TPU v7x, 32 devices: a whole 2x2x4 slice. The times are simulated.
32 devices in a mesh: clip: 2 (over y), pos: 16 (over z, x, core).
Axes of the slice: x: 2, y: 2, z: 4, core: 2. Of those that a mesh axis runs over, the one named last changes fastest.
Arguments:
- tokens: bfloat16 [128, 256, 768], P('clip', 'pos'), may hold values from -6 to 6
- clip_lengths: int32 [2, 4], P('clip'), may hold values from 1 to 32, 64 in all within a row
- timesteps: int32 [2, 4], P('clip'), may hold values from 0 to 999
- embed_first: bfloat16 [256, 768], replicated, may hold values from -0.375 to 0.375
- embed_second: bfloat16 [768, 768], replicated, may hold values from -0.21875 to 0.21875
- adaln_weight: bfloat16 [768, 6912], replicated, may hold values from -0.4375 to 0.4375
- spatial_in: bfloat16 [768, 2304], replicated, may hold values from -0.21875 to 0.21875
- spatial_out: bfloat16 [768, 768], replicated, may hold values from -0.875 to 0.875
- temporal_in: bfloat16 [768, 2304], replicated, may hold values from -0.21875 to 0.21875
- temporal_out: bfloat16 [768, 768], replicated, may hold values from -0.4375 to 0.4375
- hidden_up: bfloat16 [768, 3072], replicated, may hold values from -0.21875 to 0.21875
- hidden_down: bfloat16 [3072, 768], replicated, may hold values from -0.109375 to 0.109375
- grad_output: bfloat16 [128, 256, 768], P('clip', 'pos'), may hold values from -6 to 6
Outputs:
- block_out: bfloat16 [128, 256, 768], P('clip', 'pos')
- grad_tokens: bfloat16 [128, 256, 768], P('clip', 'pos')
- grad_embed_first: float32 [256, 768], P('pos')
- grad_embed_second: float32 [768, 768], P('pos')
- grad_adaln_weight: float32 [768, 6912], P('pos')
- grad_spatial_in: float32 [768, 2304], P('pos')
- grad_spatial_out: float32 [768, 768], P('pos')
- grad_temporal_in: float32 [768, 2304], P('pos')
- grad_temporal_out: float32 [768, 768], P('pos')
- grad_hidden_up: float32 [768, 3072], P('pos')
- grad_hidden_down: float32 [3072, 768], P('pos')
Inputs may be any that keep to these rules, and one draw needn't show every extreme that they name: `clip_lengths`: row r lists in order the frame counts of the 4 clips that fill frames r * 64 to (r + 1) * 64 - 1; every row sums to 64 and its longest clip has 32 frames. `timesteps`: one diffusion timestep index per clip, in the order of clip_lengths.
All inputs are finite; a program needn't handle non-finite values.
Results may differ from a plain program's by a relative error of at most 0.02.
Values may be sent and summed in bfloat16 or wider, within the bound.
A program may use at most 448 MiB of HBM per device.

v0:
```python
from functools import partial
import math

import jax
import jax.numpy as jnp
from jax import lax
from jax.sharding import PartitionSpec as P

HEADS = 12
HEAD_DIM = 64
FREQ = 256


epsilon = 1e-06
highest = lax.Precision.HIGHEST
masked_score = -1000000000.0


def frequency(step_ids):
    half_width = FREQ // 2
    rate_table = jnp.exp(
        -math.log(10000.0) * jnp.arange(half_width, dtype=jnp.float32) / half_width
    )
    angles = step_ids.astype(jnp.float32)[:, None] * rate_table[None, :]
    return jnp.concatenate([jnp.cos(angles), jnp.sin(angles)], axis=1)


def modulation(step_ids, first_w, second_w, adaln_w):
    hidden_cond = jax.nn.silu(
        jnp.dot(frequency(step_ids), first_w, precision=highest, preferred_element_type=jnp.float32)
    )
    cond_vec = jnp.dot(hidden_cond, second_w, precision=highest, preferred_element_type=jnp.float32)
    return jnp.dot(
        jax.nn.silu(cond_vec), adaln_w, precision=highest, preferred_element_type=jnp.float32
    )


def clip_onehot(lengths, frames):
    clip_ends = jnp.cumsum(lengths)
    frame_ids = jnp.arange(frames, dtype=jnp.int32)
    clip_ids = jnp.sum((frame_ids[:, None] >= clip_ends[None, :]).astype(jnp.int32), axis=1)
    onehot = (clip_ids[:, None] == jnp.arange(lengths.shape[0], dtype=jnp.int32)[None, :]).astype(
        jnp.float32
    )
    return (onehot, clip_ids)


def norm_mod(values, shift_vec, scale_vec):
    centre = values - jnp.mean(values, axis=-1, keepdims=True)
    spread = jnp.mean(centre * centre, axis=-1, keepdims=True)
    return centre * lax.rsqrt(spread + epsilon) * (1.0 + scale_vec) + shift_vec


def gelu_tanh(values):
    return jax.nn.gelu(values, approximate=True)


def project(normed, weight):
    frames, places, model_width = normed.shape
    joined = jnp.dot(
        normed.reshape(frames * places, model_width), weight, preferred_element_type=jnp.float32
    )
    return joined.astype(jnp.bfloat16).reshape(frames, places, 3, HEADS, HEAD_DIM)


def weight_grad(left, right):
    return jnp.einsum("rd,rk->dk", left, right, preferred_element_type=jnp.float32)


def input_grad(grad_rows, weight):
    return jnp.einsum("rk,dk->rd", grad_rows, weight, preferred_element_type=jnp.float32)


def score_block(query_heads, key_heads, factor):
    return (
        jnp.einsum("fqhd,fkhd->fhqk", query_heads, key_heads, preferred_element_type=jnp.float32)
        * factor
    )


def on_device(
    tokens,
    clip_lengths,
    timesteps,
    embed_first,
    embed_second,
    adaln_weight,
    spatial_in,
    spatial_out,
    temporal_in,
    temporal_out,
    hidden_up,
    hidden_down,
    grad_output,
):
    frames, places, model_width = tokens.shape
    row_count = frames * places
    factor = 1.0 / math.sqrt(HEAD_DIM)
    modulated, cond_pull = jax.vjp(
        partial(modulation, timesteps[0]),
        embed_first.astype(jnp.float32),
        embed_second.astype(jnp.float32),
        adaln_weight.astype(jnp.float32),
    )
    onehot, clip_ids = clip_onehot(clip_lengths[0], frames)
    per_frame = jnp.einsum(
        "fc,cm->fm", onehot, modulated, precision=highest, preferred_element_type=jnp.float32
    )
    pieces = [
        per_frame[:, None, slot_index * model_width : (slot_index + 1) * model_width]
        for slot_index in range(9)
    ]
    token_x = tokens.astype(jnp.float32)
    normed_one, norm_pull_one = jax.vjp(norm_mod, token_x, pieces[0], pieces[1])
    h_one = normed_one.astype(jnp.bfloat16)
    qkv_one = project(h_one, spatial_in)
    q_space = qkv_one[:, :, 0]
    k_local = qkv_one[:, :, 1].reshape(frames, places, model_width)
    v_local = qkv_one[:, :, 2].reshape(frames, places, model_width)
    k_all, v_all = (
        lax.all_gather(k_local, "pos", axis=1, tiled=True),
        lax.all_gather(v_local, "pos", axis=1, tiled=True),
    )
    patch_count = k_all.shape[1]
    k_heads = k_all.reshape(frames, patch_count, HEADS, HEAD_DIM)
    v_heads = v_all.reshape(frames, patch_count, HEADS, HEAD_DIM)
    space_scores = score_block(q_space, k_heads, factor)
    space_top = jnp.max(space_scores, axis=-1, keepdims=True)
    space_lse = space_top + jnp.log(
        jnp.sum(jnp.exp(space_scores - space_top), axis=-1, keepdims=True)
    )
    space_probs = jnp.exp(space_scores - space_lse).astype(jnp.bfloat16)
    o_one = jnp.einsum("fhqk,fkhd->fqhd", space_probs, v_heads, preferred_element_type=jnp.float32)
    o_one = o_one.astype(jnp.bfloat16).reshape(row_count, model_width)
    y_one = jnp.dot(o_one, spatial_out, preferred_element_type=jnp.float32).reshape(
        frames, places, model_width
    )
    x_one = token_x + pieces[2] * y_one
    normed_two, norm_pull_two = jax.vjp(norm_mod, x_one, pieces[3], pieces[4])
    h_two = normed_two.astype(jnp.bfloat16)
    qkv_two = project(h_two, temporal_in)
    q_time = qkv_two[:, :, 0]
    k_time = qkv_two[:, :, 1]
    v_time = qkv_two[:, :, 2]
    same_clip = (clip_ids[:, None] == clip_ids[None, :])[None, None]
    time_scores = (
        jnp.einsum("fphd,gphd->phfg", q_time, k_time, preferred_element_type=jnp.float32) * factor
    )
    time_scores = jnp.where(same_clip, time_scores, masked_score)
    time_top = jnp.max(time_scores, axis=-1, keepdims=True)
    time_lse = time_top + jnp.log(jnp.sum(jnp.exp(time_scores - time_top), axis=-1, keepdims=True))
    time_probs = jnp.exp(time_scores - time_lse)
    time_low = time_probs.astype(jnp.bfloat16)
    o_two = jnp.einsum("phfg,gphd->fphd", time_low, v_time, preferred_element_type=jnp.float32)
    o_two = o_two.astype(jnp.bfloat16).reshape(row_count, model_width)
    y_two = jnp.dot(o_two, temporal_out, preferred_element_type=jnp.float32).reshape(
        frames, places, model_width
    )
    x_two = x_one + pieces[5] * y_two
    normed_three, norm_pull_three = jax.vjp(norm_mod, x_two, pieces[6], pieces[7])
    h_three = normed_three.astype(jnp.bfloat16).reshape(row_count, model_width)
    upward = jnp.dot(h_three, hidden_up, preferred_element_type=jnp.float32)
    activated, gelu_pull = jax.vjp(gelu_tanh, upward)
    act_low = activated.astype(jnp.bfloat16)
    z_out = jnp.dot(act_low, hidden_down, preferred_element_type=jnp.float32).reshape(
        frames, places, model_width
    )
    block_out = (x_two + pieces[8] * z_out).astype(jnp.bfloat16)
    grad_top = grad_output.astype(jnp.float32)
    grad_gate_three = jnp.sum(grad_top * z_out, axis=1)
    grad_z = (pieces[8] * grad_top).astype(jnp.bfloat16).reshape(row_count, model_width)
    grad_hidden_down = weight_grad(act_low, grad_z)
    grad_act = input_grad(grad_z, hidden_down)
    grad_up_rows = gelu_pull(grad_act)[0].astype(jnp.bfloat16)
    grad_hidden_up = weight_grad(h_three, grad_up_rows)
    grad_h_three = input_grad(grad_up_rows, hidden_up).reshape(frames, places, model_width)
    grad_norm_three, grad_shift_three, grad_scale_three = norm_pull_three(grad_h_three)
    grad_two = grad_top + grad_norm_three
    grad_gate_two = jnp.sum(grad_two * y_two, axis=1)
    grad_y_two = (pieces[5] * grad_two).astype(jnp.bfloat16).reshape(row_count, model_width)
    grad_temporal_out = weight_grad(o_two, grad_y_two)
    grad_o_two = (
        input_grad(grad_y_two, temporal_out)
        .astype(jnp.bfloat16)
        .reshape(frames, places, HEADS, HEAD_DIM)
    )
    grad_time_probs = jnp.einsum(
        "fphd,gphd->phfg", grad_o_two, v_time, preferred_element_type=jnp.float32
    )
    time_inner = jnp.sum(grad_time_probs * time_probs, axis=-1, keepdims=True)
    grad_time_scores = (time_probs * (grad_time_probs - time_inner)).astype(jnp.bfloat16)
    grad_q_time = (
        jnp.einsum("phfg,gphd->fphd", grad_time_scores, k_time, preferred_element_type=jnp.float32)
        * factor
    )
    grad_k_time = (
        jnp.einsum("phfg,fphd->gphd", grad_time_scores, q_time, preferred_element_type=jnp.float32)
        * factor
    )
    grad_v_time = jnp.einsum(
        "phfg,fphd->gphd", time_low, grad_o_two, preferred_element_type=jnp.float32
    )
    grad_qkv_two = (
        jnp.stack([grad_q_time, grad_k_time, grad_v_time], axis=2)
        .astype(jnp.bfloat16)
        .reshape(row_count, 3 * model_width)
    )
    grad_temporal_in = weight_grad(h_two.reshape(row_count, model_width), grad_qkv_two)
    grad_h_two = input_grad(grad_qkv_two, temporal_in).reshape(frames, places, model_width)
    grad_norm_two, grad_shift_two, grad_scale_two = norm_pull_two(grad_h_two)
    grad_one = grad_two + grad_norm_two
    grad_gate_one = jnp.sum(grad_one * y_one, axis=1)
    grad_y_one = (pieces[2] * grad_one).astype(jnp.bfloat16).reshape(row_count, model_width)
    grad_spatial_out = weight_grad(o_one, grad_y_one)
    grad_o_one = (
        input_grad(grad_y_one, spatial_out)
        .astype(jnp.bfloat16)
        .reshape(frames, places, model_width)
    )
    k_back, v_back = (k_all, v_all)
    k_back_heads = k_back.reshape(frames, patch_count, HEADS, HEAD_DIM)
    v_back_heads = v_back.reshape(frames, patch_count, HEADS, HEAD_DIM)
    grad_o_heads = grad_o_one.reshape(frames, places, HEADS, HEAD_DIM)
    again_probs = jnp.exp(score_block(q_space, k_back_heads, factor) - space_lse)
    grad_space_probs = jnp.einsum(
        "fqhd,fkhd->fhqk", grad_o_heads, v_back_heads, preferred_element_type=jnp.float32
    )
    space_inner = jnp.sum(grad_space_probs * again_probs, axis=-1, keepdims=True)
    grad_space_scores = (again_probs * (grad_space_probs - space_inner)).astype(jnp.bfloat16)
    grad_q_space = (
        jnp.einsum(
            "fhqk,fkhd->fqhd", grad_space_scores, k_back_heads, preferred_element_type=jnp.float32
        )
        * factor
    )
    key_terms = (
        jnp.einsum(
            "fhqk,fqhd->fkhd", grad_space_scores, q_space, preferred_element_type=jnp.float32
        )
        * factor
    )
    value_terms = jnp.einsum(
        "fhqk,fqhd->fkhd",
        again_probs.astype(jnp.bfloat16),
        grad_o_heads,
        preferred_element_type=jnp.float32,
    )
    grad_keys, grad_values = (
        lax.psum_scatter(
            key_terms.reshape(frames, patch_count, model_width).astype(jnp.bfloat16),
            "pos",
            scatter_dimension=1,
            tiled=True,
        ).astype(jnp.float32),
        lax.psum_scatter(
            value_terms.reshape(frames, patch_count, model_width).astype(jnp.bfloat16),
            "pos",
            scatter_dimension=1,
            tiled=True,
        ).astype(jnp.float32),
    )
    grad_qkv_one = jnp.stack(
        [grad_q_space.reshape(frames, places, model_width), grad_keys, grad_values], axis=2
    )
    grad_qkv_one = grad_qkv_one.astype(jnp.bfloat16).reshape(row_count, 3 * model_width)
    grad_spatial_in = weight_grad(h_one.reshape(row_count, model_width), grad_qkv_one)
    grad_h_one = input_grad(grad_qkv_one, spatial_in).reshape(frames, places, model_width)
    grad_norm_one, grad_shift_one, grad_scale_one = norm_pull_one(grad_h_one)
    grad_tokens = (grad_one + grad_norm_one).astype(jnp.bfloat16)
    grad_frames = jnp.concatenate(
        [
            grad_shift_one[:, 0],
            grad_scale_one[:, 0],
            grad_gate_one,
            grad_shift_two[:, 0],
            grad_scale_two[:, 0],
            grad_gate_two,
            grad_shift_three[:, 0],
            grad_scale_three[:, 0],
            grad_gate_three,
        ],
        axis=1,
    )
    grad_modulation = jnp.einsum(
        "fc,fm->cm", onehot, grad_frames, precision=highest, preferred_element_type=jnp.float32
    )
    grad_embed_first, grad_embed_second, grad_adaln_weight = cond_pull(grad_modulation)
    summed = (
        lax.psum_scatter(
            grad_embed_first.astype(jnp.bfloat16), "pos", scatter_dimension=0, tiled=True
        ).astype(jnp.float32),
        lax.psum_scatter(
            grad_embed_second.astype(jnp.bfloat16), "pos", scatter_dimension=0, tiled=True
        ).astype(jnp.float32),
        lax.psum_scatter(
            grad_adaln_weight.astype(jnp.bfloat16), "pos", scatter_dimension=0, tiled=True
        ).astype(jnp.float32),
        lax.psum_scatter(
            grad_spatial_in.astype(jnp.bfloat16), "pos", scatter_dimension=0, tiled=True
        ).astype(jnp.float32),
        lax.psum_scatter(
            grad_spatial_out.astype(jnp.bfloat16), "pos", scatter_dimension=0, tiled=True
        ).astype(jnp.float32),
        lax.psum_scatter(
            grad_temporal_in.astype(jnp.bfloat16), "pos", scatter_dimension=0, tiled=True
        ).astype(jnp.float32),
        lax.psum_scatter(
            grad_temporal_out.astype(jnp.bfloat16), "pos", scatter_dimension=0, tiled=True
        ).astype(jnp.float32),
        lax.psum_scatter(
            grad_hidden_up.astype(jnp.bfloat16), "pos", scatter_dimension=0, tiled=True
        ).astype(jnp.float32),
        lax.psum_scatter(
            grad_hidden_down.astype(jnp.bfloat16), "pos", scatter_dimension=0, tiled=True
        ).astype(jnp.float32),
    )
    summed = (
        lax.psum(summed[0].astype(jnp.bfloat16), "clip").astype(jnp.float32),
        lax.psum(summed[1].astype(jnp.bfloat16), "clip").astype(jnp.float32),
        lax.psum(summed[2].astype(jnp.bfloat16), "clip").astype(jnp.float32),
        lax.psum(summed[3].astype(jnp.bfloat16), "clip").astype(jnp.float32),
        lax.psum(summed[4].astype(jnp.bfloat16), "clip").astype(jnp.float32),
        lax.psum(summed[5].astype(jnp.bfloat16), "clip").astype(jnp.float32),
        lax.psum(summed[6].astype(jnp.bfloat16), "clip").astype(jnp.float32),
        lax.psum(summed[7].astype(jnp.bfloat16), "clip").astype(jnp.float32),
        lax.psum(summed[8].astype(jnp.bfloat16), "clip").astype(jnp.float32),
    )
    return (
        block_out,
        grad_tokens,
        summed[0],
        summed[1],
        summed[2],
        summed[3],
        summed[4],
        summed[5],
        summed[6],
        summed[7],
        summed[8],
    )


def solution(mesh):
    in_specs = (
        P("clip", "pos", None),
        P("clip", None),
        P("clip", None),
        P(),
        P(),
        P(),
        P(),
        P(),
        P(),
        P(),
        P(),
        P(),
        P("clip", "pos", None),
    )
    out_specs = (
        P("clip", "pos", None),
        P("clip", "pos", None),
        P("pos", None),
        P("pos", None),
        P("pos", None),
        P("pos", None),
        P("pos", None),
        P("pos", None),
        P("pos", None),
        P("pos", None),
        P("pos", None),
    )
    return jax.shard_map(
        on_device, mesh=mesh, in_specs=in_specs, out_specs=out_specs, check_vma=False
    )
```

profile of v0, /device:TPU:0, one launch (start us, length us, event | category | flops | bytes accessed | tf_op | source)
XLA Modules:
  0.0 1902.6 jit_solution(2923653464098898793)
XLA Ops:
  31.7 15.0 reshape.275
  68.8 124.6 %all-gather.5.cloned.1.call-done = bf16[64,256,768]{2,1,0:T(8,128)(2,1)} async-done(((bf16[64,16,768]{2,1,0:T(8,128)(2,1)}), bf16[64,256,768]{2,1,0:T(8,128)(2,1)}) %all-gather.5.cloned.1.call-update) | async-done | bytes 25165840 | tf_op jit(solution)/shard_map/all_gather | solution.py:121
  193.5 30.7 %copy.79 = bf16[64,256,768]{1,2,0:T(8,128)(2,1)} copy(bf16[64,256,768]{2,1,0:T(8,128)(2,1)} %all-gather.5.cloned.1.call-done) | data formatting | bytes 50331648 | tf_op jit(solution)/shard_map/all_gather | solution.py:121
  224.2 18.9 multiply_reduce_fusion.1
  252.7 71.5 %all-gather.3.cloned.1.call-done = bf16[64,256,768]{2,1,0:T(8,128)(2,1)} async-done(((bf16[64,16,768]{2,1,0:T(8,128)(2,1)}), bf16[64,256,768]{2,1,0:T(8,128)(2,1)}) %all-gather.3.cloned.1.call-update) | async-done | bytes 25165840 | tf_op jit(solution)/shard_map/all_gather | solution.py:122
  324.1 31.5 %copy.77 = bf16[64,256,768]{1,2,0:T(8,128)(2,1)} copy(bf16[64,256,768]{2,1,0:T(8,128)(2,1)} %all-gather.3.cloned.1.call-done) | data formatting | bytes 50331648 | tf_op jit(solution)/shard_map/all_gather | solution.py:122
  355.6 16.2 convert_bitcast_fusion
  397.0 15.0 reshape.279
  471.7 16.5 fusion.6
  565.3 12.3 copy.97
  577.6 15.8 convert_element_type.240
  616.8 17.5 convolution_convert_fusion
  634.3 32.6 %copy.102 = bf16[64,256,768]{2,1,0:T(8,128)(2,1)} copy(bf16[64,256,768]{1,2,0:T(8,128)(2,1)} %bitcast.161) | data formatting | bytes 50331648 | tf_op jit(solution)/shard_map/convert_element_type | solution.py:256
  667.0 26.9 %multiply_reduce_fusion = (f32[64,12,16]{2,1,0:T(8,128)S(1)}, f32[64,12,16,256]{3,2,1,0:T(8,128)}) fusion(f32[64,12,16,256]{3,2,1,0:T(8,128)} %get-tuple-element.58, f32[64,12,16]{2,1,0:T(8,128)S(1)} %copy-done.14, bf16[64,256,12,64]{1,3,2,0:T(8,128)(2,1)} %bitcast.156, bf16[64,16,12,64]{3,2,1,0:T(8,128)(2,1)} %reshape_reshape.3), kind=kOutput, calls=%fused_computation.13 | convolution fusion | flops 415223808 | bytes 52002816 | tf_op jit(solution)/shard_map/fqhd,fkhd->fhqk/dot_general | solution.py:225
  693.9 12.4 multiply_convert_fusion.1
  706.3 14.0 multiply_convert_fusion
  720.3 30.1 %copy.100 = bf16[64,256,768]{2,1,0:T(8,128)(2,1)} copy(bf16[64,256,768]{1,2,0:T(8,128)(2,1)} %bitcast.162) | data formatting | bytes 50331648 | tf_op jit(solution)/shard_map/convert_element_type | solution.py:250
  774.2 16.0 convert_element_type.264
  799.3 11.6 convolution_convert_fusion.4
  821.9 13.6 multiply_bitcast_fusion
  843.8 66.5 %reduce-scatter.14.cloned.1.call-done = bf16[64,16,768]{2,1,0:T(8,128)(2,1)} async-done(((bf16[64,256,768]{2,1,0:T(8,128)(2,1)}), bf16[64,16,768]{2,1,0:T(8,128)(2,1)}) %reduce-scatter.14.cloned.1.call-update) | async-done | bytes 1572880 | tf_op jit(solution)/shard_map/reduce_scatter | solution.py:255
  910.4 246.4 %reduce-scatter.12.cloned.1.call-done = bf16[64,16,768]{2,1,0:T(8,128)(2,1)} async-done(((bf16[64,256,768]{2,1,0:T(8,128)(2,1)}), bf16[64,16,768]{2,1,0:T(8,128)(2,1)}) %reduce-scatter.12.cloned.1.call-update) | async-done | bytes 1572880 | tf_op jit(solution)/shard_map/reduce_scatter | solution.py:249
  1198.6 19.3 %convolution_convert_fusion.1 = bf16[768,6912]{1,0:T(8,128)(2,1)} fusion(f32[4,6912]{1,0:T(4,128)S(1)} %fusion.48, f32[4,768]{1,0:T(4,128)S(1)} %copy-done.71), kind=kOutput, calls=%fused_computation.17 | convolution fusion | flops 260124672 | bytes 10739712 | tf_op jit(solution)/shard_map/transpose(jvp())/dot_general | solution.py:33
  1221.9 56.2 %reduce-scatter.24.cloned.1.call-done = bf16[48,768]{1,0:T(8,128)(2,1)} async-done(((bf16[768,768]{1,0:T(8,128)(2,1)}), bf16[48,768]{1,0:T(8,128)(2,1)}) %reduce-scatter.24.cloned.1.call-update) | async-done | bytes 73744 | tf_op jit(solution)/shard_map/reduce_scatter | solution.py:301
  1278.2 71.0 %reduce-scatter.26.cloned.1.call-done = bf16[48,2304]{1,0:T(8,128)(2,1)} async-done(((bf16[768,2304]{1,0:T(8,128)(2,1)}), bf16[48,2304]{1,0:T(8,128)(2,1)}) %reduce-scatter.26.cloned.1.call-update) | async-done | bytes 221200 | tf_op jit(solution)/shard_map/reduce_scatter | solution.py:304
  1349.2 78.5 %reduce-scatter.32.cloned.1.call-done = bf16[192,768]{1,0:T(8,128)(2,1)} async-done(((bf16[3072,768]{1,0:T(8,128)(2,1)}), bf16[192,768]{1,0:T(8,128)(2,1)}) %reduce-scatter.32.cloned.1.call-update) | async-done | bytes 294928 | tf_op jit(solution)/shard_map/reduce_scatter | solution.py:313
  1427.7 78.6 %reduce-scatter.30.cloned.1.call-done = bf16[48,3072]{1,0:T(8,128)(2,1)} async-done(((bf16[768,3072]{1,0:T(8,128)(2,1)}), bf16[48,3072]{1,0:T(8,128)(2,1)}) %reduce-scatter.30.cloned.1.call-update) | async-done | bytes 294928 | tf_op jit(solution)/shard_map/reduce_scatter | solution.py:310
  1506.3 61.5 %reduce-scatter.18.cloned.1.call-done = bf16[48,768]{1,0:T(8,128)(2,1)} async-done(((bf16[768,768]{1,0:T(8,128)(2,1)}), bf16[48,768]{1,0:T(8,128)(2,1)}) %reduce-scatter.18.cloned.1.call-update) | async-done | bytes 73744 | tf_op jit(solution)/shard_map/reduce_scatter | solution.py:292
  1567.8 71.0 %reduce-scatter.22.cloned.1.call-done = bf16[48,2304]{1,0:T(8,128)(2,1)} async-done(((bf16[768,2304]{1,0:T(8,128)(2,1)}), bf16[48,2304]{1,0:T(8,128)(2,1)}) %reduce-scatter.22.cloned.1.call-update) | async-done | bytes 221200 | tf_op jit(solution)/shard_map/reduce_scatter | solution.py:298
  1638.8 123.6 %reduce-scatter.20.cloned.1.call-done = bf16[48,6912]{1,0:T(8,128)(2,1)} async-done(((bf16[768,6912]{1,0:T(8,128)(2,1)}), bf16[48,6912]{1,0:T(8,128)(2,1)}) %reduce-scatter.20.cloned.1.call-update) | async-done | bytes 663568 | tf_op jit(solution)/shard_map/reduce_scatter | solution.py:295
  1767.5 54.7 %reduce-scatter.16.cloned.1.call-done = bf16[16,768]{1,0:T(8,128)(2,1)} async-done(((bf16[256,768]{1,0:T(8,128)(2,1)}), bf16[16,768]{1,0:T(8,128)(2,1)}) %reduce-scatter.16.cloned.1.call-update) | async-done | bytes 24592 | tf_op jit(solution)/shard_map/reduce_scatter | solution.py:289
  1833.0 49.9 %all-reduce.3.cloned.1.call-done = (bf16[48,768]{1,0:T(8,128)(2,1)}, bf16[48,6912]{1,0:T(8,128)(2,1)}, bf16[48,2304]{1,0:T(8,128)(2,1)}, bf16[48,768]{1,0:T(8,12...) async-done(((bf16[48,768]{1,0:T(8,128)(2,1)}, bf16[48,6912]{1,0:T(8,128)(2,1)}, ...) | async-done | bytes 1916944 | tf_op jit(solution)/shard_map/psum | solution.py:319
  (342 shorter events, 367.2 us)
Async XLA Ops:
  7.2 384.4 %copy-start = (bf16[768,2304]{1,0:T(8,128)(2,1)S(1)}, bf16[768,2304]{1,0:T(8,128)(2,1)}, u32[]{:S(2)}) copy-start(bf16[768,2304]{1,0:T(8,128)(2,1)} %param.21) | copy-start | bytes 10616836
  7.2 186.3 %all-gather.5.cloned.1.call-start = ((), (), s32[]{:S(2)}) async-start(), calls=%async_computation.12 | async-start | bytes 26738688 | tf_op jit(solution)/shard_map/all_gather | solution.py:121
  8.3 60.4 %copy-start.87 = (s32[64]{0:T(128)}, s32[64]{0:T(128)S(1)}, u32[]{:S(2)}) copy-start(s32[64]{0:T(128)S(1)} %convert_reduce_fusion.1) | copy-start | bytes 772
  10.8 12.2 copy-start.54
  12.8 10.2 copy-start.66
  62.0 262.1 %all-gather.3.cloned.1.call-start = ((), (), s32[]{:S(2)}) async-start(), calls=%async_computation.11 | async-start | bytes 26738688 | tf_op jit(solution)/shard_map/all_gather | solution.py:122
  68.2 842.2 %reduce-scatter.14.cloned.1.call-start = ((), (), s32[]{:S(2)}) async-start(), calls=%async_computation.14 | async-start | bytes 26738688 | tf_op jit(solution)/shard_map/reduce_scatter | solution.py:255
  243.1 8.7 copy-start.25
  454.8 9.5 slice-start.5
  471.7 28.3 %copy-start.19 = (f32[1024,768]{1,0:T(8,128)}, f32[1024,768]{1,0:T(8,128)S(1)}, u32[]{:S(2)}) copy-start(f32[1024,768]{1,0:T(8,128)S(1)} %fusion.86) | copy-start | bytes 9437188
  525.6 15.5 slice-start
  593.5 10.5 copy-start.20
  593.5 10.5 copy-start.21
  593.5 10.5 copy-start.22
  666.9 489.8 %reduce-scatter.12.cloned.1.call-start = ((), (), s32[]{:S(2)}) async-start(), calls=%async_computation.13 | async-start | bytes 26738688 | tf_op jit(solution)/shard_map/reduce_scatter | solution.py:249
  706.3 14.0 copy-start.5
  750.4 471.5 %reduce-scatter.28.cloned.1.call-start = ((), (), s32[]{:S(2)}) async-start(), calls=%async_computation.21 | async-start | bytes 1253376 | tf_op jit(solution)/shard_map/reduce_scatter | solution.py:307
  766.2 512.0 %reduce-scatter.24.cloned.1.call-start = ((), (), s32[]{:S(2)}) async-start(), calls=%async_computation.19 | async-start | bytes 1253376 | tf_op jit(solution)/shard_map/reduce_scatter | solution.py:301
  774.1 16.0 copy-start.43
  774.1 575.1 %reduce-scatter.26.cloned.1.call-start = ((), (), s32[]{:S(2)}) async-start(), calls=%async_computation.20 | async-start | bytes 3760128 | tf_op jit(solution)/shard_map/reduce_scatter | solution.py:304
  797.9 629.7 %reduce-scatter.32.cloned.1.call-start = ((), (), s32[]{:S(2)}) async-start(), calls=%async_computation.23 | async-start | bytes 5013504 | tf_op jit(solution)/shard_map/reduce_scatter | solution.py:313
  810.9 695.4 %reduce-scatter.30.cloned.1.call-start = ((), (), s32[]{:S(2)}) async-start(), calls=%async_computation.22 | async-start | bytes 5013504 | tf_op jit(solution)/shard_map/reduce_scatter | solution.py:310
  821.9 745.9 %reduce-scatter.18.cloned.1.call-start = ((), (), s32[]{:S(2)}) async-start(), calls=%async_computation.16 | async-start | bytes 1253376 | tf_op jit(solution)/shard_map/reduce_scatter | solution.py:292
  1159.2 10.5 slice-start.2
  1169.7 8.3 copy-start.71
  1181.2 457.6 %reduce-scatter.22.cloned.1.call-start = ((), (), s32[]{:S(2)}) async-start(), calls=%async_computation.18 | async-start | bytes 3760128 | tf_op jit(solution)/shard_map/reduce_scatter | solution.py:298
  1198.6 563.8 %reduce-scatter.20.cloned.1.call-start = ((), (), s32[]{:S(2)}) async-start(), calls=%async_computation.17 | async-start | bytes 11280384 | tf_op jit(solution)/shard_map/reduce_scatter | solution.py:295
  1217.9 544.5 %copy-start.82 = (f32[64,16]{1,0:T(8,128)S(1)}, f32[64,16]{1,0:T(8,128)}, u32[]{:S(2)}) copy-start(f32[64,16]{1,0:T(8,128)} %get-tuple-element.14) | copy-start | bytes 12292
  1218.0 604.2 %reduce-scatter.16.cloned.1.call-start = ((), (), s32[]{:S(2)}) async-start(), calls=%async_computation.15 | async-start | bytes 417792 | tf_op jit(solution)/shard_map/reduce_scatter | solution.py:289
  1221.9 661.0 %all-reduce.3.cloned.1.call-start = ((), (), s32[]{:S(2)}) async-start(), calls=%async_computation.24 | async-start | bytes 3833856 | tf_op jit(solution)/shard_map/psum | solution.py:319
  1762.5 133.4 %copy-start.1 = (bf16[768,2304]{1,0:T(8,128)(2,1)S(1)}, bf16[768,2304]{1,0:T(8,128)(2,1)}, u32[]{:S(2)}) copy-start(bf16[768,2304]{1,0:T(8,128)(2,1)} %param.21) | copy-start | bytes 10616836
  1882.9 11.8 copy-start.65
  (81 other events, 311.8 us)
Sparse Core Ops, SparseCore 0:
  62.2 131.2 all-gather.4
  195.6 128.5 all-gather.2
  667.1 243.2 reduce-scatter.13
  914.3 242.3 reduce-scatter.11
  1160.2 57.2 reduce-scatter.27
  1221.0 57.1 reduce-scatter.23
  1282.1 67.1 reduce-scatter.25
  1353.1 74.5 reduce-scatter.31
  1431.5 74.7 reduce-scatter.29
  1510.3 57.4 reduce-scatter.17
  1571.7 67.1 reduce-scatter.21
  1642.7 119.6 reduce-scatter.19
  1766.5 55.6 reduce-scatter.15
  1824.7 58.1 all-reduce.2
where the time goes:
time: 1920 us; the launch traced here: 1900 us
  waiting for transfers between devices  1150 us (60%)
  local copies, waits for them, and re-layouts  321 us (17%)
  matrix products  304 us (16%)
  other arithmetic  97.4 us (5%)
    reduce_scatter x1, waiting for transfers between devices, on_device(): lax.psum_scatter(key_terms.reshape(frames, patch_count, model_width).asty...  246 us
    all_gather x1, waiting for transfers between devices, on_device(): lax.all_gather(k_local, 'pos', axis=1, tiled=True)  125 us
    reduce_scatter x1, waiting for transfers between devices, on_device(): lax.psum_scatter(grad_adaln_weight.astype(jnp.bfloat16), 'pos', scatter_d...  124 us
    reduce_scatter x1, waiting for transfers between devices, on_device(): lax.psum_scatter(grad_hidden_up.astype(jnp.bfloat16), 'pos', scatter_dime...  78.6 us
    reduce_scatter x1, waiting for transfers between devices, on_device(): lax.psum_scatter(grad_hidden_down.astype(jnp.bfloat16), 'pos', scatter_di...  78.5 us
    all_gather x1, waiting for transfers between devices, on_device(): lax.all_gather(v_local, 'pos', axis=1, tiled=True)  71.5 us
    reduce_scatter x1, waiting for transfers between devices, on_device(): lax.psum_scatter(grad_spatial_in.astype(jnp.bfloat16), 'pos', scatter_dim...  71 us
    reduce_scatter x1, waiting for transfers between devices, on_device(): lax.psum_scatter(grad_temporal_in.astype(jnp.bfloat16), 'pos', scatter_di...  71 us
  transfers between devices with their start and end apart: 14, of which 13 were waited for; matrix products, arithmetic and copies ran while one was open for 16% of the time, Pallas kernels for 0%

commit v1 on v0

v1 whole, which is shorter than its diff:
```python
from functools import partial
import math

import jax
import jax.numpy as jnp
from jax import lax
from jax.experimental import pallas as pl
from jax.experimental.pallas import tpu as pltpu
from jax.sharding import PartitionSpec as P

HEADS = 12
HEAD_DIM = 64
FREQ = 256

epsilon = 1e-06
highest = lax.Precision.HIGHEST
masked_score = -1000000000.0
f32 = jnp.float32
bf16 = jnp.bfloat16


def frequency(step_ids):
    half_width = FREQ // 2
    rate_table = jnp.exp(
        -math.log(10000.0) * jnp.arange(half_width, dtype=jnp.float32) / half_width
    )
    angles = step_ids.astype(jnp.float32)[:, None] * rate_table[None, :]
    return jnp.concatenate([jnp.cos(angles), jnp.sin(angles)], axis=1)


def dot_high(left, right):
    return jnp.dot(left, right, precision=highest, preferred_element_type=f32)


def silu_grad(values):
    gate = jax.nn.sigmoid(values)
    return gate * (1.0 + values * (1.0 - gate))


def clip_onehot(lengths, frames):
    clip_ends = jnp.cumsum(lengths)
    frame_ids = jnp.arange(frames, dtype=jnp.int32)
    clip_ids = jnp.sum((frame_ids[:, None] >= clip_ends[None, :]).astype(jnp.int32), axis=1)
    onehot = (clip_ids[:, None] == jnp.arange(lengths.shape[0], dtype=jnp.int32)[None, :]).astype(
        jnp.float32
    )
    return (onehot, clip_ids)


def weight_grad(left, right):
    return jnp.einsum("rd,rk->dk", left, right, preferred_element_type=f32).astype(bf16)


def bdot(left, right):
    return lax.dot_general(left, right, (((1,), (0,)), ((), ())), preferred_element_type=f32)


def bdot_nt(left, right):
    return lax.dot_general(left, right, (((1,), (1,)), ((), ())), preferred_element_type=f32)


def bdot_tn(left, right):
    return lax.dot_general(left, right, (((0,), (0,)), ((), ())), preferred_element_type=f32)


def norm_rows(values):
    width = values.shape[-1]
    centre = values - jnp.sum(values, axis=-1, keepdims=True) * (1.0 / width)
    spread = jnp.sum(centre * centre, axis=-1, keepdims=True) * (1.0 / width)
    inverse = lax.rsqrt(spread + epsilon)
    return centre * inverse, inverse


def norm_rows_back(normed, inverse, scale_vec, grad):
    width = grad.shape[-1]
    inner = grad * (1.0 + scale_vec)
    mean_one = jnp.sum(inner, axis=-1, keepdims=True) * (1.0 / width)
    mean_two = jnp.sum(inner * normed, axis=-1, keepdims=True) * (1.0 / width)
    return inverse * (inner - mean_one - normed * mean_two)


def pair_masks(scale):
    lanes = lax.broadcasted_iota(jnp.int32, (1, 2 * HEAD_DIM), 1)
    low_half = jnp.where(lanes < HEAD_DIM, scale, 0.0).astype(bf16)
    high_half = jnp.where(lanes < HEAD_DIM, 0.0, scale).astype(bf16)
    return low_half, high_half


ROWS = 32


def load_rows(ref, step):
    places, width = ref.shape[2:]
    count = max(1, ROWS // places)
    part = ref[pl.ds(step * count, count), 0].astype(f32)
    return part.reshape(count * places, width)


def store_rows(ref, step, values):
    places, width = ref.shape[2:]
    count = max(1, ROWS // places)
    ref[pl.ds(step * count, count), 0] = values.reshape(count, places, width).astype(bf16)


def space_forward(x_ref, mod_ref, w_ref, h_ref, qkv_ref, o_ref, lse_ref):
    patches, width = h_ref.shape[1:]
    places = x_ref.shape[2]
    pair = 2 * HEAD_DIM
    shift, scale = mod_ref[0, 0:1, :], mod_ref[0, 1:2, :]

    def norm_step(step, _):
        normed, _inverse = norm_rows(load_rows(x_ref, step))
        h_ref[0, pl.ds(step * ROWS, ROWS), :] = (normed * (1.0 + scale) + shift).astype(bf16)
        return 0

    lax.fori_loop(0, patches // ROWS, norm_step, 0)
    for part in range(3):
        cols = slice(part * width, (part + 1) * width)
        qkv_ref[0, :, cols] = bdot(h_ref[0], w_ref[:, cols]).astype(bf16)
    masks = pair_masks(1.0 / math.sqrt(HEAD_DIM))
    lane_ids = lax.broadcasted_iota(jnp.int32, (1, pair), 1)
    lse_ref[0] = jnp.zeros((patches, pair), f32)

    def head_pair(index, _):
        at = pl.multiple_of(index * pair, pair)
        q = qkv_ref[0, :, pl.ds(at, pair)]
        k = qkv_ref[0, :, pl.ds(pl.multiple_of(width + at, pair), pair)]
        v = qkv_ref[0, :, pl.ds(pl.multiple_of(2 * width + at, pair), pair)]
        outs = []
        lse = lse_ref[0]
        for half in range(2):
            scores = bdot_nt(q * masks[half], k)
            top = jnp.max(scores, axis=-1, keepdims=True)
            exps = jnp.exp(scores - top)
            total = jnp.sum(exps, axis=-1, keepdims=True)
            probs = (exps * (1.0 / total)).astype(bf16)
            outs.append(bdot(probs, v))
            lse = jnp.where(lane_ids == 2 * index + half, top + jnp.log(total), lse)
        lse_ref[0] = lse
        both = jnp.where(lane_ids < HEAD_DIM, outs[0], outs[1])
        o_ref[:, 0, :, pl.ds(at, pair)] = both.reshape(patches // places, places, pair).astype(bf16)
        return 0

    lax.fori_loop(0, HEADS // 2, head_pair, 0)


def space_backward(
    go_ref, qkv_ref, lse_ref, x_ref, mod_ref, w_ref, dqkv_ref, dv_ref, sum_ref, e_ref
):
    patches = qkv_ref.shape[1]
    width = x_ref.shape[3]
    places = x_ref.shape[2]
    pair = 2 * HEAD_DIM
    scale = mod_ref[0, 1:2, :]
    factor = 1.0 / math.sqrt(HEAD_DIM)
    masks_q = pair_masks(factor)
    masks = pair_masks(1.0)
    lane_ids = lax.broadcasted_iota(jnp.int32, (1, pair), 1)

    def head_pair(index, _):
        at = pl.multiple_of(index * pair, pair)
        k_at = pl.multiple_of(width + at, pair)
        v_at = pl.multiple_of(2 * width + at, pair)
        q = qkv_ref[0, :, pl.ds(at, pair)]
        k = qkv_ref[0, :, pl.ds(k_at, pair)]
        v = qkv_ref[0, :, pl.ds(v_at, pair)]
        go = go_ref[:, 0, :, pl.ds(at, pair)].astype(f32).reshape(patches, pair).astype(bf16)
        lse_all = lse_ref[0]
        gq, gk, gv = None, None, None
        for half in range(2):
            lse = jnp.sum(
                jnp.where(lane_ids == 2 * index + half, lse_all, 0.0), axis=-1, keepdims=True
            )
            q_half = q * masks_q[half]
            go_half = go * masks[half]
            probs = jnp.exp(bdot_nt(q_half, k) - lse)
            grad_p = bdot_nt(go_half, v)
            inner = jnp.sum(grad_p * probs, axis=-1, keepdims=True)
            grad_s = (probs * (grad_p - inner)).astype(bf16)
            part_q = bdot(grad_s, k * masks_q[half])
            part_k = bdot_tn(grad_s, q_half)
            part_v = bdot_tn(probs.astype(bf16), go_half)
            gq = part_q if gq is None else gq + part_q
            gk = part_k if gk is None else gk + part_k
            gv = part_v if gv is None else gv + part_v
        dqkv_ref[0, :, pl.ds(at, pair)] = gq.astype(bf16)
        dqkv_ref[0, :, pl.ds(k_at, pair)] = gk.astype(bf16)
        dqkv_ref[0, :, pl.ds(v_at, pair)] = gv.astype(bf16)
        return 0

    lax.fori_loop(0, HEADS // 2, head_pair, 0)
    e_ref[...] = bdot_nt(dqkv_ref[0], w_ref[...])

    def norm_step(step, sums):
        grad = e_ref[pl.ds(step * ROWS, ROWS), :]
        normed, inverse = norm_rows(load_rows(x_ref, step))
        store_rows(dv_ref, step, norm_rows_back(normed, inverse, scale, grad))
        folded = grad.reshape(ROWS // 8, 8, width).sum(axis=0)
        folded_n = (grad * normed).reshape(ROWS // 8, 8, width).sum(axis=0)
        return sums[0] + folded, sums[1] + folded_n

    zero = jnp.zeros((8, width), f32)
    shift_sum, scale_sum = lax.fori_loop(0, patches // ROWS, norm_step, (zero, zero))
    sum_ref[0, 0:1, :] = jnp.sum(shift_sum, axis=0, keepdims=True)
    sum_ref[0, 1:2, :] = jnp.sum(scale_sum, axis=0, keepdims=True)


GELU_C = math.sqrt(2.0 / math.pi)


def middle(
    o1_ref, x_ref, g_ref, mod_ref, clip_ref, wso_ref, wti_ref, wto_ref, wup_ref, wdn_ref,
    out_ref, act_ref, dz_ref, h3_ref, du_ref, o2_ref, dy2_ref, h2_ref, dqkv_ref, dy1_ref, do1_ref,
    dx1_ref, sum_ref,
    qkv_ref, p_ref, y1_ref, y2_ref, n2_ref, n3_ref, r2_ref, r3_ref, xa_ref, gp_ref, e_ref,
):
    count, frames, width = x_ref.shape
    rows = count * frames
    pair = 2 * HEAD_DIM
    hidden = act_ref.shape[1]
    factor = 1.0 / math.sqrt(HEAD_DIM)
    per = frames // ROWS
    steps = rows // ROWS

    @pl.when(pl.program_id(0) == 0)
    def _():
        sum_ref[...] = jnp.zeros_like(sum_ref)

    def at_rows(step):
        return step // per, pl.ds(lax.rem(step, per) * ROWS, ROWS), pl.ds(step * ROWS, ROWS)

    def mod(index, part):
        return mod_ref[index, part, :]

    y1_ref[...] = bdot(o1_ref[...].reshape(rows, width), wso_ref[...])

    def step_one(step, _):
        place, part, flat = at_rows(step)
        x_one = x_ref[place, part, :].astype(f32) + mod(2, part) * y1_ref[flat, :]
        xa_ref[flat, :] = x_one
        normed, inverse = norm_rows(x_one)
        n2_ref[flat, :] = normed
        r2_ref[flat, :] = jnp.broadcast_to(inverse, (ROWS, pair))
        h2_ref[flat, :] = (normed * (1.0 + mod(4, part)) + mod(3, part)).astype(bf16)
        return 0

    lax.fori_loop(0, steps, step_one, 0)
    for third in range(3):
        cols = slice(third * width, (third + 1) * width)
        qkv_ref[:, cols] = bdot(h2_ref[...], wti_ref[:, cols]).astype(bf16)

    masks = pair_masks(1.0)
    masks_q = pair_masks(factor)
    lane_ids = lax.broadcasted_iota(jnp.int32, (1, pair), 1)
    is_low = lane_ids < HEAD_DIM
    allowed = clip_ref[...] > 0.5

    def halves(values, reduce, neutral):
        low_part = reduce(jnp.where(is_low, values, neutral), axis=-1, keepdims=True)
        high_part = reduce(jnp.where(is_low, neutral, values), axis=-1, keepdims=True)
        return jnp.where(is_low, low_part, high_part)

    def stacked(values, pair_of_masks):
        return jnp.concatenate([values * pair_of_masks[0], values * pair_of_masks[1]], axis=0)

    def pair_at(index):
        at = pl.multiple_of(index * pair, pair)
        return (
            pl.ds(at, pair),
            pl.ds(pl.multiple_of(width + at, pair), pair),
            pl.ds(pl.multiple_of(2 * width + at, pair), pair),
        )

    def time_pair(index, _):
        q_at, k_at, v_at = pair_at(index)
        for place in range(count):
            part = slice(place * frames, (place + 1) * frames)
            q = qkv_ref[part, q_at]
            keys = stacked(qkv_ref[part, k_at], masks_q)
            values = stacked(qkv_ref[part, v_at], masks)
            scores = jnp.where(allowed, bdot_nt(q, keys), masked_score)
            exps = jnp.exp(scores - halves(scores, jnp.max, -jnp.inf))
            probs = exps / halves(exps, jnp.sum, 0.0)
            p_ref[index, part, :] = probs
            o2_ref[part, q_at] = bdot(probs.astype(bf16), values).astype(bf16)
        return 0

    lax.fori_loop(0, HEADS // 2, time_pair, 0)

    y2_ref[...] = bdot(o2_ref[...], wto_ref[...])

    def step_two(step, _):
        place, part, flat = at_rows(step)
        x_two = xa_ref[flat, :] + mod(5, part) * y2_ref[flat, :]
        xa_ref[flat, :] = x_two
        normed, inverse = norm_rows(x_two)
        n3_ref[flat, :] = normed
        r3_ref[flat, :] = jnp.broadcast_to(inverse, (ROWS, pair))
        h3_ref[flat, :] = (normed * (1.0 + mod(7, part)) + mod(6, part)).astype(bf16)
        dz_ref[flat, :] = (mod(8, part) * g_ref[place, part, :].astype(f32)).astype(bf16)
        return 0

    lax.fori_loop(0, steps, step_two, 0)

    tile = 256

    def up_tile(index, _):
        cols = pl.ds(pl.multiple_of(index * tile, tile), tile)
        u = bdot(h3_ref[...], wup_ref[:, cols])
        square = u * u
        tanh = jnp.tanh(GELU_C * (u * (1.0 + 0.044715 * square)))
        half = 0.5 * (1.0 + tanh)
        act_ref[:, cols] = (u * half).astype(bf16)
        slope = half + (0.5 * GELU_C) * u * (1.0 - tanh * tanh) * (1.0 + (3.0 * 0.044715) * square)
        du = bdot_nt(dz_ref[...], wdn_ref[cols, :]) * slope
        du_ref[:, cols] = du.astype(bf16)
        return 0

    lax.fori_loop(0, hidden // tile, up_tile, 0)
    e_ref[...] = bdot(act_ref[...], wdn_ref[...])

    def step_three(step, _):
        place, part, flat = at_rows(step)
        z = e_ref[flat, :]
        grad = g_ref[place, part, :].astype(f32)
        out_ref[place, part, :] = (xa_ref[flat, :] + mod(8, part) * z).astype(bf16)
        sum_ref[6, part, :] += grad * z
        return 0

    lax.fori_loop(0, steps, step_three, 0)
    e_ref[...] = bdot_nt(du_ref[...], wup_ref[...])

    def step_four(step, _):
        place, part, flat = at_rows(step)
        grad = e_ref[flat, :]
        normed = n3_ref[flat, :]
        sum_ref[4, part, :] += grad
        sum_ref[5, part, :] += grad * normed
        back = norm_rows_back(normed, r3_ref[flat, 0:1], mod(7, part), grad)
        grad_two = g_ref[place, part, :].astype(f32) + back
        xa_ref[flat, :] = grad_two
        sum_ref[3, part, :] += grad_two * y2_ref[flat, :]
        dy2_ref[flat, :] = (mod(5, part) * grad_two).astype(bf16)
        return 0

    lax.fori_loop(0, steps, step_four, 0)
    y2_ref[...] = bdot_nt(dy2_ref[...], wto_ref[...])

    def time_pair_back(index, _):
        q_at, k_at, v_at = pair_at(index)
        for place in range(count):
            part = slice(place * frames, (place + 1) * frames)
            go = y2_ref[part, q_at].astype(bf16)
            q = qkv_ref[part, q_at] * factor
            keys = stacked(qkv_ref[part, k_at], masks_q)
            values = stacked(qkv_ref[part, v_at], masks)
            probs = p_ref[index, part, :]
            grad_p = bdot_nt(go, values)
            inner = halves(grad_p * probs, jnp.sum, 0.0)
            grad_s = (probs * (grad_p - inner)).astype(bf16)
            dqkv_ref[part, q_at] = bdot(grad_s, keys).astype(bf16)
            grad_k = bdot_tn(grad_s, q)
            grad_v = bdot_tn(probs.astype(bf16), go)
            dqkv_ref[part, k_at] = jnp.where(is_low, grad_k[:frames], grad_k[frames:]).astype(bf16)
            dqkv_ref[part, v_at] = jnp.where(is_low, grad_v[:frames], grad_v[frames:]).astype(bf16)
        return 0

    lax.fori_loop(0, HEADS // 2, time_pair_back, 0)
    e_ref[...] = bdot_nt(dqkv_ref[...], wti_ref[...])

    def step_five(step, _):
        place, part, flat = at_rows(step)
        grad = e_ref[flat, :]
        normed = n2_ref[flat, :]
        sum_ref[1, part, :] += grad
        sum_ref[2, part, :] += grad * normed
        grad_one = xa_ref[flat, :] + norm_rows_back(normed, r2_ref[flat, 0:1], mod(4, part), grad)
        dx1_ref[place, part, :] = grad_one
        sum_ref[0, part, :] += grad_one * y1_ref[flat, :]
        dy1_ref[flat, :] = (mod(2, part) * grad_one).astype(bf16)
        return 0

    lax.fori_loop(0, steps, step_five, 0)
    do1_ref[...] = bdot_nt(dy1_ref[...], wso_ref[...]).astype(bf16).reshape(count, frames, width)


VMEM_LIMIT = 62 * 1024 * 1024


def resident(shape):
    return pl.BlockSpec(shape, lambda i: (0,) * len(shape), pipeline_mode=pl.Buffered(1))


def call_space_forward(x, mods, weight):
    n_pos, own, places, width = x.shape
    patches = n_pos * places
    pair = 2 * HEAD_DIM
    spread = pl.BlockSpec((n_pos, 1, places, width), lambda i: (0, i, 0, 0))

    def by_frame(*shape):
        return pl.BlockSpec((1,) + shape, lambda i: (i, 0, 0))

    rows = own * patches
    return pl.pallas_call(
        space_forward,
        grid=(own,),
        in_specs=[spread, by_frame(2, width), resident(weight.shape)],
        out_specs=[
            by_frame(patches, width),
            by_frame(patches, 3 * width),
            spread,
            by_frame(patches, pair),
        ],
        out_shape=[
            jax.ShapeDtypeStruct((own, patches, width), bf16),
            jax.ShapeDtypeStruct((own, patches, 3 * width), bf16),
            jax.ShapeDtypeStruct(x.shape, bf16),
            jax.ShapeDtypeStruct((own, patches, pair), f32),
        ],
        compiler_params=pltpu.CompilerParams(vmem_limit_bytes=VMEM_LIMIT),
        cost_estimate=pl.CostEstimate(
            flops=2 * rows * width * 3 * width + 4 * rows * patches * width,
            bytes_accessed=rows * width * 12 + weight.size * 2,
            transcendentals=rows * patches * HEADS,
        ),
        name="space_forward",
    )(x, mods, weight)


def call_space_backward(go, qkv, lse, x, mods, weight):
    n_pos, own, places, width = x.shape
    patches = n_pos * places
    pair = 2 * HEAD_DIM
    spread = pl.BlockSpec((n_pos, 1, places, width), lambda i: (0, i, 0, 0))

    def by_frame(*shape):
        return pl.BlockSpec((1,) + shape, lambda i: (i, 0, 0))

    rows = own * patches
    return pl.pallas_call(
        space_backward,
        grid=(own,),
        in_specs=[
            spread,
            by_frame(patches, 3 * width),
            by_frame(patches, pair),
            spread,
            by_frame(2, width),
            resident(weight.shape),
        ],
        out_specs=[by_frame(patches, 3 * width), spread, by_frame(2, width)],
        out_shape=[
            jax.ShapeDtypeStruct((own, patches, 3 * width), bf16),
            jax.ShapeDtypeStruct(x.shape, bf16),
            jax.ShapeDtypeStruct((own, 2, width), f32),
        ],
        scratch_shapes=[pltpu.VMEM((patches, width), f32)],
        compiler_params=pltpu.CompilerParams(vmem_limit_bytes=VMEM_LIMIT),
        cost_estimate=pl.CostEstimate(
            flops=2 * rows * width * 3 * width + 10 * rows * patches * width,
            bytes_accessed=rows * width * 16 + weight.size * 2,
            transcendentals=rows * patches * HEADS,
        ),
        name="space_backward",
    )(go, qkv, lse, x, mods, weight)


def call_middle(o_one, x, grad, mods, same_clip, wso, wti, wto, wup, wdn):
    places, frames, width = x.shape
    count = max(1, min(places, 256 // frames))
    rows = count * frames
    hidden = wup.shape[1]
    pair = 2 * HEAD_DIM
    total = places * frames
    chunk = pl.BlockSpec((count, frames, width), lambda i: (i, 0, 0))

    def flat(cols):
        return pl.BlockSpec((rows, cols), lambda i: (i, 0))

    def flat_shape(cols):
        return jax.ShapeDtypeStruct((total, cols), bf16)

    def scratch(cols, dtype=f32):
        return pltpu.VMEM((rows, cols), dtype)

    lanes = jnp.concatenate([same_clip, same_clip], axis=1)
    flops = 2 * total * (2 * (wso.size + wti.size + wto.size + wup.size + wdn.size))
    return pl.pallas_call(
        middle,
        grid=(places // count,),
        in_specs=[chunk, chunk, chunk, resident(mods.shape), resident(lanes.shape)]
        + [resident(w.shape) for w in (wso, wti, wto, wup, wdn)],
        out_specs=[
            chunk,
            flat(hidden),
            flat(width),
            flat(width),
            flat(hidden),
            flat(width),
            flat(width),
            flat(width),
            flat(3 * width),
            flat(width),
            chunk,
            chunk,
            pl.BlockSpec((7, frames, width), lambda i: (0, 0, 0)),
        ],
        out_shape=[
            jax.ShapeDtypeStruct(x.shape, bf16),
            flat_shape(hidden),
            flat_shape(width),
            flat_shape(width),
            flat_shape(hidden),
            flat_shape(width),
            flat_shape(width),
            flat_shape(width),
            flat_shape(3 * width),
            flat_shape(width),
            jax.ShapeDtypeStruct(x.shape, bf16),
            jax.ShapeDtypeStruct(x.shape, f32),
            jax.ShapeDtypeStruct((7, frames, width), f32),
        ],
        scratch_shapes=[
            scratch(3 * width, bf16),
            pltpu.VMEM((HEADS // 2, rows, pair), f32),
            scratch(width),
            scratch(width),
            scratch(width),
            scratch(width),
            scratch(pair),
            scratch(pair),
            scratch(width),
            pltpu.VMEM((8, pair), f32),
            scratch(width),
        ],
        compiler_params=pltpu.CompilerParams(vmem_limit_bytes=VMEM_LIMIT),
        cost_estimate=pl.CostEstimate(
            flops=flops, bytes_accessed=total * 40000, transcendentals=total * hidden
        ),
        name="middle",
    )(o_one, x, grad, mods, lanes, wso, wti, wto, wup, wdn)


def on_device(
    tokens,
    clip_lengths,
    timesteps,
    embed_first,
    embed_second,
    adaln_weight,
    spatial_in,
    spatial_out,
    temporal_in,
    temporal_out,
    hidden_up,
    hidden_down,
    grad_output,
    n_pos=16,
    n_clip=2,
):
    frames, places, width = tokens.shape
    rows = frames * places
    own = frames // n_pos
    patches = places * n_pos
    me = lax.axis_index("pos")
    clip_at = lax.axis_index("clip")
    clips = clip_lengths.shape[1]

    def exchange(values):
        sent = values.reshape(frames, places, width)
        got = lax.all_to_all(sent, "pos", split_axis=0, concat_axis=0, tiled=True)
        return got.reshape(n_pos, own, places, width)

    x_space = exchange(tokens)

    all_steps = lax.all_gather(timesteps[0], "clip", axis=0, tiled=True)
    freq = frequency(all_steps)
    first_w, second_w, adaln_w = (
        embed_first.astype(f32),
        embed_second.astype(f32),
        adaln_weight.astype(f32),
    )
    pre_cond = dot_high(freq, first_w)
    hidden_cond = jax.nn.silu(pre_cond)
    cond = dot_high(hidden_cond, second_w)
    cond_act = jax.nn.silu(cond)
    own_act = lax.dynamic_slice_in_dim(cond_act, clip_at * clips, clips, 0)
    modulated = dot_high(own_act, adaln_w)
    onehot, clip_ids = clip_onehot(clip_lengths[0], frames)
    per_frame = dot_high(onehot, modulated)
    own_frames = lax.dynamic_slice_in_dim(per_frame, me * own, own, 0)

    own_mods = own_frames[:, : 2 * width].reshape(own, 2, width)
    h_one, qkv_one, o_one_space, lse_one = call_space_forward(x_space, own_mods, spatial_in)
    o_one = exchange(o_one_space).reshape(frames, places, width)

    def turn(values):
        return values.transpose(1, 0, 2)

    o_one = turn(o_one)
    mods = per_frame.reshape(frames, 9, width).transpose(1, 0, 2)
    same_clip = jnp.dot(onehot, onehot.T)
    (block_turned, act, grad_z, h_three, grad_u, o_two, grad_y_two, h_two, grad_qkv_two, grad_y_one, grad_o_one,
     grad_one, sums) = call_middle(
        o_one, turn(tokens), turn(grad_output), mods, same_clip, spatial_out, temporal_in, temporal_out,
        hidden_up, hidden_down,
    )
    block_out = turn(block_turned)
    grad_o_space = exchange(turn(grad_o_one))
    grad_qkv_one, back_one, sums_one = call_space_backward(
        grad_o_space, qkv_one, lse_one, x_space, own_mods, spatial_in
    )
    back_places = exchange(back_one).reshape(frames, places, width)
    grad_tokens = (turn(grad_one) + back_places.astype(f32)).astype(bf16)
    g_hidden_down = weight_grad(act, grad_z)
    g_hidden_up = weight_grad(h_three, grad_u)
    g_temporal_out = weight_grad(o_two, grad_y_two)
    g_temporal_in = weight_grad(h_two, grad_qkv_two)
    g_spatial_out = weight_grad(o_one.reshape(rows, width), grad_y_one)
    patches = n_pos * places
    g_spatial_in = weight_grad(
        h_one.reshape(own * patches, width), grad_qkv_one.reshape(own * patches, 3 * width)
    )
    shift_own, scale_own = sums_one[:, 0], sums_one[:, 1]

    own_hot = lax.dynamic_slice_in_dim(onehot, me * own, own, 0)
    dmod_own = dot_high(own_hot.T, jnp.concatenate([shift_own, scale_own], axis=1))
    dmod_rest = dot_high(onehot.T, sums.transpose(1, 0, 2).reshape(frames, 7 * width))
    dmod = lax.psum(jnp.concatenate([dmod_own, dmod_rest], axis=1), "pos")
    dmod_all = lax.all_gather(dmod, "clip", axis=0, tiled=True)

    def own_columns(values):
        block = values.shape[1] // n_pos
        return lax.dynamic_slice_in_dim(values, me * block, block, 1)

    g_adaln = dot_high(own_columns(cond_act).T, dmod_all)
    grad_cond = dot_high(dmod_all, adaln_w.T) * silu_grad(cond)
    g_second = dot_high(own_columns(hidden_cond).T, grad_cond)
    grad_pre = dot_high(grad_cond, second_w.T) * silu_grad(pre_cond)
    g_first = dot_high(own_columns(freq).T, grad_pre)

    quarter = g_hidden_down.shape[0] // width
    down = g_hidden_down.reshape(n_pos, quarter, width // n_pos, width)
    down = [down[:, j].reshape(width, width) for j in range(quarter)]

    def reduce(parts):
        joined = jnp.concatenate(parts, axis=1)
        scattered = lax.psum_scatter(joined, "pos", scatter_dimension=0, tiled=True)
        return lax.psum(scattered, "clip").astype(f32)

    mlp = reduce([g_hidden_up] + down)
    rest = reduce([g_temporal_in, g_temporal_out, g_spatial_out, g_spatial_in])
    wide = 3 * width
    up_cols = g_hidden_up.shape[1]
    return (
        block_out,
        grad_tokens,
        g_first,
        g_second,
        g_adaln,
        rest[:, wide + 2 * width :],
        rest[:, wide + width : wide + 2 * width],
        rest[:, :wide],
        rest[:, wide : wide + width],
        mlp[:, :up_cols],
        jnp.concatenate(
            [mlp[:, up_cols + j * width : up_cols + (j + 1) * width] for j in range(quarter)], axis=0
        ),
    )


def solution(mesh):
    in_specs = (
        P("clip", "pos", None),
        P("clip", None),
        P("clip", None),
        P(),
        P(),
        P(),
        P(),
        P(),
        P(),
        P(),
        P(),
        P(),
        P("clip", "pos", None),
    )
    out_specs = (P("clip", "pos", None),) * 2 + (P("pos", None),) * 9
    body = partial(on_device, n_pos=mesh.shape["pos"], n_clip=mesh.shape["clip"])
    return jax.shard_map(body, mesh=mesh, in_specs=in_specs, out_specs=out_specs, check_vma=False)
```

time: 1920 us -> 763 us (0.40)
  waiting for transfers between devices: 1150 us -> 358 us
  local copies, waits for them, and re-layouts: 321 us -> 36.2 us
  matrix products: 304 us -> 56.9 us
  Pallas kernels: 0 us -> 231 us
  other arithmetic: 97.4 us -> 12.8 us
  starting transfers between devices: 1.05 us -> 36.4 us
    reduce_scatter x11 -> x2, waiting for transfers between devices: 908 us -> 215 us  [reduce(): scattered = lax.psum_scatter(joined, 'pos', scatter_dimension=0, tiled=True)]
    dot_general x40 -> x18, matrix products: 304 us -> 56.9 us  [the longest x6 30.8 us: weight_grad(): jnp.einsum('rd,rk->dk', left, right, preferred_element_type=f32)]
    pallas_call x0 -> x3, Pallas kernels: none -> 231 us  [the longest x1 156 us: call_middle(): pl.pallas_call(middle, grid=(places // count,), in_specs=[chunk, chunk, c...]
    all_gather x2 -> x0, waiting for transfers between devices: 196 us -> none  [the longest x1 125 us: on_device(): lax.all_gather(k_local, 'pos', axis=1, tiled=True)]
    convert_element_type x9 -> x0, local copies, waits for them, and re-layouts: 125 us -> none  [the longest x3 44.1 us: on_device(): grad_qkv_two = jnp.stack([grad_q_time, grad_k_time, grad_v_time], axis=2)...]
    all_gather x2 -> x0, local copies, waits for them, and re-layouts: 62.2 us -> none  [the longest x1 31.5 us: on_device(): lax.all_gather(v_local, 'pos', axis=1, tiled=True)]
    convert_element_type x19 -> x1, other arithmetic: 56.8 us -> 2.59 us  [on_device(): grad_tokens = (turn(grad_one) + back_places.astype(f32)).astype(bf16)]
    reshape x6 -> x3, local copies, waits for them, and re-layouts: 53.1 us -> 2.16 us  [the longest x1 1.43 us: on_device(): mods = per_frame.reshape(frames, 9, width).transpose(1, 0, 2)]
  transfers between devices with their start and end apart: 14 -> 8, of which waited for: 13 -> 7; matrix products, arithmetic and copies ran while one was open for 16% -> 11% of each run, Pallas kernels for 0% -> 0%
where the time goes in v1:
time: 763 us; the launch traced here: 758 us
  waiting for transfers between devices  358 us (47%)
  Pallas kernels  231 us (30%)
  matrix products  56.9 us (7%)
  starting transfers between devices  36.4 us (5%)
  local copies, waits for them, and re-layouts  36.2 us (5%)
  between operations  15.1 us (2%)
  other arithmetic  12.8 us (2%)
  blocking collectives  10.9 us (1%)
    reduce_scatter x2, waiting for transfers between devices, reduce(): scattered = lax.psum_scatter(joined, 'pos', scatter_dimension=0, tiled=True)  215 us
    pallas_call x1, Pallas kernels, call_middle(): pl.pallas_call(middle, grid=(places // count,), in_specs=[chunk, chunk, c...  156 us
    psum x1, waiting for transfers between devices, on_device(): dmod = lax.psum(jnp.concatenate([dmod_own, dmod_rest], axis=1), 'pos')  58.5 us
    all_to_all x4, waiting for transfers between devices, exchange(): got = lax.all_to_all(sent, 'pos', split_axis=0, concat_axis=0, tiled=True)  49.7 us
    pallas_call x1, Pallas kernels, call_space_backward(): pl.pallas_call(space_backward, grid=(own,), in_specs=[spread, by_frame(pa...  39 us
    pallas_call x1, Pallas kernels, call_space_forward(): pl.pallas_call(space_forward, grid=(own,), in_specs=[spread, by_frame(2,...  36.1 us
    all_to_all x4, starting transfers between devices, exchange(): got = lax.all_to_all(sent, 'pos', split_axis=0, concat_axis=0, tiled=True)  35.8 us
    psum x1, waiting for transfers between devices, reduce(): return lax.psum(scattered, 'clip').astype(f32)  34.8 us
  transfers between devices with their start and end apart: 8, of which 7 were waited for; matrix products, arithmetic and copies ran while one was open for 11% of the time, Pallas kernels for 0%

profile of v1, /device:TPU:0, one launch (start us, length us, event | category | flops | bytes accessed | tf_op | source)
XLA Modules:
  0.0 757.7 jit_solution(3371194538347833275)
XLA Ops:
  7.2 7.6 all-to-all-start
  16.2 4.3 all-reduce
  21.7 7.0 fusion.14
  31.6 15.2 %all-to-all-done = bf16[64,16,768]{2,1,0:T(8,128)(2,1)} async-done(((bf16[64,16,768]{2,1,0:T(8,128)(2,1)}), bf16[64,16,768]{2,1,0:T(8,128)(2,1)}, u32[]{:S(2)}, u32[]{:S(2)}) %all-to-all-start) | async-done | bytes 1572896 | tf_op jit(solution)/shard_map/all_to_all | solution.py:571
  46.7 36.1 %space_forward.1 = (bf16[4,256,768]{2,1,0:T(8,128)(2,1)}, bf16[4,256,2304]{2,1,0:T(8,128)(2,1)}, bf16[16,4,16,768]{3,2,1,0:T(8,128)(2,1)}, f32[4,256,128]{2,1,0:T(8,128)}) custom-call(bf16[16,4,16,768]{3,2,1,0:T(8,128)(2,1)} %bitcast.x_ref, f32[4,2,768]{2,1,0:T(2,128)} %reshape.85.mod_ref, bf16[768,2304]{1,0:T(8,128)(2,1)} %w_ref.3), custom_call_target="tpu_custom_call" | custom-call | flops 4429185024 | bytes 12976128 | tf_op jit(solution)/shard_map/space_forward/pallas_call | solution.py:404
  82.8 9.8 %all-to-all-start.1 = ((bf16[64,16,768]{2,1,0:T(8,128)(2,1)}), bf16[64,16,768]{2,1,0:T(8,128)(2,1)}, u32[]{:S(2)}, u32[]{:S(2)}) async-start(bf16[64,16,768]{2,1,0:T(8,128)(2,1)} %bitcast.94), calls=%async_computation.1 | async-start | bytes 3145728 | tf_op jit(solution)/shard_map/all_to_all | solution.py:571
  98.3 26.2 %all-to-all-done.1 = bf16[64,16,768]{2,1,0:T(8,128)(2,1)} async-done(((bf16[64,16,768]{2,1,0:T(8,128)(2,1)}), bf16[64,16,768]{2,1,0:T(8,128)(2,1)}, u32[]{:S(2)}, u32[]{:S(2)}) %all-to-all-start.1) | async-done | bytes 1572896 | tf_op jit(solution)/shard_map/all_to_all | solution.py:571
  124.5 3.0 copy.110
  127.5 156.3 %middle.1 = (bf16[16,64,768]{2,1,0:T(8,128)(2,1)}, bf16[1024,3072]{1,0:T(8,128)(2,1)}, bf16[1024,768]{1,0:T(8,128)(2,1)}, bf16[1024,768]{1,0:T(8,128)(2,1)}, bf1...) custom-call(bf16[16,64,768]{2,1,0:T(8,128)(2,1)} %bitcast.89, ...), custom_call_target="tpu_custom_call" | custom-call | flops 31406948352 | bytes 40960000 | tf_op jit(solution)/shard_map/middle/pallas_call | solution.py:488
  283.9 3.5 copy.77
  287.3 9.3 %all-to-all-start.2 = ((bf16[64,16,768]{2,1,0:T(8,128)(2,1)}), bf16[64,16,768]{2,1,0:T(8,128)(2,1)}, u32[]{:S(2)}, u32[]{:S(2)}) async-start(bf16[64,16,768]{2,1,0:T(8,128)(2,1)} %copy.77), calls=%async_computation.2 | async-start | bytes 3145728 | tf_op jit(solution)/shard_map/all_to_all | solution.py:571
  296.8 8.6 %convolution_convert_fusion = bf16[3072,768]{1,0:T(8,128)(2,1)S(1)} fusion(bf16[1024,3072]{1,0:T(8,128)(2,1)} %get-tuple-element.49, bf16[1024,768]{1,0:T(8,128)(2,1)S(1)} %copy-done.17), kind=kOutput, calls=%fused_computation.2 | convolution fusion | flops 4834197504 | bytes 12582912 | tf_op jit(solution)/shard_map/rd,rk->dk/dot_general | solution.py:51
  309.2 6.9 fusion
  320.2 8.3 %all-to-all-done.2 = bf16[64,16,768]{2,1,0:T(8,128)(2,1)} async-done(((bf16[64,16,768]{2,1,0:T(8,128)(2,1)}), bf16[64,16,768]{2,1,0:T(8,128)(2,1)}, u32[]{:S(2)}, u32[]{:S(2)}) %all-to-all-start.2) | async-done | bytes 1572896 | tf_op jit(solution)/shard_map/all_to_all | solution.py:571
  328.5 39.0 %space_backward.1 = (bf16[4,256,2304]{2,1,0:T(8,128)(2,1)}, bf16[16,4,16,768]{3,2,1,0:T(8,128)(2,1)}, f32[4,2,768]{2,1,0:T(2,128)}) custom-call(bf16[16,4,16,768]{3,2,1,0:T(8,128)(2,1)} %bitcast.13.go_ref, bf16[4,256,2304]{2,1,0:T(8,128)(2,1)} %get-tuple-element.35.qkv_ref, f32[4,256,128]{2,1,0:T(8,128)} %get-tuple-element.36.lse_ref, ...), custom_call_target="tpu_custom_call" | custom-call | flops 5637144576 | bytes 16121856 | tf_op jit(solution)/shard_map/space_backward/pallas_call | solution.py:440
  370.0 2.4 constant_dynamic-update-slice_fusion
  373.8 3.0 convolution_convert_fusion.3
  378.4 6.7 convolution_convert_fusion.2
  385.1 4.1 bitcast_convert_fusion
  389.2 7.5 pad_maximum_fusion
  396.8 9.1 %all-to-all-start.3 = ((bf16[64,16,768]{2,1,0:T(8,128)(2,1)}), bf16[64,16,768]{2,1,0:T(8,128)(2,1)S(1)}, u32[]{:S(2)}, u32[]{:S(2)}) async-start(bf16[64,16,768]{2,1,0:T(8,128)(2,1)} %bitcast.88), calls=%async_computation.3 | async-start | bytes 3145728 | tf_op jit(solution)/shard_map/all_to_all | solution.py:571
  406.0 3.4 copy.88
  409.4 58.5 %all-reduce.5.cloned.1.call-done = f32[4,6912]{1,0:T(4,128)} async-done(((f32[4,6912]{1,0:T(4,128)}), f32[4,6912]{1,0:T(4,128)}) %all-reduce.5.cloned.1.call-update) | async-done | bytes 110608 | tf_op jit(solution)/shard_map/psum | solution.py:629
  467.9 6.7 all-gather.1
  474.7 11.0 %convolution_multiply_fusion.1 = f32[8,768]{1,0:T(8,128)S(1)} fusion(f32[8,6912]{1,0:T(8,128)S(1)} %reshape.99, bf16[768,6912]{1,0:T(8,128)(2,1)} %param.18, f32[8,768]{1,0:T(8,128)S(1)} %get-tuple-element.114), kind=kOutput, calls=%fused_computation.14 | convolution fusion | flops 509657088 | bytes 10887168 | tf_op jit(solution)/shard_map/dot_general | solution.py:32
  485.6 99.9 %reduce-scatter.5.cloned.1.call-done = bf16[48,6144]{1,0:T(8,128)(2,1)} async-done(((bf16[768,6144]{1,0:T(8,128)(2,1)}), bf16[48,6144]{1,0:T(8,128)(2,1)}) %reduce-scatter.5.cloned.1.call-update) | async-done | bytes 589840 | tf_op jit(solution)/shard_map/reduce_scatter | solution.py:648
  585.6 115.0 %reduce-scatter.3.cloned.1.call-done = bf16[48,6144]{1,0:T(8,128)(2,1)} async-done(((bf16[768,6144]{1,0:T(8,128)(2,1)}), bf16[48,6144]{1,0:T(8,128)(2,1)}) %reduce-scatter.3.cloned.1.call-update) | async-done | bytes 589840 | tf_op jit(solution)/shard_map/reduce_scatter | solution.py:648
  703.7 2.4 fusion.20
  706.0 2.6 fusion.1
  708.6 2.0 copy.89
  710.6 34.8 %all-reduce.7.cloned.1.call-done = (bf16[48,6144]{1,0:T(8,128)(2,1)}, bf16[48,6144]{1,0:T(8,128)(2,1)}) async-done(((bf16[48,6144]{1,0:T(8,128)(2,1)}, bf16[48,6144]{1,0:T(8,128)(2,1)}), (bf16[48,6144]{1,0:T(8,128)(2,1)}, bf16[48,6144]{1,0:T(8,128)(2,1)})) %all-reduce.7.cloned.1.call-update) | async-done | bytes 1179664 | tf_op jit(solution)/shard_map/psum | solution.py:649
  747.1 2.0 fusion.39
  (94 shorter events, 30.5 us)
Async XLA Ops:
  7.2 14.0 %copy-start = (bf16[768,768]{1,0:T(8,128)(2,1)S(1)}, bf16[768,768]{1,0:T(8,128)(2,1)}, u32[]{:S(2)}) copy-start(bf16[768,768]{1,0:T(8,128)(2,1)} %param.17) | copy-start | bytes 3538948
  7.2 7.6 %copy-start.11 = (u32[32]{0:T(128)S(1)}, u32[32]{0:T(128)}, u32[]{:S(2)}) copy-start(u32[32]{0:T(128)} %constant.42) | copy-start | bytes 388
  7.2 8.9 %copy-start.9 = (s32[1,4]{1,0:T(1,128)S(1)}, s32[1,4]{1,0:T(1,128)}, u32[]{:S(2)}) copy-start(s32[1,4]{1,0:T(1,128)} %param.15) | copy-start | bytes 52
  7.2 13.2 %copy-start.10 = (s32[1,4]{1,0:T(1,128)S(1)}, s32[1,4]{1,0:T(1,128)}, u32[]{:S(2)}) copy-start(s32[1,4]{1,0:T(1,128)} %param.14) | copy-start | bytes 52
  7.2 13.6 %copy-start.8 = (bf16[256,768]{1,0:T(8,128)(2,1)S(1)}, bf16[256,768]{1,0:T(8,128)(2,1)}, u32[]{:S(2)}) copy-start(bf16[256,768]{1,0:T(8,128)(2,1)} %param.16) | copy-start | bytes 1179652
  7.2 39.5 %all-to-all-start = ((bf16[64,16,768]{2,1,0:T(8,128)(2,1)}), bf16[64,16,768]{2,1,0:T(8,128)(2,1)}, u32[]{:S(2)}, u32[]{:S(2)}) async-start(bf16[64,16,768]{2,1,0:T(8,128)(2,1)} %param.13), calls=%async_computation | async-start | bytes 3145728 | tf_op jit(solution)/shard_map/all_to_all | solution.py:571
  29.7 1.2 copy-start.1
  82.8 9.8 %copy-start.3 = (bf16[64,16,768]{2,1,0:T(8,128)(2,1)S(1)}, bf16[64,16,768]{2,1,0:T(8,128)(2,1)}, u32[]{:S(2)}) copy-start(bf16[64,16,768]{2,1,0:T(8,128)(2,1)} %param.13) | copy-start | bytes 4718596
  82.8 41.7 %all-to-all-start.1 = ((bf16[64,16,768]{2,1,0:T(8,128)(2,1)}), bf16[64,16,768]{2,1,0:T(8,128)(2,1)}, u32[]{:S(2)}, u32[]{:S(2)}) async-start(bf16[64,16,768]{2,1,0:T(8,128)(2,1)} %bitcast.94), calls=%async_computation.1 | async-start | bytes 3145728 | tf_op jit(solution)/shard_map/all_to_all | solution.py:571
  92.6 1.6 copy-start.5
  94.3 1.7 copy-start.2
  287.3 9.5 %copy-start.17 = (bf16[1024,768]{1,0:T(8,128)(2,1)S(1)}, bf16[1024,768]{1,0:T(8,128)(2,1)}, u32[]{:S(2)}) copy-start(bf16[1024,768]{1,0:T(8,128)(2,1)} %get-tuple-element.50) | copy-start | bytes 4718596
  287.3 41.2 %all-to-all-start.2 = ((bf16[64,16,768]{2,1,0:T(8,128)(2,1)}), bf16[64,16,768]{2,1,0:T(8,128)(2,1)}, u32[]{:S(2)}, u32[]{:S(2)}) async-start(bf16[64,16,768]{2,1,0:T(8,128)(2,1)} %copy.77), calls=%async_computation.2 | async-start | bytes 3145728 | tf_op jit(solution)/shard_map/all_to_all | solution.py:571
  296.6 171.3 %all-reduce.5.cloned.1.call-start = ((), (), s32[]{:S(2)}) async-start(), calls=%async_computation.6 | async-start | bytes 221184 | tf_op jit(solution)/shard_map/psum | solution.py:629
  296.8 8.7 %copy-start.7 = (f32[7,64,768]{2,1,0:T(8,128)S(1)}, f32[7,64,768]{2,1,0:T(8,128)}, u32[]{:S(2)}) copy-start(f32[7,64,768]{2,1,0:T(8,128)} %get-tuple-element.39) | copy-start | bytes 4128772
  305.5 2.6 slice-start.2
  305.6 3.2 slice-start.3
  305.6 3.6 copy-start.15
  369.9 215.6 %reduce-scatter.5.cloned.1.call-start = ((), (), s32[]{:S(2)}) async-start(), calls=%async_computation.8 | async-start | bytes 10027008 | tf_op jit(solution)/shard_map/reduce_scatter | solution.py:648
  372.4 1.4 copy-start.6
  372.4 328.1 %reduce-scatter.3.cloned.1.call-start = ((), (), s32[]{:S(2)}) async-start(), calls=%async_computation.7 | async-start | bytes 10027008 | tf_op jit(solution)/shard_map/reduce_scatter | solution.py:648
  373.8 3.0 copy-start.12
  373.8 3.0 copy-start.13
  376.8 1.5 copy-start.16
  376.8 8.2 %slice-start = ((s8[4718592]{0:T(1024)(128)(4,1)}), s8[4194304]{0:T(1024)(128)(4,1)S(1)}, s32[]{:S(2)}) async-start(s8[4718592]{0:T(1024)(128)(4,1)} %bitcast.99), calls=%async_computation.10 | async-start | bytes 8388608
  378.3 6.7 slice-start.1
  378.3 6.7 copy-start.14
  396.8 309.3 %all-to-all-start.3 = ((bf16[64,16,768]{2,1,0:T(8,128)(2,1)}), bf16[64,16,768]{2,1,0:T(8,128)(2,1)S(1)}, u32[]{:S(2)}, u32[]{:S(2)}) async-start(bf16[64,16,768]{2,1,0:T(8,128)(2,1)} %bitcast.88), calls=%async_computation.3 | async-start | bytes 3145728 | tf_op jit(solution)/shard_map/all_to_all | solution.py:571
  405.9 339.5 %all-reduce.7.cloned.1.call-start = ((), (), s32[]{:S(2)}) async-start(), calls=%async_computation.9 | async-start | bytes 2359296 | tf_op jit(solution)/shard_map/psum | solution.py:649
  745.4 3.7 copy-start.4
Sparse Core Ops, SparseCore 0:
  370.1 97.8 all-reduce.4
  472.0 113.5 reduce-scatter.4
  589.7 110.8 reduce-scatter.2
  702.8 42.5 all-reduce.6

commit v2 on v1

--- a/solution.py
+++ b/solution.py
@@ -541,6 +541,72 @@
     )(o_one, x, grad, mods, lanes, wso, wti, wto, wup, wdn)
 
 
+def swap(values, axis, size, bit):
+    return lax.ppermute(values, axis, [(i, i ^ bit) for i in range(size)])
+
+
+def bits_of(size):
+    return [1 << i for i in range(size.bit_length() - 1)]
+
+
+def by_distance(values, axis, size):
+    for bit in bits_of(size):
+        values = jnp.concatenate([values, swap(values, axis, size, bit)], axis=0)
+    return values
+
+
+def butterfly(values, axis, size):
+    for bit in bits_of(size):
+        values = values + swap(values, axis, size, bit)
+    return values
+
+
+def halve(values, index, axis):
+    def pick(at):
+        return lax.dynamic_index_in_dim(values, at, axis, keepdims=False)
+
+    return pick(index), pick(1 - index)
+
+
+def reduce_rows(grad, n_pos, n_clip, clip_first):
+    rows, cols = grad.shape
+    block = rows // n_pos
+    me, clip_at = lax.axis_index("pos"), lax.axis_index("clip")
+    values = grad.reshape(n_pos, block, cols)
+
+    def add(keep, got):
+        return (keep.astype(f32) + got.astype(f32)).astype(bf16)
+
+    def pos_step(values, bit):
+        left = values.shape[0] // 2
+        split = values.reshape(left, 2, *values.shape[1:])
+        keep, send = halve(split, lax.rem(me // bit, 2), 1)
+        return add(keep, swap(send, "pos", n_pos, bit))
+
+    bits = bits_of(n_pos)
+    values = pos_step(values, bits[0])
+    if clip_first:
+        for bit in reversed(bits_of(n_clip)):
+            split = values.reshape(*values.shape[:2], 2, values.shape[2] // 2)
+            keep, send = halve(split, lax.rem(clip_at // bit, 2), 2)
+            values = add(keep, swap(send, "clip", n_clip, bit))
+    for bit in bits[1:]:
+        values = pos_step(values, bit)
+    values = values[0]
+    for bit in bits_of(n_clip):
+        got = swap(values, "clip", n_clip, bit)
+        if clip_first:
+            upper = lax.rem(clip_at // bit, 2) == 1
+            values = jnp.concatenate(
+                [jnp.where(upper, got, values), jnp.where(upper, values, got)], axis=1
+            )
+        elif 2 * bit == n_clip:
+            return values.astype(f32) + got.astype(f32)
+        else:
+            values = add(values, got)
+    return values.astype(f32)
+
+
 def on_device(
     tokens,
     clip_lengths,
@@ -563,7 +629,6 @@
     own = frames // n_pos
     patches = places * n_pos
     me = lax.axis_index("pos")
-    clip_at = lax.axis_index("clip")
     clips = clip_lengths.shape[1]
 
     def exchange(values):
@@ -573,7 +638,7 @@
 
     x_space = exchange(tokens)
 
-    all_steps = lax.all_gather(timesteps[0], "clip", axis=0, tiled=True)
+    all_steps = by_distance(timesteps[0], "clip", n_clip)
     freq = frequency(all_steps)
     first_w, second_w, adaln_w = (
         embed_first.astype(f32),
@@ -584,8 +649,7 @@
     hidden_cond = jax.nn.silu(pre_cond)
     cond = dot_high(hidden_cond, second_w)
     cond_act = jax.nn.silu(cond)
-    own_act = lax.dynamic_slice_in_dim(cond_act, clip_at * clips, clips, 0)
-    modulated = dot_high(own_act, adaln_w)
+    modulated = dot_high(cond_act[:clips], adaln_w)
     onehot, clip_ids = clip_onehot(clip_lengths[0], frames)
     per_frame = dot_high(onehot, modulated)
     own_frames = lax.dynamic_slice_in_dim(per_frame, me * own, own, 0)
@@ -612,60 +676,65 @@
     )
     back_places = exchange(back_one).reshape(frames, places, width)
     grad_tokens = (turn(grad_one) + back_places.astype(f32)).astype(bf16)
-    g_hidden_down = weight_grad(act, grad_z)
-    g_hidden_up = weight_grad(h_three, grad_u)
-    g_temporal_out = weight_grad(o_two, grad_y_two)
-    g_temporal_in = weight_grad(h_two, grad_qkv_two)
-    g_spatial_out = weight_grad(o_one.reshape(rows, width), grad_y_one)
-    patches = n_pos * places
-    g_spatial_in = weight_grad(
-        h_one.reshape(own * patches, width), grad_qkv_one.reshape(own * patches, 3 * width)
-    )
-    shift_own, scale_own = sums_one[:, 0], sums_one[:, 1]
-
-    own_hot = lax.dynamic_slice_in_dim(onehot, me * own, own, 0)
-    dmod_own = dot_high(own_hot.T, jnp.concatenate([shift_own, scale_own], axis=1))
-    dmod_rest = dot_high(onehot.T, sums.transpose(1, 0, 2).reshape(frames, 7 * width))
-    dmod = lax.psum(jnp.concatenate([dmod_own, dmod_rest], axis=1), "pos")
-    dmod_all = lax.all_gather(dmod, "clip", axis=0, tiled=True)
 
     def own_columns(values):
         block = values.shape[1] // n_pos
         return lax.dynamic_slice_in_dim(values, me * block, block, 1)
 
-    g_adaln = dot_high(own_columns(cond_act).T, dmod_all)
-    grad_cond = dot_high(dmod_all, adaln_w.T) * silu_grad(cond)
+    def total(values):
+        return by_distance(butterfly(values, "pos", n_pos), "clip", n_clip)
+
+    own_act = own_columns(cond_act).T
+    first_cols = 2 * width
+    dmod_rest = total(dot_high(onehot.T, sums.transpose(1, 0, 2).reshape(frames, 7 * width)))
+    g_adaln_rest = dot_high(own_act, dmod_rest)
+    back_rest = dot_high(dmod_rest, adaln_w[:, first_cols:].T)
+    own_hot = lax.dynamic_slice_in_dim(onehot, me * own, own, 0)
+    dmod_first = total(dot_high(own_hot.T, sums_one.reshape(own, first_cols)))
+    g_adaln_first = dot_high(own_act, dmod_first)
+    back_first = dot_high(dmod_first, adaln_w[:, :first_cols].T)
+    g_adaln = jnp.concatenate([g_adaln_first, g_adaln_rest], axis=1)
+    grad_cond = (back_first + back_rest) * silu_grad(cond)
     g_second = dot_high(own_columns(hidden_cond).T, grad_cond)
     grad_pre = dot_high(grad_cond, second_w.T) * silu_grad(pre_cond)
     g_first = dot_high(own_columns(freq).T, grad_pre)
 
-    quarter = g_hidden_down.shape[0] // width
-    down = g_hidden_down.reshape(n_pos, quarter, width // n_pos, width)
-    down = [down[:, j].reshape(width, width) for j in range(quarter)]
-
-    def reduce(parts):
-        joined = jnp.concatenate(parts, axis=1)
-        scattered = lax.psum_scatter(joined, "pos", scatter_dimension=0, tiled=True)
-        return lax.psum(scattered, "clip").astype(f32)
-
-    mlp = reduce([g_hidden_up] + down)
-    rest = reduce([g_temporal_in, g_temporal_out, g_spatial_out, g_spatial_in])
-    wide = 3 * width
-    up_cols = g_hidden_up.shape[1]
+    early = partial(reduce_rows, n_pos=n_pos, n_clip=n_clip, clip_first=False)
+    late = partial(reduce_rows, n_pos=n_pos, n_clip=n_clip, clip_first=True)
+    g_hidden_up = early(weight_grad(h_three, grad_u))
+    g_hidden_down = late(weight_grad(act, grad_z))
+    g_temporal_in = early(weight_grad(h_two, grad_qkv_two))
+    outs = late(
+        jnp.concatenate(
+            [
+                weight_grad(o_two, grad_y_two),
+                weight_grad(o_one.reshape(rows, width), grad_y_one),
+            ],
+            axis=1,
+        )
+    )
+    h_flat = h_one.reshape(own * patches, width)
+    grad_flat = grad_qkv_one.reshape(own * patches, 3 * width)
+    half = grad_flat.shape[1] // 2
+    g_spatial_in = jnp.concatenate(
+        [
+            early(weight_grad(h_flat, grad_flat[:, :half])),
+            late(weight_grad(h_flat, grad_flat[:, half:])),
+        ],
+        axis=1,
+    )
     return (
         block_out,
         grad_tokens,
         g_first,
         g_second,
         g_adaln,
-        rest[:, wide + 2 * width :],
-        rest[:, wide + width : wide + 2 * width],
-        rest[:, :wide],
-        rest[:, wide : wide + width],
-        mlp[:, :up_cols],
-        jnp.concatenate(
-            [mlp[:, up_cols + j * width : up_cols + (j + 1) * width] for j in range(quarter)], axis=0
-        ),
+        g_spatial_in,
+        outs[:, width:],
+        g_temporal_in,
+        outs[:, :width],
+        g_hidden_up,
+        g_hidden_down,
     )
 
 

time: 763 us -> 604 us (0.79)
  waiting for transfers between devices: 358 us -> 120 us
  starting transfers between devices: 36.4 us -> 78.8 us
  other arithmetic: 12.8 us -> 46.6 us
  local copies, waits for them, and re-layouts: 36.2 us -> 54.5 us
  between operations: 15.1 us -> 2.03 us
  blocking collectives: 10.9 us -> 0 us
  matrix products: 56.9 us -> 64.6 us
    reduce_scatter x2 -> x0, waiting for transfers between devices: 215 us -> none  [reduce(): scattered = lax.psum_scatter(joined, 'pos', scatter_dimension=0, tiled=True)]
    psum x2 -> x0, waiting for transfers between devices: 93.3 us -> none  [the longest x1 58.5 us: on_device(): dmod = lax.psum(jnp.concatenate([dmod_own, dmod_rest], axis=1), 'pos')]
    ppermute x0 -> x44, waiting for transfers between devices: none -> 79.4 us  [swap(): return lax.ppermute(values, axis, [(i, i ^ bit) for i in range(size)])]
    ppermute x0 -> x44, starting transfers between devices: none -> 52.5 us  [swap(): return lax.ppermute(values, axis, [(i, i ^ bit) for i in range(size)])]
    convert_element_type x0 -> x24, other arithmetic: none -> 23.8 us  [the longest x21 22.8 us: add(): return (keep.astype(f32) + got.astype(f32)).astype(bf16)]
    squeeze x1 -> x24, local copies, waits for them, and re-layouts: 0.01 us -> 12.9 us  [pick(): return lax.dynamic_index_in_dim(values, at, axis, keepdims=False)]
    reshape x0 -> x3, local copies, waits for them, and re-layouts: none -> 10.5 us  [reduce_rows(): split = values.reshape(*values.shape[:2], 2, values.shape[2] // 2)]
    all_to_all x4, starting transfers between devices: 35.8 us -> 26.3 us  [exchange(): got = lax.all_to_all(sent, 'pos', split_axis=0, concat_axis=0, tiled=True)]
  transfers between devices with their start and end apart: 8 -> 48, of which waited for: 7 -> 22; matrix products, arithmetic and copies ran while one was open for 11% -> 24% of each run, Pallas kernels for 0% -> 7%
where the time goes in v2:
time: 604 us; the launch traced here: 598 us
  Pallas kernels  231 us (38%)
  waiting for transfers between devices  120 us (20%)
  starting transfers between devices  78.8 us (13%)
  matrix products  64.6 us (11%)
  local copies, waits for them, and re-layouts  54.5 us (9%)
  other arithmetic  46.6 us (8%)
    pallas_call x1, Pallas kernels, call_middle(): pl.pallas_call(middle, grid=(places // count,), in_specs=[chunk, chunk, c...  156 us
    ppermute x44, waiting for transfers between devices, swap(): return lax.ppermute(values, axis, [(i, i ^ bit) for i in range(size)])  79.4 us
    ppermute x44, starting transfers between devices, swap(): return lax.ppermute(values, axis, [(i, i ^ bit) for i in range(size)])  52.5 us
    all_to_all x4, waiting for transfers between devices, exchange(): got = lax.all_to_all(sent, 'pos', split_axis=0, concat_axis=0, tiled=True)  40.9 us
    pallas_call x1, Pallas kernels, call_space_backward(): pl.pallas_call(space_backward, grid=(own,), in_specs=[spread, by_frame(pa...  39 us
    pallas_call x1, Pallas kernels, call_space_forward(): pl.pallas_call(space_forward, grid=(own,), in_specs=[spread, by_frame(2,...  36.1 us
    dot_general x7, matrix products, weight_grad(): jnp.einsum('rd,rk->dk', left, right, preferred_element_type=f32)  32.6 us
    dot_general x13, matrix products, dot_high(): return jnp.dot(left, right, precision=highest, preferred_element_type=f32)  31.7 us
  transfers between devices with their start and end apart: 48, of which 22 were waited for; matrix products, arithmetic and copies ran while one was open for 24% of the time, Pallas kernels for 7%

profile of v2, /device:TPU:0, one launch (start us, length us, event | category | flops | bytes accessed | tf_op | source)
XLA Modules:
  0.0 598.1 jit_solution(3049827818018010793)
XLA Ops:
  0.7 7.6 %all-to-all-start = ((bf16[64,16,768]{2,1,0:T(8,128)(2,1)}), bf16[64,16,768]{2,1,0:T(8,128)(2,1)}, u32[]{:S(2)}, u32[]{:S(2)}) async-start(bf16[64,16,768]{2,1,0:T(8,128)(2,1)} %param.13), calls=%async_computation | async-start | bytes 3145728 | tf_op jit(solution)/shard_map/all_to_all | solution.py:636
  14.2 7.0 %fusion.50 = f32[4,6912]{1,0:T(4,128)S(1)} fusion(bf16[768,6912]{1,0:T(8,128)(2,1)} %param.18, f32[8,768]{1,0:T(8,128)S(1)} %get-tuple-element.124), kind=kOutput, calls=%fused_computation.146 | convolution fusion | flops 254803968 | bytes 10739712 | tf_op jit(solution)/shard_map/dot_general | solution.py:32
  24.0 16.2 %all-to-all-done = bf16[64,16,768]{2,1,0:T(8,128)(2,1)} async-done(((bf16[64,16,768]{2,1,0:T(8,128)(2,1)}), bf16[64,16,768]{2,1,0:T(8,128)(2,1)}, u32[]{:S(2)}, u32[]{:S(2)}) %all-to-all-start) | async-done | bytes 1572896 | tf_op jit(solution)/shard_map/all_to_all | solution.py:636
  40.2 36.1 %space_forward.1 = (bf16[4,256,768]{2,1,0:T(8,128)(2,1)}, bf16[4,256,2304]{2,1,0:T(8,128)(2,1)}, bf16[16,4,16,768]{3,2,1,0:T(8,128)(2,1)}, f32[4,256,128]{2,1,0:T(8,128)}) custom-call(bf16[16,4,16,768]{3,2,1,0:T(8,128)(2,1)} %bitcast.x_ref, f32[4,2,768]{2,1,0:T(2,128)} %reshape.233.mod_ref, bf16[768,2304]{1,0:T(8,128)(2,1)} %w_ref.3), custom_call_target="tpu_custom_call" | custom-call | flops 4429185024 | bytes 12976128 | tf_op jit(solution)/shard_map/space_forward/pallas_call | solution.py:404
  76.2 9.5 %all-to-all-start.1 = ((bf16[64,16,768]{2,1,0:T(8,128)(2,1)}), bf16[64,16,768]{2,1,0:T(8,128)(2,1)}, u32[]{:S(2)}, u32[]{:S(2)}) async-start(bf16[64,16,768]{2,1,0:T(8,128)(2,1)} %bitcast.256), calls=%async_computation.1 | async-start | bytes 3145728 | tf_op jit(solution)/shard_map/all_to_all | solution.py:636
  87.4 3.2 copy.136
  93.0 24.7 %all-to-all-done.1 = bf16[64,16,768]{2,1,0:T(8,128)(2,1)} async-done(((bf16[64,16,768]{2,1,0:T(8,128)(2,1)}), bf16[64,16,768]{2,1,0:T(8,128)(2,1)}, u32[]{:S(2)}, u32[]{:S(2)}) %all-to-all-start.1) | async-done | bytes 1572896 | tf_op jit(solution)/shard_map/all_to_all | solution.py:636
  120.7 156.2 %middle.1 = (bf16[16,64,768]{2,1,0:T(8,128)(2,1)}, bf16[1024,3072]{1,0:T(8,128)(2,1)}, bf16[1024,768]{1,0:T(8,128)(2,1)}, bf16[1024,768]{1,0:T(8,128)(2,1)}, bf1...) custom-call(bf16[16,64,768]{2,1,0:T(8,128)(2,1)} %bitcast.260, ...), custom_call_target="tpu_custom_call" | custom-call | flops 31406948352 | bytes 40960000 | tf_op jit(solution)/shard_map/middle/pallas_call | solution.py:488
  276.9 8.1 %convolution_convert_fusion = bf16[3072,768]{1,0:T(8,128)(2,1)S(1)} fusion(bf16[1024,3072]{1,0:T(8,128)(2,1)} %get-tuple-element.49, bf16[1024,768]{1,0:T(8,128)(2,1)} %get-tuple-element.50), kind=kOutput, calls=%fused_computation.2 | convolution fusion | flops 4834197504 | bytes 12582912 | tf_op jit(solution)/shard_map/rd,rk->dk/dot_general | solution.py:51
  300.0 6.4 %convolution_convert_fusion.2 = bf16[768,2304]{1,0:T(8,128)(2,1)S(1)} fusion(bf16[1024,768]{1,0:T(8,128)(2,1)S(1)} %copy-done.41, bf16[1024,2304]{1,0:T(8,128)(2,1)} %get-tuple-element.46), kind=kOutput, calls=%fused_computation.4 | convolution fusion | flops 3625648128 | bytes 9830400 | tf_op jit(solution)/shard_map/rd,rk->dk/dot_general | solution.py:51
  313.3 4.2 collective-permute-start.8
  326.1 8.3 %convolution_convert_fusion.1 = bf16[768,3072]{1,0:T(8,128)(2,1)S(1)} fusion(bf16[1024,768]{1,0:T(8,128)(2,1)S(1)} %copy-done.40, bf16[1024,3072]{1,0:T(8,128)(2,1)} %get-tuple-element.48), kind=kOutput, calls=%fused_computation.3 | convolution fusion | flops 4834197504 | bytes 12582912 | tf_op jit(solution)/shard_map/rd,rk->dk/dot_general | solution.py:51
  342.2 4.4 all-to-all-start.2
  346.6 3.4 copy.102
  355.8 9.6 %fusion = f32[8,768]{1,0:T(8,128)} fusion(bf16[768,6912]{1,0:T(8,128)(2,1)} %param.18, f32[4,5376]{1,0:T(4,128)S(1)} %collective-permute-done.10, f32[4,5376]{1,0:T(4,128)S(1)} %add.268), kind=kOutput, calls=%fused_computation | convolution fusion | flops 396404736 | bytes 8454144 | tf_op jit(solution)/shard_map/dot_general | solution.py:32
  371.9 4.3 collective-permute-done.25
  376.3 4.5 collective-permute-start.26
  383.3 4.1 collective-permute-done.26
  389.4 3.7 fusion.2
  393.1 4.9 reshape.255
  398.0 5.9 constant_dynamic-slice_fusion.2
  406.0 3.3 fusion.3
  416.1 39.0 %space_backward.1 = (bf16[4,256,2304]{2,1,0:T(8,128)(2,1)}, bf16[16,4,16,768]{3,2,1,0:T(8,128)(2,1)}, f32[4,2,768]{2,1,0:T(2,128)}) custom-call(bf16[16,4,16,768]{3,2,1,0:T(8,128)(2,1)} %bitcast.12.go_ref, bf16[4,256,2304]{2,1,0:T(8,128)(2,1)} %get-tuple-element.35.qkv_ref, f32[4,256,128]{2,1,0:T(8,128)} %get-tuple-element.36.lse_ref, ...), custom_call_target="tpu_custom_call" | custom-call | flops 5637144576 | bytes 16121856 | tf_op jit(solution)/shard_map/space_backward/pallas_call | solution.py:440
  458.1 4.5 convolution_convert_fusion.4
  467.0 3.5 collective-permute-done.3
  471.8 3.5 collective-permute-done.4
  477.6 4.8 all-to-all-start.3
  485.3 3.7 fusion.22
  495.5 34.1 %collective-permute-done.31 = bf16[1,48,2304]{2,1,0:T(8,128)(2,1)S(1)} collective-permute-done((bf16[1,48,2304]{2,1,0:T(8,128)(2,1)S(1)}, bf16[1,48,2304]{2,1,0:T(8,128)(2,1)S(1)}, u32[]{:S(2)}, u32[]{:S(2)}) %collective-permute-start.31) | collective-permute-done | bytes 221216 | tf_op jit(solution)/shard_map/ppermute | solution.py:545
  564.0 6.7 %collective-permute-done.36 = bf16[1,48,3072]{2,1,0:T(8,128)(2,1)S(1)} collective-permute-done((bf16[1,48,3072]{2,1,0:T(8,128)(2,1)S(1)}, bf16[1,48,3072]{2,1,0:T(8,128)(2,1)S(1)}, u32[]{:S(2)}, u32[]{:S(2)}) %collective-permute-start.36) | collective-permute-done | bytes 294944 | tf_op jit(solution)/shard_map/ppermute | solution.py:545
  570.8 4.2 collective-permute-start.37
  583.3 3.3 collective-permute-done.20
  (283 shorter events, 153.4 us)
Async XLA Ops:
  0.7 39.5 %all-to-all-start = ((bf16[64,16,768]{2,1,0:T(8,128)(2,1)}), bf16[64,16,768]{2,1,0:T(8,128)(2,1)}, u32[]{:S(2)}, u32[]{:S(2)}) async-start(bf16[64,16,768]{2,1,0:T(8,128)(2,1)} %param.13), calls=%async_computation | async-start | bytes 3145728 | tf_op jit(solution)/shard_map/all_to_all | solution.py:636
  76.2 41.4 %all-to-all-start.1 = ((bf16[64,16,768]{2,1,0:T(8,128)(2,1)}), bf16[64,16,768]{2,1,0:T(8,128)(2,1)}, u32[]{:S(2)}, u32[]{:S(2)}) async-start(bf16[64,16,768]{2,1,0:T(8,128)(2,1)} %bitcast.256), calls=%async_computation.1 | async-start | bytes 3145728 | tf_op jit(solution)/shard_map/all_to_all | solution.py:636
  288.5 100.9 %collective-permute-start.38 = (bf16[8,192,768]{2,1,0:T(8,128)(2,1)}, bf16[8,192,768]{2,1,0:T(8,128)(2,1)}, u32[]{:S(2)}, u32[]{:S(2)}) collective-permute-start(bf16[8,192,768]{2,1,0:T(8,128)(2,1)} %dynamic-slice_bitcast_fusion), channel_id=1, source_target_pairs={{0,1},{1,0},{2,3},{3,2},{4,5},{5,4},{6,7},{7,6},{8,9},{9,8},{10,11... | collective-permute-start | bytes 7077896 | tf_op jit(solution)/shard_map/ppermute | solution.py:545
  297.3 20.2 %collective-permute-start.22 = (bf16[8,48,1536]{2,1,0:T(8,128)(2,1)S(1)}, bf16[8,48,1536]{2,1,0:T(8,128)(2,1)S(1)}, u32[]{:S(2)}, u32[]{:S(2)}) collective-permute-start(bf16[8,48,1536]{2,1,0:T(8,128)(2,1)S(1)} %dynamic-slice_bitcast_fusion.4), channel_id=1, source_target_pairs={{0,1},{1,0},{2,3},{3,2},{4,5},{5,4},{6,7},{7,6},{8,9},{9,8},{10,11... | collective-permute-start | bytes 3538952 | tf_op jit(solution)/shard_map/ppermute | solution.py:545
  310.6 59.3 %collective-permute-start.28 = (bf16[8,48,2304]{2,1,0:T(8,128)(2,1)}, bf16[8,48,2304]{2,1,0:T(8,128)(2,1)}, u32[]{:S(2)}, u32[]{:S(2)}) collective-permute-start(bf16[8,48,2304]{2,1,0:T(8,128)(2,1)} %dynamic-slice_bitcast_fusion.2), channel_id=1, source_target_pairs={{0,1},{1,0},{2,3},{3,2},{4,5},{5,4},{6,7},{7,6},{8,9},{9,8},{10,11... | collective-permute-start | bytes 5308424 | tf_op jit(solution)/shard_map/ppermute | solution.py:545
  313.3 21.2 %collective-permute-start.8 = (f32[4,5376]{1,0:T(4,128)}, f32[4,5376]{1,0:T(4,128)}, u32[]{:S(2)}, u32[]{:S(2)}) collective-permute-start(f32[4,5376]{1,0:T(4,128)} %add.266), channel_id=1, source_target_pairs={{0,4},{1,5},{2,6},{3,7},{4,0},{5,1},{6,2},{7,3},{8,12},{9,13},{10,... | collective-permute-start | bytes 258056 | tf_op jit(solution)/shard_map/ppermute | solution.py:545
  324.5 27.8 %collective-permute-start.23 = (bf16[8,48,768]{2,1,0:T(8,128)(2,1)S(1)}, bf16[8,48,768]{2,1,0:T(8,128)(2,1)S(1)}, u32[]{:S(2)}, u32[]{:S(2)}) collective-permute-start(bf16[8,48,768]{2,1,0:T(8,128)(2,1)S(1)} %bitcast.267), channel_id=1, source_target_pairs={{0,16},{16,0},{1,17},{17,1},{2,18},{18,2},{3,19},{19,3},{4,20},{20... | collective-permute-start | bytes 1769480 | tf_op jit(solution)/shard_map/ppermute | solution.py:545
  336.6 13.4 %collective-permute-start.9 = (f32[4,5376]{1,0:T(4,128)}, f32[4,5376]{1,0:T(4,128)}, u32[]{:S(2)}, u32[]{:S(2)}) collective-permute-start(f32[4,5376]{1,0:T(4,128)} %add.267), channel_id=1, source_target_pairs={{0,8},{1,9},{2,10},{3,11},{4,12},{5,13},{6,14},{7,15},{8,0},{9,1},... | collective-permute-start | bytes 258056 | tf_op jit(solution)/shard_map/ppermute | solution.py:545
  339.5 66.4 %collective-permute-start.33 = (bf16[8,48,3072]{2,1,0:T(8,128)(2,1)}, bf16[8,48,3072]{2,1,0:T(8,128)(2,1)}, u32[]{:S(2)}, u32[]{:S(2)}) collective-permute-start(bf16[8,48,3072]{2,1,0:T(8,128)(2,1)} %dynamic-slice_bitcast_fusion.1), channel_id=1, source_target_pairs={{0,1},{1,0},{2,3},{3,2},{4,5},{5,4},{6,7},{7,6},{8,9},{9,8},{10,11... | collective-permute-start | bytes 7077896 | tf_op jit(solution)/shard_map/ppermute | solution.py:545
  342.2 73.8 %all-to-all-start.2 = ((bf16[64,16,768]{2,1,0:T(8,128)(2,1)}), bf16[64,16,768]{2,1,0:T(8,128)(2,1)}, u32[]{:S(2)}, u32[]{:S(2)}) async-start(bf16[64,16,768]{2,1,0:T(8,128)(2,1)} %copy.88), calls=%async_computation.2 | async-start | bytes 3145728 | tf_op jit(solution)/shard_map/all_to_all | solution.py:636
  352.5 16.0 %collective-permute-start.24 = (bf16[4,48,768]{2,1,0:T(8,128)(2,1)S(1)}, bf16[4,48,768]{2,1,0:T(8,128)(2,1)S(1)}, u32[]{:S(2)}, u32[]{:S(2)}) collective-permute-start(bf16[4,48,768]{2,1,0:T(8,128)(2,1)S(1)} %dynamic-slice_bitcast_fusion.13), channel_id=1, source_target_pairs={{0,2},{1,3},{2,0},{3,1},{4,6},{5,7},{6,4},{7,5},{8,10},{9,11},{10,... | collective-permute-start | bytes 884744 | tf_op jit(solution)/shard_map/ppermute | solution.py:545
  376.3 11.2 %collective-permute-start.26 = (bf16[1,48,768]{2,1,0:T(8,128)(2,1)S(1)}, bf16[1,48,768]{2,1,0:T(8,128)(2,1)S(1)}, u32[]{:S(2)}, u32[]{:S(2)}) collective-permute-start(bf16[1,48,768]{2,1,0:T(8,128)(2,1)S(1)} %constant_dynamic-slice_fusion.5), channel_id=1, source_target_pairs={{0,8},{1,9},{2,10},{3,11},{4,12},{5,13},{6,14},{7,15},{8,0},{9,1},... | collective-permute-start | bytes 221192 | tf_op jit(solution)/shard_map/ppermute | solution.py:545
  381.8 32.0 %collective-permute-start.29 = (bf16[4,48,2304]{2,1,0:T(8,128)(2,1)}, bf16[4,48,2304]{2,1,0:T(8,128)(2,1)}, u32[]{:S(2)}, u32[]{:S(2)}) collective-permute-start(bf16[4,48,2304]{2,1,0:T(8,128)(2,1)} %dynamic-slice_bitcast_fusion.5), channel_id=1, source_target_pairs={{0,2},{1,3},{2,0},{3,1},{4,6},{5,7},{6,4},{7,5},{8,10},{9,11},{10,... | collective-permute-start | bytes 2654216 | tf_op jit(solution)/shard_map/ppermute | solution.py:545
  388.1 23.9 %collective-permute-start.27 = (bf16[48,768]{1,0:T(8,128)(2,1)}, bf16[48,768]{1,0:T(8,128)(2,1)}, u32[]{:S(2)}, u32[]{:S(2)}) collective-permute-start(bf16[48,768]{1,0:T(8,128)(2,1)} %fusion.39), channel_id=1, source_target_pairs={{0,16},{16,0},{1,17},{17,1},{2,18},{18,2},{3,19},{19,3},{4,20},{20... | collective-permute-start | bytes 221192 | tf_op jit(solution)/shard_map/ppermute | solution.py:545
  405.2 125.3 %collective-permute-start.39 = (bf16[8,192,384]{2,1,0:T(8,128)(2,1)}, bf16[8,192,384]{2,1,0:T(8,128)(2,1)}, u32[]{:S(2)}, u32[]{:S(2)}) collective-permute-start(bf16[8,192,384]{2,1,0:T(8,128)(2,1)} %bitcast.214), channel_id=1, source_target_pairs={{0,16},{16,0},{1,17},{17,1},{2,18},{18,2},{3,19},{19,3},{4,20},{20... | collective-permute-start | bytes 3538952 | tf_op jit(solution)/shard_map/ppermute | solution.py:545
  410.5 124.1 %collective-permute-start.34 = (bf16[4,48,3072]{2,1,0:T(8,128)(2,1)}, bf16[4,48,3072]{2,1,0:T(8,128)(2,1)}, u32[]{:S(2)}, u32[]{:S(2)}) collective-permute-start(bf16[4,48,3072]{2,1,0:T(8,128)(2,1)} %dynamic-slice_bitcast_fusion.3), channel_id=1, source_target_pairs={{0,2},{1,3},{2,0},{3,1},{4,6},{5,7},{6,4},{7,5},{8,10},{9,11},{10,... | collective-permute-start | bytes 3538952 | tf_op jit(solution)/shard_map/ppermute | solution.py:545
  457.4 34.4 %collective-permute-start.30 = (bf16[2,48,2304]{2,1,0:T(8,128)(2,1)S(1)}, bf16[2,48,2304]{2,1,0:T(8,128)(2,1)S(1)}, u32[]{:S(2)}, u32[]{:S(2)}) collective-permute-start(bf16[2,48,2304]{2,1,0:T(8,128)(2,1)S(1)} %dynamic-slice_bitcast_fusion.10), channel_id=1, source_target_pairs={{0,4},{1,5},{2,6},{3,7},{4,0},{5,1},{6,2},{7,3},{8,12},{9,13},{10,... | collective-permute-start | bytes 1327112 | tf_op jit(solution)/shard_map/ppermute | solution.py:545
  471.8 66.2 %collective-permute-start.11 = (bf16[8,48,1152]{2,1,0:T(8,128)(2,1)}, bf16[8,48,1152]{2,1,0:T(8,128)(2,1)}, u32[]{:S(2)}, u32[]{:S(2)}) collective-permute-start(bf16[8,48,1152]{2,1,0:T(8,128)(2,1)} %dynamic-slice_bitcast_fusion.7), channel_id=1, source_target_pairs={{0,1},{1,0},{2,3},{3,2},{4,5},{5,4},{6,7},{7,6},{8,9},{9,8},{10,11... | collective-permute-start | bytes 2654216 | tf_op jit(solution)/shard_map/ppermute | solution.py:545
  477.6 115.1 %all-to-all-start.3 = ((bf16[64,16,768]{2,1,0:T(8,128)(2,1)}), bf16[64,16,768]{2,1,0:T(8,128)(2,1)}, u32[]{:S(2)}, u32[]{:S(2)}) async-start(bf16[64,16,768]{2,1,0:T(8,128)(2,1)} %bitcast.254), calls=%async_computation.3 | async-start | bytes 3145728 | tf_op jit(solution)/shard_map/all_to_all | solution.py:636
  482.5 58.9 %collective-permute-start.16 = (bf16[8,48,1152]{2,1,0:T(8,128)(2,1)}, bf16[8,48,1152]{2,1,0:T(8,128)(2,1)S(1)}, u32[]{:S(2)}, u32[]{:S(2)}) collective-permute-start(bf16[8,48,1152]{2,1,0:T(8,128)(2,1)} %dynamic-slice_bitcast_fusion.6), channel_id=1, source_target_pairs={{0,1},{1,0},{2,3},{3,2},{4,5},{5,4},{6,7},{7,6},{8,9},{9,8},{10,11... | collective-permute-start | bytes 2654216 | tf_op jit(solution)/shard_map/ppermute | solution.py:545
  491.9 37.6 %collective-permute-start.31 = (bf16[1,48,2304]{2,1,0:T(8,128)(2,1)S(1)}, bf16[1,48,2304]{2,1,0:T(8,128)(2,1)S(1)}, u32[]{:S(2)}, u32[]{:S(2)}) collective-permute-start(bf16[1,48,2304]{2,1,0:T(8,128)(2,1)S(1)} %constant_dynamic-slice_fusion.4), channel_id=1, source_target_pairs={{0,8},{1,9},{2,10},{3,11},{4,12},{5,13},{6,14},{7,15},{8,0},{9,1},... | collective-permute-start | bytes 663560 | tf_op jit(solution)/shard_map/ppermute | solution.py:545
  533.1 16.5 %collective-permute-start.40 = (bf16[4,192,384]{2,1,0:T(8,128)(2,1)}, bf16[4,192,384]{2,1,0:T(8,128)(2,1)}, u32[]{:S(2)}, u32[]{:S(2)}) collective-permute-start(bf16[4,192,384]{2,1,0:T(8,128)(2,1)} %dynamic-slice_bitcast_fusion.8), channel_id=1, source_target_pairs={{0,2},{1,3},{2,0},{3,1},{4,6},{5,7},{6,4},{7,5},{8,10},{9,11},{10,... | collective-permute-start | bytes 1769480 | tf_op jit(solution)/shard_map/ppermute | solution.py:545
  537.2 15.2 %collective-permute-start.35 = (bf16[2,48,3072]{2,1,0:T(8,128)(2,1)}, bf16[2,48,3072]{2,1,0:T(8,128)(2,1)}, u32[]{:S(2)}, u32[]{:S(2)}) collective-permute-start(bf16[2,48,3072]{2,1,0:T(8,128)(2,1)} %dynamic-slice_bitcast_fusion.9), channel_id=1, source_target_pairs={{0,4},{1,5},{2,6},{3,7},{4,0},{5,1},{6,2},{7,3},{8,12},{9,13},{10,... | collective-permute-start | bytes 1769480 | tf_op jit(solution)/shard_map/ppermute | solution.py:545
  540.9 16.5 %collective-permute-start.12 = (bf16[4,48,1152]{2,1,0:T(8,128)(2,1)}, bf16[4,48,1152]{2,1,0:T(8,128)(2,1)}, u32[]{:S(2)}, u32[]{:S(2)}) collective-permute-start(bf16[4,48,1152]{2,1,0:T(8,128)(2,1)} %dynamic-slice_bitcast_fusion.11), channel_id=1, source_target_pairs={{0,2},{1,3},{2,0},{3,1},{4,6},{5,7},{6,4},{7,5},{8,10},{9,11},{10,... | collective-permute-start | bytes 1327112 | tf_op jit(solution)/shard_map/ppermute | solution.py:545
  547.2 12.0 %collective-permute-start.17 = (bf16[8,48,576]{2,1,0:T(8,128)(2,1)S(1)}, bf16[8,48,576]{2,1,0:T(8,128)(2,1)S(1)}, u32[]{:S(2)}, u32[]{:S(2)}) collective-permute-start(bf16[8,48,576]{2,1,0:T(8,128)(2,1)S(1)} %bitcast.268), channel_id=1, source_target_pairs={{0,16},{16,0},{1,17},{17,1},{2,18},{18,2},{3,19},{19,3},{4,20},{20... | collective-permute-start | bytes 1327112 | tf_op jit(solution)/shard_map/ppermute | solution.py:545
  550.9 12.1 %collective-permute-start.41 = (bf16[2,192,384]{2,1,0:T(8,128)(2,1)S(1)}, bf16[2,192,384]{2,1,0:T(8,128)(2,1)S(1)}, u32[]{:S(2)}, u32[]{:S(2)}) collective-permute-start(bf16[2,192,384]{2,1,0:T(8,128)(2,1)S(1)} %dynamic-slice_bitcast_fusion.12), channel_id=1, source_target_pairs={{0,4},{1,5},{2,6},{3,7},{4,0},{5,1},{6,2},{7,3},{8,12},{9,13},{10,... | collective-permute-start | bytes 884744 | tf_op jit(solution)/shard_map/ppermute | solution.py:545
  553.7 17.0 %collective-permute-start.36 = (bf16[1,48,3072]{2,1,0:T(8,128)(2,1)S(1)}, bf16[1,48,3072]{2,1,0:T(8,128)(2,1)S(1)}, u32[]{:S(2)}, u32[]{:S(2)}) collective-permute-start(bf16[1,48,3072]{2,1,0:T(8,128)(2,1)S(1)} %constant_dynamic-slice_fusion.3), channel_id=1, source_target_pairs={{0,8},{1,9},{2,10},{3,11},{4,12},{5,13},{6,14},{7,15},{8,0},{9,1},... | collective-permute-start | bytes 884744 | tf_op jit(solution)/shard_map/ppermute | solution.py:545
  558.6 16.4 %collective-permute-start.13 = (bf16[2,48,1152]{2,1,0:T(8,128)(2,1)S(1)}, bf16[2,48,1152]{2,1,0:T(8,128)(2,1)S(1)}, u32[]{:S(2)}, u32[]{:S(2)}) collective-permute-start(bf16[2,48,1152]{2,1,0:T(8,128)(2,1)S(1)} %dynamic-slice_bitcast_fusion.15), channel_id=1, source_target_pairs={{0,4},{1,5},{2,6},{3,7},{4,0},{5,1},{6,2},{7,3},{8,12},{9,13},{10,... | collective-permute-start | bytes 663560 | tf_op jit(solution)/shard_map/ppermute | solution.py:545
  559.3 15.8 %collective-permute-start.18 = (bf16[4,48,576]{2,1,0:T(8,128)(2,1)S(1)}, bf16[4,48,576]{2,1,0:T(8,128)(2,1)S(1)}, u32[]{:S(2)}, u32[]{:S(2)}) collective-permute-start(bf16[4,48,576]{2,1,0:T(8,128)(2,1)S(1)} %dynamic-slice_bitcast_fusion.14), channel_id=1, source_target_pairs={{0,2},{1,3},{2,0},{3,1},{4,6},{5,7},{6,4},{7,5},{8,10},{9,11},{10,... | collective-permute-start | bytes 663560 | tf_op jit(solution)/shard_map/ppermute | solution.py:545
  563.1 14.3 %collective-permute-start.42 = (bf16[1,192,384]{2,1,0:T(8,128)(2,1)S(1)}, bf16[1,192,384]{2,1,0:T(8,128)(2,1)S(1)}, u32[]{:S(2)}, u32[]{:S(2)}) collective-permute-start(bf16[1,192,384]{2,1,0:T(8,128)(2,1)S(1)} %constant_dynamic-slice_fusion.1), channel_id=1, source_target_pairs={{0,8},{1,9},{2,10},{3,11},{4,12},{5,13},{6,14},{7,15},{8,0},{9,1},... | collective-permute-start | bytes 442376 | tf_op jit(solution)/shard_map/ppermute | solution.py:545
  570.8 21.1 %collective-permute-start.37 = (bf16[48,3072]{1,0:T(8,128)(2,1)S(1)}, bf16[48,3072]{1,0:T(8,128)(2,1)S(1)}, u32[]{:S(2)}, u32[]{:S(2)}) collective-permute-start(bf16[48,3072]{1,0:T(8,128)(2,1)S(1)} %fusion.32), channel_id=1, source_target_pairs={{0,16},{16,0},{1,17},{17,1},{2,18},{18,2},{3,19},{19,3},{4,20},{20... | collective-permute-start | bytes 884744 | tf_op jit(solution)/shard_map/ppermute | solution.py:545
  577.5 10.6 %collective-permute-start.43 = (bf16[192,384]{1,0:T(8,128)(2,1)S(1)}, bf16[192,384]{1,0:T(8,128)(2,1)S(1)}, u32[]{:S(2)}, u32[]{:S(2)}) collective-permute-start(bf16[192,384]{1,0:T(8,128)(2,1)S(1)} %fusion.36), channel_id=1, source_target_pairs={{0,16},{16,0},{1,17},{17,1},{2,18},{18,2},{3,19},{19,3},{4,20},{20... | collective-permute-start | bytes 442376 | tf_op jit(solution)/shard_map/ppermute | solution.py:545
  (62 other events, 474.3 us)

commit v3 on v2

--- a/solution.py
+++ b/solution.py
@@ -96,13 +96,84 @@
     return part.reshape(count * places, width)
 
 
-def store_rows(ref, step, values):
-    places, width = ref.shape[2:]
-    count = max(1, ROWS // places)
-    ref[pl.ds(step * count, count), 0] = values.reshape(count, places, width).astype(bf16)
-
-
-def space_forward(x_ref, mod_ref, w_ref, h_ref, qkv_ref, o_ref, lse_ref):
+class Spread:
+
+    def __init__(self, n_pos, step, steps, hold, out, send_sem, recv_sem, own_sem):
+        self.n_pos, self.step, self.steps = n_pos, step, steps
+        self.hold, self.out = hold, out
+        self.send_sem, self.recv_sem, self.own_sem = send_sem, recv_sem, own_sem
+        self.me = lax.axis_index("pos")
+
+    def greet(self):
+        barrier = pltpu.get_barrier_semaphore()
+
+        def signal(shift, _):
+            target = lax.rem(self.me + shift, self.n_pos)
+            pl.semaphore_signal(
+                barrier, inc=1, device_id={"pos": target}, device_id_type=pl.DeviceIdType.MESH
+            )
+            return 0
+
+        lax.fori_loop(1, self.n_pos, signal, 0)
+        pl.semaphore_wait(barrier, self.n_pos - 1)
+
+    def copy(self, step, shift, source):
+        target = lax.rem(self.me + shift, self.n_pos)
+        return pltpu.make_async_remote_copy(
+            self.hold.at[step, target],
+            self.out.at[source * self.steps + step],
+            self.send_sem.at[step, shift],
+            self.recv_sem.at[step, shift],
+            device_id={"pos": target},
+            device_id_type=pl.DeviceIdType.MESH,
+        )
+
+    def stay(self, step):
+        return pltpu.make_async_copy(
+            self.hold.at[step, self.me],
+            self.out.at[self.me * self.steps + step],
+            self.own_sem.at[step],
+        )
+
+    def send(self):
+        def one(shift, _):
+            self.copy(self.step, shift, self.me).start()
+            return 0
+
+        lax.fori_loop(1, self.n_pos, one, 0)
+        self.stay(self.step).start()
+
+    def finish(self):
+        def one_step(step, _):
+            def one(shift, _):
+                self.copy(step, shift, self.me).wait_send()
+                source = lax.rem(self.me + self.n_pos - shift, self.n_pos)
+                self.copy(step, shift, source).wait_recv()
+                return 0
+
+            lax.fori_loop(1, self.n_pos, one, 0)
+            self.stay(step).wait()
+            return 0
+
+        lax.fori_loop(0, self.steps, one_step, 0)
+
+
+def spread_scratch(own, n_pos, places, width):
+    return [
+        pltpu.VMEM((own, n_pos, places, width), bf16),
+        pltpu.SemaphoreType.DMA((own, n_pos)),
+        pltpu.SemaphoreType.DMA((own, n_pos)),
+        pltpu.SemaphoreType.DMA((own,)),
+    ]
+
+
+def space_forward(
+    x_ref, mod_ref, w_ref, h_ref, qkv_ref, o_ref, lse_ref, hold, send_sem, recv_sem, own_sem
+):
+    own, n_pos = hold.shape[:2]
+    frame = pl.program_id(0)
+    spread = Spread(n_pos, frame, own, hold, o_ref, send_sem, recv_sem, own_sem)
+    pl.when(frame == 0)(spread.greet)
     patches, width = h_ref.shape[1:]
     places = x_ref.shape[2]
     pair = 2 * HEAD_DIM
@@ -138,15 +209,22 @@
             lse = jnp.where(lane_ids == 2 * index + half, top + jnp.log(total), lse)
         lse_ref[0] = lse
         both = jnp.where(lane_ids < HEAD_DIM, outs[0], outs[1])
-        o_ref[:, 0, :, pl.ds(at, pair)] = both.reshape(patches // places, places, pair).astype(bf16)
+        hold[frame, :, :, pl.ds(at, pair)] = both.reshape(n_pos, places, pair).astype(bf16)
         return 0
 
     lax.fori_loop(0, HEADS // 2, head_pair, 0)
+    spread.send()
+    pl.when(frame == own - 1)(spread.finish)
 
 
 def space_backward(
-    go_ref, qkv_ref, lse_ref, x_ref, mod_ref, w_ref, dqkv_ref, dv_ref, sum_ref, e_ref
+    go_ref, qkv_ref, lse_ref, x_ref, mod_ref, w_ref, dqkv_ref, dv_ref, sum_ref, e_ref,
+    hold, send_sem, recv_sem, own_sem,
 ):
+    own, n_pos = hold.shape[:2]
+    frame = pl.program_id(0)
+    spread = Spread(n_pos, frame, own, hold, dv_ref, send_sem, recv_sem, own_sem)
+    pl.when(frame == 0)(spread.greet)
     patches = qkv_ref.shape[1]
     width = x_ref.shape[3]
     places = x_ref.shape[2]
@@ -194,15 +272,20 @@
     def norm_step(step, sums):
         grad = e_ref[pl.ds(step * ROWS, ROWS), :]
         normed, inverse = norm_rows(load_rows(x_ref, step))
-        store_rows(dv_ref, step, norm_rows_back(normed, inverse, scale, grad))
+        back = norm_rows_back(normed, inverse, scale, grad)
+        count = max(1, ROWS // places)
+        back = back.reshape(count, places, width).astype(bf16)
+        hold[frame, pl.ds(step * count, count)] = back
         folded = grad.reshape(ROWS // 8, 8, width).sum(axis=0)
         folded_n = (grad * normed).reshape(ROWS // 8, 8, width).sum(axis=0)
         return sums[0] + folded, sums[1] + folded_n
 
     zero = jnp.zeros((8, width), f32)
     shift_sum, scale_sum = lax.fori_loop(0, patches // ROWS, norm_step, (zero, zero))
+    spread.send()
     sum_ref[0, 0:1, :] = jnp.sum(shift_sum, axis=0, keepdims=True)
     sum_ref[0, 1:2, :] = jnp.sum(scale_sum, axis=0, keepdims=True)
+    pl.when(frame == own - 1)(spread.finish)
 
 
 GELU_C = math.sqrt(2.0 / math.pi)
@@ -408,16 +491,19 @@
         out_specs=[
             by_frame(patches, width),
             by_frame(patches, 3 * width),
-            spread,
+            pl.BlockSpec(memory_space=pl.ANY),
             by_frame(patches, pair),
         ],
         out_shape=[
             jax.ShapeDtypeStruct((own, patches, width), bf16),
             jax.ShapeDtypeStruct((own, patches, 3 * width), bf16),
-            jax.ShapeDtypeStruct(x.shape, bf16),
+            jax.ShapeDtypeStruct((n_pos * own, places, width), bf16),
             jax.ShapeDtypeStruct((own, patches, pair), f32),
         ],
-        compiler_params=pltpu.CompilerParams(vmem_limit_bytes=VMEM_LIMIT),
+        scratch_shapes=spread_scratch(own, n_pos, places, width),
+        compiler_params=pltpu.CompilerParams(
+            vmem_limit_bytes=VMEM_LIMIT, collective_id=0, has_side_effects=True
+        ),
         cost_estimate=pl.CostEstimate(
             flops=2 * rows * width * 3 * width + 4 * rows * patches * width,
             bytes_accessed=rows * width * 12 + weight.size * 2,
@@ -448,14 +534,21 @@
             by_frame(2, width),
             resident(weight.shape),
         ],
-        out_specs=[by_frame(patches, 3 * width), spread, by_frame(2, width)],
+        out_specs=[
+            by_frame(patches, 3 * width),
+            pl.BlockSpec(memory_space=pl.ANY),
+            by_frame(2, width),
+        ],
         out_shape=[
             jax.ShapeDtypeStruct((own, patches, 3 * width), bf16),
-            jax.ShapeDtypeStruct(x.shape, bf16),
+            jax.ShapeDtypeStruct((n_pos * own, places, width), bf16),
             jax.ShapeDtypeStruct((own, 2, width), f32),
         ],
-        scratch_shapes=[pltpu.VMEM((patches, width), f32)],
-        compiler_params=pltpu.CompilerParams(vmem_limit_bytes=VMEM_LIMIT),
+        scratch_shapes=[pltpu.VMEM((patches, width), f32)]
+        + spread_scratch(own, n_pos, places, width),
+        compiler_params=pltpu.CompilerParams(
+            vmem_limit_bytes=VMEM_LIMIT, collective_id=1, has_side_effects=True
+        ),
         cost_estimate=pl.CostEstimate(
             flops=2 * rows * width * 3 * width + 10 * rows * patches * width,
             bytes_accessed=rows * width * 16 + weight.size * 2,
@@ -655,8 +748,7 @@
     own_frames = lax.dynamic_slice_in_dim(per_frame, me * own, own, 0)
 
     own_mods = own_frames[:, : 2 * width].reshape(own, 2, width)
-    h_one, qkv_one, o_one_space, lse_one = call_space_forward(x_space, own_mods, spatial_in)
-    o_one = exchange(o_one_space).reshape(frames, places, width)
+    h_one, qkv_one, o_one, lse_one = call_space_forward(x_space, own_mods, spatial_in)
 
     def turn(values):
         return values.transpose(1, 0, 2)
@@ -671,10 +763,9 @@
     )
     block_out = turn(block_turned)
     grad_o_space = exchange(turn(grad_o_one))
-    grad_qkv_one, back_one, sums_one = call_space_backward(
+    grad_qkv_one, back_places, sums_one = call_space_backward(
         grad_o_space, qkv_one, lse_one, x_space, own_mods, spatial_in
     )
-    back_places = exchange(back_one).reshape(frames, places, width)
     grad_tokens = (turn(grad_one) + back_places.astype(f32)).astype(bf16)
 
     def own_columns(values):
@@ -699,6 +790,9 @@
     grad_pre = dot_high(grad_cond, second_w.T) * silu_grad(pre_cond)
     g_first = dot_high(own_columns(freq).T, grad_pre)
 
+    h_two, grad_qkv_two, o_two, grad_y_two, o_one, grad_y_one, grad_qkv_one = lax.optimization_barrier(
+        (h_two, grad_qkv_two, o_two, grad_y_two, o_one, grad_y_one, grad_qkv_one)
+    )
     early = partial(reduce_rows, n_pos=n_pos, n_clip=n_clip, clip_first=False)
     late = partial(reduce_rows, n_pos=n_pos, n_clip=n_clip, clip_first=True)
     g_hidden_up = early(weight_grad(h_three, grad_u))

time: 604 us -> 624 us (1.033)
  Pallas kernels: 231 us -> 261 us
  starting transfers between devices: 78.8 us -> 68.1 us
    ppermute x44, waiting for transfers between devices: 79.4 us -> 106 us  [swap(): return lax.ppermute(values, axis, [(i, i ^ bit) for i in range(size)])]
    all_to_all x4 -> x2, waiting for transfers between devices: 40.9 us -> 15.2 us  [exchange(): got = lax.all_to_all(sent, 'pos', split_axis=0, concat_axis=0, tiled=True)]
    pallas_call x1, Pallas kernels: 36.1 us -> 53 us  [call_space_forward(): pl.pallas_call(space_forward, grid=(own,), in_specs=[spread, by_frame(2,...]
    all_to_all x4 -> x2, starting transfers between devices: 26.3 us -> 12.9 us  [exchange(): got = lax.all_to_all(sent, 'pos', split_axis=0, concat_axis=0, tiled=True)]
    pallas_call x1, Pallas kernels: 39 us -> 51.1 us  [call_space_backward(): pl.pallas_call(space_backward, grid=(own,), in_specs=[spread, by_frame(pa...]
    unnamed x100 -> x104, local copies, waits for them, and re-layouts: 17.5 us -> 14.5 us
  transfers between devices with their start and end apart: 48 -> 46, of which waited for: 22 -> 17; matrix products, arithmetic and copies ran while one was open for 24% -> 23% of each run, Pallas kernels for 7% -> 8%
where the time goes in v3:
time: 624 us; the launch traced here: 618 us
  Pallas kernels  261 us (42%)
  waiting for transfers between devices  122 us (20%)
  starting transfers between devices  68.1 us (11%)
  matrix products  63.7 us (10%)
  local copies, waits for them, and re-layouts  52.6 us (8%)
  other arithmetic  49.3 us (8%)
    pallas_call x1, Pallas kernels, call_middle(): pl.pallas_call(middle, grid=(places // count,), in_specs=[chunk, chunk, c...  156 us
    ppermute x44, waiting for transfers between devices, swap(): return lax.ppermute(values, axis, [(i, i ^ bit) for i in range(size)])  106 us
    ppermute x44, starting transfers between devices, swap(): return lax.ppermute(values, axis, [(i, i ^ bit) for i in range(size)])  55.3 us
    pallas_call x1, Pallas kernels, call_space_forward(): pl.pallas_call(space_forward, grid=(own,), in_specs=[spread, by_frame(2,...  53 us
    pallas_call x1, Pallas kernels, call_space_backward(): pl.pallas_call(space_backward, grid=(own,), in_specs=[spread, by_frame(pa...  51.1 us
    dot_general x13, matrix products, dot_high(): return jnp.dot(left, right, precision=highest, preferred_element_type=f32)  33.9 us
    dot_general x7, matrix products, weight_grad(): jnp.einsum('rd,rk->dk', left, right, preferred_element_type=f32)  29.7 us
    convert_element_type x21, other arithmetic, add(): return (keep.astype(f32) + got.astype(f32)).astype(bf16)  21.3 us
  transfers between devices with their start and end apart: 46, of which 17 were waited for; matrix products, arithmetic and copies ran while one was open for 23% of the time, Pallas kernels for 8%

profile of v3, /device:TPU:0, one launch (start us, length us, event | category | flops | bytes accessed | tf_op | source)
XLA Modules:
  0.0 618.1 jit_solution(6743849760704195175)
XLA Ops:
  0.7 7.7 %all-to-all-start = ((bf16[64,16,768]{2,1,0:T(8,128)(2,1)}), bf16[64,16,768]{2,1,0:T(8,128)(2,1)}, u32[]{:S(2)}, u32[]{:S(2)}) async-start(bf16[64,16,768]{2,1,0:T(8,128)(2,1)} %param.13), calls=%async_computation | async-start | bytes 3145728 | tf_op jit(solution)/shard_map/all_to_all | solution.py:729
  15.1 7.0 %fusion.50 = f32[4,6912]{1,0:T(4,128)S(1)} fusion(bf16[768,6912]{1,0:T(8,128)(2,1)} %param.18, f32[8,768]{1,0:T(8,128)S(1)} %get-tuple-element.136), kind=kOutput, calls=%fused_computation.147 | convolution fusion | flops 254803968 | bytes 10739712 | tf_op jit(solution)/shard_map/dot_general | solution.py:32
  25.1 15.2 %all-to-all-done = bf16[64,16,768]{2,1,0:T(8,128)(2,1)} async-done(((bf16[64,16,768]{2,1,0:T(8,128)(2,1)}), bf16[64,16,768]{2,1,0:T(8,128)(2,1)}, u32[]{:S(2)}, u32[]{:S(2)}) %all-to-all-start) | async-done | bytes 1572896 | tf_op jit(solution)/shard_map/all_to_all | solution.py:729
  40.3 53.0 %space_forward.1 = (bf16[4,256,768]{2,1,0:T(8,128)(2,1)}, bf16[4,256,2304]{2,1,0:T(8,128)(2,1)}, bf16[64,16,768]{2,1,0:T(8,128)(2,1)}, f32[4,256,128]{2,1,0:T(8,128)}) custom-call(bf16[16,4,16,768]{3,2,1,0:T(8,128)(2,1)} %bitcast.x_ref, f32[4,2,768]{2,1,0:T(2,128)} %reshape.227.mod_ref, bf16[768,2304]{1,0:T(8,128)(2,1)} %w_ref.3), custom_call_target="tpu_custom_call" | custom-call | flops 4429185024 | bytes 12976128 | tf_op jit(solution)/shard_map/space_forward/pallas_call | solution.py:487
  93.3 4.6 copy_bitcast_fusion
  97.9 156.5 %middle.1 = (bf16[16,64,768]{2,1,0:T(8,128)(2,1)}, bf16[1024,3072]{1,0:T(8,128)(2,1)}, bf16[1024,768]{1,0:T(8,128)(2,1)}, bf16[1024,768]{1,0:T(8,128)(2,1)}, bf1...) custom-call(bf16[16,64,768]{2,1,0:T(8,128)(2,1)} %get-tuple-element., ...), custom_call_target="tpu_custom_call" | custom-call | flops 31406948352 | bytes 40960000 | tf_op jit(solution)/shard_map/middle/pallas_call | solution.py:581
  254.4 7.9 %convolution_convert_fusion = bf16[3072,768]{1,0:T(8,128)(2,1)S(1)} fusion(bf16[1024,3072]{1,0:T(8,128)(2,1)} %get-tuple-element.63, bf16[1024,768]{1,0:T(8,128)(2,1)} %get-tuple-element.64), kind=kOutput, calls=%fused_computation.2 | convolution fusion | flops 4834197504 | bytes 12582912 | tf_op jit(solution)/shard_map/rd,rk->dk/dot_general | solution.py:51
  265.8 5.4 convolution_convert_fusion.1
  275.4 3.6 collective-permute-done.6
  289.1 5.2 all-to-all-start.1
  298.3 37.5 %collective-permute-done.9 = f32[4,5376]{1,0:T(4,128)S(1)} collective-permute-done((f32[4,5376]{1,0:T(4,128)S(1)}, f32[4,5376]{1,0:T(4,128)S(1)}, u32[]{:S(2)}, u32[]{:S(2)}) %collective-permute-start.9) | collective-permute-done | bytes 86048 | tf_op jit(solution)/shard_map/ppermute | solution.py:638
  338.7 3.4 copy.98
  345.3 10.6 %fusion = f32[8,768]{1,0:T(8,128)} fusion(bf16[768,6912]{1,0:T(8,128)(2,1)} %param.18, f32[4,5376]{1,0:T(4,128)} %collective-permute-done.10, f32[4,5376]{1,0:T(4,128)} %add.268), kind=kOutput, calls=%fused_computation | convolution fusion | flops 396404736 | bytes 8454144 | tf_op jit(solution)/shard_map/dot_general | solution.py:32
  358.1 4.7 reshape.247
  362.8 6.0 constant_dynamic-slice_fusion.2
  370.6 3.3 fusion.3
  378.0 51.1 %space_backward.1 = (bf16[4,256,2304]{2,1,0:T(8,128)(2,1)}, bf16[64,16,768]{2,1,0:T(8,128)(2,1)}, f32[4,2,768]{2,1,0:T(2,128)}) custom-call(bf16[16,4,16,768]{3,2,1,0:T(8,128)(2,1)} %bitcast.11.go_ref, bf16[4,256,2304]{2,1,0:T(8,128)(2,1)} %get-tuple-element.42.qkv_ref, f32[4,256,128]{2,1,0:T(8,128)} %get-tuple-element.43.lse_ref, ...), custom_call_target="tpu_custom_call" | custom-call | flops 5637144576 | bytes 16121856 | tf_op jit(solution)/shard_map/space_backward/pallas_call | solution.py:526
  429.1 5.8 convolution_convert_fusion.4
  434.9 3.5 convolution_convert_fusion.3
  438.4 4.1 convolution_convert_fusion.2
  462.3 5.0 fusion.5
  468.8 3.3 collective-permute-done.4
  476.0 3.7 fusion.22
  496.9 3.5 reshape.236
  500.4 4.4 constant_dynamic-slice_fusion.9
  532.0 3.8 collective-permute-done.13
  540.6 3.4 collective-permute-done.19
  547.6 4.0 collective-permute-done.20
  559.8 18.7 %collective-permute-done.24 = bf16[4,48,768]{2,1,0:T(8,128)(2,1)S(1)} collective-permute-done((bf16[4,48,768]{2,1,0:T(8,128)(2,1)S(1)}, bf16[4,48,768]{2,1,0:T(8,128)(2,1)S(1)}, u32[]{:S(2)}, u32[]{:S(2)}) %collective-permute-start.24) | collective-permute-done | bytes 294944 | tf_op jit(solution)/shard_map/ppermute | solution.py:638
  594.6 6.8 %collective-permute-done.30 = bf16[2,48,2304]{2,1,0:T(8,128)(2,1)S(1)} collective-permute-done((bf16[2,48,2304]{2,1,0:T(8,128)(2,1)S(1)}, bf16[2,48,2304]{2,1,0:T(8,128)(2,1)S(1)}, u32[]{:S(2)}, u32[]{:S(2)}) %collective-permute-start.30) | collective-permute-done | bytes 442400 | tf_op jit(solution)/shard_map/ppermute | solution.py:638
  604.5 6.3 %collective-permute-done.31 = bf16[1,48,2304]{2,1,0:T(8,128)(2,1)S(1)} collective-permute-done((bf16[1,48,2304]{2,1,0:T(8,128)(2,1)S(1)}, bf16[1,48,2304]{2,1,0:T(8,128)(2,1)S(1)}, u32[]{:S(2)}, u32[]{:S(2)}) %collective-permute-start.31) | collective-permute-done | bytes 221216 | tf_op jit(solution)/shard_map/ppermute | solution.py:638
  613.3 3.6 collective-permute-done.32
  (283 shorter events, 153.6 us)
Async XLA Ops:
  0.7 39.6 %all-to-all-start = ((bf16[64,16,768]{2,1,0:T(8,128)(2,1)}), bf16[64,16,768]{2,1,0:T(8,128)(2,1)}, u32[]{:S(2)}, u32[]{:S(2)}) async-start(bf16[64,16,768]{2,1,0:T(8,128)(2,1)} %param.13), calls=%async_computation | async-start | bytes 3145728 | tf_op jit(solution)/shard_map/all_to_all | solution.py:729
  265.2 90.8 %collective-permute-start.38 = (bf16[8,192,768]{2,1,0:T(8,128)(2,1)}, bf16[8,192,768]{2,1,0:T(8,128)(2,1)S(1)}, u32[]{:S(2)}, u32[]{:S(2)}) collective-permute-start(bf16[8,192,768]{2,1,0:T(8,128)(2,1)} %dynamic-slice_bitcast_fusion), channel_id=1, source_target_pairs={{0,1},{1,0},{2,3},{3,2},{4,5},{5,4},{6,7},{7,6},{8,9},{9,8},{10,11... | collective-permute-start | bytes 7077896 | tf_op jit(solution)/shard_map/ppermute | solution.py:638
  274.1 96.5 %collective-permute-start.33 = (bf16[8,48,3072]{2,1,0:T(8,128)(2,1)}, bf16[8,48,3072]{2,1,0:T(8,128)(2,1)}, u32[]{:S(2)}, u32[]{:S(2)}) collective-permute-start(bf16[8,48,3072]{2,1,0:T(8,128)(2,1)} %dynamic-slice_bitcast_fusion.1), channel_id=1, source_target_pairs={{0,1},{1,0},{2,3},{3,2},{4,5},{5,4},{6,7},{7,6},{8,9},{9,8},{10,11... | collective-permute-start | bytes 7077896 | tf_op jit(solution)/shard_map/ppermute | solution.py:638
  284.7 9.6 %collective-permute-start.8 = (f32[4,5376]{1,0:T(4,128)}, f32[4,5376]{1,0:T(4,128)}, u32[]{:S(2)}, u32[]{:S(2)}) collective-permute-start(f32[4,5376]{1,0:T(4,128)} %add.266), channel_id=1, source_target_pairs={{0,4},{1,5},{2,6},{3,7},{4,0},{5,1},{6,2},{7,3},{8,12},{9,13},{10,... | collective-permute-start | bytes 258056 | tf_op jit(solution)/shard_map/ppermute | solution.py:638
  289.1 88.8 %all-to-all-start.1 = ((bf16[64,16,768]{2,1,0:T(8,128)(2,1)}), bf16[64,16,768]{2,1,0:T(8,128)(2,1)}, u32[]{:S(2)}, u32[]{:S(2)}) async-start(bf16[64,16,768]{2,1,0:T(8,128)(2,1)} %copy.85), calls=%async_computation.1 | async-start | bytes 3145728 | tf_op jit(solution)/shard_map/all_to_all | solution.py:729
  295.3 40.5 %collective-permute-start.9 = (f32[4,5376]{1,0:T(4,128)S(1)}, f32[4,5376]{1,0:T(4,128)S(1)}, u32[]{:S(2)}, u32[]{:S(2)}) collective-permute-start(f32[4,5376]{1,0:T(4,128)S(1)} %add.267), channel_id=1, source_target_pairs={{0,8},{1,9},{2,10},{3,11},{4,12},{5,13},{6,14},{7,15},{8,0},{9,1},... | collective-permute-start | bytes 258056 | tf_op jit(solution)/shard_map/ppermute | solution.py:638
  370.0 115.8 %collective-permute-start.39 = (bf16[8,192,384]{2,1,0:T(8,128)(2,1)}, bf16[8,192,384]{2,1,0:T(8,128)(2,1)}, u32[]{:S(2)}, u32[]{:S(2)}) collective-permute-start(bf16[8,192,384]{2,1,0:T(8,128)(2,1)} %bitcast.210), channel_id=1, source_target_pairs={{0,16},{16,0},{1,17},{17,1},{2,18},{18,2},{3,19},{19,3},{4,20},{20... | collective-permute-start | bytes 3538952 | tf_op jit(solution)/shard_map/ppermute | solution.py:638
  376.5 112.6 %collective-permute-start.34 = (bf16[4,48,3072]{2,1,0:T(8,128)(2,1)}, bf16[4,48,3072]{2,1,0:T(8,128)(2,1)}, u32[]{:S(2)}, u32[]{:S(2)}) collective-permute-start(bf16[4,48,3072]{2,1,0:T(8,128)(2,1)} %dynamic-slice_bitcast_fusion.3), channel_id=1, source_target_pairs={{0,2},{1,3},{2,0},{3,1},{4,6},{5,7},{6,4},{7,5},{8,10},{9,11},{10,... | collective-permute-start | bytes 3538952 | tf_op jit(solution)/shard_map/ppermute | solution.py:638
  445.3 110.2 %collective-permute-start.28 = (bf16[8,48,2304]{2,1,0:T(8,128)(2,1)}, bf16[8,48,2304]{2,1,0:T(8,128)(2,1)}, u32[]{:S(2)}, u32[]{:S(2)}) collective-permute-start(bf16[8,48,2304]{2,1,0:T(8,128)(2,1)} %dynamic-slice_bitcast_fusion.2), channel_id=1, source_target_pairs={{0,1},{1,0},{2,3},{3,2},{4,5},{5,4},{6,7},{7,6},{8,9},{9,8},{10,11... | collective-permute-start | bytes 5308424 | tf_op jit(solution)/shard_map/ppermute | solution.py:638
  446.8 8.1 %collective-permute-start.1 = (f32[4,1536]{1,0:T(4,128)}, f32[4,1536]{1,0:T(4,128)}, u32[]{:S(2)}, u32[]{:S(2)}) collective-permute-start(f32[4,1536]{1,0:T(4,128)} %fusion.57), channel_id=1, source_target_pairs={{0,1},{1,0},{2,3},{3,2},{4,5},{5,4},{6,7},{7,6},{8,9},{9,8},{10,11... | collective-permute-start | bytes 73736 | tf_op jit(solution)/shard_map/ppermute | solution.py:638
  458.6 54.8 %collective-permute-start.22 = (bf16[8,48,1536]{2,1,0:T(8,128)(2,1)}, bf16[8,48,1536]{2,1,0:T(8,128)(2,1)}, u32[]{:S(2)}, u32[]{:S(2)}) collective-permute-start(bf16[8,48,1536]{2,1,0:T(8,128)(2,1)} %dynamic-slice_bitcast_fusion.4), channel_id=1, source_target_pairs={{0,1},{1,0},{2,3},{3,2},{4,5},{5,4},{6,7},{7,6},{8,9},{9,8},{10,11... | collective-permute-start | bytes 3538952 | tf_op jit(solution)/shard_map/ppermute | solution.py:638
  476.0 16.9 %collective-permute-start.11 = (bf16[8,48,1152]{2,1,0:T(8,128)(2,1)S(1)}, bf16[8,48,1152]{2,1,0:T(8,128)(2,1)S(1)}, u32[]{:S(2)}, u32[]{:S(2)}) collective-permute-start(bf16[8,48,1152]{2,1,0:T(8,128)(2,1)S(1)} %dynamic-slice_bitcast_fusion.7), channel_id=1, source_target_pairs={{0,1},{1,0},{2,3},{3,2},{4,5},{5,4},{6,7},{7,6},{8,9},{9,8},{10,11... | collective-permute-start | bytes 2654216 | tf_op jit(solution)/shard_map/ppermute | solution.py:638
  485.9 9.1 %collective-permute-start.16 = (bf16[8,48,1152]{2,1,0:T(8,128)(2,1)S(1)}, bf16[8,48,1152]{2,1,0:T(8,128)(2,1)S(1)}, u32[]{:S(2)}, u32[]{:S(2)}) collective-permute-start(bf16[8,48,1152]{2,1,0:T(8,128)(2,1)S(1)} %dynamic-slice_bitcast_fusion.6), channel_id=1, source_target_pairs={{0,1},{1,0},{2,3},{3,2},{4,5},{5,4},{6,7},{7,6},{8,9},{9,8},{10,11... | collective-permute-start | bytes 2654216 | tf_op jit(solution)/shard_map/ppermute | solution.py:638
  489.1 16.7 %collective-permute-start.40 = (bf16[4,192,384]{2,1,0:T(8,128)(2,1)}, bf16[4,192,384]{2,1,0:T(8,128)(2,1)}, u32[]{:S(2)}, u32[]{:S(2)}) collective-permute-start(bf16[4,192,384]{2,1,0:T(8,128)(2,1)} %dynamic-slice_bitcast_fusion.8), channel_id=1, source_target_pairs={{0,2},{1,3},{2,0},{3,1},{4,6},{5,7},{6,4},{7,5},{8,10},{9,11},{10,... | collective-permute-start | bytes 1769480 | tf_op jit(solution)/shard_map/ppermute | solution.py:638
  492.9 16.3 %collective-permute-start.35 = (bf16[2,48,3072]{2,1,0:T(8,128)(2,1)}, bf16[2,48,3072]{2,1,0:T(8,128)(2,1)}, u32[]{:S(2)}, u32[]{:S(2)}) collective-permute-start(bf16[2,48,3072]{2,1,0:T(8,128)(2,1)} %dynamic-slice_bitcast_fusion.9), channel_id=1, source_target_pairs={{0,4},{1,5},{2,6},{3,7},{4,0},{5,1},{6,2},{7,3},{8,12},{9,13},{10,... | collective-permute-start | bytes 1769480 | tf_op jit(solution)/shard_map/ppermute | solution.py:638
  494.9 28.5 %collective-permute-start.12 = (bf16[4,48,1152]{2,1,0:T(8,128)(2,1)}, bf16[4,48,1152]{2,1,0:T(8,128)(2,1)}, u32[]{:S(2)}, u32[]{:S(2)}) collective-permute-start(bf16[4,48,1152]{2,1,0:T(8,128)(2,1)} %dynamic-slice_bitcast_fusion.11), channel_id=1, source_target_pairs={{0,2},{1,3},{2,0},{3,1},{4,6},{5,7},{6,4},{7,5},{8,10},{9,11},{10,... | collective-permute-start | bytes 1327112 | tf_op jit(solution)/shard_map/ppermute | solution.py:638
  505.7 19.9 %collective-permute-start.17 = (bf16[8,48,576]{2,1,0:T(8,128)(2,1)}, bf16[8,48,576]{2,1,0:T(8,128)(2,1)}, u32[]{:S(2)}, u32[]{:S(2)}) collective-permute-start(bf16[8,48,576]{2,1,0:T(8,128)(2,1)} %bitcast.212), channel_id=1, source_target_pairs={{0,16},{16,0},{1,17},{17,1},{2,18},{18,2},{3,19},{19,3},{4,20},{20... | collective-permute-start | bytes 1327112 | tf_op jit(solution)/shard_map/ppermute | solution.py:638
  509.3 17.7 %collective-permute-start.41 = (bf16[2,192,384]{2,1,0:T(8,128)(2,1)}, bf16[2,192,384]{2,1,0:T(8,128)(2,1)}, u32[]{:S(2)}, u32[]{:S(2)}) collective-permute-start(bf16[2,192,384]{2,1,0:T(8,128)(2,1)} %dynamic-slice_bitcast_fusion.12), channel_id=1, source_target_pairs={{0,4},{1,5},{2,6},{3,7},{4,0},{5,1},{6,2},{7,3},{8,12},{9,13},{10,... | collective-permute-start | bytes 884744 | tf_op jit(solution)/shard_map/ppermute | solution.py:638
  513.4 15.9 %collective-permute-start.36 = (bf16[1,48,3072]{2,1,0:T(8,128)(2,1)}, bf16[1,48,3072]{2,1,0:T(8,128)(2,1)}, u32[]{:S(2)}, u32[]{:S(2)}) collective-permute-start(bf16[1,48,3072]{2,1,0:T(8,128)(2,1)} %constant_dynamic-slice_fusion.3), channel_id=1, source_target_pairs={{0,8},{1,9},{2,10},{3,11},{4,12},{5,13},{6,14},{7,15},{8,0},{9,1},... | collective-permute-start | bytes 884744 | tf_op jit(solution)/shard_map/ppermute | solution.py:638
  523.4 34.2 %collective-permute-start.23 = (bf16[8,48,768]{2,1,0:T(8,128)(2,1)S(1)}, bf16[8,48,768]{2,1,0:T(8,128)(2,1)S(1)}, u32[]{:S(2)}, u32[]{:S(2)}) collective-permute-start(bf16[8,48,768]{2,1,0:T(8,128)(2,1)S(1)} %bitcast.259), channel_id=1, source_target_pairs={{0,16},{16,0},{1,17},{17,1},{2,18},{18,2},{3,19},{19,3},{4,20},{20... | collective-permute-start | bytes 1769480 | tf_op jit(solution)/shard_map/ppermute | solution.py:638
  525.6 10.2 %collective-permute-start.13 = (bf16[2,48,1152]{2,1,0:T(8,128)(2,1)S(1)}, bf16[2,48,1152]{2,1,0:T(8,128)(2,1)S(1)}, u32[]{:S(2)}, u32[]{:S(2)}) collective-permute-start(bf16[2,48,1152]{2,1,0:T(8,128)(2,1)S(1)} %dynamic-slice_bitcast_fusion.15), channel_id=1, source_target_pairs={{0,4},{1,5},{2,6},{3,7},{4,0},{5,1},{6,2},{7,3},{8,12},{9,13},{10,... | collective-permute-start | bytes 663560 | tf_op jit(solution)/shard_map/ppermute | solution.py:638
  527.0 9.0 %collective-permute-start.18 = (bf16[4,48,576]{2,1,0:T(8,128)(2,1)S(1)}, bf16[4,48,576]{2,1,0:T(8,128)(2,1)S(1)}, u32[]{:S(2)}, u32[]{:S(2)}) collective-permute-start(bf16[4,48,576]{2,1,0:T(8,128)(2,1)S(1)} %dynamic-slice_bitcast_fusion.14), channel_id=1, source_target_pairs={{0,2},{1,3},{2,0},{3,1},{4,6},{5,7},{6,4},{7,5},{8,10},{9,11},{10,... | collective-permute-start | bytes 663560 | tf_op jit(solution)/shard_map/ppermute | solution.py:638
  529.3 9.8 %collective-permute-start.42 = (bf16[1,192,384]{2,1,0:T(8,128)(2,1)S(1)}, bf16[1,192,384]{2,1,0:T(8,128)(2,1)S(1)}, u32[]{:S(2)}, u32[]{:S(2)}) collective-permute-start(bf16[1,192,384]{2,1,0:T(8,128)(2,1)S(1)} %constant_dynamic-slice_fusion.1), channel_id=1, source_target_pairs={{0,8},{1,9},{2,10},{3,11},{4,12},{5,13},{6,14},{7,15},{8,0},{9,1},... | collective-permute-start | bytes 442376 | tf_op jit(solution)/shard_map/ppermute | solution.py:638
  535.8 18.8 %collective-permute-start.37 = (bf16[48,3072]{1,0:T(8,128)(2,1)S(1)}, bf16[48,3072]{1,0:T(8,128)(2,1)S(1)}, u32[]{:S(2)}, u32[]{:S(2)}) collective-permute-start(bf16[48,3072]{1,0:T(8,128)(2,1)S(1)} %fusion.32), channel_id=1, source_target_pairs={{0,16},{16,0},{1,17},{17,1},{2,18},{18,2},{3,19},{19,3},{4,20},{20... | collective-permute-start | bytes 884744 | tf_op jit(solution)/shard_map/ppermute | solution.py:638
  535.9 10.5 %collective-permute-start.14 = (bf16[1,48,1152]{2,1,0:T(8,128)(2,1)S(1)}, bf16[1,48,1152]{2,1,0:T(8,128)(2,1)S(1)}, u32[]{:S(2)}, u32[]{:S(2)}) collective-permute-start(bf16[1,48,1152]{2,1,0:T(8,128)(2,1)S(1)} %constant_dynamic-slice_fusion.10), channel_id=1, source_target_pairs={{0,8},{1,9},{2,10},{3,11},{4,12},{5,13},{6,14},{7,15},{8,0},{9,1},... | collective-permute-start | bytes 331784 | tf_op jit(solution)/shard_map/ppermute | solution.py:638
  544.0 7.9 %collective-permute-start.43 = (bf16[192,384]{1,0:T(8,128)(2,1)S(1)}, bf16[192,384]{1,0:T(8,128)(2,1)S(1)}, u32[]{:S(2)}, u32[]{:S(2)}) collective-permute-start(bf16[192,384]{1,0:T(8,128)(2,1)S(1)} %fusion.36), channel_id=1, source_target_pairs={{0,16},{16,0},{1,17},{17,1},{2,18},{18,2},{3,19},{19,3},{4,20},{20... | collective-permute-start | bytes 442376 | tf_op jit(solution)/shard_map/ppermute | solution.py:638
  551.6 8.2 %collective-permute-start.15 = (bf16[48,1152]{1,0:T(8,128)(2,1)S(1)}, bf16[48,1152]{1,0:T(8,128)(2,1)S(1)}, u32[]{:S(2)}, u32[]{:S(2)}) collective-permute-start(bf16[48,1152]{1,0:T(8,128)(2,1)S(1)} %fusion.38), channel_id=1, source_target_pairs={{0,16},{16,0},{1,17},{17,1},{2,18},{18,2},{3,19},{19,3},{4,20},{20... | collective-permute-start | bytes 331784 | tf_op jit(solution)/shard_map/ppermute | solution.py:638
  551.8 29.0 %collective-permute-start.21 = (bf16[48,576]{1,0:T(8,128)(2,1)S(1)}, bf16[48,576]{1,0:T(8,128)(2,1)S(1)}, u32[]{:S(2)}, u32[]{:S(2)}) collective-permute-start(bf16[48,576]{1,0:T(8,128)(2,1)S(1)} %fusion.40), channel_id=1, source_target_pairs={{0,16},{16,0},{1,17},{17,1},{2,18},{18,2},{3,19},{19,3},{4,20},{20... | collective-permute-start | bytes 165896 | tf_op jit(solution)/shard_map/ppermute | solution.py:638
  557.5 33.2 %collective-permute-start.29 = (bf16[4,48,2304]{2,1,0:T(8,128)(2,1)S(1)}, bf16[4,48,2304]{2,1,0:T(8,128)(2,1)S(1)}, u32[]{:S(2)}, u32[]{:S(2)}) collective-permute-start(bf16[4,48,2304]{2,1,0:T(8,128)(2,1)S(1)} %dynamic-slice_bitcast_fusion.5), channel_id=1, source_target_pairs={{0,2},{1,3},{2,0},{3,1},{4,6},{5,7},{6,4},{7,5},{8,10},{9,11},{10,... | collective-permute-start | bytes 2654216 | tf_op jit(solution)/shard_map/ppermute | solution.py:638
  557.7 20.8 %collective-permute-start.24 = (bf16[4,48,768]{2,1,0:T(8,128)(2,1)S(1)}, bf16[4,48,768]{2,1,0:T(8,128)(2,1)S(1)}, u32[]{:S(2)}, u32[]{:S(2)}) collective-permute-start(bf16[4,48,768]{2,1,0:T(8,128)(2,1)S(1)} %dynamic-slice_bitcast_fusion.13), channel_id=1, source_target_pairs={{0,2},{1,3},{2,0},{3,1},{4,6},{5,7},{6,4},{7,5},{8,10},{9,11},{10,... | collective-permute-start | bytes 884744 | tf_op jit(solution)/shard_map/ppermute | solution.py:638
  591.0 10.4 %collective-permute-start.30 = (bf16[2,48,2304]{2,1,0:T(8,128)(2,1)S(1)}, bf16[2,48,2304]{2,1,0:T(8,128)(2,1)S(1)}, u32[]{:S(2)}, u32[]{:S(2)}) collective-permute-start(bf16[2,48,2304]{2,1,0:T(8,128)(2,1)S(1)} %dynamic-slice_bitcast_fusion.10), channel_id=1, source_target_pairs={{0,4},{1,5},{2,6},{3,7},{4,0},{5,1},{6,2},{7,3},{8,12},{9,13},{10,... | collective-permute-start | bytes 1327112 | tf_op jit(solution)/shard_map/ppermute | solution.py:638
  601.5 9.3 %collective-permute-start.31 = (bf16[1,48,2304]{2,1,0:T(8,128)(2,1)S(1)}, bf16[1,48,2304]{2,1,0:T(8,128)(2,1)S(1)}, u32[]{:S(2)}, u32[]{:S(2)}) collective-permute-start(bf16[1,48,2304]{2,1,0:T(8,128)(2,1)S(1)} %constant_dynamic-slice_fusion.4), channel_id=1, source_target_pairs={{0,8},{1,9},{2,10},{3,11},{4,12},{5,13},{6,14},{7,15},{8,0},{9,1},... | collective-permute-start | bytes 663560 | tf_op jit(solution)/shard_map/ppermute | solution.py:638
  (63 other events, 598.0 us)

commit v4 on v3

--- a/solution.py
+++ b/solution.py
@@ -648,56 +648,257 @@
     return values
 
 
-def butterfly(values, axis, size):
-    for bit in bits_of(size):
-        values = values + swap(values, axis, size, bit)
-    return values
-
-
-def halve(values, index, axis):
-    def pick(at):
-        return lax.dynamic_index_in_dim(values, at, axis, keepdims=False)
-
-    return pick(index), pick(1 - index)
-
-
-def reduce_rows(grad, n_pos, n_clip, clip_first):
-    rows, cols = grad.shape
-    block = rows // n_pos
-    me, clip_at = lax.axis_index("pos"), lax.axis_index("clip")
-    values = grad.reshape(n_pos, block, cols)
-
-    def add(keep, got):
-        return (keep.astype(f32) + got.astype(f32)).astype(bf16)
-
-    def pos_step(values, bit):
-        left = values.shape[0] // 2
-        split = values.reshape(left, 2, *values.shape[1:])
-        keep, send = halve(split, lax.rem(me // bit, 2), 1)
-        return add(keep, swap(send, "pos", n_pos, bit))
-
-    bits = bits_of(n_pos)
-    values = pos_step(values, bits[0])
-    if clip_first:
-        for bit in reversed(bits_of(n_clip)):
-            split = values.reshape(*values.shape[:2], 2, values.shape[2] // 2)
-            keep, send = halve(split, lax.rem(clip_at // bit, 2), 2)
-            values = add(keep, swap(send, "clip", n_clip, bit))
-    for bit in bits[1:]:
-        values = pos_step(values, bit)
-    values = values[0]
-    for bit in bits_of(n_clip):
-        got = swap(values, "clip", n_clip, bit)
-        if clip_first:
-            upper = lax.rem(clip_at // bit, 2) == 1
-            values = jnp.concatenate(
-                [jnp.where(upper, got, values), jnp.where(upper, values, got)], axis=1
-            )
-        elif 2 * bit == n_clip:
-            return values.astype(f32) + got.astype(f32)
+def dot_exact(left, right):
+    parts = []
+    for _ in range(3):
+        part = left.astype(bf16)
+        parts.append(part)
+        left = left - part.astype(f32)
+    count = parts[0].shape[0]
+    got = jnp.dot(jnp.concatenate(parts, axis=0), right, preferred_element_type=f32)
+    return got[:count] + (got[count : 2 * count] + got[2 * count :])
+
+
+def flow_stages(n_pos, n_clip, clip_first):
+    pos = [("pos", bit, "halve") for bit in bits_of(n_pos)]
+    clip = bits_of(n_clip)
+    if not clip_first:
+        return pos + [("clip", bit, "sum") for bit in clip]
+    first = [("clip", clip[0], "columns")]
+    last = [("clip", clip[0], "gather")]
+    return pos[:1] + first + pos[1:] + [("clip", bit, "sum") for bit in clip[1:]] + last
+
+
+def flow_shapes(stages, n_pos, block, cols):
+    lead = n_pos.bit_length() - 1
+    shapes = []
+    for _, _, what in stages:
+        if what == "halve":
+            lead -= 1
+        elif what == "columns":
+            cols //= 2
+        shapes.append((2,) * lead + (block, cols))
+    return shapes
+
+
+class Flow:
+    def __init__(self, number, stages, grad, out, keep, gots, sems, place):
+        self.number, self.stages = number, stages
+        self.grad, self.out, self.keep, self.gots = grad, out, keep, gots
+        self.send_sem, self.recv_sem, self.keep_sem = sems
+        self.place = place
+
+    def side(self, stage):
+        axis, bit, _ = self.stages[stage]
+        return lax.rem(self.place[axis] // bit, 2)
+
+    def columns(self, side, width):
+        return pl.ds(pl.multiple_of(side * width, width), width)
+
+    def part(self, ref, stage, side):
+        what = self.stages[stage][2]
+        lead = len(ref.shape) - 2
+        if what == "halve":
+            return (slice(None),) * (lead - 1) + (side,)
+        if what == "columns":
+            half = ref.shape[-1] // 2
+            return (slice(None),) * (lead + 1) + (self.columns(side, half),)
+        return None
+
+    def held(self, stage):
+        if stage == 0:
+            return self.grad
+        return self.keep if stage == 1 else self.gots[stage - 1]
+
+    def copy(self, stage):
+        axis, bit, _ = self.stages[stage]
+        side = self.side(stage)
+        source = self.held(stage)
+        at = self.part(source, stage, 1 - side)
+        return pltpu.make_async_remote_copy(
+            source if at is None else source.at[at],
+            self.gots[stage],
+            self.send_sem.at[self.number, stage],
+            self.recv_sem.at[self.number, stage],
+            device_id={axis: self.place[axis] + bit * (1 - 2 * side)},
+            device_id_type=pl.DeviceIdType.MESH,
+        )
+
+    def own(self):
+        at = self.part(self.grad, 0, self.side(0))
+        return pltpu.make_async_copy(self.grad.at[at], self.keep, self.keep_sem.at[self.number])
+
+    def start(self):
+        self.copy(0).start()
+        self.own().start()
+
+    def take(self, stage):
+        self.copy(stage).wait_recv()
+        if stage == 0:
+            self.own().wait()
+        what = self.stages[stage][2]
+        got = self.gots[stage]
+        side = self.side(stage)
+        last = stage == len(self.stages) - 1
+        lead = len(got.shape) - 2
+        if what == "gather":
+            half = got.shape[-1]
+            self.out[:, self.columns(side, half)] = self.held(stage)[...].astype(f32)
+            self.out[:, self.columns(1 - side, half)] = got[...].astype(f32)
+            return
+        if last:
+            self.out[...] = self.held(stage)[...].astype(f32) + got[...].astype(f32)
+            return
+        target = self.keep if stage == 0 else got
+
+        def one(index, _):
+            at = tuple(lax.rem(index // (1 << i), 2) for i in range(lead))
+            if stage == 0:
+                mine = self.keep[at]
+            elif what == "halve":
+                mine = self.held(stage)[at + (side,)]
+            elif what == "columns":
+                mine = self.held(stage)[at + (slice(None), self.columns(side, got.shape[-1]))]
+            else:
+                mine = self.held(stage)[at]
+            target[at] = mine + got[at]
+            return 0
+
+        lax.fori_loop(0, 1 << lead, one, 0)
+        self.copy(stage + 1).start()
+
+    def finish(self):
+        for stage in range(len(self.stages)):
+            self.copy(stage).wait_send()
+
+
+class Butterfly:
+    def __init__(self, n_pos, n_clip, values, out, got, acc, sems, place):
+        self.pos_bits, self.clip_bits = bits_of(n_pos), bits_of(n_clip)
+        self.values, self.out, self.got, self.acc = values, out, got, acc
+        self.send_sem, self.recv_sem = sems
+        self.place = place
+        self.count = len(self.pos_bits) + len(self.clip_bits)
+
+    def copy(self, stage):
+        if stage < len(self.pos_bits):
+            axis, bit = "pos", self.pos_bits[stage]
+            source = self.values if stage == 0 else self.acc.at[stage - 1]
+            target = self.got.at[stage]
         else:
-            values = add(values, got)
-    return values.astype(f32)
+            axis, bit = "clip", self.clip_bits[stage - len(self.pos_bits)]
+            source, target = self.out.at[pl.ds(0, bit)], self.out.at[pl.ds(bit, bit)]
+        side = lax.rem(self.place[axis] // bit, 2)
+        return pltpu.make_async_remote_copy(
+            source,
+            target,
+            self.send_sem.at[stage],
+            self.recv_sem.at[stage],
+            device_id={axis: self.place[axis] + bit * (1 - 2 * side)},
+            device_id_type=pl.DeviceIdType.MESH,
+        )
+
+    def start(self):
+        self.copy(0).start()
+
+    def take(self, stage):
+        self.copy(stage).wait_recv()
+        last = len(self.pos_bits) - 1
+        if stage <= last:
+            mine = self.values[...] if stage == 0 else self.acc[stage - 1]
+            if stage < last:
+                self.acc[stage] = mine + self.got[stage]
+            else:
+                self.out[0] = mine + self.got[stage]
+        if stage + 1 < self.count:
+            self.copy(stage + 1).start()
+
+    def finish(self):
+        for stage in range(self.count):
+            self.copy(stage).wait_send()
+
+
+def combine(n_pos, n_clip, kinds, *refs):
+    count = len(kinds)
+    grads, small = refs[:count], refs[count]
+    outs, small_out = refs[count + 1 : 2 * count + 1], refs[2 * count + 1]
+    rest = list(refs[2 * count + 2 :])
+    place = {"pos": lax.axis_index("pos"), "clip": lax.axis_index("clip")}
+    partners = [("pos", bit) for bit in bits_of(n_pos)] + [("clip", bit) for bit in bits_of(n_clip)]
+    barrier = pltpu.get_barrier_semaphore()
+    for axis, bit in partners:
+        side = lax.rem(place[axis] // bit, 2)
+        pl.semaphore_signal(
+            barrier,
+            inc=1,
+            device_id={axis: place[axis] + bit * (1 - 2 * side)},
+            device_id_type=pl.DeviceIdType.MESH,
+        )
+    pl.semaphore_wait(barrier, len(partners))
+
+    sems = rest[:3]
+    small_sems = rest[3:5]
+    got, acc = rest[5:7]
+    rest = rest[7:]
+    flows = []
+    for number, clip_first in enumerate(kinds):
+        stages = flow_stages(n_pos, n_clip, clip_first)
+        keep, gots = rest[0], rest[1 : 1 + len(stages)]
+        rest = rest[1 + len(stages) :]
+        flows.append(Flow(number, stages, grads[number], outs[number], keep, gots, sems, place))
+    tree = Butterfly(n_pos, n_clip, small, small_out, got, acc, small_sems, place)
+    tree.start()
+    for flow in flows:
+        flow.start()
+    for stage in range(max(tree.count, max(len(flow.stages) for flow in flows))):
+        if stage < tree.count:
+            tree.take(stage)
+        for flow in flows:
+            if stage < len(flow.stages):
+                flow.take(stage)
+    tree.finish()
+    for flow in flows:
+        flow.finish()
+
+
+def call_combine(grads, kinds, small, n_pos, n_clip):
+    lead = n_pos.bit_length() - 1
+    most = lead + len(bits_of(n_clip)) + 1
+    views, out_shape, buffers = [], [], []
+    for grad, clip_first in zip(grads, kinds):
+        rows, cols = grad.shape
+        block = rows // n_pos
+        views.append(grad.reshape((2,) * lead + (block, cols)))
+        out_shape.append(jax.ShapeDtypeStruct((block, cols), f32))
+        stages = flow_stages(n_pos, n_clip, clip_first)
+        shapes = flow_shapes(stages, n_pos, block, cols)
+        buffers += [pltpu.VMEM(shape, bf16) for shape in [shapes[0]] + shapes]
+    clips, wide = small.shape
+    out_shape.append(jax.ShapeDtypeStruct((n_clip, clips, wide), f32))
+    dma = pltpu.SemaphoreType.DMA
+    whole = pl.BlockSpec(memory_space=pltpu.VMEM)
+    sizes = sum(grad.size for grad in grads)
+    return pl.pallas_call(
+        partial(combine, n_pos, n_clip, kinds),
+        in_specs=[pl.BlockSpec(memory_space=pl.ANY)] * len(grads) + [whole],
+        out_specs=[whole] * len(out_shape),
+        out_shape=out_shape,
+        scratch_shapes=[
+            dma((len(grads), most)),
+            dma((len(grads), most)),
+            dma((len(grads),)),
+            dma((most,)),
+            dma((most,)),
+            pltpu.VMEM((lead, clips, wide), f32),
+            pltpu.VMEM((lead, clips, wide), f32),
+        ]
+        + buffers,
+        compiler_params=pltpu.CompilerParams(
+            vmem_limit_bytes=VMEM_LIMIT, collective_id=2, has_side_effects=True
+        ),
+        cost_estimate=pl.CostEstimate(flops=sizes, bytes_accessed=sizes * 4, transcendentals=0),
+        name="combine",
+    )(*views, small)
 
 
 def on_device(
@@ -733,16 +934,11 @@
 
     all_steps = by_distance(timesteps[0], "clip", n_clip)
     freq = frequency(all_steps)
-    first_w, second_w, adaln_w = (
-        embed_first.astype(f32),
-        embed_second.astype(f32),
-        adaln_weight.astype(f32),
-    )
-    pre_cond = dot_high(freq, first_w)
+    pre_cond = dot_exact(freq, embed_first)
     hidden_cond = jax.nn.silu(pre_cond)
-    cond = dot_high(hidden_cond, second_w)
+    cond = dot_exact(hidden_cond, embed_second)
     cond_act = jax.nn.silu(cond)
-    modulated = dot_high(cond_act[:clips], adaln_w)
+    modulated = dot_exact(cond_act[:clips], adaln_weight)
     onehot, clip_ids = clip_onehot(clip_lengths[0], frames)
     per_frame = dot_high(onehot, modulated)
     own_frames = lax.dynamic_slice_in_dim(per_frame, me * own, own, 0)
@@ -768,55 +964,35 @@
     )
     grad_tokens = (turn(grad_one) + back_places.astype(f32)).astype(bf16)
 
+    h_flat = h_one.reshape(own * patches, width)
+    grad_flat = grad_qkv_one.reshape(own * patches, 3 * width)
+    own_hot = lax.dynamic_slice_in_dim(onehot, me * own, own, 0)
+    dmod_first = dot_high(own_hot.T, sums_one.reshape(own, 2 * width))
+    dmod_rest = dot_high(onehot.T, sums.transpose(1, 0, 2).reshape(frames, 7 * width))
+    grads = (
+        weight_grad(h_three, grad_u),
+        weight_grad(act, grad_z),
+        weight_grad(h_two, grad_qkv_two),
+        weight_grad(h_flat, grad_flat),
+        weight_grad(o_two, grad_y_two),
+        weight_grad(o_one.reshape(rows, width), grad_y_one),
+    )
+    kinds = (False, True, False, True, False, True)
+    dmod_local = jnp.concatenate([dmod_first, dmod_rest], axis=1)
+    (
+        g_hidden_up, g_hidden_down, g_temporal_in, g_spatial_in, g_temporal_out, g_spatial_out, dmod
+    ) = call_combine(grads, kinds, dmod_local, n_pos, n_clip)
+    dmod = dmod.reshape(n_clip * clips, 9 * width)
+
     def own_columns(values):
         block = values.shape[1] // n_pos
         return lax.dynamic_slice_in_dim(values, me * block, block, 1)
 
-    def total(values):
-        return by_distance(butterfly(values, "pos", n_pos), "clip", n_clip)
-
-    own_act = own_columns(cond_act).T
-    first_cols = 2 * width
-    dmod_rest = total(dot_high(onehot.T, sums.transpose(1, 0, 2).reshape(frames, 7 * width)))
-    g_adaln_rest = dot_high(own_act, dmod_rest)
-    back_rest = dot_high(dmod_rest, adaln_w[:, first_cols:].T)
-    own_hot = lax.dynamic_slice_in_dim(onehot, me * own, own, 0)
-    dmod_first = total(dot_high(own_hot.T, sums_one.reshape(own, first_cols)))
-    g_adaln_first = dot_high(own_act, dmod_first)
-    back_first = dot_high(dmod_first, adaln_w[:, :first_cols].T)
-    g_adaln = jnp.concatenate([g_adaln_first, g_adaln_rest], axis=1)
-    grad_cond = (back_first + back_rest) * silu_grad(cond)
+    g_adaln = dot_high(own_columns(cond_act).T, dmod)
+    grad_cond = dot_exact(dmod, adaln_weight.T) * silu_grad(cond)
     g_second = dot_high(own_columns(hidden_cond).T, grad_cond)
-    grad_pre = dot_high(grad_cond, second_w.T) * silu_grad(pre_cond)
+    grad_pre = dot_exact(grad_cond, embed_second.T) * silu_grad(pre_cond)
     g_first = dot_high(own_columns(freq).T, grad_pre)
-
-    h_two, grad_qkv_two, o_two, grad_y_two, o_one, grad_y_one, grad_qkv_one = lax.optimization_barrier(
-        (h_two, grad_qkv_two, o_two, grad_y_two, o_one, grad_y_one, grad_qkv_one)
-    )
-    early = partial(reduce_rows, n_pos=n_pos, n_clip=n_clip, clip_first=False)
-    late = partial(reduce_rows, n_pos=n_pos, n_clip=n_clip, clip_first=True)
-    g_hidden_up = early(weight_grad(h_three, grad_u))
-    g_hidden_down = late(weight_grad(act, grad_z))
-    g_temporal_in = early(weight_grad(h_two, grad_qkv_two))
-    outs = late(
-        jnp.concatenate(
-            [
-                weight_grad(o_two, grad_y_two),
-                weight_grad(o_one.reshape(rows, width), grad_y_one),
-            ],
-            axis=1,
-        )
-    )
-    h_flat = h_one.reshape(own * patches, width)
-    grad_flat = grad_qkv_one.reshape(own * patches, 3 * width)
-    half = grad_flat.shape[1] // 2
-    g_spatial_in = jnp.concatenate(
-        [
-            early(weight_grad(h_flat, grad_flat[:, :half])),
-            late(weight_grad(h_flat, grad_flat[:, half:])),
-        ],
-        axis=1,
-    )
     return (
         block_out,
         grad_tokens,
@@ -824,9 +1000,9 @@
         g_second,
         g_adaln,
         g_spatial_in,
-        outs[:, width:],
+        g_spatial_out,
         g_temporal_in,
-        outs[:, :width],
+        g_temporal_out,
         g_hidden_up,
         g_hidden_down,
     )

time: 624 us -> 509 us (0.82)
  Pallas kernels: 261 us -> 384 us
  waiting for transfers between devices: 122 us -> 23.1 us
  starting transfers between devices: 68.1 us -> 16.6 us
  other arithmetic: 49.3 us -> 4.95 us
  local copies, waits for them, and re-layouts: 52.6 us -> 21.6 us
  matrix products: 63.7 us -> 52.5 us
    pallas_call x0 -> x1, Pallas kernels: none -> 118 us  [call_combine(): pl.pallas_call(partial(combine, n_pos, n_clip, kinds), in_specs=[pl.Block...]
    ppermute x44 -> x1, waiting for transfers between devices: 106 us -> 0.01 us  [swap(): return lax.ppermute(values, axis, [(i, i ^ bit) for i in range(size)])]
    ppermute x44 -> x1, starting transfers between devices: 55.3 us -> 3.06 us  [swap(): return lax.ppermute(values, axis, [(i, i ^ bit) for i in range(size)])]
    dot_general x13 -> x6, matrix products: 33.9 us -> 6.12 us  [dot_high(): return jnp.dot(left, right, precision=highest, preferred_element_type=f32)]
    convert_element_type x24 -> x8, other arithmetic: 22.2 us -> 0.13 us  [dot_exact(): part = left.astype(bf16)]
    dot_general x0 -> x5, matrix products: none -> 13.5 us  [dot_exact(): jnp.dot(jnp.concatenate(parts, axis=0), right, preferred_element_type=f32)]
    squeeze x24 -> x0, local copies, waits for them, and re-layouts: 11.4 us -> none  [pick(): return lax.dynamic_index_in_dim(values, at, axis, keepdims=False)]
    dynamic_slice x2 -> x0, other arithmetic: 10.5 us -> none  [pick(): return lax.dynamic_index_in_dim(values, at, axis, keepdims=False)]
  transfers between devices with their start and end apart: 46 -> 3, of which waited for: 17 -> 2; matrix products, arithmetic and copies ran while one was open for 23% -> 8% of each run, Pallas kernels for 8% -> 0%
where the time goes in v4:
time: 509 us; the launch traced here: 504 us
  Pallas kernels  384 us (75%)
  matrix products  52.5 us (10%)
  waiting for transfers between devices  23.1 us (5%)
  local copies, waits for them, and re-layouts  21.6 us (4%)
  starting transfers between devices  16.6 us (3%)
    pallas_call x1, Pallas kernels, call_middle(): pl.pallas_call(middle, grid=(places // count,), in_specs=[chunk, chunk, c...  157 us
    pallas_call x1, Pallas kernels, call_combine(): pl.pallas_call(partial(combine, n_pos, n_clip, kinds), in_specs=[pl.Block...  118 us
    pallas_call x1, Pallas kernels, call_space_backward(): pl.pallas_call(space_backward, grid=(own,), in_specs=[spread, by_frame(pa...  56.1 us
    pallas_call x1, Pallas kernels, call_space_forward(): pl.pallas_call(space_forward, grid=(own,), in_specs=[spread, by_frame(2,...  53 us
    dot_general x6, matrix products, weight_grad(): jnp.einsum('rd,rk->dk', left, right, preferred_element_type=f32)  32.8 us
    all_to_all x2, waiting for transfers between devices, exchange(): got = lax.all_to_all(sent, 'pos', split_axis=0, concat_axis=0, tiled=True)  23.1 us
    all_to_all x2, starting transfers between devices, exchange(): got = lax.all_to_all(sent, 'pos', split_axis=0, concat_axis=0, tiled=True)  13.5 us
    dot_general x5, matrix products, dot_exact(): jnp.dot(jnp.concatenate(parts, axis=0), right, preferred_element_type=f32)  13.5 us
  transfers between devices with their start and end apart: 3, of which 2 were waited for; matrix products, arithmetic and copies ran while one was open for 8% of the time, Pallas kernels for 0%

profile of v4, /device:TPU:0, one launch (start us, length us, event | category | flops | bytes accessed | tf_op | source)
XLA Modules:
  0.0 504.0 jit_solution(10320739471797302867)
XLA Ops:
  0.7 3.1 collective-permute-start
  3.7 6.0 %all-to-all-start = ((bf16[64,16,768]{2,1,0:T(8,128)(2,1)}), bf16[64,16,768]{2,1,0:T(8,128)(2,1)}, u32[]{:S(2)}, u32[]{:S(2)}) async-start(bf16[64,16,768]{2,1,0:T(8,128)(2,1)} %param.13), calls=%async_computation | async-start | bytes 3145728 | tf_op jit(solution)/shard_map/all_to_all | solution.py:930
  9.8 1.7 copy.69
  13.5 5.5 %fusion.37 = f32[12,6912]{1,0:T(8,128)S(1)} fusion(bf16[768,6912]{1,0:T(8,128)(2,1)} %param.18, bf16[4,768]{1,0:T(4,128)(2,1)S(1)} %get-tuple-element.111, bf16[4,768]{1,0:T(4,128)(2,1)S(1)} %get-tuple-element.112, bf16[4,768]{1,0:T(4,128)(2,1)S(1)} %get-tuple-element.113), kind=kOutput, calls=%fused_computation.55 | convolution fusion | flops 127457280 | bytes 10967040 | tf_op jit(solution)/shard_map/dot_general | solution.py:658
  19.0 0.9 fusion.9
  20.6 1.4 copy.68
  22.0 19.6 %all-to-all-done = bf16[64,16,768]{2,1,0:T(8,128)(2,1)} async-done(((bf16[64,16,768]{2,1,0:T(8,128)(2,1)}), bf16[64,16,768]{2,1,0:T(8,128)(2,1)}, u32[]{:S(2)}, u32[]{:S(2)}) %all-to-all-start) | async-done | bytes 1572896 | tf_op jit(solution)/shard_map/all_to_all | solution.py:930
  41.6 53.0 %space_forward.1 = (bf16[4,256,768]{2,1,0:T(8,128)(2,1)}, bf16[4,256,2304]{2,1,0:T(8,128)(2,1)}, bf16[64,16,768]{2,1,0:T(8,128)(2,1)}, f32[4,256,128]{2,1,0:T(8,128)}) custom-call(bf16[16,4,16,768]{3,2,1,0:T(8,128)(2,1)} %bitcast.x_ref, f32[4,2,768]{2,1,0:T(2,128)} %reshape.115.mod_ref, bf16[768,2304]{1,0:T(8,128)(2,1)} %w_ref.3), custom_call_target="tpu_custom_call" | custom-call | flops 4429185024 | bytes 12976128 | tf_op jit(solution)/shard_map/space_forward/pallas_call | solution.py:487
  94.6 4.7 fusion.89
  99.3 156.5 %middle.1 = (bf16[16,64,768]{2,1,0:T(8,128)(2,1)}, bf16[1024,3072]{1,0:T(8,128)(2,1)}, bf16[1024,768]{1,0:T(8,128)(2,1)}, bf16[1024,768]{1,0:T(8,128)(2,1)}, bf1...) custom-call(bf16[16,64,768]{2,1,0:T(8,128)(2,1)} %get-tuple-element., ...), custom_call_target="tpu_custom_call" | custom-call | flops 31406948352 | bytes 40960000 | tf_op jit(solution)/shard_map/middle/pallas_call | solution.py:581
  255.8 3.5 copy.54
  259.3 7.6 %all-to-all-start.1 = ((bf16[64,16,768]{2,1,0:T(8,128)(2,1)}), bf16[64,16,768]{2,1,0:T(8,128)(2,1)}, u32[]{:S(2)}, u32[]{:S(2)}) async-start(bf16[64,16,768]{2,1,0:T(8,128)(2,1)} %copy.54), calls=%async_computation.1 | async-start | bytes 3145728 | tf_op jit(solution)/shard_map/all_to_all | solution.py:930
  267.0 1.3 copy-done.3
  268.3 2.0 copy.57
  270.3 2.5 convolution_convert_fusion.4
  272.8 2.5 convolution_convert_fusion.3
  275.3 6.9 %convolution_convert_fusion.1 = bf16[768,3072]{1,0:T(8,128)(2,1)} fusion(bf16[1024,768]{1,0:T(8,128)(2,1)S(1)} %copy-done.19, bf16[1024,3072]{1,0:T(8,128)(2,1)S(1)} %bitcast.82), kind=kOutput, calls=%fused_computation.2 | convolution fusion | flops 4834197504 | bytes 12582912 | tf_op jit(solution)/shard_map/rd,rk->dk/dot_general | solution.py:51
  282.9 5.4 %convolution_convert_fusion.2 = bf16[768,2304]{1,0:T(8,128)(2,1)} fusion(bf16[1024,768]{1,0:T(8,128)(2,1)S(1)} %copy-done.20, bf16[1024,2304]{1,0:T(8,128)(2,1)S(1)} %bitcast.84), kind=kOutput, calls=%fused_computation.3 | convolution fusion | flops 3625648128 | bytes 9830400 | tf_op jit(solution)/shard_map/rd,rk->dk/dot_general | solution.py:51
  288.3 6.9 %convolution_convert_fusion = bf16[3072,768]{1,0:T(8,128)(2,1)} fusion(bf16[1024,3072]{1,0:T(8,128)(2,1)S(1)} %bitcast.86, bf16[1024,768]{1,0:T(8,128)(2,1)S(1)} %copy-done.21), kind=kOutput, calls=%fused_computation.1 | convolution fusion | flops 4834197504 | bytes 12582912 | tf_op jit(solution)/shard_map/rd,rk->dk/dot_general | solution.py:51
  295.2 3.5 all-to-all-done.1
  298.8 56.1 %space_backward.1 = (bf16[4,256,2304]{2,1,0:T(8,128)(2,1)}, bf16[64,16,768]{2,1,0:T(8,128)(2,1)}, f32[4,2,768]{2,1,0:T(2,128)}) custom-call(bf16[16,4,16,768]{3,2,1,0:T(8,128)(2,1)} %bitcast.11.go_ref, bf16[4,256,2304]{2,1,0:T(8,128)(2,1)} %get-tuple-element.42.qkv_ref, f32[4,256,128]{2,1,0:T(8,128)} %get-tuple-element.43.lse_ref, ...), custom_call_target="tpu_custom_call" | custom-call | flops 5637144576 | bytes 16121856 | tf_op jit(solution)/shard_map/space_backward/pallas_call | solution.py:526
  356.5 8.6 %bitcast_convert_fusion = bf16[768,2304]{1,0:T(8,128)(2,1)} fusion(bf16[4,256,768]{2,1,0:T(8,128)(2,1)} %get-tuple-element.51, bf16[4,256,2304]{2,1,0:T(8,128)(2,1)} %get-tuple-element.52), kind=kOutput, calls=%fused_computation | convolution fusion | flops 3625648128 | bytes 9830400 | tf_op jit(solution)/shard_map/rd,rk->dk/dot_general | solution.py:51
  365.1 118.1 %combine.1 = (f32[48,3072]{1,0:T(8,128)}, f32[192,768]{1,0:T(8,128)}, f32[48,2304]{1,0:T(8,128)}, f32[48,2304]{1,0:T(8,128)}, f32[48,768]{1,0:T(8,128)}, /*index=5*/f32[48,768]{1,0:T(8,128)}, f32[2,4,6912]{2,1,0:T(4,128)}) custom-call(bf16[2,2,2,2,48,3072]{5,4,3,2,1,0:T(8,128)(2,1)} %bitcast.63, bf16[2,2,2,2,192,768]{5,4,3,2,1,0:T(8,128)(2,1)} %bitcast.64, ...), custom_call_target="tpu_custom_call" | custom-call | flops 9437184 | bytes 37748736 | tf_op jit(solution)/shard_map/combine/pallas_call | solution.py:881
  483.2 1.0 reshape.127
  484.2 2.4 fusion.66
  486.6 7.0 %fusion.1 = f32[24,768]{1,0:T(8,128)S(1)} fusion(bf16[768,6912]{1,0:T(8,128)(2,1)} %param.18, bf16[8,6912]{1,0:T(8,128)(2,1)S(1)} %get-tuple-element.119, bf16[8,6912]{1,0:T(8,128)(2,1)S(1)} %get-tuple-element.120, bf16[8,6912]{1,0:T(8,128)(2,1)S(1)} %get-tuple-element.118), kind=kOutput, calls=%fused_computation.11 | convolution fusion | flops 255799296 | bytes 11022336 | tf_op jit(solution)/shard_map/dot_general | solution.py:658
  493.7 1.1 fusion.68
  495.2 1.0 fusion.29
  496.2 2.9 fusion
  499.1 0.8 copy.76
  501.9 0.8 copy.80
  502.7 0.8 copy.81
  (89 shorter events, 7.7 us)
Async XLA Ops:
  0.6 12.5 %copy-start = (bf16[768,768]{1,0:T(8,128)(2,1)S(1)}, bf16[768,768]{1,0:T(8,128)(2,1)}, u32[]{:S(2)}) copy-start(bf16[768,768]{1,0:T(8,128)(2,1)} %param.17) | copy-start | bytes 3538948
  0.7 9.1 %copy-start.1 = (bf16[64,16,768]{2,1,0:T(8,128)(2,1)S(1)}, bf16[64,16,768]{2,1,0:T(8,128)(2,1)}, u32[]{:S(2)}) copy-start(bf16[64,16,768]{2,1,0:T(8,128)(2,1)} %param.13) | copy-start | bytes 4718596
  0.7 12.0 %collective-permute-start = (s32[4]{0:T(128)}, s32[4]{0:T(128)S(1)}, u32[]{:S(2)}, u32[]{:S(2)}) collective-permute-start(s32[4]{0:T(128)} %bitcast.78), channel_id=1, source_target_pairs={{0,16},{16,0},{1,17},{17,1},{2,18},{18,2},{3,19},{19,3},{4,20},{20... | collective-permute-start | bytes 56 | tf_op jit(solution)/shard_map/ppermute | solution.py:638
  3.7 37.9 %all-to-all-start = ((bf16[64,16,768]{2,1,0:T(8,128)(2,1)}), bf16[64,16,768]{2,1,0:T(8,128)(2,1)}, u32[]{:S(2)}, u32[]{:S(2)}) async-start(bf16[64,16,768]{2,1,0:T(8,128)(2,1)} %param.13), calls=%async_computation | async-start | bytes 3145728 | tf_op jit(solution)/shard_map/all_to_all | solution.py:930
  9.7 1.7 copy-start.14
  9.7 3.0 copy-start.15
  9.7 3.2 copy-start.11
  259.3 7.6 %copy-start.6 = (f32[7,64,768]{2,1,0:T(8,128)S(1)}, f32[7,64,768]{2,1,0:T(8,128)}, u32[]{:S(2)}) copy-start(f32[7,64,768]{2,1,0:T(8,128)} %get-tuple-element.57) | copy-start | bytes 4128772
  259.3 39.5 %all-to-all-start.1 = ((bf16[64,16,768]{2,1,0:T(8,128)(2,1)}), bf16[64,16,768]{2,1,0:T(8,128)(2,1)}, u32[]{:S(2)}, u32[]{:S(2)}) async-start(bf16[64,16,768]{2,1,0:T(8,128)(2,1)} %copy.54), calls=%async_computation.1 | async-start | bytes 3145728 | tf_op jit(solution)/shard_map/all_to_all | solution.py:930
  266.9 1.4 copy-start.3
  268.3 2.0 copy-start.17
  268.3 2.0 copy-start.18
  270.3 2.5 copy-start.5
  270.3 2.5 copy-start.16
  270.3 5.0 slice-start
  270.3 5.0 copy-start.19
  272.8 2.5 slice-start.1
  272.8 10.0 %slice-start.2 = ((s8[4718592]{0:T(1024)(128)(4,1)}), s8[4194304]{0:T(1024)(128)(4,1)S(1)}, s32[]{:S(2)}) async-start(s8[4718592]{0:T(1024)(128)(4,1)} %bitcast.83), calls=%async_computation.4 | async-start | bytes 8388608
  275.3 7.5 %slice-start.3 = ((s8[4718592]{0:T(1024)(128)(4,1)}), s8[524288]{0:T(1024)(128)(4,1)S(1)}, s32[]{:S(2)}) async-start(s8[4718592]{0:T(1024)(128)(4,1)} %bitcast.83), calls=%async_computation.5 | async-start | bytes 1048576
  275.3 7.5 %copy-start.20 = (bf16[1024,768]{1,0:T(8,128)(2,1)S(1)}, bf16[1024,768]{1,0:T(8,128)(2,1)}, u32[]{:S(2)}) copy-start(bf16[1024,768]{1,0:T(8,128)(2,1)} %get-tuple-element.49) | copy-start | bytes 4718596
  282.2 6.1 %slice-start.4 = ((s8[6291456]{0:T(1024)(128)(4,1)}), s8[2097152]{0:T(1024)(128)(4,1)S(1)}, s32[]{:S(2)}) async-start(s8[6291456]{0:T(1024)(128)(4,1)} %bitcast.85), calls=%async_computation.6 | async-start | bytes 4194304
  282.9 5.4 %slice-start.5 = ((s8[6291456]{0:T(1024)(128)(4,1)}), s8[4194304]{0:T(1024)(128)(4,1)S(1)}, s32[]{:S(2)}) async-start(s8[6291456]{0:T(1024)(128)(4,1)} %bitcast.85), calls=%async_computation.7 | async-start | bytes 8388608
  282.9 5.4 %copy-start.21 = (bf16[1024,768]{1,0:T(8,128)(2,1)S(1)}, bf16[1024,768]{1,0:T(8,128)(2,1)}, u32[]{:S(2)}) copy-start(bf16[1024,768]{1,0:T(8,128)(2,1)} %get-tuple-element.48) | copy-start | bytes 4718596
  486.6 9.6 %copy-start.2 = (f32[16,64,768]{2,1,0:T(8,128)S(1)}, f32[16,64,768]{2,1,0:T(8,128)}, u32[]{:S(2)}) copy-start(f32[16,64,768]{2,1,0:T(8,128)} %get-tuple-element.40) | copy-start | bytes 9437188
  493.6 2.5 copy-start.4
  496.2 2.9 copy-start.10
  496.2 3.7 copy-start.13
  496.2 4.3 copy-start.9
  499.1 2.2 copy-start.12
  499.1 2.9 copy-start.8
  499.1 3.7 copy-start.7

commit v5 on v3

--- a/solution.py
+++ b/solution.py
@@ -96,6 +96,235 @@
     return part.reshape(count * places, width)
 
 
+def swap(values, axis, size, bit):
+    return lax.ppermute(values, axis, [(i, i ^ bit) for i in range(size)])
+
+
+def bits_of(size):
+    return [1 << i for i in range(size.bit_length() - 1)]
+
+
+def by_distance(values, axis, size):
+    for bit in bits_of(size):
+        values = jnp.concatenate([values, swap(values, axis, size, bit)], axis=0)
+    return values
+
+
+def dot_exact(left, right):
+    parts = []
+    for _ in range(3):
+        part = left.astype(bf16)
+        parts.append(part)
+        left = left - part.astype(f32)
+    count = parts[0].shape[0]
+    got = jnp.dot(jnp.concatenate(parts, axis=0), right, preferred_element_type=f32)
+    return got[:count] + (got[count : 2 * count] + got[2 * count :])
+
+
+def flow_stages(n_pos, n_clip, clip_first):
+    pos = [("pos", bit, "halve") for bit in bits_of(n_pos)]
+    clip = bits_of(n_clip)
+    if not clip_first:
+        return pos + [("clip", bit, "sum") for bit in clip]
+    first = [("clip", clip[0], "columns")]
+    last = [("clip", clip[0], "gather")]
+    return pos[:1] + first + pos[1:] + [("clip", bit, "sum") for bit in clip[1:]] + last
+
+
+def flow_shapes(stages, n_pos, block, cols):
+    lead = n_pos.bit_length() - 1
+    shapes = []
+    for _, _, what in stages:
+        if what == "halve":
+            lead -= 1
+        elif what == "columns":
+            cols //= 2
+        shapes.append((2,) * lead + (block, cols))
+    return shapes
+
+
+class Flow:
+    def __init__(self, number, stages, grad, out, keep, gots, sems, place):
+        self.number, self.stages = number, stages
+        self.grad, self.out, self.keep, self.gots = grad, out, keep, gots
+        self.send_sem, self.recv_sem, self.keep_sem = sems
+        self.place = place
+
+    def side(self, stage):
+        axis, bit, _ = self.stages[stage]
+        return lax.rem(self.place[axis] // bit, 2)
+
+    def columns(self, side, width):
+        return pl.ds(pl.multiple_of(side * width, width), width)
+
+    def part(self, ref, stage, side):
+        what = self.stages[stage][2]
+        lead = len(ref.shape) - 2
+        if what == "halve":
+            return (slice(None),) * (lead - 1) + (side,)
+        if what == "columns":
+            half = ref.shape[-1] // 2
+            return (slice(None),) * (lead + 1) + (self.columns(side, half),)
+        return None
+
+    def held(self, stage):
+        if stage == 0:
+            return self.grad
+        return self.keep if stage == 1 else self.gots[stage - 1]
+
+    def copy(self, stage):
+        axis, bit, _ = self.stages[stage]
+        side = self.side(stage)
+        source = self.held(stage)
+        at = self.part(source, stage, 1 - side)
+        return pltpu.make_async_remote_copy(
+            source if at is None else source.at[at],
+            self.gots[stage],
+            self.send_sem.at[self.number, stage],
+            self.recv_sem.at[self.number, stage],
+            device_id={axis: self.place[axis] + bit * (1 - 2 * side)},
+            device_id_type=pl.DeviceIdType.MESH,
+        )
+
+    def own(self):
+        at = self.part(self.grad, 0, self.side(0))
+        return pltpu.make_async_copy(self.grad.at[at], self.keep, self.keep_sem.at[self.number])
+
+    def start(self):
+        self.copy(0).start()
+        self.own().start()
+
+    def take(self, stage):
+        self.copy(stage).wait_recv()
+        if stage == 0:
+            self.own().wait()
+        what = self.stages[stage][2]
+        got = self.gots[stage]
+        side = self.side(stage)
+        last = stage == len(self.stages) - 1
+        lead = len(got.shape) - 2
+        if what == "gather":
+            half = got.shape[-1]
+            self.out[:, self.columns(side, half)] = self.held(stage)[...].astype(f32)
+            self.out[:, self.columns(1 - side, half)] = got[...].astype(f32)
+            return
+        if last:
+            self.out[...] = self.held(stage)[...].astype(f32) + got[...].astype(f32)
+            return
+        target = self.keep if stage == 0 else got
+
+        def one(index, _):
+            at = tuple(lax.rem(index // (1 << i), 2) for i in range(lead))
+            if stage == 0:
+                mine = self.keep[at]
+            elif what == "halve":
+                mine = self.held(stage)[at + (side,)]
+            elif what == "columns":
+                mine = self.held(stage)[at + (slice(None), self.columns(side, got.shape[-1]))]
+            else:
+                mine = self.held(stage)[at]
+            target[at] = mine + got[at]
+            return 0
+
+        lax.fori_loop(0, 1 << lead, one, 0)
+        self.copy(stage + 1).start()
+
+    def finish(self):
+        for stage in range(len(self.stages)):
+            self.copy(stage).wait_send()
+
+
+class Butterfly:
+    def __init__(self, n_pos, n_clip, values, out, got, acc, sems, place):
+        self.pos_bits, self.clip_bits = bits_of(n_pos), bits_of(n_clip)
+        self.values, self.out, self.got, self.acc = values, out, got, acc
+        self.send_sem, self.recv_sem = sems
+        self.place = place
+        self.count = len(self.pos_bits) + len(self.clip_bits)
+
+    def copy(self, stage):
+        if stage < len(self.pos_bits):
+            axis, bit = "pos", self.pos_bits[stage]
+            source = self.values if stage == 0 else self.acc.at[stage - 1]
+            target = self.got.at[stage]
+        else:
+            axis, bit = "clip", self.clip_bits[stage - len(self.pos_bits)]
+            source, target = self.out.at[pl.ds(0, bit)], self.out.at[pl.ds(bit, bit)]
+        side = lax.rem(self.place[axis] // bit, 2)
+        return pltpu.make_async_remote_copy(
+            source,
+            target,
+            self.send_sem.at[stage],
+            self.recv_sem.at[stage],
+            device_id={axis: self.place[axis] + bit * (1 - 2 * side)},
+            device_id_type=pl.DeviceIdType.MESH,
+        )
+
+    def start(self):
+        self.copy(0).start()
+
+    def take(self, stage):
+        self.copy(stage).wait_recv()
+        last = len(self.pos_bits) - 1
+        if stage <= last:
+            mine = self.values[...] if stage == 0 else self.acc[stage - 1]
+            if stage < last:
+                self.acc[stage] = mine + self.got[stage]
+            else:
+                self.out[0] = mine + self.got[stage]
+        if stage + 1 < self.count:
+            self.copy(stage + 1).start()
+
+    def finish(self):
+        for stage in range(self.count):
+            self.copy(stage).wait_send()
+
+
+def partner_list(n_pos, n_clip):
+    return [("pos", bit) for bit in bits_of(n_pos)] + [("clip", bit) for bit in bits_of(n_clip)]
+
+
+def here():
+    return {"pos": lax.axis_index("pos"), "clip": lax.axis_index("clip")}
+
+
+def signal_swap(barrier, place, axis, bit):
+    side = lax.rem(place[axis] // bit, 2)
+    pl.semaphore_signal(
+        barrier,
+        inc=1,
+        device_id={axis: place[axis] + bit * (1 - 2 * side)},
+        device_id_type=pl.DeviceIdType.MESH,
+    )
+
+
+def make_flows(n_pos, n_clip, kinds, grads, outs, scratch):
+    sems, rest = scratch[:3], list(scratch[3:])
+    flows = []
+    for number, clip_first in enumerate(kinds):
+        stages = flow_stages(n_pos, n_clip, clip_first)
+        keep, gots = rest[0], rest[1 : 1 + len(stages)]
+        rest = rest[1 + len(stages) :]
+        flows.append(Flow(number, stages, grads[number], outs[number], keep, gots, sems, here()))
+    return flows
+
+
+def flow_plan(grads, kinds, n_pos, n_clip):
+    lead = n_pos.bit_length() - 1
+    most = lead + len(bits_of(n_clip)) + 1
+    dma = pltpu.SemaphoreType.DMA
+    scratch = [dma((len(grads), most)), dma((len(grads), most)), dma((len(grads),))]
+    views, out_shape = [], []
+    for grad, clip_first in zip(grads, kinds):
+        rows, cols = grad.shape
+        block = rows // n_pos
+        views.append(grad.reshape((2,) * lead + (block, cols)))
+        out_shape.append(jax.ShapeDtypeStruct((block, cols), f32))
+        shapes = flow_shapes(flow_stages(n_pos, n_clip, clip_first), n_pos, block, cols)
+        scratch += [pltpu.VMEM(shape, bf16) for shape in [shapes[0]] + shapes]
+    return views, out_shape, scratch
+
+
 class Spread:
 
     def __init__(self, n_pos, step, steps, hold, out, send_sem, recv_sem, own_sem):
@@ -104,7 +333,7 @@
         self.send_sem, self.recv_sem, self.own_sem = send_sem, recv_sem, own_sem
         self.me = lax.axis_index("pos")
 
-    def greet(self):
+    def greet(self, more=0):
         barrier = pltpu.get_barrier_semaphore()
 
         def signal(shift, _):
@@ -115,7 +344,7 @@
             return 0
 
         lax.fori_loop(1, self.n_pos, signal, 0)
-        pl.semaphore_wait(barrier, self.n_pos - 1)
+        pl.semaphore_wait(barrier, self.n_pos - 1 + more)
 
     def copy(self, step, shift, source):
         target = lax.rem(self.me + shift, self.n_pos)
@@ -217,14 +446,37 @@
     pl.when(frame == own - 1)(spread.finish)
 
 
-def space_backward(
-    go_ref, qkv_ref, lse_ref, x_ref, mod_ref, w_ref, dqkv_ref, dv_ref, sum_ref, e_ref,
-    hold, send_sem, recv_sem, own_sem,
-):
+def space_backward(n_clip, kinds, *refs):
+    flow_count = len(kinds)
+    go_ref, qkv_ref, lse_ref, x_ref, mod_ref, w_ref = refs[:6]
+    grads, refs = refs[6 : 6 + flow_count], refs[6 + flow_count :]
+    dqkv_ref, dv_ref, sum_ref = refs[:3]
+    outs, refs = refs[3 : 3 + flow_count], refs[3 + flow_count :]
+    e_ref, hold, send_sem, recv_sem, own_sem = refs[:5]
     own, n_pos = hold.shape[:2]
     frame = pl.program_id(0)
     spread = Spread(n_pos, frame, own, hold, dv_ref, send_sem, recv_sem, own_sem)
-    pl.when(frame == 0)(spread.greet)
+    flows = make_flows(n_pos, n_clip, kinds, grads, outs, refs[5:])
+    stages = max(len(flow.stages) for flow in flows)
+    order = [(i, stage) for stage in range(stages) for i in range(flow_count)]
+    order = [(i, stage) for i, stage in order if stage < len(flows[i].stages)]
+    cuts = [2, flow_count, flow_count + 2]
+
+    @pl.when(frame == 0)
+    def _():
+        place = here()
+        others = [("clip", bit) for bit in bits_of(n_clip)]
+        barrier = pltpu.get_barrier_semaphore()
+        for axis, bit in others:
+            signal_swap(barrier, place, axis, bit)
+        spread.greet(len(others))
+        for flow in flows:
+            flow.start()
+
+    def advance(first, last):
+        for i, stage in order[first:last]:
+            flows[i].take(stage)
+
     patches = qkv_ref.shape[1]
     width = x_ref.shape[3]
     places = x_ref.shape[2]
@@ -285,7 +537,17 @@
     spread.send()
     sum_ref[0, 0:1, :] = jnp.sum(shift_sum, axis=0, keepdims=True)
     sum_ref[0, 1:2, :] = jnp.sum(scale_sum, axis=0, keepdims=True)
-    pl.when(frame == own - 1)(spread.finish)
+    done = 0
+    for index, cut in enumerate(cuts[: own - 1]):
+        pl.when(frame == index)(partial(advance, done, cut))
+        done = cut
+
+    @pl.when(frame == own - 1)
+    def _():
+        advance(done, len(order))
+        spread.finish()
+        for flow in flows:
+            flow.finish()
 
 
 GELU_C = math.sqrt(2.0 / math.pi)
@@ -354,21 +616,35 @@
             pl.ds(pl.multiple_of(2 * width + at, pair), pair),
         )
 
+    parts = [slice(place * frames, (place + 1) * frames) for place in range(count)]
+    same_half = (
+        lax.broadcasted_iota(jnp.int32, (pair, pair), 0) // HEAD_DIM
+        == lax.broadcasted_iota(jnp.int32, (pair, pair), 1) // HEAD_DIM
+    )
+    ones = jnp.where(same_half, 1.0, 0.0).astype(bf16)
+
+    def half_sums(values):
+        high = values.astype(bf16)
+        low = (values - high.astype(f32)).astype(bf16)
+        return bdot(high, ones) + bdot(low, ones)
+
     def time_pair(index, _):
-        q_at, k_at, v_at = pair_at(index)
-        for place in range(count):
-            part = slice(place * frames, (place + 1) * frames)
-            q = qkv_ref[part, q_at]
-            keys = stacked(qkv_ref[part, k_at], masks_q)
-            values = stacked(qkv_ref[part, v_at], masks)
-            scores = jnp.where(allowed, bdot_nt(q, keys), masked_score)
-            exps = jnp.exp(scores - halves(scores, jnp.max, -jnp.inf))
-            probs = exps / halves(exps, jnp.sum, 0.0)
-            p_ref[index, part, :] = probs
-            o2_ref[part, q_at] = bdot(probs.astype(bf16), values).astype(bf16)
+        jobs = [(2 * index + i, part) + pair_at(2 * index + i) for i in range(2) for part in parts]
+        keys = [stacked(qkv_ref[part, k_at], masks_q) for _i, part, q_at, k_at, v_at in jobs]
+        scores = [bdot_nt(qkv_ref[job[1], job[2]], key) for job, key in zip(jobs, keys)]
+        scores = [jnp.where(allowed, score, masked_score) for score in scores]
+        tops = [halves(score, jnp.max, -jnp.inf) for score in scores]
+        exps = [jnp.exp(score - top) for score, top in zip(scores, tops)]
+        sums = [half_sums(exp) for exp in exps]
+        probs = [exp / total for exp, total in zip(exps, sums)]
+        values = [stacked(qkv_ref[job[1], job[4]], masks) for job in jobs]
+        outs = [bdot(prob.astype(bf16), value) for prob, value in zip(probs, values)]
+        for (i, part, q_at, _k, _v), prob, out in zip(jobs, probs, outs):
+            p_ref[i, part, :] = prob
+            o2_ref[part, q_at] = out.astype(bf16)
         return 0
 
-    lax.fori_loop(0, HEADS // 2, time_pair, 0)
+    lax.fori_loop(0, HEADS // 4, time_pair, 0)
 
     y2_ref[...] = bdot(o2_ref[...], wto_ref[...])
 
@@ -431,21 +707,23 @@
 
     def time_pair_back(index, _):
         q_at, k_at, v_at = pair_at(index)
-        for place in range(count):
-            part = slice(place * frames, (place + 1) * frames)
-            go = y2_ref[part, q_at].astype(bf16)
-            q = qkv_ref[part, q_at] * factor
-            keys = stacked(qkv_ref[part, k_at], masks_q)
-            values = stacked(qkv_ref[part, v_at], masks)
-            probs = p_ref[index, part, :]
-            grad_p = bdot_nt(go, values)
-            inner = halves(grad_p * probs, jnp.sum, 0.0)
-            grad_s = (probs * (grad_p - inner)).astype(bf16)
-            dqkv_ref[part, q_at] = bdot(grad_s, keys).astype(bf16)
-            grad_k = bdot_tn(grad_s, q)
-            grad_v = bdot_tn(probs.astype(bf16), go)
-            dqkv_ref[part, k_at] = jnp.where(is_low, grad_k[:frames], grad_k[frames:]).astype(bf16)
-            dqkv_ref[part, v_at] = jnp.where(is_low, grad_v[:frames], grad_v[frames:]).astype(bf16)
+        gos = [y2_ref[part, q_at].astype(bf16) for part in parts]
+        values = [stacked(qkv_ref[part, v_at], masks) for part in parts]
+        grads = [bdot_nt(go, value) for go, value in zip(gos, values)]
+        probs = [p_ref[index, part, :] for part in parts]
+        inner = [half_sums(grad * prob) for grad, prob in zip(grads, probs)]
+        scores = [
+            (prob * (grad - mean)).astype(bf16) for prob, grad, mean in zip(probs, grads, inner)
+        ]
+        keys = [stacked(qkv_ref[part, k_at], masks_q) for part in parts]
+        qs = [qkv_ref[part, q_at] * factor for part in parts]
+        grad_q = [bdot(score, key) for score, key in zip(scores, keys)]
+        grad_k = [bdot_tn(score, q) for score, q in zip(scores, qs)]
+        grad_v = [bdot_tn(prob.astype(bf16), go) for prob, go in zip(probs, gos)]
+        for part, g_q, g_k, g_v in zip(parts, grad_q, grad_k, grad_v):
+            dqkv_ref[part, q_at] = g_q.astype(bf16)
+            dqkv_ref[part, k_at] = jnp.where(is_low, g_k[:frames], g_k[frames:]).astype(bf16)
+            dqkv_ref[part, v_at] = jnp.where(is_low, g_v[:frames], g_v[frames:]).astype(bf16)
         return 0
 
     lax.fori_loop(0, HEADS // 2, time_pair_back, 0)
@@ -513,18 +791,21 @@
     )(x, mods, weight)
 
 
-def call_space_backward(go, qkv, lse, x, mods, weight):
+def call_space_backward(go, qkv, lse, x, mods, weight, grads, kinds, n_clip):
     n_pos, own, places, width = x.shape
     patches = n_pos * places
     pair = 2 * HEAD_DIM
     spread = pl.BlockSpec((n_pos, 1, places, width), lambda i: (0, i, 0, 0))
+    anywhere = pl.BlockSpec(memory_space=pl.ANY)
 
     def by_frame(*shape):
         return pl.BlockSpec((1,) + shape, lambda i: (i, 0, 0))
 
     rows = own * patches
+    views, flow_outs, flow_scratch = flow_plan(grads, kinds, n_pos, n_clip)
+    sizes = sum(grad.size for grad in grads)
     return pl.pallas_call(
-        space_backward,
+        partial(space_backward, n_clip, kinds),
         grid=(own,),
         in_specs=[
             spread,
@@ -533,29 +814,29 @@
             spread,
             by_frame(2, width),
             resident(weight.shape),
-        ],
-        out_specs=[
-            by_frame(patches, 3 * width),
-            pl.BlockSpec(memory_space=pl.ANY),
-            by_frame(2, width),
-        ],
+        ]
+        + [anywhere] * len(grads),
+        out_specs=[by_frame(patches, 3 * width), anywhere, by_frame(2, width)]
+        + [resident(out.shape) for out in flow_outs],
         out_shape=[
             jax.ShapeDtypeStruct((own, patches, 3 * width), bf16),
             jax.ShapeDtypeStruct((n_pos * own, places, width), bf16),
             jax.ShapeDtypeStruct((own, 2, width), f32),
-        ],
+        ]
+        + flow_outs,
         scratch_shapes=[pltpu.VMEM((patches, width), f32)]
-        + spread_scratch(own, n_pos, places, width),
+        + spread_scratch(own, n_pos, places, width)
+        + flow_scratch,
         compiler_params=pltpu.CompilerParams(
             vmem_limit_bytes=VMEM_LIMIT, collective_id=1, has_side_effects=True
         ),
         cost_estimate=pl.CostEstimate(
             flops=2 * rows * width * 3 * width + 10 * rows * patches * width,
-            bytes_accessed=rows * width * 16 + weight.size * 2,
+            bytes_accessed=rows * width * 16 + weight.size * 2 + sizes * 4,
             transcendentals=rows * patches * HEADS,
         ),
         name="space_backward",
-    )(go, qkv, lse, x, mods, weight)
+    )(go, qkv, lse, x, mods, weight, *views)
 
 
 def call_middle(o_one, x, grad, mods, same_clip, wso, wti, wto, wup, wdn):
@@ -634,70 +915,60 @@
     )(o_one, x, grad, mods, lanes, wso, wti, wto, wup, wdn)
 
 
-def swap(values, axis, size, bit):
-    return lax.ppermute(values, axis, [(i, i ^ bit) for i in range(size)])
-
-
-def bits_of(size):
-    return [1 << i for i in range(size.bit_length() - 1)]
-
-
-def by_distance(values, axis, size):
-    for bit in bits_of(size):
-        values = jnp.concatenate([values, swap(values, axis, size, bit)], axis=0)
-    return values
-
-
-def butterfly(values, axis, size):
-    for bit in bits_of(size):
-        values = values + swap(values, axis, size, bit)
-    return values
-
-
-def halve(values, index, axis):
-    def pick(at):
-        return lax.dynamic_index_in_dim(values, at, axis, keepdims=False)
-
-    return pick(index), pick(1 - index)
-
-
-def reduce_rows(grad, n_pos, n_clip, clip_first):
-    rows, cols = grad.shape
-    block = rows // n_pos
-    me, clip_at = lax.axis_index("pos"), lax.axis_index("clip")
-    values = grad.reshape(n_pos, block, cols)
-
-    def add(keep, got):
-        return (keep.astype(f32) + got.astype(f32)).astype(bf16)
-
-    def pos_step(values, bit):
-        left = values.shape[0] // 2
-        split = values.reshape(left, 2, *values.shape[1:])
-        keep, send = halve(split, lax.rem(me // bit, 2), 1)
-        return add(keep, swap(send, "pos", n_pos, bit))
-
-    bits = bits_of(n_pos)
-    values = pos_step(values, bits[0])
-    if clip_first:
-        for bit in reversed(bits_of(n_clip)):
-            split = values.reshape(*values.shape[:2], 2, values.shape[2] // 2)
-            keep, send = halve(split, lax.rem(clip_at // bit, 2), 2)
-            values = add(keep, swap(send, "clip", n_clip, bit))
-    for bit in bits[1:]:
-        values = pos_step(values, bit)
-    values = values[0]
-    for bit in bits_of(n_clip):
-        got = swap(values, "clip", n_clip, bit)
-        if clip_first:
-            upper = lax.rem(clip_at // bit, 2) == 1
-            values = jnp.concatenate(
-                [jnp.where(upper, got, values), jnp.where(upper, values, got)], axis=1
-            )
-        elif 2 * bit == n_clip:
-            return values.astype(f32) + got.astype(f32)
-        else:
-            values = add(values, got)
-    return values.astype(f32)
+def combine(n_pos, n_clip, kinds, *refs):
+    count = len(kinds)
+    grads, small = refs[:count], refs[count]
+    outs, small_out = refs[count + 1 : 2 * count + 1], refs[2 * count + 1]
+    small_sems, got, acc = refs[2 * count + 2 : 2 * count + 4], refs[2 * count + 4], refs[2 * count + 5]
+    place = here()
+    partners = partner_list(n_pos, n_clip)
+    barrier = pltpu.get_barrier_semaphore()
+    for axis, bit in partners:
+        signal_swap(barrier, place, axis, bit)
+    pl.semaphore_wait(barrier, len(partners))
+    flows = make_flows(n_pos, n_clip, kinds, grads, outs, refs[2 * count + 6 :])
+    tree = Butterfly(n_pos, n_clip, small, small_out, got, acc, small_sems, place)
+    tree.start()
+    for flow in flows:
+        flow.start()
+    for stage in range(max(tree.count, max(len(flow.stages) for flow in flows))):
+        if stage < tree.count:
+            tree.take(stage)
+        for flow in flows:
+            if stage < len(flow.stages):
+                flow.take(stage)
+    tree.finish()
+    for flow in flows:
+        flow.finish()
+
+
+def call_combine(grads, kinds, small, n_pos, n_clip):
+    lead = n_pos.bit_length() - 1
+    most = lead + len(bits_of(n_clip))
+    views, out_shape, scratch = flow_plan(grads, kinds, n_pos, n_clip)
+    clips, wide = small.shape
+    out_shape.append(jax.ShapeDtypeStruct((n_clip, clips, wide), f32))
+    dma = pltpu.SemaphoreType.DMA
+    whole = pl.BlockSpec(memory_space=pltpu.VMEM)
+    sizes = sum(grad.size for grad in grads)
+    return pl.pallas_call(
+        partial(combine, n_pos, n_clip, kinds),
+        in_specs=[pl.BlockSpec(memory_space=pl.ANY)] * len(grads) + [whole],
+        out_specs=[whole] * len(out_shape),
+        out_shape=out_shape,
+        scratch_shapes=[
+            dma((most,)),
+            dma((most,)),
+            pltpu.VMEM((lead, clips, wide), f32),
+            pltpu.VMEM((lead, clips, wide), f32),
+        ]
+        + scratch,
+        compiler_params=pltpu.CompilerParams(
+            vmem_limit_bytes=VMEM_LIMIT, collective_id=2, has_side_effects=True
+        ),
+        cost_estimate=pl.CostEstimate(flops=sizes, bytes_accessed=sizes * 4, transcendentals=0),
+        name="combine",
+    )(*views, small)
 
 
 def on_device(
@@ -733,16 +1004,11 @@
 
     all_steps = by_distance(timesteps[0], "clip", n_clip)
     freq = frequency(all_steps)
-    first_w, second_w, adaln_w = (
-        embed_first.astype(f32),
-        embed_second.astype(f32),
-        adaln_weight.astype(f32),
-    )
-    pre_cond = dot_high(freq, first_w)
+    pre_cond = dot_exact(freq, embed_first)
     hidden_cond = jax.nn.silu(pre_cond)
-    cond = dot_high(hidden_cond, second_w)
+    cond = dot_exact(hidden_cond, embed_second)
     cond_act = jax.nn.silu(cond)
-    modulated = dot_high(cond_act[:clips], adaln_w)
+    modulated = dot_exact(cond_act[:clips], adaln_weight)
     onehot, clip_ids = clip_onehot(clip_lengths[0], frames)
     per_frame = dot_high(onehot, modulated)
     own_frames = lax.dynamic_slice_in_dim(per_frame, me * own, own, 0)
@@ -763,60 +1029,43 @@
     )
     block_out = turn(block_turned)
     grad_o_space = exchange(turn(grad_o_one))
-    grad_qkv_one, back_places, sums_one = call_space_backward(
-        grad_o_space, qkv_one, lse_one, x_space, own_mods, spatial_in
+    early = (
+        weight_grad(h_three, grad_u),
+        weight_grad(act, grad_z),
+        weight_grad(h_two, grad_qkv_two),
+        weight_grad(o_one.reshape(rows, width), grad_y_one),
+        weight_grad(o_two, grad_y_two),
+    )
+    (
+        grad_qkv_one, back_places, sums_one,
+        g_hidden_up, g_hidden_down, g_temporal_in, g_spatial_out, g_temporal_out,
+    ) = call_space_backward(
+        grad_o_space, qkv_one, lse_one, x_space, own_mods, spatial_in,
+        early, (False, True, False, True, True), n_clip,
     )
     grad_tokens = (turn(grad_one) + back_places.astype(f32)).astype(bf16)
+
+    h_flat = h_one.reshape(own * patches, width)
+    grad_flat = grad_qkv_one.reshape(own * patches, 3 * width)
+    cut = grad_flat.shape[1] // 512 * 256
+    own_hot = lax.dynamic_slice_in_dim(onehot, me * own, own, 0)
+    dmod_first = dot_high(own_hot.T, sums_one.reshape(own, 2 * width))
+    dmod_rest = dot_high(onehot.T, sums.transpose(1, 0, 2).reshape(frames, 7 * width))
+    dmod_local = jnp.concatenate([dmod_first, dmod_rest], axis=1)
+    late = (weight_grad(h_flat, grad_flat[:, :cut]), weight_grad(h_flat, grad_flat[:, cut:]))
+    in_low, in_high, dmod = call_combine(late, (True, False), dmod_local, n_pos, n_clip)
+    g_spatial_in = jnp.concatenate([in_low, in_high], axis=1)
+    dmod = dmod.reshape(n_clip * clips, 9 * width)
 
     def own_columns(values):
         block = values.shape[1] // n_pos
         return lax.dynamic_slice_in_dim(values, me * block, block, 1)
 
-    def total(values):
-        return by_distance(butterfly(values, "pos", n_pos), "clip", n_clip)
-
-    own_act = own_columns(cond_act).T
-    first_cols = 2 * width
-    dmod_rest = total(dot_high(onehot.T, sums.transpose(1, 0, 2).reshape(frames, 7 * width)))
-    g_adaln_rest = dot_high(own_act, dmod_rest)
-    back_rest = dot_high(dmod_rest, adaln_w[:, first_cols:].T)
-    own_hot = lax.dynamic_slice_in_dim(onehot, me * own, own, 0)
-    dmod_first = total(dot_high(own_hot.T, sums_one.reshape(own, first_cols)))
-    g_adaln_first = dot_high(own_act, dmod_first)
-    back_first = dot_high(dmod_first, adaln_w[:, :first_cols].T)
-    g_adaln = jnp.concatenate([g_adaln_first, g_adaln_rest], axis=1)
-    grad_cond = (back_first + back_rest) * silu_grad(cond)
+    g_adaln = dot_high(own_columns(cond_act).T, dmod)
+    grad_cond = dot_exact(dmod, adaln_weight.T) * silu_grad(cond)
     g_second = dot_high(own_columns(hidden_cond).T, grad_cond)
-    grad_pre = dot_high(grad_cond, second_w.T) * silu_grad(pre_cond)
+    grad_pre = dot_exact(grad_cond, embed_second.T) * silu_grad(pre_cond)
     g_first = dot_high(own_columns(freq).T, grad_pre)
-
-    h_two, grad_qkv_two, o_two, grad_y_two, o_one, grad_y_one, grad_qkv_one = lax.optimization_barrier(
-        (h_two, grad_qkv_two, o_two, grad_y_two, o_one, grad_y_one, grad_qkv_one)
-    )
-    early = partial(reduce_rows, n_pos=n_pos, n_clip=n_clip, clip_first=False)
-    late = partial(reduce_rows, n_pos=n_pos, n_clip=n_clip, clip_first=True)
-    g_hidden_up = early(weight_grad(h_three, grad_u))
-    g_hidden_down = late(weight_grad(act, grad_z))
-    g_temporal_in = early(weight_grad(h_two, grad_qkv_two))
-    outs = late(
-        jnp.concatenate(
-            [
-                weight_grad(o_two, grad_y_two),
-                weight_grad(o_one.reshape(rows, width), grad_y_one),
-            ],
-            axis=1,
-        )
-    )
-    h_flat = h_one.reshape(own * patches, width)
-    grad_flat = grad_qkv_one.reshape(own * patches, 3 * width)
-    half = grad_flat.shape[1] // 2
-    g_spatial_in = jnp.concatenate(
-        [
-            early(weight_grad(h_flat, grad_flat[:, :half])),
-            late(weight_grad(h_flat, grad_flat[:, half:])),
-        ],
-        axis=1,
-    )
     return (
         block_out,
         grad_tokens,
@@ -824,9 +1073,9 @@
         g_second,
         g_adaln,
         g_spatial_in,
-        outs[:, width:],
+        g_spatial_out,
         g_temporal_in,
-        outs[:, :width],
+        g_temporal_out,
         g_hidden_up,
         g_hidden_down,
     )

time: 624 us -> 460 us (0.74)
  waiting for transfers between devices: 122 us -> 23.3 us
  Pallas kernels: 261 us -> 333 us
  starting transfers between devices: 68.1 us -> 16.6 us
  other arithmetic: 49.3 us -> 5.74 us
  local copies, waits for them, and re-layouts: 52.6 us -> 20.1 us
  matrix products: 63.7 us -> 54.4 us
    pallas_call x1 -> x2, Pallas kernels: 51.1 us -> 167 us  [the longest x1 126 us: call_space_backward(): pl.pallas_call(partial(space_backward, n_clip, kinds), grid=(own,), in_sp...]
    ppermute x44 -> x1, waiting for transfers between devices: 106 us -> 0.01 us  [swap(): return lax.ppermute(values, axis, [(i, i ^ bit) for i in range(size)])]
    ppermute x44 -> x1, starting transfers between devices: 55.3 us -> 3.06 us  [swap(): return lax.ppermute(values, axis, [(i, i ^ bit) for i in range(size)])]
    pallas_call x1, Pallas kernels: 156 us -> 113 us  [call_middle(): pl.pallas_call(middle, grid=(places // count,), in_specs=[chunk, chunk, c...]
    dot_general x13 -> x6, matrix products: 33.9 us -> 6.12 us  [dot_high(): return jnp.dot(left, right, precision=highest, preferred_element_type=f32)]
    convert_element_type x24 -> x8, other arithmetic: 22.2 us -> 0.13 us  [dot_exact(): part = left.astype(bf16)]
    dot_general x0 -> x5, matrix products: none -> 13.5 us  [dot_exact(): jnp.dot(jnp.concatenate(parts, axis=0), right, preferred_element_type=f32)]
    squeeze x24 -> x0, local copies, waits for them, and re-layouts: 11.4 us -> none  [pick(): return lax.dynamic_index_in_dim(values, at, axis, keepdims=False)]
  transfers between devices with their start and end apart: 46 -> 3, of which waited for: 17 -> 2; matrix products, arithmetic and copies ran while one was open for 23% -> 9% of each run, Pallas kernels for 8% -> 0%
where the time goes in v5:
time: 460 us; the launch traced here: 454 us
  Pallas kernels  333 us (72%)
  matrix products  54.4 us (12%)
  waiting for transfers between devices  23.3 us (5%)
  local copies, waits for them, and re-layouts  20.1 us (4%)
  starting transfers between devices  16.6 us (4%)
  other arithmetic  5.74 us (1%)
    pallas_call x1, Pallas kernels, call_space_backward(): pl.pallas_call(partial(space_backward, n_clip, kinds), grid=(own,), in_sp...  126 us
    pallas_call x1, Pallas kernels, call_middle(): pl.pallas_call(middle, grid=(places // count,), in_specs=[chunk, chunk, c...  113 us
    pallas_call x1, Pallas kernels, call_space_forward(): pl.pallas_call(space_forward, grid=(own,), in_specs=[spread, by_frame(2,...  53 us
    pallas_call x1, Pallas kernels, call_combine(): pl.pallas_call(partial(combine, n_pos, n_clip, kinds), in_specs=[pl.Block...  41.5 us
    dot_general x7, matrix products, weight_grad(): jnp.einsum('rd,rk->dk', left, right, preferred_element_type=f32)  34.6 us
    all_to_all x2, waiting for transfers between devices, exchange(): got = lax.all_to_all(sent, 'pos', split_axis=0, concat_axis=0, tiled=True)  23.2 us
    all_to_all x2, starting transfers between devices, exchange(): got = lax.all_to_all(sent, 'pos', split_axis=0, concat_axis=0, tiled=True)  13.5 us
    dot_general x5, matrix products, dot_exact(): jnp.dot(jnp.concatenate(parts, axis=0), right, preferred_element_type=f32)  13.5 us
  transfers between devices with their start and end apart: 3, of which 2 were waited for; matrix products, arithmetic and copies ran while one was open for 9% of the time, Pallas kernels for 0%

profile of v5, /device:TPU:0, one launch (start us, length us, event | category | flops | bytes accessed | tf_op | source)
XLA Modules:
  0.0 454.3 jit_solution(10225186996459882783)
XLA Ops:
  0.7 3.1 collective-permute-start
  3.7 6.0 %all-to-all-start = ((bf16[64,16,768]{2,1,0:T(8,128)(2,1)}), bf16[64,16,768]{2,1,0:T(8,128)(2,1)}, u32[]{:S(2)}, u32[]{:S(2)}) async-start(bf16[64,16,768]{2,1,0:T(8,128)(2,1)} %param.13), calls=%async_computation | async-start | bytes 3145728 | tf_op jit(solution)/shard_map/all_to_all | solution.py:1000
  9.8 1.6 copy.64
  13.4 5.5 %fusion.43 = f32[12,6912]{1,0:T(8,128)S(1)} fusion(bf16[768,6912]{1,0:T(8,128)(2,1)} %param.18, bf16[4,768]{1,0:T(4,128)(2,1)S(1)} %get-tuple-element.113, bf16[4,768]{1,0:T(4,128)(2,1)S(1)} %get-tuple-element.114, bf16[4,768]{1,0:T(4,128)(2,1)S(1)} %get-tuple-element.115), kind=kOutput, calls=%fused_computation.60 | convolution fusion | flops 127457280 | bytes 10967040 | tf_op jit(solution)/shard_map/dot_general | solution.py:120
  18.9 0.9 fusion.15
  20.5 1.5 copy.63
  22.0 19.6 %all-to-all-done = bf16[64,16,768]{2,1,0:T(8,128)(2,1)} async-done(((bf16[64,16,768]{2,1,0:T(8,128)(2,1)}), bf16[64,16,768]{2,1,0:T(8,128)(2,1)}, u32[]{:S(2)}, u32[]{:S(2)}) %all-to-all-start) | async-done | bytes 1572896 | tf_op jit(solution)/shard_map/all_to_all | solution.py:1000
  41.6 53.0 %space_forward.1 = (bf16[4,256,768]{2,1,0:T(8,128)(2,1)}, bf16[4,256,2304]{2,1,0:T(8,128)(2,1)}, bf16[64,16,768]{2,1,0:T(8,128)(2,1)}, f32[4,256,128]{2,1,0:T(8,128)}) custom-call(bf16[16,4,16,768]{3,2,1,0:T(8,128)(2,1)} %bitcast.x_ref.refs_3_, f32[4,2,768]{2,1,0:T(2,128)} %reshape.122.mod_ref.refs_4_, bf16[768,2304]{1,0:T(8,128)(2,1)} %refs_5_.1), custom_call_target="tpu_custom_call" | custom-call | flops 4429185024 | bytes 12976128 | tf_op jit(solution)/shard_map/space_forward/pallas_call | solution.py:765
  94.6 4.7 %fusion.95 = (bf16[64,16,768]{2,0,1:T(8,128)(2,1)}, bf16[16,64,768]{2,1,0:T(8,128)(2,1)}, bf16[16,64,768]{2,1,0:T(8,128)(2,1)}) fusion(bf16[64,16,768]{2,1,0:T(8,128)(2,1)} %get-tuple-element.39, bf16[64,16,768]{2,1,0:T(8,128)(2,1)} %param.25), kind=kLoop, calls=%fused_computation.129 | loop fusion | bytes 7864320 | tf_op jit(solution)/shard_map/space_forward/pallas_call | solution.py:765
  99.3 112.6 %middle.1 = (bf16[16,64,768]{2,1,0:T(8,128)(2,1)}, bf16[1024,3072]{1,0:T(8,128)(2,1)}, bf16[1024,768]{1,0:T(8,128)(2,1)}, bf16[1024,768]{1,0:T(8,128)(2,1)}, bf1...) custom-call(bf16[16,64,768]{2,1,0:T(8,128)(2,1)} %get-tuple-element., ...), custom_call_target="tpu_custom_call" | custom-call | flops 31406948352 | bytes 40960000 | tf_op jit(solution)/shard_map/middle/pallas_call | solution.py:862
  211.9 3.4 copy.51
  215.4 7.6 %all-to-all-start.1 = ((bf16[64,16,768]{2,1,0:T(8,128)(2,1)}), bf16[64,16,768]{2,1,0:T(8,128)(2,1)}, u32[]{:S(2)}, u32[]{:S(2)}) async-start(bf16[64,16,768]{2,1,0:T(8,128)(2,1)} %copy.51), calls=%async_computation.1 | async-start | bytes 3145728 | tf_op jit(solution)/shard_map/all_to_all | solution.py:1000
  223.1 1.3 copy-done.3
  224.4 2.0 copy.53
  226.4 2.5 convolution_convert_fusion.4
  228.9 2.5 convolution_convert_fusion.5
  231.4 6.8 %convolution_convert_fusion.1 = bf16[768,3072]{1,0:T(8,128)(2,1)} fusion(bf16[1024,768]{1,0:T(8,128)(2,1)S(1)} %copy-done.22, bf16[1024,3072]{1,0:T(8,128)(2,1)S(1)} %bitcast.88), kind=kOutput, calls=%fused_computation.1 | convolution fusion | flops 4834197504 | bytes 12582912 | tf_op jit(solution)/shard_map/rd,rk->dk/dot_general | solution.py:51
  238.9 5.3 %convolution_convert_fusion.2 = bf16[768,2304]{1,0:T(8,128)(2,1)} fusion(bf16[1024,768]{1,0:T(8,128)(2,1)S(1)} %copy-done.23, bf16[1024,2304]{1,0:T(8,128)(2,1)S(1)} %bitcast.90), kind=kOutput, calls=%fused_computation.2 | convolution fusion | flops 3625648128 | bytes 9830400 | tf_op jit(solution)/shard_map/rd,rk->dk/dot_general | solution.py:51
  244.3 6.9 %convolution_convert_fusion = bf16[3072,768]{1,0:T(8,128)(2,1)} fusion(bf16[1024,3072]{1,0:T(8,128)(2,1)S(1)} %bitcast.92, bf16[1024,768]{1,0:T(8,128)(2,1)S(1)} %copy-done.24), kind=kOutput, calls=%fused_computation | convolution fusion | flops 4834197504 | bytes 12582912 | tf_op jit(solution)/shard_map/rd,rk->dk/dot_general | solution.py:51
  251.2 3.6 all-to-all-done.1
  254.8 125.7 %space_backward.1 = (bf16[4,256,2304]{2,1,0:T(8,128)(2,1)}, bf16[64,16,768]{2,1,0:T(8,128)(2,1)}, f32[4,2,768]{2,1,0:T(2,128)}, f32[48,3072]{1,0:T(8,128)}, f32[...) custom-call(bf16[16,4,16,768]{3,2,1,0:T(8,128)(2,1)} %bitcast.11.refs_0_, ...), custom_call_target="tpu_custom_call" | custom-call | flops 5637144576 | bytes 46792704 | tf_op jit(solution)/shard_map/space_backward/pallas_call | solution.py:807
  380.6 5.9 %convolution_convert_fusion.3 = bf16[768,1280]{1,0:T(8,128)(2,1)} fusion(bf16[1024,768]{1,0:T(8,128)(2,1)} %bitcast.84, bf16[1024,2304]{1,0:T(8,128)(2,1)} %bitcast.79), kind=kOutput, calls=%fused_computation.3 | convolution fusion | flops 2014248960 | bytes 6160384 | tf_op jit(solution)/shard_map/rd,rk->dk/dot_general | solution.py:51
  386.5 4.6 %fusion.4 = bf16[768,1024]{1,0:T(8,128)(2,1)} fusion(bf16[1024,768]{1,0:T(8,128)(2,1)S(1)} %bitcast.85, bf16[1024,2304]{1,0:T(8,128)(2,1)} %bitcast.80), kind=kOutput, calls=%fused_computation.10 | convolution fusion | flops 1611399168 | bytes 5242880 | tf_op jit(solution)/shard_map/rd,rk->dk/dot_general | solution.py:51
  392.0 41.5 %combine.1 = (f32[48,1024]{1,0:T(8,128)}, f32[48,1280]{1,0:T(8,128)}, f32[2,4,6912]{2,1,0:T(4,128)}) custom-call(bf16[2,2,2,2,48,1024]{5,4,3,2,1,0:T(8,128)(2,1)} %bitcast.72, bf16[2,2,2,2,48,1280]{5,4,3,2,1,0:T(8,128)(2,1)} %bitcast.67, f32[4,6912]{1,0:T(4,128)} %pad_maximum_fusion.1.refs_2_), custom_call_target="tpu_custom_call" | custom-call | flops 1769472 | bytes 7077888 | tf_op jit(solution)/shard_map/combine/pallas_call | solution.py:954
  433.6 1.0 reshape.137
  434.6 2.4 fusion.72
  437.0 7.0 %fusion.7 = f32[24,768]{1,0:T(8,128)S(1)} fusion(bf16[768,6912]{1,0:T(8,128)(2,1)} %param.18, bf16[8,6912]{1,0:T(8,128)(2,1)S(1)} %get-tuple-element.121, bf16[8,6912]{1,0:T(8,128)(2,1)S(1)} %get-tuple-element.122, bf16[8,6912]{1,0:T(8,128)(2,1)S(1)} %get-tuple-element.120), kind=kOutput, calls=%fused_computation.16 | convolution fusion | flops 255799296 | bytes 11022336 | tf_op jit(solution)/shard_map/dot_general | solution.py:120
  444.1 1.1 fusion.74
  446.4 1.0 fusion.35
  447.4 2.9 fusion
  452.4 0.8 copy.73
  453.2 0.8 copy.74
  (96 shorter events, 7.8 us)
Async XLA Ops:
  0.6 12.4 %copy-start = (bf16[768,768]{1,0:T(8,128)(2,1)S(1)}, bf16[768,768]{1,0:T(8,128)(2,1)}, u32[]{:S(2)}) copy-start(bf16[768,768]{1,0:T(8,128)(2,1)} %param.17) | copy-start | bytes 3538948
  0.7 9.1 %copy-start.1 = (bf16[64,16,768]{2,1,0:T(8,128)(2,1)S(1)}, bf16[64,16,768]{2,1,0:T(8,128)(2,1)}, u32[]{:S(2)}) copy-start(bf16[64,16,768]{2,1,0:T(8,128)(2,1)} %param.13) | copy-start | bytes 4718596
  0.7 11.9 %collective-permute-start = (s32[4]{0:T(128)}, s32[4]{0:T(128)S(1)}, u32[]{:S(2)}, u32[]{:S(2)}) collective-permute-start(s32[4]{0:T(128)} %bitcast.82), channel_id=1, source_target_pairs={{0,16},{16,0},{1,17},{17,1},{2,18},{18,2},{3,19},{19,3},{4,20},{20... | collective-permute-start | bytes 56 | tf_op jit(solution)/shard_map/ppermute | solution.py:100
  3.7 37.9 %all-to-all-start = ((bf16[64,16,768]{2,1,0:T(8,128)(2,1)}), bf16[64,16,768]{2,1,0:T(8,128)(2,1)}, u32[]{:S(2)}, u32[]{:S(2)}) async-start(bf16[64,16,768]{2,1,0:T(8,128)(2,1)} %param.13), calls=%async_computation | async-start | bytes 3145728 | tf_op jit(solution)/shard_map/all_to_all | solution.py:1000
  9.7 2.9 copy-start.17
  9.7 3.1 copy-start.10
  215.4 7.6 %copy-start.6 = (f32[7,64,768]{2,1,0:T(8,128)S(1)}, f32[7,64,768]{2,1,0:T(8,128)}, u32[]{:S(2)}) copy-start(f32[7,64,768]{2,1,0:T(8,128)} %get-tuple-element.58) | copy-start | bytes 4128772
  215.4 39.5 %all-to-all-start.1 = ((bf16[64,16,768]{2,1,0:T(8,128)(2,1)}), bf16[64,16,768]{2,1,0:T(8,128)(2,1)}, u32[]{:S(2)}, u32[]{:S(2)}) async-start(bf16[64,16,768]{2,1,0:T(8,128)(2,1)} %copy.51), calls=%async_computation.1 | async-start | bytes 3145728 | tf_op jit(solution)/shard_map/all_to_all | solution.py:1000
  224.3 2.0 copy-start.20
  224.4 2.0 copy-start.21
  226.4 2.5 copy-start.5
  226.4 2.5 copy-start.19
  226.4 5.0 %slice-start = ((s8[6291456]{0:T(1024)(128)(4,1)}), s8[4194304]{0:T(1024)(128)(4,1)S(1)}, s32[]{:S(2)}) async-start(s8[6291456]{0:T(1024)(128)(4,1)} %bitcast.87), calls=%async_computation.2 | async-start | bytes 8388608
  226.4 5.0 %copy-start.22 = (bf16[1024,768]{1,0:T(8,128)(2,1)S(1)}, bf16[1024,768]{1,0:T(8,128)(2,1)}, u32[]{:S(2)}) copy-start(bf16[1024,768]{1,0:T(8,128)(2,1)} %get-tuple-element.45) | copy-start | bytes 4718596
  228.9 2.5 slice-start.1
  228.9 9.9 %slice-start.2 = ((s8[4718592]{0:T(1024)(128)(4,1)}), s8[4194304]{0:T(1024)(128)(4,1)S(1)}, s32[]{:S(2)}) async-start(s8[4718592]{0:T(1024)(128)(4,1)} %bitcast.89), calls=%async_computation.4 | async-start | bytes 8388608
  231.4 7.5 %slice-start.3 = ((s8[4718592]{0:T(1024)(128)(4,1)}), s8[524288]{0:T(1024)(128)(4,1)S(1)}, s32[]{:S(2)}) async-start(s8[4718592]{0:T(1024)(128)(4,1)} %bitcast.89), calls=%async_computation.5 | async-start | bytes 1048576
  231.4 7.5 %copy-start.23 = (bf16[1024,768]{1,0:T(8,128)(2,1)S(1)}, bf16[1024,768]{1,0:T(8,128)(2,1)}, u32[]{:S(2)}) copy-start(bf16[1024,768]{1,0:T(8,128)(2,1)} %get-tuple-element.49) | copy-start | bytes 4718596
  238.3 6.0 %slice-start.4 = ((s8[6291456]{0:T(1024)(128)(4,1)}), s8[2097152]{0:T(1024)(128)(4,1)S(1)}, s32[]{:S(2)}) async-start(s8[6291456]{0:T(1024)(128)(4,1)} %bitcast.91), calls=%async_computation.6 | async-start | bytes 4194304
  238.9 5.4 %slice-start.5 = ((s8[6291456]{0:T(1024)(128)(4,1)}), s8[4194304]{0:T(1024)(128)(4,1)S(1)}, s32[]{:S(2)}) async-start(s8[6291456]{0:T(1024)(128)(4,1)} %bitcast.91), calls=%async_computation.7 | async-start | bytes 8388608
  238.9 5.3 %copy-start.24 = (bf16[1024,768]{1,0:T(8,128)(2,1)S(1)}, bf16[1024,768]{1,0:T(8,128)(2,1)}, u32[]{:S(2)}) copy-start(bf16[1024,768]{1,0:T(8,128)(2,1)} %get-tuple-element.48) | copy-start | bytes 4718596
  380.6 6.0 %copy-start.18 = (bf16[4,256,768]{2,1,0:T(8,128)(2,1)S(1)}, bf16[4,256,768]{2,1,0:T(8,128)(2,1)}, u32[]{:S(2)}) copy-start(bf16[4,256,768]{2,1,0:T(8,128)(2,1)} %get-tuple-element.55) | copy-start | bytes 4718596
  386.5 4.6 %copy-start.15 = (f32[4,2,768]{2,1,0:T(2,128)S(1)}, f32[4,2,768]{2,1,0:T(2,128)}, u32[]{:S(2)}) copy-start(f32[4,2,768]{2,1,0:T(2,128)} %get-tuple-element.57) | copy-start | bytes 73732
  437.0 8.2 %copy-start.11 = (f32[48,1280]{1,0:T(8,128)S(1)}, f32[48,1280]{1,0:T(8,128)}, u32[]{:S(2)}) copy-start(f32[48,1280]{1,0:T(8,128)} %get-tuple-element.61) | copy-start | bytes 737284
  437.0 8.2 %copy-start.12 = (f32[48,1024]{1,0:T(8,128)S(1)}, f32[48,1024]{1,0:T(8,128)}, u32[]{:S(2)}) copy-start(f32[48,1024]{1,0:T(8,128)} %get-tuple-element.60) | copy-start | bytes 589828
  437.0 10.4 %copy-start.2 = (f32[16,64,768]{2,1,0:T(8,128)S(1)}, f32[16,64,768]{2,1,0:T(8,128)}, u32[]{:S(2)}) copy-start(f32[16,64,768]{2,1,0:T(8,128)} %get-tuple-element.41) | copy-start | bytes 9437188
  444.0 3.3 copy-start.4
  447.4 2.9 copy-start.14
  447.4 3.6 copy-start.9
  447.4 4.3 copy-start.13
  450.3 2.1 copy-start.8
  450.3 2.9 copy-start.7
  (2 other events, 3.0 us)

commit v6 on v5

--- a/solution.py
+++ b/solution.py
@@ -318,7 +318,10 @@
     for grad, clip_first in zip(grads, kinds):
         rows, cols = grad.shape
         block = rows // n_pos
-        views.append(grad.reshape((2,) * lead + (block, cols)))
+        if isinstance(grad, jax.ShapeDtypeStruct):
+            views.append(pltpu.VMEM((2,) * lead + (block, cols), bf16))
+        else:
+            views.append(grad.reshape((2,) * lead + (block, cols)))
         out_shape.append(jax.ShapeDtypeStruct((block, cols), f32))
         shapes = flow_shapes(flow_stages(n_pos, n_clip, clip_first), n_pos, block, cols)
         scratch += [pltpu.VMEM(shape, bf16) for shape in [shapes[0]] + shapes]
@@ -446,21 +449,26 @@
     pl.when(frame == own - 1)(spread.finish)
 
 
-def space_backward(n_clip, kinds, *refs):
-    flow_count = len(kinds)
-    go_ref, qkv_ref, lse_ref, x_ref, mod_ref, w_ref = refs[:6]
-    grads, refs = refs[6 : 6 + flow_count], refs[6 + flow_count :]
-    dqkv_ref, dv_ref, sum_ref = refs[:3]
-    outs, refs = refs[3 : 3 + flow_count], refs[3 + flow_count :]
-    e_ref, hold, send_sem, recv_sem, own_sem = refs[:5]
+def space_backward(n_clip, kinds, early, *refs):
+    go_ref, qkv_ref, lse_ref, x_ref, h_ref, mod_ref, w_ref, hot_ref, rest_ref = refs[:9]
+    grads, refs = refs[9 : 9 + early], refs[9 + early :]
+    dv_ref, dmod_ref = refs[:2]
+    outs, refs = refs[2 : 2 + len(kinds)], refs[2 + len(kinds) :]
+    e_ref, dqkv_ref, total_ref, small_ref, got_ref, acc_ref, every_ref = refs[:7]
+    small_send, small_recv, hold, send_sem, recv_sem, own_sem = refs[7:13]
+    late_grads, refs = refs[13 : 13 + len(kinds) - early], refs[13 + len(kinds) - early :]
     own, n_pos = hold.shape[:2]
     frame = pl.program_id(0)
     spread = Spread(n_pos, frame, own, hold, dv_ref, send_sem, recv_sem, own_sem)
-    flows = make_flows(n_pos, n_clip, kinds, grads, outs, refs[5:])
+    flows = make_flows(n_pos, n_clip, kinds, tuple(grads) + tuple(late_grads), outs, refs)
+    late = flows[early:]
+    tree = Butterfly(
+        n_pos, n_clip, small_ref, every_ref, got_ref, acc_ref, (small_send, small_recv), here()
+    )
     stages = max(len(flow.stages) for flow in flows)
-    order = [(i, stage) for stage in range(stages) for i in range(flow_count)]
+    order = [(i, stage) for stage in range(stages) for i in range(early)]
     order = [(i, stage) for i, stage in order if stage < len(flows[i].stages)]
-    cuts = [2, flow_count, flow_count + 2]
+    cuts = [2, early, early + 2]
 
     @pl.when(frame == 0)
     def _():
@@ -470,12 +478,33 @@
         for axis, bit in others:
             signal_swap(barrier, place, axis, bit)
         spread.greet(len(others))
-        for flow in flows:
+        for flow in flows[:early]:
             flow.start()
-
-    def advance(first, last):
-        for i, stage in order[first:last]:
+        total_ref[...] = jnp.zeros_like(total_ref)
+        small_ref[:, : 2 * x_ref.shape[3]] = jnp.zeros_like(small_ref[:, : 2 * x_ref.shape[3]])
+        small_ref[:, 2 * x_ref.shape[3] :] = rest_ref[...]
+
+    def advance(steps):
+        for i, stage in steps:
             flows[i].take(stage)
+
+    def start_late():
+        block = late_grads[0].shape[-2]
+        lead = len(late_grads[0].shape) - 2
+
+        def one(index, _):
+            at = tuple(lax.rem(index // (1 << i), 2) for i in reversed(range(lead)))
+            rows = pl.ds(pl.multiple_of(index * block, 8), block)
+            first = 0
+            for grad in late_grads:
+                cols = grad.shape[-1]
+                grad[at] = total_ref[rows, first : first + cols].astype(bf16)
+                first += cols
+            return 0
+
+        lax.fori_loop(0, n_pos, one, 0)
+        for flow in late:
+            flow.start()
 
     patches = qkv_ref.shape[1]
     width = x_ref.shape[3]
@@ -513,13 +542,13 @@
             gq = part_q if gq is None else gq + part_q
             gk = part_k if gk is None else gk + part_k
             gv = part_v if gv is None else gv + part_v
-        dqkv_ref[0, :, pl.ds(at, pair)] = gq.astype(bf16)
-        dqkv_ref[0, :, pl.ds(k_at, pair)] = gk.astype(bf16)
-        dqkv_ref[0, :, pl.ds(v_at, pair)] = gv.astype(bf16)
+        dqkv_ref[:, pl.ds(at, pair)] = gq.astype(bf16)
+        dqkv_ref[:, pl.ds(k_at, pair)] = gk.astype(bf16)
+        dqkv_ref[:, pl.ds(v_at, pair)] = gv.astype(bf16)
         return 0
 
     lax.fori_loop(0, HEADS // 2, head_pair, 0)
-    e_ref[...] = bdot_nt(dqkv_ref[0], w_ref[...])
+    e_ref[...] = bdot_nt(dqkv_ref[...], w_ref[...])
 
     def norm_step(step, sums):
         grad = e_ref[pl.ds(step * ROWS, ROWS), :]
@@ -535,17 +564,32 @@
     zero = jnp.zeros((8, width), f32)
     shift_sum, scale_sum = lax.fori_loop(0, patches // ROWS, norm_step, (zero, zero))
     spread.send()
-    sum_ref[0, 0:1, :] = jnp.sum(shift_sum, axis=0, keepdims=True)
-    sum_ref[0, 1:2, :] = jnp.sum(scale_sum, axis=0, keepdims=True)
+    hot = hot_ref[frame][:, 0:1]
+    small_ref[:, :width] += hot * jnp.sum(shift_sum, axis=0, keepdims=True)
+    small_ref[:, width : 2 * width] += hot * jnp.sum(scale_sum, axis=0, keepdims=True)
+    for third in range(3):
+        cols = slice(third * width, (third + 1) * width)
+        total_ref[:, cols] += bdot_tn(h_ref[0], dqkv_ref[:, cols])
     done = 0
     for index, cut in enumerate(cuts[: own - 1]):
-        pl.when(frame == index)(partial(advance, done, cut))
+        pl.when(frame == index)(partial(advance, order[done:cut]))
         done = cut
 
     @pl.when(frame == own - 1)
     def _():
-        advance(done, len(order))
+        tree.start()
+        start_late()
+        left = order[done:]
+        for stage in range(stages + 1):
+            advance([step for step in left if step[1] == stage])
+            if stage < tree.count:
+                tree.take(stage)
+            for flow in late:
+                if 0 <= stage - 1 < len(flow.stages):
+                    flow.take(stage - 1)
+        dmod_ref[...] = every_ref[...]
         spread.finish()
+        tree.finish()
         for flow in flows:
             flow.finish()
 
@@ -791,10 +835,12 @@
     )(x, mods, weight)
 
 
-def call_space_backward(go, qkv, lse, x, mods, weight, grads, kinds, n_clip):
+def call_space_backward(go, qkv, lse, x, h, mods, weight, hot, dmod_rest, grads, kinds, n_clip):
     n_pos, own, places, width = x.shape
     patches = n_pos * places
     pair = 2 * HEAD_DIM
+    lead = n_pos.bit_length() - 1
+    clips = dmod_rest.shape[0]
     spread = pl.BlockSpec((n_pos, 1, places, width), lambda i: (0, i, 0, 0))
     anywhere = pl.BlockSpec(memory_space=pl.ANY)
 
@@ -802,41 +848,59 @@
         return pl.BlockSpec((1,) + shape, lambda i: (i, 0, 0))
 
     rows = own * patches
-    views, flow_outs, flow_scratch = flow_plan(grads, kinds, n_pos, n_clip)
+    cut = 3 * width // 512 * 256
+    late = [jax.ShapeDtypeStruct((width, cols), bf16) for cols in (cut, 3 * width - cut)]
+    kinds = kinds + (True, False)
+    views, flow_outs, flow_scratch = flow_plan(list(grads) + late, kinds, n_pos, n_clip)
+    early = len(grads)
     sizes = sum(grad.size for grad in grads)
+    dmod_shape = (n_clip, clips, 9 * width)
+    swaps = lead + len(bits_of(n_clip))
     return pl.pallas_call(
-        partial(space_backward, n_clip, kinds),
+        partial(space_backward, n_clip, kinds, early),
         grid=(own,),
         in_specs=[
             spread,
             by_frame(patches, 3 * width),
             by_frame(patches, pair),
             spread,
+            by_frame(patches, width),
             by_frame(2, width),
             resident(weight.shape),
+            resident(hot.shape),
+            resident(dmod_rest.shape),
         ]
-        + [anywhere] * len(grads),
-        out_specs=[by_frame(patches, 3 * width), anywhere, by_frame(2, width)]
-        + [resident(out.shape) for out in flow_outs],
+        + [anywhere] * early,
+        out_specs=[anywhere, resident(dmod_shape)] + [resident(out.shape) for out in flow_outs],
         out_shape=[
-            jax.ShapeDtypeStruct((own, patches, 3 * width), bf16),
             jax.ShapeDtypeStruct((n_pos * own, places, width), bf16),
-            jax.ShapeDtypeStruct((own, 2, width), f32),
+            jax.ShapeDtypeStruct(dmod_shape, f32),
         ]
         + flow_outs,
-        scratch_shapes=[pltpu.VMEM((patches, width), f32)]
+        scratch_shapes=[
+            pltpu.VMEM((patches, width), f32),
+            pltpu.VMEM((patches, 3 * width), bf16),
+            pltpu.VMEM((width, 3 * width), f32),
+            pltpu.VMEM((clips, 9 * width), f32),
+            pltpu.VMEM((lead, clips, 9 * width), f32),
+            pltpu.VMEM((lead, clips, 9 * width), f32),
+            pltpu.VMEM(dmod_shape, f32),
+            pltpu.SemaphoreType.DMA((swaps,)),
+            pltpu.SemaphoreType.DMA((swaps,)),
+        ]
         + spread_scratch(own, n_pos, places, width)
+        + views[early:]
         + flow_scratch,
         compiler_params=pltpu.CompilerParams(
             vmem_limit_bytes=VMEM_LIMIT, collective_id=1, has_side_effects=True
         ),
         cost_estimate=pl.CostEstimate(
-            flops=2 * rows * width * 3 * width + 10 * rows * patches * width,
+            flops=4 * rows * width * 3 * width + 10 * rows * patches * width,
             bytes_accessed=rows * width * 16 + weight.size * 2 + sizes * 4,
             transcendentals=rows * patches * HEADS,
         ),
         name="space_backward",
-    )(go, qkv, lse, x, mods, weight, *views)
+    )(go, qkv, lse, x, h, mods, weight, hot, dmod_rest, *views[:early])
 
 
 def call_middle(o_one, x, grad, mods, same_clip, wso, wti, wto, wup, wdn):
@@ -915,62 +979,6 @@
     )(o_one, x, grad, mods, lanes, wso, wti, wto, wup, wdn)
 
 
-def combine(n_pos, n_clip, kinds, *refs):
-    count = len(kinds)
-    grads, small = refs[:count], refs[count]
-    outs, small_out = refs[count + 1 : 2 * count + 1], refs[2 * count + 1]
-    small_sems, got, acc = refs[2 * count + 2 : 2 * count + 4], refs[2 * count + 4], refs[2 * count + 5]
-    place = here()
-    partners = partner_list(n_pos, n_clip)
-    barrier = pltpu.get_barrier_semaphore()
-    for axis, bit in partners:
-        signal_swap(barrier, place, axis, bit)
-    pl.semaphore_wait(barrier, len(partners))
-    flows = make_flows(n_pos, n_clip, kinds, grads, outs, refs[2 * count + 6 :])
-    tree = Butterfly(n_pos, n_clip, small, small_out, got, acc, small_sems, place)
-    tree.start()
-    for flow in flows:
-        flow.start()
-    for stage in range(max(tree.count, max(len(flow.stages) for flow in flows))):
-        if stage < tree.count:
-            tree.take(stage)
-        for flow in flows:
-            if stage < len(flow.stages):
-                flow.take(stage)
-    tree.finish()
-    for flow in flows:
-        flow.finish()
-
-
-def call_combine(grads, kinds, small, n_pos, n_clip):
-    lead = n_pos.bit_length() - 1
-    most = lead + len(bits_of(n_clip))
-    views, out_shape, scratch = flow_plan(grads, kinds, n_pos, n_clip)
-    clips, wide = small.shape
-    out_shape.append(jax.ShapeDtypeStruct((n_clip, clips, wide), f32))
-    dma = pltpu.SemaphoreType.DMA
-    whole = pl.BlockSpec(memory_space=pltpu.VMEM)
-    sizes = sum(grad.size for grad in grads)
-    return pl.pallas_call(
-        partial(combine, n_pos, n_clip, kinds),
-        in_specs=[pl.BlockSpec(memory_space=pl.ANY)] * len(grads) + [whole],
-        out_specs=[whole] * len(out_shape),
-        out_shape=out_shape,
-        scratch_shapes=[
-            dma((most,)),
-            dma((most,)),
-            pltpu.VMEM((lead, clips, wide), f32),
-            pltpu.VMEM((lead, clips, wide), f32),
-        ]
-        + scratch,
-        compiler_params=pltpu.CompilerParams(
-            vmem_limit_bytes=VMEM_LIMIT, collective_id=2, has_side_effects=True
-        ),
-        cost_estimate=pl.CostEstimate(flops=sizes, bytes_accessed=sizes * 4, transcendentals=0),
-        name="combine",
-    )(*views, small)
-
-
 def on_device(
     tokens,
     clip_lengths,
@@ -1036,24 +1044,17 @@
         weight_grad(o_one.reshape(rows, width), grad_y_one),
         weight_grad(o_two, grad_y_two),
     )
+    own_hot = lax.dynamic_slice_in_dim(onehot, me * own, own, 0)
+    hot = jnp.broadcast_to(own_hot[:, :, None], (own, clips, 128))
+    dmod_rest = dot_high(onehot.T, sums.transpose(1, 0, 2).reshape(frames, 7 * width))
     (
-        grad_qkv_one, back_places, sums_one,
-        g_hidden_up, g_hidden_down, g_temporal_in, g_spatial_out, g_temporal_out,
+        back_places, dmod, g_hidden_up, g_hidden_down, g_temporal_in, g_spatial_out, g_temporal_out,
+        in_low, in_high,
     ) = call_space_backward(
-        grad_o_space, qkv_one, lse_one, x_space, own_mods, spatial_in,
-        early, (False, True, False, True, True), n_clip,
+        grad_o_space, qkv_one, lse_one, x_space, h_one, own_mods, spatial_in, hot, dmod_rest,
+        early, (False, True, True, True, True), n_clip,
     )
     grad_tokens = (turn(grad_one) + back_places.astype(f32)).astype(bf16)
-
-    h_flat = h_one.reshape(own * patches, width)
-    grad_flat = grad_qkv_one.reshape(own * patches, 3 * width)
-    cut = grad_flat.shape[1] // 512 * 256
-    own_hot = lax.dynamic_slice_in_dim(onehot, me * own, own, 0)
-    dmod_first = dot_high(own_hot.T, sums_one.reshape(own, 2 * width))
-    dmod_rest = dot_high(onehot.T, sums.transpose(1, 0, 2).reshape(frames, 7 * width))
-    dmod_local = jnp.concatenate([dmod_first, dmod_rest], axis=1)
-    late = (weight_grad(h_flat, grad_flat[:, :cut]), weight_grad(h_flat, grad_flat[:, cut:]))
-    in_low, in_high, dmod = call_combine(late, (True, False), dmod_local, n_pos, n_clip)
     g_spatial_in = jnp.concatenate([in_low, in_high], axis=1)
     dmod = dmod.reshape(n_clip * clips, 9 * width)
 

time: 460 us -> 420 us (0.913)
  Pallas kernels: 333 us -> 304 us
  matrix products: 54.4 us -> 44.3 us
    pallas_call x2 -> x1, Pallas kernels: 167 us -> 138 us  [call_space_backward(): pl.pallas_call(partial(space_backward, n_clip, kinds, early), grid=(own,)...]
    dot_general x7 -> x5, matrix products: 34.6 us -> 24.1 us  [weight_grad(): jnp.einsum('rd,rk->dk', left, right, preferred_element_type=f32)]
  transfers between devices with their start and end apart: 3 -> 3, of which waited for: 2 -> 2; matrix products, arithmetic and copies ran while one was open for 9% -> 10% of each run, Pallas kernels for 0% -> 0%
where the time goes in v6:
time: 420 us; the launch traced here: 414 us
  Pallas kernels  304 us (72%)
  matrix products  44.3 us (11%)
  waiting for transfers between devices  22.6 us (5%)
  local copies, waits for them, and re-layouts  20.7 us (5%)
  starting transfers between devices  16.6 us (4%)
  other arithmetic  5.07 us (1%)
    pallas_call x1, Pallas kernels, call_space_backward(): pl.pallas_call(partial(space_backward, n_clip, kinds, early), grid=(own,)...  138 us
    pallas_call x1, Pallas kernels, call_middle(): pl.pallas_call(middle, grid=(places // count,), in_specs=[chunk, chunk, c...  112 us
    pallas_call x1, Pallas kernels, call_space_forward(): pl.pallas_call(space_forward, grid=(own,), in_specs=[spread, by_frame(2,...  53 us
    dot_general x5, matrix products, weight_grad(): jnp.einsum('rd,rk->dk', left, right, preferred_element_type=f32)  24.1 us
    all_to_all x2, waiting for transfers between devices, exchange(): got = lax.all_to_all(sent, 'pos', split_axis=0, concat_axis=0, tiled=True)  22.6 us
    all_to_all x2, starting transfers between devices, exchange(): got = lax.all_to_all(sent, 'pos', split_axis=0, concat_axis=0, tiled=True)  13.5 us
    dot_general x5, matrix products, dot_exact(): jnp.dot(jnp.concatenate(parts, axis=0), right, preferred_element_type=f32)  13.4 us
    unnamed x65, local copies, waits for them, and re-layouts  8.75 us
  transfers between devices with their start and end apart: 3, of which 2 were waited for; matrix products, arithmetic and copies ran while one was open for 10% of the time, Pallas kernels for 0%

profile of v6, /device:TPU:0, one launch (start us, length us, event | category | flops | bytes accessed | tf_op | source)
XLA Modules:
  0.0 414.2 jit_solution(6631155387990635360)
XLA Ops:
  0.7 3.1 collective-permute-start
  3.7 6.0 %all-to-all-start = ((bf16[64,16,768]{2,1,0:T(8,128)(2,1)}), bf16[64,16,768]{2,1,0:T(8,128)(2,1)}, u32[]{:S(2)}, u32[]{:S(2)}) async-start(bf16[64,16,768]{2,1,0:T(8,128)(2,1)} %param.13), calls=%async_computation | async-start | bytes 3145728 | tf_op jit(solution)/shard_map/all_to_all | solution.py:1008
  9.8 1.6 copy.63
  13.4 5.5 %fusion.37 = f32[12,6912]{1,0:T(8,128)S(1)} fusion(bf16[768,6912]{1,0:T(8,128)(2,1)} %param.18, bf16[4,768]{1,0:T(4,128)(2,1)S(1)} %get-tuple-element.109, bf16[4,768]{1,0:T(4,128)(2,1)S(1)} %get-tuple-element.110, bf16[4,768]{1,0:T(4,128)(2,1)S(1)} %get-tuple-element.111), kind=kOutput, calls=%fused_computation.54 | convolution fusion | flops 127457280 | bytes 10967040 | tf_op jit(solution)/shard_map/dot_general | solution.py:120
  19.0 0.9 fusion.9
  20.5 1.4 copy.62
  21.9 19.7 %all-to-all-done = bf16[64,16,768]{2,1,0:T(8,128)(2,1)} async-done(((bf16[64,16,768]{2,1,0:T(8,128)(2,1)}), bf16[64,16,768]{2,1,0:T(8,128)(2,1)}, u32[]{:S(2)}, u32[]{:S(2)}) %all-to-all-start) | async-done | bytes 1572896 | tf_op jit(solution)/shard_map/all_to_all | solution.py:1008
  41.6 53.0 %space_forward.1 = (bf16[4,256,768]{2,1,0:T(8,128)(2,1)}, bf16[4,256,2304]{2,1,0:T(8,128)(2,1)}, bf16[64,16,768]{2,1,0:T(8,128)(2,1)}, f32[4,256,128]{2,1,0:T(8,128)}) custom-call(bf16[16,4,16,768]{3,2,1,0:T(8,128)(2,1)} %bitcast.x_ref.refs_3_, f32[4,2,768]{2,1,0:T(2,128)} %reshape.108.mod_ref.refs_5_, bf16[768,2304]{1,0:T(8,128)(2,1)} %refs_6_.1), custom_call_target="tpu_custom_call" | custom-call | flops 4429185024 | bytes 12976128 | tf_op jit(solution)/shard_map/space_forward/pallas_call | solution.py:809
  94.6 4.7 %fusion.86 = (bf16[64,16,768]{2,0,1:T(8,128)(2,1)}, bf16[16,64,768]{2,1,0:T(8,128)(2,1)}, bf16[16,64,768]{2,1,0:T(8,128)(2,1)}) fusion(bf16[64,16,768]{2,1,0:T(8,128)(2,1)} %get-tuple-element.37, bf16[64,16,768]{2,1,0:T(8,128)(2,1)} %param.25), kind=kLoop, calls=%fused_computation.121 | loop fusion | bytes 7864320 | tf_op jit(solution)/shard_map/space_forward/pallas_call | solution.py:809
  99.3 112.3 %middle.1 = (bf16[16,64,768]{2,1,0:T(8,128)(2,1)}, bf16[1024,3072]{1,0:T(8,128)(2,1)}, bf16[1024,768]{1,0:T(8,128)(2,1)}, bf16[1024,768]{1,0:T(8,128)(2,1)}, bf1...) custom-call(bf16[16,64,768]{2,1,0:T(8,128)(2,1)} %get-tuple-element., ...), custom_call_target="tpu_custom_call" | custom-call | flops 31406948352 | bytes 40960000 | tf_op jit(solution)/shard_map/middle/pallas_call | solution.py:926
  211.7 3.4 copy.51
  215.1 7.6 %all-to-all-start.1 = ((bf16[64,16,768]{2,1,0:T(8,128)(2,1)}), bf16[64,16,768]{2,1,0:T(8,128)(2,1)}, u32[]{:S(2)}, u32[]{:S(2)}) async-start(bf16[64,16,768]{2,1,0:T(8,128)(2,1)} %copy.51), calls=%async_computation.1 | async-start | bytes 3145728 | tf_op jit(solution)/shard_map/all_to_all | solution.py:1008
  222.8 1.3 copy-done.3
  224.1 2.0 copy.53
  226.1 2.5 convolution_convert_fusion.3
  228.6 2.5 convolution_convert_fusion.4
  231.1 6.9 %convolution_convert_fusion.1 = bf16[768,3072]{1,0:T(8,128)(2,1)} fusion(bf16[1024,768]{1,0:T(8,128)(2,1)S(1)} %copy-done.20, bf16[1024,3072]{1,0:T(8,128)(2,1)S(1)} %bitcast.71), kind=kOutput, calls=%fused_computation.1 | convolution fusion | flops 4834197504 | bytes 12582912 | tf_op jit(solution)/shard_map/rd,rk->dk/dot_general | solution.py:51
  238.0 1.2 fusion.25.refs_8_
  239.3 5.3 %convolution_convert_fusion.2 = bf16[768,2304]{1,0:T(8,128)(2,1)} fusion(bf16[1024,768]{1,0:T(8,128)(2,1)S(1)} %copy-done.21, bf16[1024,2304]{1,0:T(8,128)(2,1)S(1)} %bitcast.73), kind=kOutput, calls=%fused_computation.2 | convolution fusion | flops 3625648128 | bytes 9830400 | tf_op jit(solution)/shard_map/rd,rk->dk/dot_general | solution.py:51
  244.7 7.0 %convolution_convert_fusion = bf16[3072,768]{1,0:T(8,128)(2,1)} fusion(bf16[1024,3072]{1,0:T(8,128)(2,1)S(1)} %bitcast.75, bf16[1024,768]{1,0:T(8,128)(2,1)S(1)} %copy-done.22), kind=kOutput, calls=%fused_computation | convolution fusion | flops 4834197504 | bytes 12582912 | tf_op jit(solution)/shard_map/rd,rk->dk/dot_general | solution.py:51
  251.6 2.9 all-to-all-done.1
  255.2 138.1 %space_backward.1 = (bf16[64,16,768]{2,1,0:T(8,128)(2,1)}, f32[2,4,6912]{2,1,0:T(4,128)}, f32[48,3072]{1,0:T(8,128)}, f32[192,768]{1,0:T(8,128)}, f32[48,2304]{1...) custom-call(bf16[16,4,16,768]{3,2,1,0:T(8,128)(2,1)} %bitcast.11.refs_0_, ...), custom_call_target="tpu_custom_call" | custom-call | flops 9261023232 | bytes 46792704 | tf_op jit(solution)/shard_map/space_backward/pallas_call | solution.py:859
  393.4 1.0 reshape.118
  394.4 7.0 %fusion.1 = f32[24,768]{1,0:T(8,128)S(1)} fusion(bf16[768,6912]{1,0:T(8,128)(2,1)} %param.18, bf16[8,6912]{1,0:T(8,128)(2,1)S(1)} %get-tuple-element.117, bf16[8,6912]{1,0:T(8,128)(2,1)S(1)} %get-tuple-element.118, bf16[8,6912]{1,0:T(8,128)(2,1)S(1)} %get-tuple-element.116), kind=kOutput, calls=%fused_computation.11 | convolution fusion | flops 255799296 | bytes 11022336 | tf_op jit(solution)/shard_map/dot_general | solution.py:120
  401.5 1.1 fusion.68
  402.6 2.4 fusion.66
  404.9 0.8 pad_maximum_fusion
  406.2 1.0 fusion.29
  407.2 2.9 fusion
  410.7 0.8 copy.70
  412.1 0.8 copy.72
  413.0 0.8 copy.73
  (88 shorter events, 5.4 us)
Async XLA Ops:
  0.6 12.5 %copy-start = (bf16[768,768]{1,0:T(8,128)(2,1)S(1)}, bf16[768,768]{1,0:T(8,128)(2,1)}, u32[]{:S(2)}) copy-start(bf16[768,768]{1,0:T(8,128)(2,1)} %param.17) | copy-start | bytes 3538948
  0.7 9.1 %copy-start.1 = (bf16[64,16,768]{2,1,0:T(8,128)(2,1)S(1)}, bf16[64,16,768]{2,1,0:T(8,128)(2,1)}, u32[]{:S(2)}) copy-start(bf16[64,16,768]{2,1,0:T(8,128)(2,1)} %param.13) | copy-start | bytes 4718596
  0.7 12.0 %collective-permute-start = (s32[4]{0:T(128)}, s32[4]{0:T(128)S(1)}, u32[]{:S(2)}, u32[]{:S(2)}) collective-permute-start(s32[4]{0:T(128)} %bitcast.62), channel_id=1, source_target_pairs={{0,16},{16,0},{1,17},{17,1},{2,18},{18,2},{3,19},{19,3},{4,20},{20... | collective-permute-start | bytes 56 | tf_op jit(solution)/shard_map/ppermute | solution.py:100
  3.7 37.9 %all-to-all-start = ((bf16[64,16,768]{2,1,0:T(8,128)(2,1)}), bf16[64,16,768]{2,1,0:T(8,128)(2,1)}, u32[]{:S(2)}, u32[]{:S(2)}) async-start(bf16[64,16,768]{2,1,0:T(8,128)(2,1)} %param.13), calls=%async_computation | async-start | bytes 3145728 | tf_op jit(solution)/shard_map/all_to_all | solution.py:1008
  9.7 1.6 copy-start.15
  9.7 2.9 copy-start.16
  9.7 3.1 copy-start.10
  215.1 7.6 %copy-start.6 = (f32[7,64,768]{2,1,0:T(8,128)S(1)}, f32[7,64,768]{2,1,0:T(8,128)}, u32[]{:S(2)}) copy-start(f32[7,64,768]{2,1,0:T(8,128)} %get-tuple-element.44) | copy-start | bytes 4128772
  215.1 39.5 %all-to-all-start.1 = ((bf16[64,16,768]{2,1,0:T(8,128)(2,1)}), bf16[64,16,768]{2,1,0:T(8,128)(2,1)}, u32[]{:S(2)}, u32[]{:S(2)}) async-start(bf16[64,16,768]{2,1,0:T(8,128)(2,1)} %copy.51), calls=%async_computation.1 | async-start | bytes 3145728 | tf_op jit(solution)/shard_map/all_to_all | solution.py:1008
  222.7 1.4 copy-start.3
  224.1 2.0 copy-start.18
  224.1 2.0 copy-start.19
  226.1 2.5 copy-start.5
  226.1 2.5 copy-start.17
  226.1 5.0 %slice-start = ((s8[6291456]{0:T(1024)(128)(4,1)}), s8[4194304]{0:T(1024)(128)(4,1)S(1)}, s32[]{:S(2)}) async-start(s8[6291456]{0:T(1024)(128)(4,1)} %bitcast.70), calls=%async_computation.2 | async-start | bytes 8388608
  226.1 5.0 %copy-start.20 = (bf16[1024,768]{1,0:T(8,128)(2,1)S(1)}, bf16[1024,768]{1,0:T(8,128)(2,1)}, u32[]{:S(2)}) copy-start(bf16[1024,768]{1,0:T(8,128)(2,1)} %get-tuple-element.45) | copy-start | bytes 4718596
  228.6 2.5 slice-start.1
  228.6 10.7 %slice-start.2 = ((s8[4718592]{0:T(1024)(128)(4,1)}), s8[4194304]{0:T(1024)(128)(4,1)S(1)}, s32[]{:S(2)}) async-start(s8[4718592]{0:T(1024)(128)(4,1)} %bitcast.72), calls=%async_computation.4 | async-start | bytes 8388608
  231.1 8.2 %slice-start.3 = ((s8[4718592]{0:T(1024)(128)(4,1)}), s8[524288]{0:T(1024)(128)(4,1)S(1)}, s32[]{:S(2)}) async-start(s8[4718592]{0:T(1024)(128)(4,1)} %bitcast.72), calls=%async_computation.5 | async-start | bytes 1048576
  231.1 8.2 %copy-start.21 = (bf16[1024,768]{1,0:T(8,128)(2,1)S(1)}, bf16[1024,768]{1,0:T(8,128)(2,1)}, u32[]{:S(2)}) copy-start(bf16[1024,768]{1,0:T(8,128)(2,1)} %get-tuple-element.49) | copy-start | bytes 4718596
  238.0 6.6 %slice-start.4 = ((s8[6291456]{0:T(1024)(128)(4,1)}), s8[2097152]{0:T(1024)(128)(4,1)S(1)}, s32[]{:S(2)}) async-start(s8[6291456]{0:T(1024)(128)(4,1)} %bitcast.74), calls=%async_computation.6 | async-start | bytes 4194304
  239.3 5.4 %slice-start.5 = ((s8[6291456]{0:T(1024)(128)(4,1)}), s8[4194304]{0:T(1024)(128)(4,1)S(1)}, s32[]{:S(2)}) async-start(s8[6291456]{0:T(1024)(128)(4,1)} %bitcast.74), calls=%async_computation.7 | async-start | bytes 8388608
  239.3 5.4 %copy-start.22 = (bf16[1024,768]{1,0:T(8,128)(2,1)S(1)}, bf16[1024,768]{1,0:T(8,128)(2,1)}, u32[]{:S(2)}) copy-start(bf16[1024,768]{1,0:T(8,128)(2,1)} %get-tuple-element.48) | copy-start | bytes 4718596
  394.4 12.7 %copy-start.4 = (bf16[64,16,768]{2,1,0:T(8,128)(2,1)S(1)}, bf16[64,16,768]{2,1,0:T(8,128)(2,1)}, u32[]{:S(2)}) copy-start(bf16[64,16,768]{2,1,0:T(8,128)(2,1)} %get-tuple-element.54) | copy-start | bytes 4718596
  401.4 3.5 copy-start.11
  401.4 3.5 copy-start.12
  402.6 4.6 %copy-start.2 = (f32[16,64,768]{2,1,0:T(8,128)S(1)}, f32[16,64,768]{2,1,0:T(8,128)}, u32[]{:S(2)}) copy-start(f32[16,64,768]{2,1,0:T(8,128)} %get-tuple-element.39) | copy-start | bytes 9437188
  407.1 2.9 copy-start.14
  407.1 3.6 copy-start.9
  407.2 4.3 %copy-start.13 = (f32[48,768]{1,0:T(8,128)S(1)}, f32[48,768]{1,0:T(8,128)}, u32[]{:S(2)}) copy-start(f32[48,768]{1,0:T(8,128)} %get-tuple-element.147) | copy-start | bytes 442372
  410.0 2.1 copy-start.8
  410.0 2.9 copy-start.7

commit v7 on v6

--- a/solution.py
+++ b/solution.py
@@ -421,26 +421,22 @@
         cols = slice(part * width, (part + 1) * width)
         qkv_ref[0, :, cols] = bdot(h_ref[0], w_ref[:, cols]).astype(bf16)
     masks = pair_masks(1.0 / math.sqrt(HEAD_DIM))
-    lane_ids = lax.broadcasted_iota(jnp.int32, (1, pair), 1)
-    lse_ref[0] = jnp.zeros((patches, pair), f32)
+    is_low = lax.broadcasted_iota(jnp.int32, (1, pair), 1) < HEAD_DIM
 
     def head_pair(index, _):
         at = pl.multiple_of(index * pair, pair)
         q = qkv_ref[0, :, pl.ds(at, pair)]
         k = qkv_ref[0, :, pl.ds(pl.multiple_of(width + at, pair), pair)]
         v = qkv_ref[0, :, pl.ds(pl.multiple_of(2 * width + at, pair), pair)]
-        outs = []
-        lse = lse_ref[0]
-        for half in range(2):
-            scores = bdot_nt(q * masks[half], k)
-            top = jnp.max(scores, axis=-1, keepdims=True)
-            exps = jnp.exp(scores - top)
-            total = jnp.sum(exps, axis=-1, keepdims=True)
-            probs = (exps * (1.0 / total)).astype(bf16)
-            outs.append(bdot(probs, v))
-            lse = jnp.where(lane_ids == 2 * index + half, top + jnp.log(total), lse)
-        lse_ref[0] = lse
-        both = jnp.where(lane_ids < HEAD_DIM, outs[0], outs[1])
+        one = jnp.ones_like(v)
+        values = [jnp.where(is_low, v, one), jnp.where(is_low, one, v)]
+        scores = [bdot_nt(q * mask, k) for mask in masks]
+        tops = [jnp.max(score, axis=-1, keepdims=True) for score in scores]
+        exps = [jnp.exp(score - top).astype(bf16) for score, top in zip(scores, tops)]
+        outs = [bdot(exp, value) for exp, value in zip(exps, values)]
+        total = pltpu.roll(jnp.where(is_low, outs[1], outs[0]), HEAD_DIM, 1)
+        both = jnp.where(is_low, outs[0], outs[1]) / total
+        lse_ref[0, index] = jnp.where(is_low, tops[0], tops[1]) + jnp.log(total)
         hold[frame, :, :, pl.ds(at, pair)] = both.reshape(n_pos, places, pair).astype(bf16)
         return 0
 
@@ -514,7 +510,13 @@
     factor = 1.0 / math.sqrt(HEAD_DIM)
     masks_q = pair_masks(factor)
     masks = pair_masks(1.0)
-    lane_ids = lax.broadcasted_iota(jnp.int32, (1, pair), 1)
+    ones = jnp.ones((patches, pair), bf16)
+
+    def key_sums(values):
+        high = values.astype(bf16)
+        low = (values - high.astype(f32)).astype(bf16)
+        total = bdot(high, ones) + bdot(low, ones)
+        return jnp.concatenate([total] * (patches // pair), axis=1)
 
     def head_pair(index, _):
         at = pl.multiple_of(index * pair, pair)
@@ -524,24 +526,19 @@
         k = qkv_ref[0, :, pl.ds(k_at, pair)]
         v = qkv_ref[0, :, pl.ds(v_at, pair)]
         go = go_ref[:, 0, :, pl.ds(at, pair)].astype(f32).reshape(patches, pair).astype(bf16)
-        lse_all = lse_ref[0]
-        gq, gk, gv = None, None, None
-        for half in range(2):
-            lse = jnp.sum(
-                jnp.where(lane_ids == 2 * index + half, lse_all, 0.0), axis=-1, keepdims=True
-            )
-            q_half = q * masks_q[half]
-            go_half = go * masks[half]
-            probs = jnp.exp(bdot_nt(q_half, k) - lse)
-            grad_p = bdot_nt(go_half, v)
-            inner = jnp.sum(grad_p * probs, axis=-1, keepdims=True)
-            grad_s = (probs * (grad_p - inner)).astype(bf16)
-            part_q = bdot(grad_s, k * masks_q[half])
-            part_k = bdot_tn(grad_s, q_half)
-            part_v = bdot_tn(probs.astype(bf16), go_half)
-            gq = part_q if gq is None else gq + part_q
-            gk = part_k if gk is None else gk + part_k
-            gv = part_v if gv is None else gv + part_v
+        lse_pair = lse_ref[0, index]
+        lses = [lse_pair[:, 0:1], lse_pair[:, HEAD_DIM : HEAD_DIM + 1]]
+        q_halves = [q * mask for mask in masks_q]
+        go_halves = [go * mask for mask in masks]
+        probs = [jnp.exp(bdot_nt(half, k) - lse) for half, lse in zip(q_halves, lses)]
+        grads = [bdot_nt(half, v) for half in go_halves]
+        inner = [key_sums(grad * prob) for grad, prob in zip(grads, probs)]
+        scores = [
+            (prob * (grad - mean)).astype(bf16) for prob, grad, mean in zip(probs, grads, inner)
+        ]
+        gq = sum(bdot(score, k * mask) for score, mask in zip(scores, masks_q))
+        gk = sum(bdot_tn(score, half) for score, half in zip(scores, q_halves))
+        gv = sum(bdot_tn(prob.astype(bf16), half) for prob, half in zip(probs, go_halves))
         dqkv_ref[:, pl.ds(at, pair)] = gq.astype(bf16)
         dqkv_ref[:, pl.ds(k_at, pair)] = gk.astype(bf16)
         dqkv_ref[:, pl.ds(v_at, pair)] = gv.astype(bf16)
@@ -601,7 +598,8 @@
     o1_ref, x_ref, g_ref, mod_ref, clip_ref, wso_ref, wti_ref, wto_ref, wup_ref, wdn_ref,
     out_ref, act_ref, dz_ref, h3_ref, du_ref, o2_ref, dy2_ref, h2_ref, dqkv_ref, dy1_ref, do1_ref,
     dx1_ref, sum_ref,
-    qkv_ref, p_ref, y1_ref, y2_ref, n2_ref, n3_ref, r2_ref, r3_ref, xa_ref, gp_ref, e_ref,
+    qkv_ref, p_ref, y1_ref, y2_ref, n2_ref, n3_ref, r2_ref, r3_ref, xa_ref, e_ref,
+    ua_ref, aa_ref, ub_ref, ab_ref,
 ):
     count, frames, width = x_ref.shape
     rows = count * frames
@@ -707,19 +705,32 @@
 
     tile = 256
 
-    def up_tile(index, _):
+    def products(index, u_ref, a_ref):
         cols = pl.ds(pl.multiple_of(index * tile, tile), tile)
-        u = bdot(h3_ref[...], wup_ref[:, cols])
+        u_ref[...] = bdot(h3_ref[...], wup_ref[:, cols])
+        a_ref[...] = bdot_nt(dz_ref[...], wdn_ref[cols, :])
+
+    def pointwise(index, u_ref, a_ref):
+        cols = pl.ds(pl.multiple_of(index * tile, tile), tile)
+        u = u_ref[...]
         square = u * u
-        tanh = jnp.tanh(GELU_C * (u * (1.0 + 0.044715 * square)))
-        half = 0.5 * (1.0 + tanh)
-        act_ref[:, cols] = (u * half).astype(bf16)
-        slope = half + (0.5 * GELU_C) * u * (1.0 - tanh * tanh) * (1.0 + (3.0 * 0.044715) * square)
-        du = bdot_nt(dz_ref[...], wdn_ref[cols, :]) * slope
-        du_ref[:, cols] = du.astype(bf16)
+        half = 0.5 + 0.5 * jnp.tanh(u * (GELU_C + (0.044715 * GELU_C) * square))
+        value = u * half
+        act_ref[:, cols] = value.astype(bf16)
+        slope = half + (value - value * half) * (2.0 * GELU_C + (6.0 * 0.044715 * GELU_C) * square)
+        du_ref[:, cols] = (a_ref[...] * slope).astype(bf16)
+
+    tiles = hidden // tile
+
+    def two_tiles(index, _):
+        products(2 * index + 1, ub_ref, ab_ref)
+        pointwise(2 * index, ua_ref, aa_ref)
+        products(jnp.minimum(2 * index + 2, tiles - 1), ua_ref, aa_ref)
+        pointwise(2 * index + 1, ub_ref, ab_ref)
         return 0
 
-    lax.fori_loop(0, hidden // tile, up_tile, 0)
+    products(0, ua_ref, aa_ref)
+    lax.fori_loop(0, tiles // 2, two_tiles, 0)
     e_ref[...] = bdot(act_ref[...], wdn_ref[...])
 
     def step_three(step, _):
@@ -814,13 +825,13 @@
             by_frame(patches, width),
             by_frame(patches, 3 * width),
             pl.BlockSpec(memory_space=pl.ANY),
-            by_frame(patches, pair),
+            pl.BlockSpec((1, HEADS // 2, patches, pair), lambda i: (i, 0, 0, 0)),
         ],
         out_shape=[
             jax.ShapeDtypeStruct((own, patches, width), bf16),
             jax.ShapeDtypeStruct((own, patches, 3 * width), bf16),
             jax.ShapeDtypeStruct((n_pos * own, places, width), bf16),
-            jax.ShapeDtypeStruct((own, patches, pair), f32),
+            jax.ShapeDtypeStruct((own, HEADS // 2, patches, pair), f32),
         ],
         scratch_shapes=spread_scratch(own, n_pos, places, width),
         compiler_params=pltpu.CompilerParams(
@@ -862,7 +873,7 @@
         in_specs=[
             spread,
             by_frame(patches, 3 * width),
-            by_frame(patches, pair),
+            pl.BlockSpec((1, HEADS // 2, patches, pair), lambda i: (i, 0, 0, 0)),
             spread,
             by_frame(patches, width),
             by_frame(2, width),
@@ -968,9 +979,9 @@
             scratch(pair),
             scratch(pair),
             scratch(width),
-            pltpu.VMEM((8, pair), f32),
             scratch(width),
-        ],
+        ]
+        + [scratch(256)] * 4,
         compiler_params=pltpu.CompilerParams(vmem_limit_bytes=VMEM_LIMIT),
         cost_estimate=pl.CostEstimate(
             flops=flops, bytes_accessed=total * 40000, transcendentals=total * hidden

time: 420 us -> 413 us (0.983)
  Pallas kernels: 304 us -> 297 us
    pallas_call x1, Pallas kernels: 112 us -> 108 us  [call_middle(): pl.pallas_call(middle, grid=(places // count,), in_specs=[chunk, chunk, c...]
where the time goes in v7:
time: 413 us; the launch traced here: 408 us
  Pallas kernels  297 us (72%)
  matrix products  44.3 us (11%)
  waiting for transfers between devices  22.5 us (5%)
  local copies, waits for them, and re-layouts  20.8 us (5%)
  starting transfers between devices  16.3 us (4%)
  other arithmetic  5.07 us (1%)
    pallas_call x1, Pallas kernels, call_space_backward(): pl.pallas_call(partial(space_backward, n_clip, kinds, early), grid=(own,)...  138 us
    pallas_call x1, Pallas kernels, call_middle(): pl.pallas_call(middle, grid=(places // count,), in_specs=[chunk, chunk, c...  108 us
    pallas_call x1, Pallas kernels, call_space_forward(): pl.pallas_call(space_forward, grid=(own,), in_specs=[spread, by_frame(2,...  51.2 us
    dot_general x5, matrix products, weight_grad(): jnp.einsum('rd,rk->dk', left, right, preferred_element_type=f32)  24.2 us
    all_to_all x2, waiting for transfers between devices, exchange(): got = lax.all_to_all(sent, 'pos', split_axis=0, concat_axis=0, tiled=True)  22.5 us
    dot_general x5, matrix products, dot_exact(): jnp.dot(jnp.concatenate(parts, axis=0), right, preferred_element_type=f32)  13.4 us
    all_to_all x2, starting transfers between devices, exchange(): got = lax.all_to_all(sent, 'pos', split_axis=0, concat_axis=0, tiled=True)  13.3 us
    unnamed x65, local copies, waits for them, and re-layouts  8.76 us
  transfers between devices with their start and end apart: 3, of which 2 were waited for; matrix products, arithmetic and copies ran while one was open for 10% of the time, Pallas kernels for 0%

profile of v7, /device:TPU:0, one launch (start us, length us, event | category | flops | bytes accessed | tf_op | source)
XLA Modules:
  0.0 407.6 jit_solution(9223869006311378409)
XLA Ops:
  0.7 3.1 collective-permute-start
  3.7 6.0 %all-to-all-start = ((bf16[64,16,768]{2,1,0:T(8,128)(2,1)}), bf16[64,16,768]{2,1,0:T(8,128)(2,1)}, u32[]{:S(2)}, u32[]{:S(2)}) async-start(bf16[64,16,768]{2,1,0:T(8,128)(2,1)} %param.13), calls=%async_computation | async-start | bytes 3145728 | tf_op jit(solution)/shard_map/all_to_all | solution.py:1019
  9.8 1.6 copy.63
  13.4 5.5 %fusion.37 = f32[12,6912]{1,0:T(8,128)S(1)} fusion(bf16[768,6912]{1,0:T(8,128)(2,1)} %param.18, bf16[4,768]{1,0:T(4,128)(2,1)S(1)} %get-tuple-element.109, bf16[4,768]{1,0:T(4,128)(2,1)S(1)} %get-tuple-element.110, bf16[4,768]{1,0:T(4,128)(2,1)S(1)} %get-tuple-element.111), kind=kOutput, calls=%fused_computation.54 | convolution fusion | flops 127457280 | bytes 10967040 | tf_op jit(solution)/shard_map/dot_general | solution.py:120
  19.0 0.9 fusion.9
  20.5 1.5 copy.62
  22.0 19.6 %all-to-all-done = bf16[64,16,768]{2,1,0:T(8,128)(2,1)} async-done(((bf16[64,16,768]{2,1,0:T(8,128)(2,1)}), bf16[64,16,768]{2,1,0:T(8,128)(2,1)}, u32[]{:S(2)}, u32[]{:S(2)}) %all-to-all-start) | async-done | bytes 1572896 | tf_op jit(solution)/shard_map/all_to_all | solution.py:1019
  41.6 51.2 %space_forward.1 = (bf16[4,256,768]{2,1,0:T(8,128)(2,1)}, bf16[4,256,2304]{2,1,0:T(8,128)(2,1)}, bf16[64,16,768]{2,1,0:T(8,128)(2,1)}, f32[4,6,256,128]{3,2,1,0:T(8,128)}) custom-call(bf16[16,4,16,768]{3,2,1,0:T(8,128)(2,1)} %bitcast.x_ref.refs_3_, f32[4,2,768]{2,1,0:T(2,128)} %reshape.108.mod_ref.refs_5_, bf16[768,2304]{1,0:T(8,128)(2,1)} %refs_6_.1), custom_call_target="tpu_custom_call" | custom-call | flops 4429185024 | bytes 12976128 | tf_op jit(solution)/shard_map/space_forward/pallas_call | solution.py:820
  92.8 4.7 %fusion.86 = (bf16[64,16,768]{2,0,1:T(8,128)(2,1)}, bf16[16,64,768]{2,1,0:T(8,128)(2,1)}, bf16[16,64,768]{2,1,0:T(8,128)(2,1)}) fusion(bf16[64,16,768]{2,1,0:T(8,128)(2,1)} %get-tuple-element.37, bf16[64,16,768]{2,1,0:T(8,128)(2,1)} %param.25), kind=kLoop, calls=%fused_computation.121 | loop fusion | bytes 7864320 | tf_op jit(solution)/shard_map/space_forward/pallas_call | solution.py:820
  97.5 107.7 %middle.1 = (bf16[16,64,768]{2,1,0:T(8,128)(2,1)}, bf16[1024,3072]{1,0:T(8,128)(2,1)}, bf16[1024,768]{1,0:T(8,128)(2,1)}, bf16[1024,768]{1,0:T(8,128)(2,1)}, bf1...) custom-call(bf16[16,64,768]{2,1,0:T(8,128)(2,1)} %get-tuple-element., ...), custom_call_target="tpu_custom_call" | custom-call | flops 31406948352 | bytes 40960000 | tf_op jit(solution)/shard_map/middle/pallas_call | solution.py:937
  205.2 3.4 copy.51
  208.7 7.3 %all-to-all-start.1 = ((bf16[64,16,768]{2,1,0:T(8,128)(2,1)}), bf16[64,16,768]{2,1,0:T(8,128)(2,1)}, u32[]{:S(2)}, u32[]{:S(2)}) async-start(bf16[64,16,768]{2,1,0:T(8,128)(2,1)} %copy.51), calls=%async_computation.1 | async-start | bytes 3145728 | tf_op jit(solution)/shard_map/all_to_all | solution.py:1019
  216.1 1.3 copy-done.3
  217.4 2.0 copy.53
  219.4 2.5 convolution_convert_fusion.3
  221.9 2.5 convolution_convert_fusion.4
  224.4 6.9 %convolution_convert_fusion.1 = bf16[768,3072]{1,0:T(8,128)(2,1)} fusion(bf16[1024,768]{1,0:T(8,128)(2,1)S(1)} %copy-done.20, bf16[1024,3072]{1,0:T(8,128)(2,1)S(1)} %bitcast.71), kind=kOutput, calls=%fused_computation.1 | convolution fusion | flops 4834197504 | bytes 12582912 | tf_op jit(solution)/shard_map/rd,rk->dk/dot_general | solution.py:51
  231.3 1.2 fusion.25.refs_8_
  232.6 5.3 %convolution_convert_fusion.2 = bf16[768,2304]{1,0:T(8,128)(2,1)} fusion(bf16[1024,768]{1,0:T(8,128)(2,1)S(1)} %copy-done.21, bf16[1024,2304]{1,0:T(8,128)(2,1)S(1)} %bitcast.73), kind=kOutput, calls=%fused_computation.2 | convolution fusion | flops 3625648128 | bytes 9830400 | tf_op jit(solution)/shard_map/rd,rk->dk/dot_general | solution.py:51
  238.0 7.0 %convolution_convert_fusion = bf16[3072,768]{1,0:T(8,128)(2,1)} fusion(bf16[1024,3072]{1,0:T(8,128)(2,1)S(1)} %bitcast.75, bf16[1024,768]{1,0:T(8,128)(2,1)S(1)} %copy-done.22), kind=kOutput, calls=%fused_computation | convolution fusion | flops 4834197504 | bytes 12582912 | tf_op jit(solution)/shard_map/rd,rk->dk/dot_general | solution.py:51
  244.9 2.9 all-to-all-done.1
  248.5 138.2 %space_backward.1 = (bf16[64,16,768]{2,1,0:T(8,128)(2,1)}, f32[2,4,6912]{2,1,0:T(4,128)}, f32[48,3072]{1,0:T(8,128)}, f32[192,768]{1,0:T(8,128)}, f32[48,2304]{1...) custom-call(bf16[16,4,16,768]{3,2,1,0:T(8,128)(2,1)} %bitcast.11.refs_0_, ...), custom_call_target="tpu_custom_call" | custom-call | flops 9261023232 | bytes 46792704 | tf_op jit(solution)/shard_map/space_backward/pallas_call | solution.py:870
  386.7 1.0 reshape.118
  387.8 7.0 %fusion.1 = f32[24,768]{1,0:T(8,128)S(1)} fusion(bf16[768,6912]{1,0:T(8,128)(2,1)} %param.18, bf16[8,6912]{1,0:T(8,128)(2,1)S(1)} %get-tuple-element.117, bf16[8,6912]{1,0:T(8,128)(2,1)S(1)} %get-tuple-element.118, bf16[8,6912]{1,0:T(8,128)(2,1)S(1)} %get-tuple-element.116), kind=kOutput, calls=%fused_computation.11 | convolution fusion | flops 255799296 | bytes 11022336 | tf_op jit(solution)/shard_map/dot_general | solution.py:120
  394.9 1.1 fusion.68
  395.9 2.4 fusion.66
  398.3 0.8 pad_maximum_fusion
  399.5 1.0 fusion.29
  400.5 2.9 fusion
  404.1 0.8 copy.70
  405.5 0.8 copy.72
  406.3 0.8 copy.73
  (88 shorter events, 5.4 us)
Async XLA Ops:
  0.6 12.5 %copy-start = (bf16[768,768]{1,0:T(8,128)(2,1)S(1)}, bf16[768,768]{1,0:T(8,128)(2,1)}, u32[]{:S(2)}) copy-start(bf16[768,768]{1,0:T(8,128)(2,1)} %param.17) | copy-start | bytes 3538948
  0.7 9.1 %copy-start.1 = (bf16[64,16,768]{2,1,0:T(8,128)(2,1)S(1)}, bf16[64,16,768]{2,1,0:T(8,128)(2,1)}, u32[]{:S(2)}) copy-start(bf16[64,16,768]{2,1,0:T(8,128)(2,1)} %param.13) | copy-start | bytes 4718596
  0.7 12.0 %collective-permute-start = (s32[4]{0:T(128)}, s32[4]{0:T(128)S(1)}, u32[]{:S(2)}, u32[]{:S(2)}) collective-permute-start(s32[4]{0:T(128)} %bitcast.62), channel_id=1, source_target_pairs={{0,16},{16,0},{1,17},{17,1},{2,18},{18,2},{3,19},{19,3},{4,20},{20... | collective-permute-start | bytes 56 | tf_op jit(solution)/shard_map/ppermute | solution.py:100
  3.7 37.9 %all-to-all-start = ((bf16[64,16,768]{2,1,0:T(8,128)(2,1)}), bf16[64,16,768]{2,1,0:T(8,128)(2,1)}, u32[]{:S(2)}, u32[]{:S(2)}) async-start(bf16[64,16,768]{2,1,0:T(8,128)(2,1)} %param.13), calls=%async_computation | async-start | bytes 3145728 | tf_op jit(solution)/shard_map/all_to_all | solution.py:1019
  9.7 1.7 copy-start.15
  9.7 2.9 copy-start.16
  9.7 3.1 copy-start.10
  208.7 7.3 %copy-start.6 = (f32[7,64,768]{2,1,0:T(8,128)S(1)}, f32[7,64,768]{2,1,0:T(8,128)}, u32[]{:S(2)}) copy-start(f32[7,64,768]{2,1,0:T(8,128)} %get-tuple-element.44) | copy-start | bytes 4128772
  208.7 39.2 %all-to-all-start.1 = ((bf16[64,16,768]{2,1,0:T(8,128)(2,1)}), bf16[64,16,768]{2,1,0:T(8,128)(2,1)}, u32[]{:S(2)}, u32[]{:S(2)}) async-start(bf16[64,16,768]{2,1,0:T(8,128)(2,1)} %copy.51), calls=%async_computation.1 | async-start | bytes 3145728 | tf_op jit(solution)/shard_map/all_to_all | solution.py:1019
  216.0 1.4 copy-start.3
  217.4 2.0 copy-start.18
  217.4 2.0 copy-start.19
  219.4 2.5 copy-start.5
  219.4 2.5 copy-start.17
  219.4 5.0 %slice-start = ((s8[6291456]{0:T(1024)(128)(4,1)}), s8[4194304]{0:T(1024)(128)(4,1)S(1)}, s32[]{:S(2)}) async-start(s8[6291456]{0:T(1024)(128)(4,1)} %bitcast.70), calls=%async_computation.2 | async-start | bytes 8388608
  219.4 5.0 %copy-start.20 = (bf16[1024,768]{1,0:T(8,128)(2,1)S(1)}, bf16[1024,768]{1,0:T(8,128)(2,1)}, u32[]{:S(2)}) copy-start(bf16[1024,768]{1,0:T(8,128)(2,1)} %get-tuple-element.45) | copy-start | bytes 4718596
  221.9 2.5 slice-start.1
  221.9 10.7 %slice-start.2 = ((s8[4718592]{0:T(1024)(128)(4,1)}), s8[4194304]{0:T(1024)(128)(4,1)S(1)}, s32[]{:S(2)}) async-start(s8[4718592]{0:T(1024)(128)(4,1)} %bitcast.72), calls=%async_computation.4 | async-start | bytes 8388608
  224.4 8.2 %slice-start.3 = ((s8[4718592]{0:T(1024)(128)(4,1)}), s8[524288]{0:T(1024)(128)(4,1)S(1)}, s32[]{:S(2)}) async-start(s8[4718592]{0:T(1024)(128)(4,1)} %bitcast.72), calls=%async_computation.5 | async-start | bytes 1048576
  224.4 8.2 %copy-start.21 = (bf16[1024,768]{1,0:T(8,128)(2,1)S(1)}, bf16[1024,768]{1,0:T(8,128)(2,1)}, u32[]{:S(2)}) copy-start(bf16[1024,768]{1,0:T(8,128)(2,1)} %get-tuple-element.49) | copy-start | bytes 4718596
  231.3 6.6 %slice-start.4 = ((s8[6291456]{0:T(1024)(128)(4,1)}), s8[2097152]{0:T(1024)(128)(4,1)S(1)}, s32[]{:S(2)}) async-start(s8[6291456]{0:T(1024)(128)(4,1)} %bitcast.74), calls=%async_computation.6 | async-start | bytes 4194304
  232.6 5.4 %slice-start.5 = ((s8[6291456]{0:T(1024)(128)(4,1)}), s8[4194304]{0:T(1024)(128)(4,1)S(1)}, s32[]{:S(2)}) async-start(s8[6291456]{0:T(1024)(128)(4,1)} %bitcast.74), calls=%async_computation.7 | async-start | bytes 8388608
  232.6 5.4 %copy-start.22 = (bf16[1024,768]{1,0:T(8,128)(2,1)S(1)}, bf16[1024,768]{1,0:T(8,128)(2,1)}, u32[]{:S(2)}) copy-start(bf16[1024,768]{1,0:T(8,128)(2,1)} %get-tuple-element.48) | copy-start | bytes 4718596
  387.8 12.7 %copy-start.4 = (bf16[64,16,768]{2,1,0:T(8,128)(2,1)S(1)}, bf16[64,16,768]{2,1,0:T(8,128)(2,1)}, u32[]{:S(2)}) copy-start(bf16[64,16,768]{2,1,0:T(8,128)(2,1)} %get-tuple-element.54) | copy-start | bytes 4718596
  394.8 3.5 copy-start.11
  394.8 3.5 copy-start.12
  395.9 4.6 %copy-start.2 = (f32[16,64,768]{2,1,0:T(8,128)S(1)}, f32[16,64,768]{2,1,0:T(8,128)}, u32[]{:S(2)}) copy-start(f32[16,64,768]{2,1,0:T(8,128)} %get-tuple-element.39) | copy-start | bytes 9437188
  400.5 2.9 copy-start.14
  400.5 3.6 copy-start.9
  400.5 4.3 %copy-start.13 = (f32[48,768]{1,0:T(8,128)S(1)}, f32[48,768]{1,0:T(8,128)}, u32[]{:S(2)}) copy-start(f32[48,768]{1,0:T(8,128)} %get-tuple-element.147) | copy-start | bytes 442372
  403.4 2.1 copy-start.8
  403.4 2.9 copy-start.7

commit v8 on v7

--- a/solution.py
+++ b/solution.py
@@ -309,22 +309,19 @@
     return flows
 
 
-def flow_plan(grads, kinds, n_pos, n_clip):
+def flow_plan(shapes, kinds, n_pos, n_clip):
     lead = n_pos.bit_length() - 1
     most = lead + len(bits_of(n_clip)) + 1
     dma = pltpu.SemaphoreType.DMA
-    scratch = [dma((len(grads), most)), dma((len(grads), most)), dma((len(grads),))]
+    scratch = [dma((len(shapes), most)), dma((len(shapes), most)), dma((len(shapes),))]
     views, out_shape = [], []
-    for grad, clip_first in zip(grads, kinds):
-        rows, cols = grad.shape
+    for (rows, cols), clip_first in zip(shapes, kinds):
         block = rows // n_pos
-        if isinstance(grad, jax.ShapeDtypeStruct):
-            views.append(pltpu.VMEM((2,) * lead + (block, cols), bf16))
-        else:
-            views.append(grad.reshape((2,) * lead + (block, cols)))
+        views.append((2,) * lead + (block, cols))
         out_shape.append(jax.ShapeDtypeStruct((block, cols), f32))
-        shapes = flow_shapes(flow_stages(n_pos, n_clip, clip_first), n_pos, block, cols)
-        scratch += [pltpu.VMEM(shape, bf16) for shape in [shapes[0]] + shapes]
+        stages = flow_stages(n_pos, n_clip, clip_first)
+        arrived = flow_shapes(stages, n_pos, block, cols)
+        scratch += [pltpu.VMEM(shape, bf16) for shape in [arrived[0]] + arrived]
     return views, out_shape, scratch
 
 
@@ -445,9 +442,17 @@
     pl.when(frame == own - 1)(spread.finish)
 
 
-def space_backward(n_clip, kinds, early, *refs):
+def space_backward(n_clip, kinds, sources, *refs):
     go_ref, qkv_ref, lse_ref, x_ref, h_ref, mod_ref, w_ref, hot_ref, rest_ref = refs[:9]
-    grads, refs = refs[9 : 9 + early], refs[9 + early :]
+    early = len(sources)
+    arrays = 1 + max(source[0] for source in sources)
+    whole, refs = refs[9 : 9 + arrays], refs[9 + arrays :]
+    grads = []
+    for at, first, cols in sources:
+        ref = whole[at]
+        if cols < ref.shape[-1]:
+            ref = ref.at[(slice(None),) * (len(ref.shape) - 1) + (pl.ds(first, cols),)]
+        grads.append(ref)
     dv_ref, dmod_ref = refs[:2]
     outs, refs = refs[2 : 2 + len(kinds)], refs[2 + len(kinds) :]
     e_ref, dqkv_ref, total_ref, small_ref, got_ref, acc_ref, every_ref = refs[:7]
@@ -462,9 +467,18 @@
         n_pos, n_clip, small_ref, every_ref, got_ref, acc_ref, (small_send, small_recv), here()
     )
     stages = max(len(flow.stages) for flow in flows)
+    points = [
+        [(0, 0)],
+        [(1, 0)],
+        [(i, 0) for i in range(2, early)],
+        [],
+        [(0, 1)],
+        [(1, 1)],
+        [(2, 1), (0, 2)],
+    ][: 2 * own - 1]
+    taken = [step for point in points for step in point]
     order = [(i, stage) for stage in range(stages) for i in range(early)]
-    order = [(i, stage) for i, stage in order if stage < len(flows[i].stages)]
-    cuts = [2, early, early + 2]
+    order = [step for step in order if step[1] < len(flows[step[0]].stages) and step not in taken]
 
     @pl.when(frame == 0)
     def _():
@@ -545,6 +559,8 @@
         return 0
 
     lax.fori_loop(0, HEADS // 2, head_pair, 0)
+    for index in range(own):
+        pl.when(frame == index)(partial(advance, points[2 * index]))
     e_ref[...] = bdot_nt(dqkv_ref[...], w_ref[...])
 
     def norm_step(step, sums):
@@ -567,23 +583,22 @@
     for third in range(3):
         cols = slice(third * width, (third + 1) * width)
         total_ref[:, cols] += bdot_tn(h_ref[0], dqkv_ref[:, cols])
-    done = 0
-    for index, cut in enumerate(cuts[: own - 1]):
-        pl.when(frame == index)(partial(advance, order[done:cut]))
-        done = cut
+    for index in range(own - 1):
+        pl.when(frame == index)(partial(advance, points[2 * index + 1]))
 
     @pl.when(frame == own - 1)
     def _():
         tree.start()
         start_late()
-        left = order[done:]
         for stage in range(stages + 1):
-            advance([step for step in left if step[1] == stage])
+            mine = [step for step in order if step[1] == stage]
+            advance([step for step in mine if step[0] > 1])
             if stage < tree.count:
                 tree.take(stage)
             for flow in late:
                 if 0 <= stage - 1 < len(flow.stages):
                     flow.take(stage - 1)
+            advance([step for step in mine if step[0] <= 1])
         dmod_ref[...] = every_ref[...]
         spread.finish()
         tree.finish()
@@ -846,7 +861,7 @@
     )(x, mods, weight)
 
 
-def call_space_backward(go, qkv, lse, x, h, mods, weight, hot, dmod_rest, grads, kinds, n_clip):
+def call_space_backward(go, qkv, lse, x, h, mods, weight, hot, dmod_rest, grads, early, n_clip):
     n_pos, own, places, width = x.shape
     patches = n_pos * places
     pair = 2 * HEAD_DIM
@@ -860,15 +875,20 @@
 
     rows = own * patches
     cut = 3 * width // 512 * 256
-    late = [jax.ShapeDtypeStruct((width, cols), bf16) for cols in (cut, 3 * width - cut)]
-    kinds = kinds + (True, False)
-    views, flow_outs, flow_scratch = flow_plan(list(grads) + late, kinds, n_pos, n_clip)
-    early = len(grads)
+    kinds = tuple(flow[3] for flow in early) + (True, False)
+    sources = tuple(flow[:3] for flow in early)
+    shapes = [(grads[at].shape[0], cols) for at, _, cols in sources]
+    shapes += [(width, cut), (width, 3 * width - cut)]
+    views, flow_outs, flow_scratch = flow_plan(shapes, kinds, n_pos, n_clip)
+    late = [pltpu.VMEM(view, bf16) for view in views[len(early) :]]
+    blocked = [
+        grad.reshape((2,) * lead + (grad.shape[0] // n_pos, grad.shape[1])) for grad in grads
+    ]
     sizes = sum(grad.size for grad in grads)
     dmod_shape = (n_clip, clips, 9 * width)
     swaps = lead + len(bits_of(n_clip))
     return pl.pallas_call(
-        partial(space_backward, n_clip, kinds, early),
+        partial(space_backward, n_clip, kinds, sources),
         grid=(own,),
         in_specs=[
             spread,
@@ -881,7 +901,7 @@
             resident(hot.shape),
             resident(dmod_rest.shape),
         ]
-        + [anywhere] * early,
+        + [anywhere] * len(blocked),
         out_specs=[anywhere, resident(dmod_shape)] + [resident(out.shape) for out in flow_outs],
         out_shape=[
             jax.ShapeDtypeStruct((n_pos * own, places, width), bf16),
@@ -900,7 +920,7 @@
             pltpu.SemaphoreType.DMA((swaps,)),
         ]
         + spread_scratch(own, n_pos, places, width)
-        + views[early:]
+        + late
         + flow_scratch,
         compiler_params=pltpu.CompilerParams(
             vmem_limit_bytes=VMEM_LIMIT, collective_id=1, has_side_effects=True
@@ -911,7 +931,7 @@
             transcendentals=rows * patches * HEADS,
         ),
         name="space_backward",
-    )(go, qkv, lse, x, h, mods, weight, hot, dmod_rest, *views[:early])
+    )(go, qkv, lse, x, h, mods, weight, hot, dmod_rest, *blocked)
 
 
 def call_middle(o_one, x, grad, mods, same_clip, wso, wti, wto, wup, wdn):
@@ -1048,25 +1068,35 @@
     )
     block_out = turn(block_turned)
     grad_o_space = exchange(turn(grad_o_one))
-    early = (
+    grads = (
         weight_grad(h_three, grad_u),
         weight_grad(act, grad_z),
         weight_grad(h_two, grad_qkv_two),
         weight_grad(o_one.reshape(rows, width), grad_y_one),
         weight_grad(o_two, grad_y_two),
     )
+    cut = 3 * width // 512 * 256
+    early = (
+        (0, 0, grads[0].shape[1], False),
+        (1, 0, width, True),
+        (2, cut, 3 * width - cut, False),
+        (2, 0, cut, True),
+        (3, 0, width, True),
+        (4, 0, width, True),
+    )
     own_hot = lax.dynamic_slice_in_dim(onehot, me * own, own, 0)
     hot = jnp.broadcast_to(own_hot[:, :, None], (own, clips, 128))
     dmod_rest = dot_high(onehot.T, sums.transpose(1, 0, 2).reshape(frames, 7 * width))
     (
-        back_places, dmod, g_hidden_up, g_hidden_down, g_temporal_in, g_spatial_out, g_temporal_out,
-        in_low, in_high,
+        back_places, dmod, g_hidden_up, g_hidden_down, time_high, time_low, g_spatial_out,
+        g_temporal_out, in_low, in_high,
     ) = call_space_backward(
         grad_o_space, qkv_one, lse_one, x_space, h_one, own_mods, spatial_in, hot, dmod_rest,
-        early, (False, True, True, True, True), n_clip,
+        grads, early, n_clip,
     )
     grad_tokens = (turn(grad_one) + back_places.astype(f32)).astype(bf16)
     g_spatial_in = jnp.concatenate([in_low, in_high], axis=1)
+    g_temporal_in = jnp.concatenate([time_low, time_high], axis=1)
     dmod = dmod.reshape(n_clip * clips, 9 * width)
 
     def own_columns(values):

time: 413 us -> 420 us (1.017)
  Pallas kernels: 297 us -> 304 us
    pallas_call x1, Pallas kernels: 138 us -> 145 us  [call_space_backward(): pl.pallas_call(partial(space_backward, n_clip, kinds, sources), grid=(own...]
    unnamed x65 -> x66, local copies, waits for them, and re-layouts: 8.76 us -> 8.02 us
where the time goes in v8:
time: 420 us; the launch traced here: 415 us
  Pallas kernels  304 us (72%)
  matrix products  44.2 us (11%)
  waiting for transfers between devices  22.5 us (5%)
  local copies, waits for them, and re-layouts  20.1 us (5%)
  starting transfers between devices  16.3 us (4%)
  other arithmetic  5.87 us (1%)
    pallas_call x1, Pallas kernels, call_space_backward(): pl.pallas_call(partial(space_backward, n_clip, kinds, sources), grid=(own...  145 us
    pallas_call x1, Pallas kernels, call_middle(): pl.pallas_call(middle, grid=(places // count,), in_specs=[chunk, chunk, c...  108 us
    pallas_call x1, Pallas kernels, call_space_forward(): pl.pallas_call(space_forward, grid=(own,), in_specs=[spread, by_frame(2,...  51.2 us
    dot_general x5, matrix products, weight_grad(): jnp.einsum('rd,rk->dk', left, right, preferred_element_type=f32)  24.1 us
    all_to_all x2, waiting for transfers between devices, exchange(): got = lax.all_to_all(sent, 'pos', split_axis=0, concat_axis=0, tiled=True)  22.5 us
    dot_general x5, matrix products, dot_exact(): jnp.dot(jnp.concatenate(parts, axis=0), right, preferred_element_type=f32)  13.4 us
    all_to_all x2, starting transfers between devices, exchange(): got = lax.all_to_all(sent, 'pos', split_axis=0, concat_axis=0, tiled=True)  13.3 us
  transfers between devices with their start and end apart: 3, of which 2 were waited for; matrix products, arithmetic and copies ran while one was open for 10% of the time, Pallas kernels for 0%

profile of v8, /device:TPU:0, one launch (start us, length us, event | category | flops | bytes accessed | tf_op | source)
XLA Modules:
  0.0 414.9 jit_solution(13784951368079145331)
XLA Ops:
  0.7 3.1 collective-permute-start
  3.7 6.0 %all-to-all-start = ((bf16[64,16,768]{2,1,0:T(8,128)(2,1)}), bf16[64,16,768]{2,1,0:T(8,128)(2,1)}, u32[]{:S(2)}, u32[]{:S(2)}) async-start(bf16[64,16,768]{2,1,0:T(8,128)(2,1)} %param.13), calls=%async_computation | async-start | bytes 3145728 | tf_op jit(solution)/shard_map/all_to_all | solution.py:1039
  9.8 1.6 copy.63
  13.5 5.5 %fusion.37 = f32[12,6912]{1,0:T(8,128)S(1)} fusion(bf16[768,6912]{1,0:T(8,128)(2,1)} %param.18, bf16[4,768]{1,0:T(4,128)(2,1)S(1)} %get-tuple-element.111, bf16[4,768]{1,0:T(4,128)(2,1)S(1)} %get-tuple-element.112, bf16[4,768]{1,0:T(4,128)(2,1)S(1)} %get-tuple-element.113), kind=kOutput, calls=%fused_computation.55 | convolution fusion | flops 127457280 | bytes 10967040 | tf_op jit(solution)/shard_map/dot_general | solution.py:120
  19.0 0.9 fusion.9
  20.6 1.5 copy.62
  22.0 19.6 %all-to-all-done = bf16[64,16,768]{2,1,0:T(8,128)(2,1)} async-done(((bf16[64,16,768]{2,1,0:T(8,128)(2,1)}), bf16[64,16,768]{2,1,0:T(8,128)(2,1)}, u32[]{:S(2)}, u32[]{:S(2)}) %all-to-all-start) | async-done | bytes 1572896 | tf_op jit(solution)/shard_map/all_to_all | solution.py:1039
  41.6 51.2 %space_forward.1 = (bf16[4,256,768]{2,1,0:T(8,128)(2,1)}, bf16[4,256,2304]{2,1,0:T(8,128)(2,1)}, bf16[64,16,768]{2,1,0:T(8,128)(2,1)}, f32[4,6,256,128]{3,2,1,0:T(8,128)}) custom-call(bf16[16,4,16,768]{3,2,1,0:T(8,128)(2,1)} %bitcast.x_ref.refs_3_, f32[4,2,768]{2,1,0:T(2,128)} %reshape.108.mod_ref.refs_5_, bf16[768,2304]{1,0:T(8,128)(2,1)} %refs_6_.1), custom_call_target="tpu_custom_call" | custom-call | flops 4429185024 | bytes 12976128 | tf_op jit(solution)/shard_map/space_forward/pallas_call | solution.py:835
  92.8 4.7 %fusion.86 = (bf16[64,16,768]{2,0,1:T(8,128)(2,1)}, bf16[16,64,768]{2,1,0:T(8,128)(2,1)}, bf16[16,64,768]{2,1,0:T(8,128)(2,1)}) fusion(bf16[64,16,768]{2,1,0:T(8,128)(2,1)} %get-tuple-element.38, bf16[64,16,768]{2,1,0:T(8,128)(2,1)} %param.25), kind=kLoop, calls=%fused_computation.122 | loop fusion | bytes 7864320 | tf_op jit(solution)/shard_map/space_forward/pallas_call | solution.py:835
  97.6 107.7 %middle.1 = (bf16[16,64,768]{2,1,0:T(8,128)(2,1)}, bf16[1024,3072]{1,0:T(8,128)(2,1)}, bf16[1024,768]{1,0:T(8,128)(2,1)}, bf16[1024,768]{1,0:T(8,128)(2,1)}, bf1...) custom-call(bf16[16,64,768]{2,1,0:T(8,128)(2,1)} %get-tuple-element., ...), custom_call_target="tpu_custom_call" | custom-call | flops 31406948352 | bytes 40960000 | tf_op jit(solution)/shard_map/middle/pallas_call | solution.py:957
  205.3 3.4 copy.51
  208.7 7.3 %all-to-all-start.1 = ((bf16[64,16,768]{2,1,0:T(8,128)(2,1)}), bf16[64,16,768]{2,1,0:T(8,128)(2,1)}, u32[]{:S(2)}, u32[]{:S(2)}) async-start(bf16[64,16,768]{2,1,0:T(8,128)(2,1)} %copy.51), calls=%async_computation.1 | async-start | bytes 3145728 | tf_op jit(solution)/shard_map/all_to_all | solution.py:1039
  216.1 1.3 copy-done.3
  217.4 2.0 copy.53
  219.5 2.5 convolution_convert_fusion.3
  222.0 2.5 convolution_convert_fusion.4
  224.5 6.9 %convolution_convert_fusion.1 = bf16[768,3072]{1,0:T(8,128)(2,1)} fusion(bf16[1024,768]{1,0:T(8,128)(2,1)S(1)} %copy-done.21, bf16[1024,3072]{1,0:T(8,128)(2,1)S(1)} %bitcast.71), kind=kOutput, calls=%fused_computation.1 | convolution fusion | flops 4834197504 | bytes 12582912 | tf_op jit(solution)/shard_map/rd,rk->dk/dot_general | solution.py:51
  231.4 1.2 fusion.25.refs_8_
  232.6 5.3 %convolution_convert_fusion.2 = bf16[768,2304]{1,0:T(8,128)(2,1)} fusion(bf16[1024,768]{1,0:T(8,128)(2,1)S(1)} %copy-done.22, bf16[1024,2304]{1,0:T(8,128)(2,1)S(1)} %bitcast.73), kind=kOutput, calls=%fused_computation.2 | convolution fusion | flops 3625648128 | bytes 9830400 | tf_op jit(solution)/shard_map/rd,rk->dk/dot_general | solution.py:51
  238.0 6.9 %convolution_convert_fusion = bf16[3072,768]{1,0:T(8,128)(2,1)} fusion(bf16[1024,3072]{1,0:T(8,128)(2,1)S(1)} %bitcast.75, bf16[1024,768]{1,0:T(8,128)(2,1)S(1)} %copy-done.23), kind=kOutput, calls=%fused_computation | convolution fusion | flops 4834197504 | bytes 12582912 | tf_op jit(solution)/shard_map/rd,rk->dk/dot_general | solution.py:51
  244.9 3.0 all-to-all-done.1
  248.6 145.5 %space_backward.1 = (bf16[64,16,768]{2,1,0:T(8,128)(2,1)}, f32[2,4,6912]{2,1,0:T(4,128)}, f32[48,3072]{1,0:T(8,128)}, f32[192,768]{1,0:T(8,128)}, f32[48,1280]{1...) custom-call(bf16[16,4,16,768]{3,2,1,0:T(8,128)(2,1)} %bitcast.11.ref, ...), custom_call_target="tpu_custom_call" | custom-call | flops 9261023232 | bytes 46792704 | tf_op jit(solution)/shard_map/space_backward/pallas_call | solution.py:890
  394.1 1.0 reshape.118
  395.1 6.9 %fusion.1 = f32[24,768]{1,0:T(8,128)S(1)} fusion(bf16[768,6912]{1,0:T(8,128)(2,1)} %param.18, bf16[8,6912]{1,0:T(8,128)(2,1)S(1)} %get-tuple-element.119, bf16[8,6912]{1,0:T(8,128)(2,1)S(1)} %get-tuple-element.120, bf16[8,6912]{1,0:T(8,128)(2,1)S(1)} %get-tuple-element.118), kind=kOutput, calls=%fused_computation.12 | convolution fusion | flops 255799296 | bytes 11022336 | tf_op jit(solution)/shard_map/dot_general | solution.py:120
  402.1 1.1 fusion.68
  403.2 2.4 fusion.66
  405.6 0.8 pad_maximum_fusion.1
  406.4 0.8 pad_maximum_fusion
  407.6 1.0 fusion.29
  408.6 2.9 fusion
  412.8 0.8 copy.70
  413.6 0.8 copy.71
  (90 shorter events, 5.4 us)
Async XLA Ops:
  0.6 12.5 %copy-start = (bf16[768,768]{1,0:T(8,128)(2,1)S(1)}, bf16[768,768]{1,0:T(8,128)(2,1)}, u32[]{:S(2)}) copy-start(bf16[768,768]{1,0:T(8,128)(2,1)} %param.17) | copy-start | bytes 3538948
  0.7 9.1 %copy-start.1 = (bf16[64,16,768]{2,1,0:T(8,128)(2,1)S(1)}, bf16[64,16,768]{2,1,0:T(8,128)(2,1)}, u32[]{:S(2)}) copy-start(bf16[64,16,768]{2,1,0:T(8,128)(2,1)} %param.13) | copy-start | bytes 4718596
  0.7 12.0 %collective-permute-start = (s32[4]{0:T(128)}, s32[4]{0:T(128)S(1)}, u32[]{:S(2)}, u32[]{:S(2)}) collective-permute-start(s32[4]{0:T(128)} %bitcast.62), channel_id=1, source_target_pairs={{0,16},{16,0},{1,17},{17,1},{2,18},{18,2},{3,19},{19,3},{4,20},{20... | collective-permute-start | bytes 56 | tf_op jit(solution)/shard_map/ppermute | solution.py:100
  3.7 37.9 %all-to-all-start = ((bf16[64,16,768]{2,1,0:T(8,128)(2,1)}), bf16[64,16,768]{2,1,0:T(8,128)(2,1)}, u32[]{:S(2)}, u32[]{:S(2)}) async-start(bf16[64,16,768]{2,1,0:T(8,128)(2,1)} %param.13), calls=%async_computation | async-start | bytes 3145728 | tf_op jit(solution)/shard_map/all_to_all | solution.py:1039
  9.7 1.7 copy-start.16
  9.7 2.9 copy-start.17
  9.7 3.1 copy-start.9
  208.7 7.3 %copy-start.6 = (f32[7,64,768]{2,1,0:T(8,128)S(1)}, f32[7,64,768]{2,1,0:T(8,128)}, u32[]{:S(2)}) copy-start(f32[7,64,768]{2,1,0:T(8,128)} %get-tuple-element.45) | copy-start | bytes 4128772
  208.7 39.2 %all-to-all-start.1 = ((bf16[64,16,768]{2,1,0:T(8,128)(2,1)}), bf16[64,16,768]{2,1,0:T(8,128)(2,1)}, u32[]{:S(2)}, u32[]{:S(2)}) async-start(bf16[64,16,768]{2,1,0:T(8,128)(2,1)} %copy.51), calls=%async_computation.1 | async-start | bytes 3145728 | tf_op jit(solution)/shard_map/all_to_all | solution.py:1039
  217.4 2.0 copy-start.19
  217.4 2.0 copy-start.20
  219.5 2.5 copy-start.5
  219.5 2.5 copy-start.18
  219.5 5.0 %slice-start = ((s8[6291456]{0:T(1024)(128)(4,1)}), s8[4194304]{0:T(1024)(128)(4,1)S(1)}, s32[]{:S(2)}) async-start(s8[6291456]{0:T(1024)(128)(4,1)} %bitcast.70), calls=%async_computation.2 | async-start | bytes 8388608
  219.5 5.0 %copy-start.21 = (bf16[1024,768]{1,0:T(8,128)(2,1)S(1)}, bf16[1024,768]{1,0:T(8,128)(2,1)}, u32[]{:S(2)}) copy-start(bf16[1024,768]{1,0:T(8,128)(2,1)} %get-tuple-element.46) | copy-start | bytes 4718596
  222.0 2.5 slice-start.1
  222.0 10.6 %slice-start.2 = ((s8[4718592]{0:T(1024)(128)(4,1)}), s8[4194304]{0:T(1024)(128)(4,1)S(1)}, s32[]{:S(2)}) async-start(s8[4718592]{0:T(1024)(128)(4,1)} %bitcast.72), calls=%async_computation.4 | async-start | bytes 8388608
  224.5 8.2 %slice-start.3 = ((s8[4718592]{0:T(1024)(128)(4,1)}), s8[524288]{0:T(1024)(128)(4,1)S(1)}, s32[]{:S(2)}) async-start(s8[4718592]{0:T(1024)(128)(4,1)} %bitcast.72), calls=%async_computation.5 | async-start | bytes 1048576
  224.5 8.1 %copy-start.22 = (bf16[1024,768]{1,0:T(8,128)(2,1)S(1)}, bf16[1024,768]{1,0:T(8,128)(2,1)}, u32[]{:S(2)}) copy-start(bf16[1024,768]{1,0:T(8,128)(2,1)} %get-tuple-element.50) | copy-start | bytes 4718596
  231.4 6.6 %slice-start.4 = ((s8[6291456]{0:T(1024)(128)(4,1)}), s8[2097152]{0:T(1024)(128)(4,1)S(1)}, s32[]{:S(2)}) async-start(s8[6291456]{0:T(1024)(128)(4,1)} %bitcast.74), calls=%async_computation.6 | async-start | bytes 4194304
  232.6 5.4 %slice-start.5 = ((s8[6291456]{0:T(1024)(128)(4,1)}), s8[4194304]{0:T(1024)(128)(4,1)S(1)}, s32[]{:S(2)}) async-start(s8[6291456]{0:T(1024)(128)(4,1)} %bitcast.74), calls=%async_computation.7 | async-start | bytes 8388608
  232.6 5.4 %copy-start.23 = (bf16[1024,768]{1,0:T(8,128)(2,1)S(1)}, bf16[1024,768]{1,0:T(8,128)(2,1)}, u32[]{:S(2)}) copy-start(bf16[1024,768]{1,0:T(8,128)(2,1)} %get-tuple-element.49) | copy-start | bytes 4718596
  395.1 10.5 %copy-start.13 = (f32[48,1024]{1,0:T(8,128)S(1)}, f32[48,1024]{1,0:T(8,128)}, u32[]{:S(2)}) copy-start(f32[48,1024]{1,0:T(8,128)} %get-tuple-element.60) | copy-start | bytes 589828
  395.1 11.2 %copy-start.12 = (f32[48,1024]{1,0:T(8,128)S(1)}, f32[48,1024]{1,0:T(8,128)}, u32[]{:S(2)}) copy-start(f32[48,1024]{1,0:T(8,128)} %get-tuple-element.57) | copy-start | bytes 589828
  402.1 3.5 copy-start.11
  402.1 4.3 %copy-start.10 = (f32[48,1280]{1,0:T(8,128)S(1)}, f32[48,1280]{1,0:T(8,128)}, u32[]{:S(2)}) copy-start(f32[48,1280]{1,0:T(8,128)} %get-tuple-element.58) | copy-start | bytes 737284
  403.2 5.4 %copy-start.4 = (bf16[64,16,768]{2,1,0:T(8,128)(2,1)S(1)}, bf16[64,16,768]{2,1,0:T(8,128)(2,1)}, u32[]{:S(2)}) copy-start(bf16[64,16,768]{2,1,0:T(8,128)(2,1)} %get-tuple-element.55) | copy-start | bytes 4718596
  405.6 3.0 copy-start.2
  408.6 2.9 copy-start.15
  408.6 3.6 copy-start.14
  408.6 4.2 %copy-start.8 = (f32[48,3072]{1,0:T(8,128)S(1)}, f32[48,3072]{1,0:T(8,128)}, u32[]{:S(2)}) copy-start(f32[48,3072]{1,0:T(8,128)} %get-tuple-element.150) | copy-start | bytes 1769476
  411.5 2.1 copy-start.7
  (1 other events, 1.4 us)

commit v9 on v7

--- a/solution.py
+++ b/solution.py
@@ -417,9 +417,13 @@
         return 0
 
     lax.fori_loop(0, patches // ROWS, norm_step, 0)
-    for part in range(3):
-        cols = slice(part * width, (part + 1) * width)
+
+    def project(third, _):
+        cols = pl.ds(pl.multiple_of(third * width, width), width)
         qkv_ref[0, :, cols] = bdot(h_ref[0], w_ref[:, cols]).astype(bf16)
+        return 0
+
+    lax.fori_loop(0, 3, project, 0)
     masks = pair_masks(1.0 / math.sqrt(HEAD_DIM))
     is_low = lax.broadcasted_iota(jnp.int32, (1, pair), 1) < HEAD_DIM
 
@@ -476,7 +480,12 @@
         spread.greet(len(others))
         for flow in flows[:early]:
             flow.start()
-        total_ref[...] = jnp.zeros_like(total_ref)
+
+        def clear(step, _):
+            total_ref[pl.ds(step * 8, 8), :] = jnp.zeros((8, total_ref.shape[1]), f32)
+            return 0
+
+        lax.fori_loop(0, total_ref.shape[0] // 8, clear, 0)
         small_ref[:, : 2 * x_ref.shape[3]] = jnp.zeros_like(small_ref[:, : 2 * x_ref.shape[3]])
         small_ref[:, 2 * x_ref.shape[3] :] = rest_ref[...]
 
@@ -564,9 +573,13 @@
     hot = hot_ref[frame][:, 0:1]
     small_ref[:, :width] += hot * jnp.sum(shift_sum, axis=0, keepdims=True)
     small_ref[:, width : 2 * width] += hot * jnp.sum(scale_sum, axis=0, keepdims=True)
-    for third in range(3):
-        cols = slice(third * width, (third + 1) * width)
+
+    def accumulate(third, _):
+        cols = pl.ds(pl.multiple_of(third * width, width), width)
         total_ref[:, cols] += bdot_tn(h_ref[0], dqkv_ref[:, cols])
+        return 0
+
+    lax.fori_loop(0, 3, accumulate, 0)
     done = 0
     for index, cut in enumerate(cuts[: own - 1]):
         pl.when(frame == index)(partial(advance, order[done:cut]))
@@ -577,13 +590,16 @@
         tree.start()
         start_late()
         left = order[done:]
-        for stage in range(stages + 1):
-            advance([step for step in left if step[1] == stage])
-            if stage < tree.count:
-                tree.take(stage)
+        for turn in range(stages):
+            mine = [step for step in left if step[1] == turn + 1]
+            if turn > 0:
+                advance([step for step in mine if step[0] < 2])
+            if turn < tree.count:
+                tree.take(turn)
             for flow in late:
-                if 0 <= stage - 1 < len(flow.stages):
-                    flow.take(stage - 1)
+                if turn < len(flow.stages):
+                    flow.take(turn)
+            advance([step for step in mine if turn == 0 or step[0] >= 2])
         dmod_ref[...] = every_ref[...]
         spread.finish()
         tree.finish()
@@ -632,9 +648,13 @@
         return 0
 
     lax.fori_loop(0, steps, step_one, 0)
-    for third in range(3):
-        cols = slice(third * width, (third + 1) * width)
+
+    def project(third, _):
+        cols = pl.ds(pl.multiple_of(third * width, width), width)
         qkv_ref[:, cols] = bdot(h2_ref[...], wti_ref[:, cols]).astype(bf16)
+        return 0
+
+    lax.fori_loop(0, 3, project, 0)
 
     masks = pair_masks(1.0)
     masks_q = pair_masks(factor)

time: 413 us -> 412 us (level); the launches traced: 408 us -> 411 us
  Pallas kernels: 297 us -> 302 us
where the time goes in v9:
time: 412 us; the launch traced here: 411 us
  Pallas kernels  302 us (73%)
  matrix products  44.3 us (11%)
  waiting for transfers between devices  22.5 us (5%)
  local copies, waits for them, and re-layouts  20.8 us (5%)
  starting transfers between devices  16.1 us (4%)
  other arithmetic  5.07 us (1%)
    pallas_call x1, Pallas kernels, call_space_backward(): pl.pallas_call(partial(space_backward, n_clip, kinds, early), grid=(own,)...  142 us
    pallas_call x1, Pallas kernels, call_middle(): pl.pallas_call(middle, grid=(places // count,), in_specs=[chunk, chunk, c...  108 us
    pallas_call x1, Pallas kernels, call_space_forward(): pl.pallas_call(space_forward, grid=(own,), in_specs=[spread, by_frame(2,...  51.6 us
    dot_general x5, matrix products, weight_grad(): jnp.einsum('rd,rk->dk', left, right, preferred_element_type=f32)  24.2 us
    all_to_all x2, waiting for transfers between devices, exchange(): got = lax.all_to_all(sent, 'pos', split_axis=0, concat_axis=0, tiled=True)  22.5 us
    dot_general x5, matrix products, dot_exact(): jnp.dot(jnp.concatenate(parts, axis=0), right, preferred_element_type=f32)  13.4 us
    all_to_all x2, starting transfers between devices, exchange(): got = lax.all_to_all(sent, 'pos', split_axis=0, concat_axis=0, tiled=True)  13 us
    unnamed x65, local copies, waits for them, and re-layouts  8.76 us
  transfers between devices with their start and end apart: 3, of which 2 were waited for; matrix products, arithmetic and copies ran while one was open for 10% of the time, Pallas kernels for 0%

profile of v9, /device:TPU:0, one launch (start us, length us, event | category | flops | bytes accessed | tf_op | source)
XLA Modules:
  0.0 411.3 jit_solution(3139872957084932031)
XLA Ops:
  0.7 3.1 collective-permute-start
  3.7 6.0 %all-to-all-start = ((bf16[64,16,768]{2,1,0:T(8,128)(2,1)}), bf16[64,16,768]{2,1,0:T(8,128)(2,1)}, u32[]{:S(2)}, u32[]{:S(2)}) async-start(bf16[64,16,768]{2,1,0:T(8,128)(2,1)} %param.13), calls=%async_computation | async-start | bytes 3145728 | tf_op jit(solution)/shard_map/all_to_all | solution.py:1039
  9.8 1.6 copy.63
  13.4 5.5 %fusion.37 = f32[12,6912]{1,0:T(8,128)S(1)} fusion(bf16[768,6912]{1,0:T(8,128)(2,1)} %param.18, bf16[4,768]{1,0:T(4,128)(2,1)S(1)} %get-tuple-element.109, bf16[4,768]{1,0:T(4,128)(2,1)S(1)} %get-tuple-element.110, bf16[4,768]{1,0:T(4,128)(2,1)S(1)} %get-tuple-element.111), kind=kOutput, calls=%fused_computation.54 | convolution fusion | flops 127457280 | bytes 10967040 | tf_op jit(solution)/shard_map/dot_general | solution.py:120
  19.0 0.9 fusion.9
  20.5 1.5 copy.62
  22.0 19.6 %all-to-all-done = bf16[64,16,768]{2,1,0:T(8,128)(2,1)} async-done(((bf16[64,16,768]{2,1,0:T(8,128)(2,1)}), bf16[64,16,768]{2,1,0:T(8,128)(2,1)}, u32[]{:S(2)}, u32[]{:S(2)}) %all-to-all-start) | async-done | bytes 1572896 | tf_op jit(solution)/shard_map/all_to_all | solution.py:1039
  41.6 51.6 %space_forward.1 = (bf16[4,256,768]{2,1,0:T(8,128)(2,1)}, bf16[4,256,2304]{2,1,0:T(8,128)(2,1)}, bf16[64,16,768]{2,1,0:T(8,128)(2,1)}, f32[4,6,256,128]{3,2,1,0:T(8,128)}) custom-call(bf16[16,4,16,768]{3,2,1,0:T(8,128)(2,1)} %bitcast.x_ref.refs_3_, f32[4,2,768]{2,1,0:T(2,128)} %reshape.108.mod_ref.refs_5_, bf16[768,2304]{1,0:T(8,128)(2,1)} %refs_6_.1), custom_call_target="tpu_custom_call" | custom-call | flops 4429185024 | bytes 12976128 | tf_op jit(solution)/shard_map/space_forward/pallas_call | solution.py:840
  93.2 4.7 %fusion.86 = (bf16[64,16,768]{2,0,1:T(8,128)(2,1)}, bf16[16,64,768]{2,1,0:T(8,128)(2,1)}, bf16[16,64,768]{2,1,0:T(8,128)(2,1)}) fusion(bf16[64,16,768]{2,1,0:T(8,128)(2,1)} %get-tuple-element.37, bf16[64,16,768]{2,1,0:T(8,128)(2,1)} %param.25), kind=kLoop, calls=%fused_computation.121 | loop fusion | bytes 7864320 | tf_op jit(solution)/shard_map/space_forward/pallas_call | solution.py:840
  97.9 108.4 %middle.1 = (bf16[16,64,768]{2,1,0:T(8,128)(2,1)}, bf16[1024,3072]{1,0:T(8,128)(2,1)}, bf16[1024,768]{1,0:T(8,128)(2,1)}, bf16[1024,768]{1,0:T(8,128)(2,1)}, bf1...) custom-call(bf16[16,64,768]{2,1,0:T(8,128)(2,1)} %get-tuple-element., ...), custom_call_target="tpu_custom_call" | custom-call | flops 31406948352 | bytes 40960000 | tf_op jit(solution)/shard_map/middle/pallas_call | solution.py:957
  206.3 3.4 copy.51
  209.7 7.1 %all-to-all-start.1 = ((bf16[64,16,768]{2,1,0:T(8,128)(2,1)}), bf16[64,16,768]{2,1,0:T(8,128)(2,1)}, u32[]{:S(2)}, u32[]{:S(2)}) async-start(bf16[64,16,768]{2,1,0:T(8,128)(2,1)} %copy.51), calls=%async_computation.1 | async-start | bytes 3145728 | tf_op jit(solution)/shard_map/all_to_all | solution.py:1039
  216.9 1.3 copy-done.3
  218.2 2.0 copy.53
  220.2 2.5 convolution_convert_fusion.3
  222.7 2.5 convolution_convert_fusion.4
  225.3 6.9 %convolution_convert_fusion.1 = bf16[768,3072]{1,0:T(8,128)(2,1)} fusion(bf16[1024,768]{1,0:T(8,128)(2,1)S(1)} %copy-done.20, bf16[1024,3072]{1,0:T(8,128)(2,1)S(1)} %bitcast.71), kind=kOutput, calls=%fused_computation.1 | convolution fusion | flops 4834197504 | bytes 12582912 | tf_op jit(solution)/shard_map/rd,rk->dk/dot_general | solution.py:51
  232.2 1.2 fusion.25.refs_8_
  233.4 5.3 %convolution_convert_fusion.2 = bf16[768,2304]{1,0:T(8,128)(2,1)} fusion(bf16[1024,768]{1,0:T(8,128)(2,1)S(1)} %copy-done.21, bf16[1024,2304]{1,0:T(8,128)(2,1)S(1)} %bitcast.73), kind=kOutput, calls=%fused_computation.2 | convolution fusion | flops 3625648128 | bytes 9830400 | tf_op jit(solution)/shard_map/rd,rk->dk/dot_general | solution.py:51
  238.8 7.0 %convolution_convert_fusion = bf16[3072,768]{1,0:T(8,128)(2,1)} fusion(bf16[1024,3072]{1,0:T(8,128)(2,1)S(1)} %bitcast.75, bf16[1024,768]{1,0:T(8,128)(2,1)S(1)} %copy-done.22), kind=kOutput, calls=%fused_computation | convolution fusion | flops 4834197504 | bytes 12582912 | tf_op jit(solution)/shard_map/rd,rk->dk/dot_general | solution.py:51
  245.8 2.9 all-to-all-done.1
  249.4 141.5 %space_backward.1 = (bf16[64,16,768]{2,1,0:T(8,128)(2,1)}, f32[2,4,6912]{2,1,0:T(4,128)}, f32[48,3072]{1,0:T(8,128)}, f32[192,768]{1,0:T(8,128)}, f32[48,2304]{1...) custom-call(bf16[16,4,16,768]{3,2,1,0:T(8,128)(2,1)} %bitcast.11.refs_0_, ...), custom_call_target="tpu_custom_call" | custom-call | flops 9261023232 | bytes 46792704 | tf_op jit(solution)/shard_map/space_backward/pallas_call | solution.py:890
  390.9 1.0 reshape.118
  392.0 7.0 %fusion.1 = f32[24,768]{1,0:T(8,128)S(1)} fusion(bf16[768,6912]{1,0:T(8,128)(2,1)} %param.18, bf16[8,6912]{1,0:T(8,128)(2,1)S(1)} %get-tuple-element.117, bf16[8,6912]{1,0:T(8,128)(2,1)S(1)} %get-tuple-element.118, bf16[8,6912]{1,0:T(8,128)(2,1)S(1)} %get-tuple-element.116), kind=kOutput, calls=%fused_computation.11 | convolution fusion | flops 255799296 | bytes 11022336 | tf_op jit(solution)/shard_map/dot_general | solution.py:120
  399.0 1.1 fusion.68
  400.1 2.4 fusion.66
  402.5 0.8 pad_maximum_fusion
  403.7 1.0 fusion.29
  404.7 2.9 fusion
  408.2 0.8 copy.70
  409.6 0.8 copy.72
  410.5 0.8 copy.73
  (88 shorter events, 5.4 us)
Async XLA Ops:
  0.6 12.5 %copy-start = (bf16[768,768]{1,0:T(8,128)(2,1)S(1)}, bf16[768,768]{1,0:T(8,128)(2,1)}, u32[]{:S(2)}) copy-start(bf16[768,768]{1,0:T(8,128)(2,1)} %param.17) | copy-start | bytes 3538948
  0.7 9.1 %copy-start.1 = (bf16[64,16,768]{2,1,0:T(8,128)(2,1)S(1)}, bf16[64,16,768]{2,1,0:T(8,128)(2,1)}, u32[]{:S(2)}) copy-start(bf16[64,16,768]{2,1,0:T(8,128)(2,1)} %param.13) | copy-start | bytes 4718596
  0.7 12.0 %collective-permute-start = (s32[4]{0:T(128)}, s32[4]{0:T(128)S(1)}, u32[]{:S(2)}, u32[]{:S(2)}) collective-permute-start(s32[4]{0:T(128)} %bitcast.62), channel_id=1, source_target_pairs={{0,16},{16,0},{1,17},{17,1},{2,18},{18,2},{3,19},{19,3},{4,20},{20... | collective-permute-start | bytes 56 | tf_op jit(solution)/shard_map/ppermute | solution.py:100
  3.7 37.9 %all-to-all-start = ((bf16[64,16,768]{2,1,0:T(8,128)(2,1)}), bf16[64,16,768]{2,1,0:T(8,128)(2,1)}, u32[]{:S(2)}, u32[]{:S(2)}) async-start(bf16[64,16,768]{2,1,0:T(8,128)(2,1)} %param.13), calls=%async_computation | async-start | bytes 3145728 | tf_op jit(solution)/shard_map/all_to_all | solution.py:1039
  9.7 1.7 copy-start.15
  9.7 2.9 copy-start.16
  9.7 3.1 copy-start.10
  209.7 7.1 %copy-start.6 = (f32[7,64,768]{2,1,0:T(8,128)S(1)}, f32[7,64,768]{2,1,0:T(8,128)}, u32[]{:S(2)}) copy-start(f32[7,64,768]{2,1,0:T(8,128)} %get-tuple-element.44) | copy-start | bytes 4128772
  209.7 39.0 %all-to-all-start.1 = ((bf16[64,16,768]{2,1,0:T(8,128)(2,1)}), bf16[64,16,768]{2,1,0:T(8,128)(2,1)}, u32[]{:S(2)}, u32[]{:S(2)}) async-start(bf16[64,16,768]{2,1,0:T(8,128)(2,1)} %copy.51), calls=%async_computation.1 | async-start | bytes 3145728 | tf_op jit(solution)/shard_map/all_to_all | solution.py:1039
  216.8 1.4 copy-start.3
  218.2 2.0 copy-start.18
  218.2 2.0 copy-start.19
  220.2 2.5 copy-start.5
  220.2 2.5 copy-start.17
  220.2 5.0 %slice-start = ((s8[6291456]{0:T(1024)(128)(4,1)}), s8[4194304]{0:T(1024)(128)(4,1)S(1)}, s32[]{:S(2)}) async-start(s8[6291456]{0:T(1024)(128)(4,1)} %bitcast.70), calls=%async_computation.2 | async-start | bytes 8388608
  220.2 5.0 %copy-start.20 = (bf16[1024,768]{1,0:T(8,128)(2,1)S(1)}, bf16[1024,768]{1,0:T(8,128)(2,1)}, u32[]{:S(2)}) copy-start(bf16[1024,768]{1,0:T(8,128)(2,1)} %get-tuple-element.45) | copy-start | bytes 4718596
  222.7 2.5 slice-start.1
  222.7 10.7 %slice-start.2 = ((s8[4718592]{0:T(1024)(128)(4,1)}), s8[4194304]{0:T(1024)(128)(4,1)S(1)}, s32[]{:S(2)}) async-start(s8[4718592]{0:T(1024)(128)(4,1)} %bitcast.72), calls=%async_computation.4 | async-start | bytes 8388608
  225.2 8.2 %slice-start.3 = ((s8[4718592]{0:T(1024)(128)(4,1)}), s8[524288]{0:T(1024)(128)(4,1)S(1)}, s32[]{:S(2)}) async-start(s8[4718592]{0:T(1024)(128)(4,1)} %bitcast.72), calls=%async_computation.5 | async-start | bytes 1048576
  225.2 8.2 %copy-start.21 = (bf16[1024,768]{1,0:T(8,128)(2,1)S(1)}, bf16[1024,768]{1,0:T(8,128)(2,1)}, u32[]{:S(2)}) copy-start(bf16[1024,768]{1,0:T(8,128)(2,1)} %get-tuple-element.49) | copy-start | bytes 4718596
  232.2 6.6 %slice-start.4 = ((s8[6291456]{0:T(1024)(128)(4,1)}), s8[2097152]{0:T(1024)(128)(4,1)S(1)}, s32[]{:S(2)}) async-start(s8[6291456]{0:T(1024)(128)(4,1)} %bitcast.74), calls=%async_computation.6 | async-start | bytes 4194304
  233.4 5.4 %slice-start.5 = ((s8[6291456]{0:T(1024)(128)(4,1)}), s8[4194304]{0:T(1024)(128)(4,1)S(1)}, s32[]{:S(2)}) async-start(s8[6291456]{0:T(1024)(128)(4,1)} %bitcast.74), calls=%async_computation.7 | async-start | bytes 8388608
  233.4 5.4 %copy-start.22 = (bf16[1024,768]{1,0:T(8,128)(2,1)S(1)}, bf16[1024,768]{1,0:T(8,128)(2,1)}, u32[]{:S(2)}) copy-start(bf16[1024,768]{1,0:T(8,128)(2,1)} %get-tuple-element.48) | copy-start | bytes 4718596
  391.9 12.7 %copy-start.4 = (bf16[64,16,768]{2,1,0:T(8,128)(2,1)S(1)}, bf16[64,16,768]{2,1,0:T(8,128)(2,1)}, u32[]{:S(2)}) copy-start(bf16[64,16,768]{2,1,0:T(8,128)(2,1)} %get-tuple-element.54) | copy-start | bytes 4718596
  399.0 3.5 copy-start.11
  399.0 3.5 copy-start.12
  400.1 4.6 %copy-start.2 = (f32[16,64,768]{2,1,0:T(8,128)S(1)}, f32[16,64,768]{2,1,0:T(8,128)}, u32[]{:S(2)}) copy-start(f32[16,64,768]{2,1,0:T(8,128)} %get-tuple-element.39) | copy-start | bytes 9437188
  404.7 2.9 copy-start.14
  404.7 3.6 copy-start.9
  404.7 4.3 %copy-start.13 = (f32[48,768]{1,0:T(8,128)S(1)}, f32[48,768]{1,0:T(8,128)}, u32[]{:S(2)}) copy-start(f32[48,768]{1,0:T(8,128)} %get-tuple-element.147) | copy-start | bytes 442372
  407.6 2.1 copy-start.8
  407.6 2.9 copy-start.7

commit v10 on v9

--- a/solution.py
+++ b/solution.py
@@ -108,6 +108,23 @@
     for bit in bits_of(size):
         values = jnp.concatenate([values, swap(values, axis, size, bit)], axis=0)
     return values
+
+
+def first_swap(grad, n_pos):
+    rows, cols = grad.shape
+    split = grad.reshape(n_pos // 2, 2, rows // n_pos, cols)
+    side = lax.rem(lax.axis_index("pos"), 2)
+    keep = lax.dynamic_index_in_dim(split, side, 1, keepdims=False)
+    send = lax.dynamic_index_in_dim(split, 1 - side, 1, keepdims=False)
+    return (keep.astype(f32) + swap(send, "pos", n_pos, 1).astype(f32)).astype(bf16)
+
+
+def column_swap(values, n_clip):
+    half = values.shape[-1] // 2
+    low, high = values[..., :half], values[..., half:]
+    upper = lax.rem(lax.axis_index("clip"), 2) == 1
+    keep, send = jnp.where(upper, high, low), jnp.where(upper, low, high)
+    return (keep.astype(f32) + swap(send, "clip", n_clip, 1).astype(f32)).astype(bf16)
 
 
 def dot_exact(left, right):
@@ -121,18 +138,18 @@
     return got[:count] + (got[count : 2 * count] + got[2 * count :])
 
 
-def flow_stages(n_pos, n_clip, clip_first):
+def flow_stages(n_pos, n_clip, clip_first, skip=0):
     pos = [("pos", bit, "halve") for bit in bits_of(n_pos)]
     clip = bits_of(n_clip)
     if not clip_first:
-        return pos + [("clip", bit, "sum") for bit in clip]
+        return (pos + [("clip", bit, "sum") for bit in clip])[skip:]
     first = [("clip", clip[0], "columns")]
     last = [("clip", clip[0], "gather")]
-    return pos[:1] + first + pos[1:] + [("clip", bit, "sum") for bit in clip[1:]] + last
-
-
-def flow_shapes(stages, n_pos, block, cols):
-    lead = n_pos.bit_length() - 1
+    stages = pos[:1] + first + pos[1:] + [("clip", bit, "sum") for bit in clip[1:]] + last
+    return stages[skip:]
+
+
+def flow_shapes(stages, lead, block, cols):
     shapes = []
     for _, _, what in stages:
         if what == "halve":
@@ -301,30 +318,29 @@
 def make_flows(n_pos, n_clip, kinds, grads, outs, scratch):
     sems, rest = scratch[:3], list(scratch[3:])
     flows = []
-    for number, clip_first in enumerate(kinds):
-        stages = flow_stages(n_pos, n_clip, clip_first)
+    for number, (clip_first, skip) in enumerate(kinds):
+        stages = flow_stages(n_pos, n_clip, clip_first, skip)
         keep, gots = rest[0], rest[1 : 1 + len(stages)]
         rest = rest[1 + len(stages) :]
         flows.append(Flow(number, stages, grads[number], outs[number], keep, gots, sems, here()))
     return flows
 
 
-def flow_plan(grads, kinds, n_pos, n_clip):
+def flow_plan(shapes, kinds, n_pos, n_clip):
     lead = n_pos.bit_length() - 1
     most = lead + len(bits_of(n_clip)) + 1
     dma = pltpu.SemaphoreType.DMA
-    scratch = [dma((len(grads), most)), dma((len(grads), most)), dma((len(grads),))]
+    scratch = [dma((len(shapes), most)), dma((len(shapes), most)), dma((len(shapes),))]
     views, out_shape = [], []
-    for grad, clip_first in zip(grads, kinds):
-        rows, cols = grad.shape
-        block = rows // n_pos
-        if isinstance(grad, jax.ShapeDtypeStruct):
-            views.append(pltpu.VMEM((2,) * lead + (block, cols), bf16))
-        else:
-            views.append(grad.reshape((2,) * lead + (block, cols)))
+    for (block, cols), (clip_first, skip) in zip(shapes, kinds):
         out_shape.append(jax.ShapeDtypeStruct((block, cols), f32))
-        shapes = flow_shapes(flow_stages(n_pos, n_clip, clip_first), n_pos, block, cols)
-        scratch += [pltpu.VMEM(shape, bf16) for shape in [shapes[0]] + shapes]
+        if clip_first and skip > 1:
+            cols //= 2
+        left = lead - min(skip, 1)
+        views.append((2,) * left + (block, cols))
+        stages = flow_stages(n_pos, n_clip, clip_first, skip)
+        arrived = flow_shapes(stages, left, block, cols)
+        scratch += [pltpu.VMEM(shape, bf16) for shape in [arrived[0]] + arrived]
     return views, out_shape, scratch
 
 
@@ -466,9 +482,18 @@
         n_pos, n_clip, small_ref, every_ref, got_ref, acc_ref, (small_send, small_recv), here()
     )
     stages = max(len(flow.stages) for flow in flows)
-    order = [(i, stage) for stage in range(stages) for i in range(early)]
-    order = [(i, stage) for i, stage in order if stage < len(flows[i].stages)]
-    cuts = [2, early, early + 2]
+    points = [
+        [(i, 0) for i in range(2, early)],
+        [(1, 0)],
+        [(2, 1), (1, 1), (0, 0)],
+    ][: own - 1]
+    taken = [step for point in points for step in point]
+    order = []
+    for turn in range(stages):
+        for i in range(early):
+            step = (i, turn - kinds[i][1])
+            if 0 <= step[1] < len(flows[i].stages) and step not in taken:
+                order.append((turn, step))
 
     @pl.when(frame == 0)
     def _():
@@ -478,8 +503,8 @@
         for axis, bit in others:
             signal_swap(barrier, place, axis, bit)
         spread.greet(len(others))
-        for flow in flows[:early]:
-            flow.start()
+        for i in [1, 0] + list(range(2, early)):
+            flows[i].start()
 
         def clear(step, _):
             total_ref[pl.ds(step * 8, 8), :] = jnp.zeros((8, total_ref.shape[1]), f32)
@@ -580,26 +605,20 @@
         return 0
 
     lax.fori_loop(0, 3, accumulate, 0)
-    done = 0
-    for index, cut in enumerate(cuts[: own - 1]):
-        pl.when(frame == index)(partial(advance, order[done:cut]))
-        done = cut
+    for index in range(own - 1):
+        pl.when(frame == index)(partial(advance, points[index]))
 
     @pl.when(frame == own - 1)
     def _():
         tree.start()
         start_late()
-        left = order[done:]
-        for turn in range(stages):
-            mine = [step for step in left if step[1] == turn + 1]
-            if turn > 0:
-                advance([step for step in mine if step[0] < 2])
+        for turn in range(stages + 1):
+            advance([step for at, step in order if at == turn])
             if turn < tree.count:
                 tree.take(turn)
             for flow in late:
-                if turn < len(flow.stages):
-                    flow.take(turn)
-            advance([step for step in mine if turn == 0 or step[0] >= 2])
+                if 0 <= turn - 1 < len(flow.stages):
+                    flow.take(turn - 1)
         dmod_ref[...] = every_ref[...]
         spread.finish()
         tree.finish()
@@ -635,6 +654,14 @@
     def mod(index, part):
         return mod_ref[index, part, :]
 
+    def by_columns(product):
+        def one(index, _):
+            cols = pl.ds(pl.multiple_of(index * 256, 256), 256)
+            e_ref[:, cols] = product(cols)
+            return 0
+
+        lax.fori_loop(0, width // 256, one, 0)
+
     y1_ref[...] = bdot(o1_ref[...].reshape(rows, width), wso_ref[...])
 
     def step_one(step, _):
@@ -751,7 +778,7 @@
 
     products(0, ua_ref, aa_ref)
     lax.fori_loop(0, tiles // 2, two_tiles, 0)
-    e_ref[...] = bdot(act_ref[...], wdn_ref[...])
+    by_columns(lambda cols: bdot(act_ref[...], wdn_ref[:, cols]))
 
     def step_three(step, _):
         place, part, flat = at_rows(step)
@@ -762,7 +789,7 @@
         return 0
 
     lax.fori_loop(0, steps, step_three, 0)
-    e_ref[...] = bdot_nt(du_ref[...], wup_ref[...])
+    by_columns(lambda cols: bdot_nt(du_ref[...], wup_ref[cols, :]))
 
     def step_four(step, _):
         place, part, flat = at_rows(step)
@@ -802,7 +829,7 @@
         return 0
 
     lax.fori_loop(0, HEADS // 2, time_pair_back, 0)
-    e_ref[...] = bdot_nt(dqkv_ref[...], wti_ref[...])
+    by_columns(lambda cols: bdot_nt(dqkv_ref[...], wti_ref[cols, :]))
 
     def step_five(step, _):
         place, part, flat = at_rows(step)
@@ -866,7 +893,9 @@
     )(x, mods, weight)
 
 
-def call_space_backward(go, qkv, lse, x, h, mods, weight, hot, dmod_rest, grads, kinds, n_clip):
+def call_space_backward(
+    go, qkv, lse, x, h, mods, weight, hot, dmod_rest, grads, shapes, kinds, n_clip
+):
     n_pos, own, places, width = x.shape
     patches = n_pos * places
     pair = 2 * HEAD_DIM
@@ -880,10 +909,13 @@
 
     rows = own * patches
     cut = 3 * width // 512 * 256
-    late = [jax.ShapeDtypeStruct((width, cols), bf16) for cols in (cut, 3 * width - cut)]
-    kinds = kinds + (True, False)
-    views, flow_outs, flow_scratch = flow_plan(list(grads) + late, kinds, n_pos, n_clip)
+    kinds = kinds + ((True, 0), (False, 0))
+    block = width // n_pos
+    flow_rows = shapes + [(block, cut), (block, 3 * width - cut)]
+    views, flow_outs, flow_scratch = flow_plan(flow_rows, kinds, n_pos, n_clip)
     early = len(grads)
+    late = [pltpu.VMEM(view, bf16) for view in views[early:]]
+    blocked = [grad.reshape(view) for grad, view in zip(grads, views)]
     sizes = sum(grad.size for grad in grads)
     dmod_shape = (n_clip, clips, 9 * width)
     swaps = lead + len(bits_of(n_clip))
@@ -901,7 +933,7 @@
             resident(hot.shape),
             resident(dmod_rest.shape),
         ]
-        + [anywhere] * early,
+        + [anywhere] * len(blocked),
         out_specs=[anywhere, resident(dmod_shape)] + [resident(out.shape) for out in flow_outs],
         out_shape=[
             jax.ShapeDtypeStruct((n_pos * own, places, width), bf16),
@@ -920,7 +952,7 @@
             pltpu.SemaphoreType.DMA((swaps,)),
         ]
         + spread_scratch(own, n_pos, places, width)
-        + views[early:]
+        + late
         + flow_scratch,
         compiler_params=pltpu.CompilerParams(
             vmem_limit_bytes=VMEM_LIMIT, collective_id=1, has_side_effects=True
@@ -931,7 +963,7 @@
             transcendentals=rows * patches * HEADS,
         ),
         name="space_backward",
-    )(go, qkv, lse, x, h, mods, weight, hot, dmod_rest, *views[:early])
+    )(go, qkv, lse, x, h, mods, weight, hot, dmod_rest, *blocked)
 
 
 def call_middle(o_one, x, grad, mods, same_clip, wso, wti, wto, wup, wdn):
@@ -1068,13 +1100,28 @@
     )
     block_out = turn(block_turned)
     grad_o_space = exchange(turn(grad_o_one))
-    early = (
-        weight_grad(h_three, grad_u),
-        weight_grad(act, grad_z),
+    down = weight_grad(act, grad_z)
+    down, h_three, grad_u = lax.optimization_barrier((down, h_three, grad_u))
+    down_block, up_block = down.shape[0] // n_pos, width // n_pos
+    up = weight_grad(h_three, grad_u)
+    up, h_two, grad_qkv_two, o_one, grad_y_one, o_two, grad_y_two = lax.optimization_barrier(
+        (up, h_two, grad_qkv_two, o_one, grad_y_one, o_two, grad_y_two)
+    )
+    grads = (
+        first_swap(up, n_pos),
+        column_swap(first_swap(down, n_pos), n_clip),
         weight_grad(h_two, grad_qkv_two),
         weight_grad(o_one.reshape(rows, width), grad_y_one),
         weight_grad(o_two, grad_y_two),
     )
+    shapes = [
+        (up_block, up.shape[1]),
+        (down_block, width),
+        (up_block, 3 * width),
+        (up_block, width),
+        (up_block, width),
+    ]
+    kinds = ((False, 1), (True, 2), (True, 0), (True, 0), (True, 0))
     own_hot = lax.dynamic_slice_in_dim(onehot, me * own, own, 0)
     hot = jnp.broadcast_to(own_hot[:, :, None], (own, clips, 128))
     dmod_rest = dot_high(onehot.T, sums.transpose(1, 0, 2).reshape(frames, 7 * width))
@@ -1083,7 +1130,7 @@
         in_low, in_high,
     ) = call_space_backward(
         grad_o_space, qkv_one, lse_one, x_space, h_one, own_mods, spatial_in, hot, dmod_rest,
-        early, (False, True, True, True, True), n_clip,
+        grads, shapes, kinds, n_clip,
     )
     grad_tokens = (turn(grad_one) + back_places.astype(f32)).astype(bf16)
     g_spatial_in = jnp.concatenate([in_low, in_high], axis=1)

time: 412 us -> 430 us (1.044)
  waiting for transfers between devices: 22.5 us -> 41.3 us
  Pallas kernels: 302 us -> 284 us
  other arithmetic: 5.07 us -> 11.3 us
  local copies, waits for them, and re-layouts: 20.8 us -> 26.3 us
  matrix products: 44.3 us -> 48.8 us
    ppermute x1 -> x4, waiting for transfers between devices: 0.01 us -> 22.8 us  [swap(): return lax.ppermute(values, axis, [(i, i ^ bit) for i in range(size)])]
    pallas_call x1, Pallas kernels: 142 us -> 124 us  [call_space_backward(): pl.pallas_call(partial(space_backward, n_clip, kinds, early), grid=(own,)...]
    convert_element_type x0 -> x3, other arithmetic: none -> 6.13 us  [the longest x2 4.68 us: first_swap(): (keep.astype(f32) + swap(send, 'pos', n_pos, 1).astype(f32)).astype(bf16)]
    pallas_call x1 -> x0, local copies, waits for them, and re-layouts: 4.7 us -> none  [call_space_forward(): pl.pallas_call(space_forward, grid=(own,), in_specs=[spread, by_frame(2,...]
    unnamed x65 -> x75, local copies, waits for them, and re-layouts: 8.76 us -> 11.3 us
  transfers between devices with their start and end apart: 3 -> 6, of which waited for: 2 -> 2; matrix products, arithmetic and copies ran while one was open for 10% -> 10% of each run, Pallas kernels for 0% -> 0%
where the time goes in v10:
time: 430 us
  Pallas kernels  284 us (66%)
  matrix products  48.8 us (11%)
  waiting for transfers between devices  41.3 us (10%)
  local copies, waits for them, and re-layouts  26.3 us (6%)
  starting transfers between devices  17.1 us (4%)
  other arithmetic  11.3 us (3%)
    pallas_call x1, Pallas kernels, call_space_backward(): pl.pallas_call(partial(space_backward, n_clip, kinds, early), grid=(own,)...  124 us
    pallas_call x1, Pallas kernels, call_middle(): pl.pallas_call(middle, grid=(places // count,), in_specs=[chunk, chunk, c...  108 us
    pallas_call x1, Pallas kernels, call_space_forward(): pl.pallas_call(space_forward, grid=(own,), in_specs=[spread, by_frame(2,...  51.6 us
    dot_general x5, matrix products, weight_grad(): jnp.einsum('rd,rk->dk', left, right, preferred_element_type=f32)  26.2 us
    ppermute x4, waiting for transfers between devices, swap(): return lax.ppermute(values, axis, [(i, i ^ bit) for i in range(size)])  22.8 us
    all_to_all x2, waiting for transfers between devices, exchange(): got = lax.all_to_all(sent, 'pos', split_axis=0, concat_axis=0, tiled=True)  18.5 us
    dot_general x5, matrix products, dot_exact(): jnp.dot(jnp.concatenate(parts, axis=0), right, preferred_element_type=f32)  13.4 us
    all_to_all x2, starting transfers between devices, exchange(): got = lax.all_to_all(sent, 'pos', split_axis=0, concat_axis=0, tiled=True)  12.9 us
  transfers between devices with their start and end apart: 6, of which 2 were waited for; matrix products, arithmetic and copies ran while one was open for 10% of the time, Pallas kernels for 0%

profile of v10, /device:TPU:0, one launch (start us, length us, event | category | flops | bytes accessed | tf_op | source)
XLA Modules:
  0.0 429.9 jit_solution(2148152341662058770)
XLA Ops:
  0.7 3.1 collective-permute-start
  3.7 6.0 %all-to-all-start = ((bf16[64,16,768]{2,1,0:T(8,128)(2,1)}), bf16[64,16,768]{2,1,0:T(8,128)(2,1)}, u32[]{:S(2)}, u32[]{:S(2)}) async-start(bf16[64,16,768]{2,1,0:T(8,128)(2,1)} %param.13), calls=%async_computation | async-start | bytes 3145728 | tf_op jit(solution)/shard_map/all_to_all | solution.py:1071
  9.8 1.6 copy.72
  14.6 5.5 %fusion.39 = f32[12,6912]{1,0:T(8,128)S(1)} fusion(bf16[768,6912]{1,0:T(8,128)(2,1)} %param.18, bf16[4,768]{1,0:T(4,128)(2,1)S(1)} %get-tuple-element.129, bf16[4,768]{1,0:T(4,128)(2,1)S(1)} %get-tuple-element.130, bf16[4,768]{1,0:T(4,128)(2,1)S(1)} %get-tuple-element.131), kind=kOutput, calls=%fused_computation.63 | convolution fusion | flops 127457280 | bytes 10967040 | tf_op jit(solution)/shard_map/dot_general | solution.py:137
  21.7 1.4 copy.71
  23.1 18.5 %all-to-all-done = bf16[64,16,768]{2,1,0:T(8,128)(2,1)} async-done(((bf16[64,16,768]{2,1,0:T(8,128)(2,1)}), bf16[64,16,768]{2,1,0:T(8,128)(2,1)}, u32[]{:S(2)}, u32[]{:S(2)}) %all-to-all-start) | async-done | bytes 1572896 | tf_op jit(solution)/shard_map/all_to_all | solution.py:1071
  41.6 51.6 %space_forward.1 = (bf16[4,256,768]{2,1,0:T(8,128)(2,1)}, bf16[4,256,2304]{2,1,0:T(8,128)(2,1)}, bf16[64,16,768]{2,1,0:T(8,128)(2,1)}, f32[4,6,256,128]{3,2,1,0:T(8,128)}) custom-call(bf16[16,4,16,768]{3,2,1,0:T(8,128)(2,1)} %bitcast.x_ref.refs_3_, f32[4,2,768]{2,1,0:T(2,128)} %reshape.118.mod_ref.refs_5_, bf16[768,2304]{1,0:T(8,128)(2,1)} %refs_6_.1), custom_call_target="tpu_custom_call" | custom-call | flops 4429185024 | bytes 12976128 | tf_op jit(solution)/shard_map/space_forward/pallas_call | solution.py:867
  93.2 4.6 %copy_bitcast_fusion = (bf16[16,64,768]{2,1,0:T(8,128)(2,1)}, bf16[16,64,768]{2,1,0:T(8,128)(2,1)}) fusion(bf16[64,16,768]{2,1,0:T(8,128)(2,1)} %param.25, bf16[64,16,768]{2,1,0:T(8,128)(2,1)} %get-tuple-element.47), kind=kLoop, calls=%fused_computation.13 | loop fusion | bytes 6291456 | tf_op jit(solution)/shard_map/transpose | solution.py:1091
  97.9 107.9 %middle.1 = (bf16[16,64,768]{2,1,0:T(8,128)(2,1)}, bf16[1024,3072]{1,0:T(8,128)(2,1)}, bf16[1024,768]{1,0:T(8,128)(2,1)}, bf16[1024,768]{1,0:T(8,128)(2,1)}, bf1...) custom-call(bf16[16,64,768]{2,1,0:T(8,128)(2,1)} %get-tuple-element., ...), custom_call_target="tpu_custom_call" | custom-call | flops 31406948352 | bytes 40960000 | tf_op jit(solution)/shard_map/middle/pallas_call | solution.py:989
  205.8 8.1 %convolution_convert_fusion.1 = bf16[3072,768]{1,0:T(8,128)(2,1)S(1)} fusion(bf16[1024,3072]{1,0:T(8,128)(2,1)} %get-tuple-element.55, bf16[1024,768]{1,0:T(8,128)(2,1)} %get-tuple-element.56), kind=kOutput, calls=%fused_computation.1 | convolution fusion | flops 4834197504 | bytes 12582912 | tf_op jit(solution)/shard_map/rd,rk->dk/dot_general | solution.py:51
  213.8 1.6 dynamic-slice_bitcast_fusion
  215.4 1.3 copy-done.3
  217.1 5.4 %convolution_convert_fusion = bf16[768,3072]{1,0:T(8,128)(2,1)S(1)} fusion(bf16[1024,768]{1,0:T(8,128)(2,1)S(1)} %copy-done.28, bf16[1024,3072]{1,0:T(8,128)(2,1)S(1)} %copy-done.24), kind=kOutput, calls=%fused_computation | convolution fusion | flops 4834197504 | bytes 12582912 | tf_op jit(solution)/shard_map/rd,rk->dk/dot_general | solution.py:51
  222.5 1.5 dynamic-slice_bitcast_fusion.1
  224.0 1.3 copy-done.2
  225.5 2.0 copy.57
  227.5 6.9 %all-to-all-start.1 = ((bf16[64,16,768]{2,1,0:T(8,128)(2,1)}), bf16[64,16,768]{2,1,0:T(8,128)(2,1)}, u32[]{:S(2)}, u32[]{:S(2)}) async-start(bf16[64,16,768]{2,1,0:T(8,128)(2,1)} %copy.57), calls=%async_computation.1 | async-start | bytes 3145728 | tf_op jit(solution)/shard_map/all_to_all | solution.py:1071
  234.5 1.5 copy.65
  237.3 2.0 copy.61
  239.3 2.5 convolution_convert_fusion.3
  241.8 7.8 %convolution_convert_fusion.2 = bf16[768,2304]{1,0:T(8,128)(2,1)} fusion(bf16[1024,768]{1,0:T(8,128)(2,1)S(1)} %copy-done.29, bf16[1024,2304]{1,0:T(8,128)(2,1)} %get-tuple-element.69), kind=kOutput, calls=%fused_computation.2 | convolution fusion | flops 3625648128 | bytes 9830400 | tf_op jit(solution)/shard_map/rd,rk->dk/dot_general | solution.py:51
  249.7 2.4 fusion
  252.9 2.5 convolution_convert_fusion.4
  255.4 2.3 fusion.1
  257.7 22.8 %collective-permute-done.3 = bf16[8,192,384]{2,1,0:T(8,128)(2,1)S(1)} collective-permute-done((bf16[8,192,384]{2,1,0:T(8,128)(2,1)S(1)}, bf16[8,192,384]{2,1,0:T(8,128)(2,1)S(1)}, u32[]{:S(2)}, u32[]{:S(2)}) %collective-permute-start.3) | collective-permute-done | bytes 1179680 | tf_op jit(solution)/shard_map/ppermute | solution.py:100
  280.5 1.5 add_convert_fusion
  282.6 124.5 %space_backward.1 = (bf16[64,16,768]{2,1,0:T(8,128)(2,1)}, f32[2,4,6912]{2,1,0:T(4,128)}, f32[48,3072]{1,0:T(8,128)}, f32[192,768]{1,0:T(8,128)}, f32[48,2304]{1...) custom-call(bf16[16,4,16,768]{3,2,1,0:T(8,128)(2,1)} %bitcast.11.refs_0_, ...), custom_call_target="tpu_custom_call" | custom-call | flops 9261023232 | bytes 34996224 | tf_op jit(solution)/shard_map/space_backward/pallas_call | solution.py:922
  408.2 7.0 %fusion.3 = f32[24,768]{1,0:T(8,128)S(1)} fusion(bf16[768,6912]{1,0:T(8,128)(2,1)} %param.18, bf16[8,6912]{1,0:T(8,128)(2,1)S(1)} %get-tuple-element.135, bf16[8,6912]{1,0:T(8,128)(2,1)S(1)} %get-tuple-element.136, bf16[8,6912]{1,0:T(8,128)(2,1)S(1)} %get-tuple-element.134), kind=kOutput, calls=%fused_computation.20 | convolution fusion | flops 255799296 | bytes 11022336 | tf_op jit(solution)/shard_map/dot_general | solution.py:137
  415.3 1.8 fusion.70
  417.1 3.2 fusion.68
  421.6 1.7 fusion.31
  423.3 2.9 fusion.2
  (109 shorter events, 14.2 us)
Async XLA Ops:
  0.6 13.1 %copy-start = (bf16[768,768]{1,0:T(8,128)(2,1)S(1)}, bf16[768,768]{1,0:T(8,128)(2,1)}, u32[]{:S(2)}) copy-start(bf16[768,768]{1,0:T(8,128)(2,1)} %param.17) | copy-start | bytes 3538948
  0.7 9.1 %copy-start.1 = (bf16[64,16,768]{2,1,0:T(8,128)(2,1)S(1)}, bf16[64,16,768]{2,1,0:T(8,128)(2,1)}, u32[]{:S(2)}) copy-start(bf16[64,16,768]{2,1,0:T(8,128)(2,1)} %param.13) | copy-start | bytes 4718596
  0.7 12.0 %collective-permute-start = (s32[4]{0:T(128)}, s32[4]{0:T(128)S(1)}, u32[]{:S(2)}, u32[]{:S(2)}) collective-permute-start(s32[4]{0:T(128)} %bitcast.87), channel_id=1, source_target_pairs={{0,16},{16,0},{1,17},{17,1},{2,18},{18,2},{3,19},{19,3},{4,20},{20... | collective-permute-start | bytes 56 | tf_op jit(solution)/shard_map/ppermute | solution.py:100
  3.7 37.9 %all-to-all-start = ((bf16[64,16,768]{2,1,0:T(8,128)(2,1)}), bf16[64,16,768]{2,1,0:T(8,128)(2,1)}, u32[]{:S(2)}, u32[]{:S(2)}) async-start(bf16[64,16,768]{2,1,0:T(8,128)(2,1)} %param.13), calls=%async_computation | async-start | bytes 3145728 | tf_op jit(solution)/shard_map/all_to_all | solution.py:1071
  9.7 2.9 copy-start.23
  9.7 3.1 copy-start.14
  205.7 11.3 %copy-start.24 = (bf16[1024,3072]{1,0:T(8,128)(2,1)S(1)}, bf16[1024,3072]{1,0:T(8,128)(2,1)}, u32[]{:S(2)}) copy-start(bf16[1024,3072]{1,0:T(8,128)(2,1)} %get-tuple-element.60) | copy-start | bytes 18874372
  213.8 2.9 copy-start.3
  213.8 3.3 copy-start.28
  216.8 32.9 %collective-permute-start.2 = (bf16[8,192,768]{2,1,0:T(8,128)(2,1)}, bf16[8,192,768]{2,1,0:T(8,128)(2,1)}, u32[]{:S(2)}, u32[]{:S(2)}) collective-permute-start(bf16[8,192,768]{2,1,0:T(8,128)(2,1)} %dynamic-slice_bitcast_fusion), channel_id=1, source_target_pairs={{0,1},{1,0},{2,3},{3,2},{4,5},{5,4},{6,7},{7,6},{8,9},{9,8},{10,11... | collective-permute-start | bytes 7077896 | tf_op jit(solution)/shard_map/ppermute | solution.py:100
  222.5 2.9 copy-start.2
  222.5 3.0 copy-start.6
  225.4 30.0 %collective-permute-start.1 = (bf16[8,48,3072]{2,1,0:T(8,128)(2,1)}, bf16[8,48,3072]{2,1,0:T(8,128)(2,1)S(1)}, u32[]{:S(2)}, u32[]{:S(2)}) collective-permute-start(bf16[8,48,3072]{2,1,0:T(8,128)(2,1)} %dynamic-slice_bitcast_fusion.1), channel_id=1, source_target_pairs={{0,1},{1,0},{2,3},{3,2},{4,5},{5,4},{6,7},{7,6},{8,9},{9,8},{10,11... | collective-permute-start | bytes 7077896 | tf_op jit(solution)/shard_map/ppermute | solution.py:100
  227.5 54.4 %all-to-all-start.1 = ((bf16[64,16,768]{2,1,0:T(8,128)(2,1)}), bf16[64,16,768]{2,1,0:T(8,128)(2,1)}, u32[]{:S(2)}, u32[]{:S(2)}) async-start(bf16[64,16,768]{2,1,0:T(8,128)(2,1)} %copy.57), calls=%async_computation.1 | async-start | bytes 3145728 | tf_op jit(solution)/shard_map/all_to_all | solution.py:1071
  234.5 2.8 copy-start.5
  239.3 2.5 copy-start.29
  239.3 10.3 %slice-start.2 = ((s8[4718592]{0:T(1024)(128)(4,1)}), s8[4194304]{0:T(1024)(128)(4,1)S(1)}, s32[]{:S(2)}) async-start(s8[4718592]{0:T(1024)(128)(4,1)} %bitcast.75), calls=%async_computation.4 | async-start | bytes 8388608
  241.8 7.8 %slice-start.3 = ((s8[4718592]{0:T(1024)(128)(4,1)}), s8[524288]{0:T(1024)(128)(4,1)S(1)}, s32[]{:S(2)}) async-start(s8[4718592]{0:T(1024)(128)(4,1)} %bitcast.75), calls=%async_computation.5 | async-start | bytes 1048576
  249.6 3.3 copy-start.7
  249.7 3.3 copy-start.25
  252.1 3.3 slice-start
  252.2 28.3 %collective-permute-start.3 = (bf16[8,192,384]{2,1,0:T(8,128)(2,1)S(1)}, bf16[8,192,384]{2,1,0:T(8,128)(2,1)S(1)}, u32[]{:S(2)}, u32[]{:S(2)}) collective-permute-start(bf16[8,192,384]{2,1,0:T(8,128)(2,1)S(1)} %broadcast_select_fusion), channel_id=1, source_target_pairs={{0,16},{16,0},{1,17},{17,1},{2,18},{18,2},{3,19},{19,3},{4,20},{20... | collective-permute-start | bytes 3538952 | tf_op jit(solution)/shard_map/ppermute | solution.py:100
  252.9 2.5 slice-start.1
  408.1 7.0 %copy-start.10 = (f32[24,768]{1,0:T(8,128)S(1)}, f32[24,768]{1,0:T(8,128)}, u32[]{:S(2)}) copy-start(f32[24,768]{1,0:T(8,128)} %copy-done.9) | copy-start | bytes 221188
  408.2 15.1 %copy-start.8 = (bf16[64,16,768]{2,1,0:T(8,128)(2,1)S(1)}, bf16[64,16,768]{2,1,0:T(8,128)(2,1)}, u32[]{:S(2)}) copy-start(bf16[64,16,768]{2,1,0:T(8,128)(2,1)} %get-tuple-element.74) | copy-start | bytes 4718596
  415.2 5.1 %copy-start.16 = (f32[48,1280]{1,0:T(8,128)S(1)}, f32[48,1280]{1,0:T(8,128)}, u32[]{:S(2)}) copy-start(f32[48,1280]{1,0:T(8,128)} %get-tuple-element.77) | copy-start | bytes 737284
  415.2 5.1 %copy-start.17 = (f32[48,1024]{1,0:T(8,128)S(1)}, f32[48,1024]{1,0:T(8,128)}, u32[]{:S(2)}) copy-start(f32[48,1024]{1,0:T(8,128)} %get-tuple-element.76) | copy-start | bytes 589828
  417.1 6.2 %copy-start.4 = (f32[16,64,768]{2,1,0:T(8,128)S(1)}, f32[16,64,768]{2,1,0:T(8,128)}, u32[]{:S(2)}) copy-start(f32[16,64,768]{2,1,0:T(8,128)} %get-tuple-element.49) | copy-start | bytes 9437188
  423.3 2.9 copy-start.19
  423.3 3.6 copy-start.13
  423.3 4.3 %copy-start.18 = (f32[48,768]{1,0:T(8,128)S(1)}, f32[48,768]{1,0:T(8,128)}, u32[]{:S(2)}) copy-start(f32[48,768]{1,0:T(8,128)} %get-tuple-element.166) | copy-start | bytes 442372
  426.2 2.9 copy-start.11
  (8 other events, 10.3 us)

commit v11 on v9

--- a/solution.py
+++ b/solution.py
@@ -590,16 +590,13 @@
         tree.start()
         start_late()
         left = order[done:]
-        for turn in range(stages):
-            mine = [step for step in left if step[1] == turn + 1]
-            if turn > 0:
-                advance([step for step in mine if step[0] < 2])
+        for turn in range(stages + 1):
+            advance([step for step in left if step[1] == turn])
             if turn < tree.count:
                 tree.take(turn)
             for flow in late:
-                if turn < len(flow.stages):
-                    flow.take(turn)
-            advance([step for step in mine if turn == 0 or step[0] >= 2])
+                if 0 <= turn - 1 < len(flow.stages):
+                    flow.take(turn - 1)
         dmod_ref[...] = every_ref[...]
         spread.finish()
         tree.finish()
@@ -762,7 +759,13 @@
         return 0
 
     lax.fori_loop(0, steps, step_three, 0)
-    e_ref[...] = bdot_nt(du_ref[...], wup_ref[...])
+
+    def back_up(index, _):
+        cols = pl.ds(pl.multiple_of(index * tile, tile), tile)
+        e_ref[:, cols] = bdot_nt(du_ref[...], wup_ref[cols, :])
+        return 0
+
+    lax.fori_loop(0, width // tile, back_up, 0)
 
     def step_four(step, _):
         place, part, flat = at_rows(step)

time: 412 us -> 407 us (0.988)
  Pallas kernels: 302 us -> 297 us
where the time goes in v11:
time: 407 us; the launch traced here: 406 us
  Pallas kernels  297 us (73%)
  matrix products  44.3 us (11%)
  waiting for transfers between devices  22.5 us (6%)
  local copies, waits for them, and re-layouts  20.8 us (5%)
  starting transfers between devices  16.1 us (4%)
  other arithmetic  5.07 us (1%)
    pallas_call x1, Pallas kernels, call_space_backward(): pl.pallas_call(partial(space_backward, n_clip, kinds, early), grid=(own,)...  138 us
    pallas_call x1, Pallas kernels, call_middle(): pl.pallas_call(middle, grid=(places // count,), in_specs=[chunk, chunk, c...  107 us
    pallas_call x1, Pallas kernels, call_space_forward(): pl.pallas_call(space_forward, grid=(own,), in_specs=[spread, by_frame(2,...  51.6 us
    dot_general x5, matrix products, weight_grad(): jnp.einsum('rd,rk->dk', left, right, preferred_element_type=f32)  24.2 us
    all_to_all x2, waiting for transfers between devices, exchange(): got = lax.all_to_all(sent, 'pos', split_axis=0, concat_axis=0, tiled=True)  22.5 us
    dot_general x5, matrix products, dot_exact(): jnp.dot(jnp.concatenate(parts, axis=0), right, preferred_element_type=f32)  13.4 us
    all_to_all x2, starting transfers between devices, exchange(): got = lax.all_to_all(sent, 'pos', split_axis=0, concat_axis=0, tiled=True)  13 us
    unnamed x65, local copies, waits for them, and re-layouts  8.76 us
  transfers between devices with their start and end apart: 3, of which 2 were waited for; matrix products, arithmetic and copies ran while one was open for 10% of the time, Pallas kernels for 0%

profile of v11, /device:TPU:0, one launch (start us, length us, event | category | flops | bytes accessed | tf_op | source)
XLA Modules:
  0.0 406.3 jit_solution(15733135423467635124)
XLA Ops:
  0.7 3.1 collective-permute-start
  3.7 6.0 %all-to-all-start = ((bf16[64,16,768]{2,1,0:T(8,128)(2,1)}), bf16[64,16,768]{2,1,0:T(8,128)(2,1)}, u32[]{:S(2)}, u32[]{:S(2)}) async-start(bf16[64,16,768]{2,1,0:T(8,128)(2,1)} %param.13), calls=%async_computation | async-start | bytes 3145728 | tf_op jit(solution)/shard_map/all_to_all | solution.py:1042
  9.8 1.6 copy.63
  13.4 5.5 %fusion.37 = f32[12,6912]{1,0:T(8,128)S(1)} fusion(bf16[768,6912]{1,0:T(8,128)(2,1)} %param.18, bf16[4,768]{1,0:T(4,128)(2,1)S(1)} %get-tuple-element.109, bf16[4,768]{1,0:T(4,128)(2,1)S(1)} %get-tuple-element.110, bf16[4,768]{1,0:T(4,128)(2,1)S(1)} %get-tuple-element.111), kind=kOutput, calls=%fused_computation.54 | convolution fusion | flops 127457280 | bytes 10967040 | tf_op jit(solution)/shard_map/dot_general | solution.py:120
  19.0 0.9 fusion.9
  20.5 1.5 copy.62
  22.0 19.6 %all-to-all-done = bf16[64,16,768]{2,1,0:T(8,128)(2,1)} async-done(((bf16[64,16,768]{2,1,0:T(8,128)(2,1)}), bf16[64,16,768]{2,1,0:T(8,128)(2,1)}, u32[]{:S(2)}, u32[]{:S(2)}) %all-to-all-start) | async-done | bytes 1572896 | tf_op jit(solution)/shard_map/all_to_all | solution.py:1042
  41.6 51.6 %space_forward.1 = (bf16[4,256,768]{2,1,0:T(8,128)(2,1)}, bf16[4,256,2304]{2,1,0:T(8,128)(2,1)}, bf16[64,16,768]{2,1,0:T(8,128)(2,1)}, f32[4,6,256,128]{3,2,1,0:T(8,128)}) custom-call(bf16[16,4,16,768]{3,2,1,0:T(8,128)(2,1)} %bitcast.x_ref.refs_3_, f32[4,2,768]{2,1,0:T(2,128)} %reshape.108.mod_ref.refs_5_, bf16[768,2304]{1,0:T(8,128)(2,1)} %refs_6_.1), custom_call_target="tpu_custom_call" | custom-call | flops 4429185024 | bytes 12976128 | tf_op jit(solution)/shard_map/space_forward/pallas_call | solution.py:843
  93.2 4.7 %fusion.86 = (bf16[64,16,768]{2,0,1:T(8,128)(2,1)}, bf16[16,64,768]{2,1,0:T(8,128)(2,1)}, bf16[16,64,768]{2,1,0:T(8,128)(2,1)}) fusion(bf16[64,16,768]{2,1,0:T(8,128)(2,1)} %get-tuple-element.37, bf16[64,16,768]{2,1,0:T(8,128)(2,1)} %param.25), kind=kLoop, calls=%fused_computation.121 | loop fusion | bytes 7864320 | tf_op jit(solution)/shard_map/space_forward/pallas_call | solution.py:843
  97.9 106.8 %middle.1 = (bf16[16,64,768]{2,1,0:T(8,128)(2,1)}, bf16[1024,3072]{1,0:T(8,128)(2,1)}, bf16[1024,768]{1,0:T(8,128)(2,1)}, bf16[1024,768]{1,0:T(8,128)(2,1)}, bf1...) custom-call(bf16[16,64,768]{2,1,0:T(8,128)(2,1)} %get-tuple-element., ...), custom_call_target="tpu_custom_call" | custom-call | flops 31406948352 | bytes 40960000 | tf_op jit(solution)/shard_map/middle/pallas_call | solution.py:960
  204.7 3.4 copy.51
  208.1 7.0 %all-to-all-start.1 = ((bf16[64,16,768]{2,1,0:T(8,128)(2,1)}), bf16[64,16,768]{2,1,0:T(8,128)(2,1)}, u32[]{:S(2)}, u32[]{:S(2)}) async-start(bf16[64,16,768]{2,1,0:T(8,128)(2,1)} %copy.51), calls=%async_computation.1 | async-start | bytes 3145728 | tf_op jit(solution)/shard_map/all_to_all | solution.py:1042
  215.3 1.3 copy-done.3
  216.6 2.0 copy.53
  218.6 2.5 convolution_convert_fusion.3
  221.1 2.5 convolution_convert_fusion.4
  223.6 6.9 %convolution_convert_fusion.1 = bf16[768,3072]{1,0:T(8,128)(2,1)} fusion(bf16[1024,768]{1,0:T(8,128)(2,1)S(1)} %copy-done.20, bf16[1024,3072]{1,0:T(8,128)(2,1)S(1)} %bitcast.71), kind=kOutput, calls=%fused_computation.1 | convolution fusion | flops 4834197504 | bytes 12582912 | tf_op jit(solution)/shard_map/rd,rk->dk/dot_general | solution.py:51
  230.5 1.2 fusion.25.refs_8_
  231.8 5.3 %convolution_convert_fusion.2 = bf16[768,2304]{1,0:T(8,128)(2,1)} fusion(bf16[1024,768]{1,0:T(8,128)(2,1)S(1)} %copy-done.21, bf16[1024,2304]{1,0:T(8,128)(2,1)S(1)} %bitcast.73), kind=kOutput, calls=%fused_computation.2 | convolution fusion | flops 3625648128 | bytes 9830400 | tf_op jit(solution)/shard_map/rd,rk->dk/dot_general | solution.py:51
  237.2 7.0 %convolution_convert_fusion = bf16[3072,768]{1,0:T(8,128)(2,1)} fusion(bf16[1024,3072]{1,0:T(8,128)(2,1)S(1)} %bitcast.75, bf16[1024,768]{1,0:T(8,128)(2,1)S(1)} %copy-done.22), kind=kOutput, calls=%fused_computation | convolution fusion | flops 4834197504 | bytes 12582912 | tf_op jit(solution)/shard_map/rd,rk->dk/dot_general | solution.py:51
  244.1 2.9 all-to-all-done.1
  247.7 138.2 %space_backward.1 = (bf16[64,16,768]{2,1,0:T(8,128)(2,1)}, f32[2,4,6912]{2,1,0:T(4,128)}, f32[48,3072]{1,0:T(8,128)}, f32[192,768]{1,0:T(8,128)}, f32[48,2304]{1...) custom-call(bf16[16,4,16,768]{3,2,1,0:T(8,128)(2,1)} %bitcast.11.refs_0_, ...), custom_call_target="tpu_custom_call" | custom-call | flops 9261023232 | bytes 46792704 | tf_op jit(solution)/shard_map/space_backward/pallas_call | solution.py:893
  385.9 1.0 reshape.118
  387.0 7.0 %fusion.1 = f32[24,768]{1,0:T(8,128)S(1)} fusion(bf16[768,6912]{1,0:T(8,128)(2,1)} %param.18, bf16[8,6912]{1,0:T(8,128)(2,1)S(1)} %get-tuple-element.117, bf16[8,6912]{1,0:T(8,128)(2,1)S(1)} %get-tuple-element.118, bf16[8,6912]{1,0:T(8,128)(2,1)S(1)} %get-tuple-element.116), kind=kOutput, calls=%fused_computation.11 | convolution fusion | flops 255799296 | bytes 11022336 | tf_op jit(solution)/shard_map/dot_general | solution.py:120
  394.1 1.1 fusion.68
  395.1 2.4 fusion.66
  397.5 0.8 pad_maximum_fusion
  398.7 1.0 fusion.29
  399.7 2.9 fusion
  403.3 0.8 copy.70
  404.7 0.8 copy.72
  405.5 0.8 copy.73
  (88 shorter events, 5.4 us)
Async XLA Ops:
  0.6 12.5 %copy-start = (bf16[768,768]{1,0:T(8,128)(2,1)S(1)}, bf16[768,768]{1,0:T(8,128)(2,1)}, u32[]{:S(2)}) copy-start(bf16[768,768]{1,0:T(8,128)(2,1)} %param.17) | copy-start | bytes 3538948
  0.7 9.1 %copy-start.1 = (bf16[64,16,768]{2,1,0:T(8,128)(2,1)S(1)}, bf16[64,16,768]{2,1,0:T(8,128)(2,1)}, u32[]{:S(2)}) copy-start(bf16[64,16,768]{2,1,0:T(8,128)(2,1)} %param.13) | copy-start | bytes 4718596
  0.7 12.0 %collective-permute-start = (s32[4]{0:T(128)}, s32[4]{0:T(128)S(1)}, u32[]{:S(2)}, u32[]{:S(2)}) collective-permute-start(s32[4]{0:T(128)} %bitcast.62), channel_id=1, source_target_pairs={{0,16},{16,0},{1,17},{17,1},{2,18},{18,2},{3,19},{19,3},{4,20},{20... | collective-permute-start | bytes 56 | tf_op jit(solution)/shard_map/ppermute | solution.py:100
  3.7 37.9 %all-to-all-start = ((bf16[64,16,768]{2,1,0:T(8,128)(2,1)}), bf16[64,16,768]{2,1,0:T(8,128)(2,1)}, u32[]{:S(2)}, u32[]{:S(2)}) async-start(bf16[64,16,768]{2,1,0:T(8,128)(2,1)} %param.13), calls=%async_computation | async-start | bytes 3145728 | tf_op jit(solution)/shard_map/all_to_all | solution.py:1042
  9.7 1.7 copy-start.15
  9.7 2.9 copy-start.16
  9.7 3.1 copy-start.10
  208.1 7.1 %copy-start.6 = (f32[7,64,768]{2,1,0:T(8,128)S(1)}, f32[7,64,768]{2,1,0:T(8,128)}, u32[]{:S(2)}) copy-start(f32[7,64,768]{2,1,0:T(8,128)} %get-tuple-element.44) | copy-start | bytes 4128772
  208.1 39.0 %all-to-all-start.1 = ((bf16[64,16,768]{2,1,0:T(8,128)(2,1)}), bf16[64,16,768]{2,1,0:T(8,128)(2,1)}, u32[]{:S(2)}, u32[]{:S(2)}) async-start(bf16[64,16,768]{2,1,0:T(8,128)(2,1)} %copy.51), calls=%async_computation.1 | async-start | bytes 3145728 | tf_op jit(solution)/shard_map/all_to_all | solution.py:1042
  215.2 1.4 copy-start.3
  216.6 2.0 copy-start.18
  216.6 2.0 copy-start.19
  218.6 2.5 copy-start.5
  218.6 2.5 copy-start.17
  218.6 5.0 %slice-start = ((s8[6291456]{0:T(1024)(128)(4,1)}), s8[4194304]{0:T(1024)(128)(4,1)S(1)}, s32[]{:S(2)}) async-start(s8[6291456]{0:T(1024)(128)(4,1)} %bitcast.70), calls=%async_computation.2 | async-start | bytes 8388608
  218.6 5.0 %copy-start.20 = (bf16[1024,768]{1,0:T(8,128)(2,1)S(1)}, bf16[1024,768]{1,0:T(8,128)(2,1)}, u32[]{:S(2)}) copy-start(bf16[1024,768]{1,0:T(8,128)(2,1)} %get-tuple-element.45) | copy-start | bytes 4718596
  221.1 2.5 slice-start.1
  221.1 10.7 %slice-start.2 = ((s8[4718592]{0:T(1024)(128)(4,1)}), s8[4194304]{0:T(1024)(128)(4,1)S(1)}, s32[]{:S(2)}) async-start(s8[4718592]{0:T(1024)(128)(4,1)} %bitcast.72), calls=%async_computation.4 | async-start | bytes 8388608
  223.6 8.2 %slice-start.3 = ((s8[4718592]{0:T(1024)(128)(4,1)}), s8[524288]{0:T(1024)(128)(4,1)S(1)}, s32[]{:S(2)}) async-start(s8[4718592]{0:T(1024)(128)(4,1)} %bitcast.72), calls=%async_computation.5 | async-start | bytes 1048576
  223.6 8.2 %copy-start.21 = (bf16[1024,768]{1,0:T(8,128)(2,1)S(1)}, bf16[1024,768]{1,0:T(8,128)(2,1)}, u32[]{:S(2)}) copy-start(bf16[1024,768]{1,0:T(8,128)(2,1)} %get-tuple-element.49) | copy-start | bytes 4718596
  230.5 6.6 %slice-start.4 = ((s8[6291456]{0:T(1024)(128)(4,1)}), s8[2097152]{0:T(1024)(128)(4,1)S(1)}, s32[]{:S(2)}) async-start(s8[6291456]{0:T(1024)(128)(4,1)} %bitcast.74), calls=%async_computation.6 | async-start | bytes 4194304
  231.8 5.4 %slice-start.5 = ((s8[6291456]{0:T(1024)(128)(4,1)}), s8[4194304]{0:T(1024)(128)(4,1)S(1)}, s32[]{:S(2)}) async-start(s8[6291456]{0:T(1024)(128)(4,1)} %bitcast.74), calls=%async_computation.7 | async-start | bytes 8388608
  231.8 5.4 %copy-start.22 = (bf16[1024,768]{1,0:T(8,128)(2,1)S(1)}, bf16[1024,768]{1,0:T(8,128)(2,1)}, u32[]{:S(2)}) copy-start(bf16[1024,768]{1,0:T(8,128)(2,1)} %get-tuple-element.48) | copy-start | bytes 4718596
  387.0 12.7 %copy-start.4 = (bf16[64,16,768]{2,1,0:T(8,128)(2,1)S(1)}, bf16[64,16,768]{2,1,0:T(8,128)(2,1)}, u32[]{:S(2)}) copy-start(bf16[64,16,768]{2,1,0:T(8,128)(2,1)} %get-tuple-element.54) | copy-start | bytes 4718596
  394.0 3.5 copy-start.11
  394.0 3.5 copy-start.12
  395.1 4.6 %copy-start.2 = (f32[16,64,768]{2,1,0:T(8,128)S(1)}, f32[16,64,768]{2,1,0:T(8,128)}, u32[]{:S(2)}) copy-start(f32[16,64,768]{2,1,0:T(8,128)} %get-tuple-element.39) | copy-start | bytes 9437188
  399.7 2.9 copy-start.14
  399.7 3.6 copy-start.9
  399.7 4.3 %copy-start.13 = (f32[48,768]{1,0:T(8,128)S(1)}, f32[48,768]{1,0:T(8,128)}, u32[]{:S(2)}) copy-start(f32[48,768]{1,0:T(8,128)} %get-tuple-element.147) | copy-start | bytes 442372
  402.6 2.1 copy-start.8
  402.6 2.9 copy-start.7

commit v12 on v11

--- a/solution.py
+++ b/solution.py
@@ -468,7 +468,7 @@
     stages = max(len(flow.stages) for flow in flows)
     order = [(i, stage) for stage in range(stages) for i in range(early)]
     order = [(i, stage) for i, stage in order if stage < len(flows[i].stages)]
-    cuts = [2, early, early + 2]
+    cuts = [2, early, early]
 
     @pl.when(frame == 0)
     def _():

time: 407 us -> 407 us (level)
  no operation moved by 1% of the time
where the time goes in v12:
time: 407 us
  Pallas kernels  297 us (73%)
  matrix products  44.3 us (11%)
  waiting for transfers between devices  22.5 us (6%)
  local copies, waits for them, and re-layouts  20.8 us (5%)
  starting transfers between devices  16.1 us (4%)
  other arithmetic  5.07 us (1%)
    pallas_call x1, Pallas kernels, call_space_backward(): pl.pallas_call(partial(space_backward, n_clip, kinds, early), grid=(own,)...  138 us
    pallas_call x1, Pallas kernels, call_middle(): pl.pallas_call(middle, grid=(places // count,), in_specs=[chunk, chunk, c...  107 us
    pallas_call x1, Pallas kernels, call_space_forward(): pl.pallas_call(space_forward, grid=(own,), in_specs=[spread, by_frame(2,...  51.6 us
    dot_general x5, matrix products, weight_grad(): jnp.einsum('rd,rk->dk', left, right, preferred_element_type=f32)  24.2 us
    all_to_all x2, waiting for transfers between devices, exchange(): got = lax.all_to_all(sent, 'pos', split_axis=0, concat_axis=0, tiled=True)  22.5 us
    dot_general x5, matrix products, dot_exact(): jnp.dot(jnp.concatenate(parts, axis=0), right, preferred_element_type=f32)  13.4 us
    all_to_all x2, starting transfers between devices, exchange(): got = lax.all_to_all(sent, 'pos', split_axis=0, concat_axis=0, tiled=True)  13 us
    unnamed x65, local copies, waits for them, and re-layouts  8.76 us
  transfers between devices with their start and end apart: 3, of which 2 were waited for; matrix products, arithmetic and copies ran while one was open for 10% of the time, Pallas kernels for 0%

profile of v12, /device:TPU:0, one launch (start us, length us, event | category | flops | bytes accessed | tf_op | source)
XLA Modules:
  0.0 406.6 jit_solution(13191538137041279939)
XLA Ops:
  0.7 3.1 collective-permute-start
  3.7 6.0 %all-to-all-start = ((bf16[64,16,768]{2,1,0:T(8,128)(2,1)}), bf16[64,16,768]{2,1,0:T(8,128)(2,1)}, u32[]{:S(2)}, u32[]{:S(2)}) async-start(bf16[64,16,768]{2,1,0:T(8,128)(2,1)} %param.13), calls=%async_computation | async-start | bytes 3145728 | tf_op jit(solution)/shard_map/all_to_all | solution.py:1042
  9.8 1.6 copy.63
  13.4 5.5 %fusion.37 = f32[12,6912]{1,0:T(8,128)S(1)} fusion(bf16[768,6912]{1,0:T(8,128)(2,1)} %param.18, bf16[4,768]{1,0:T(4,128)(2,1)S(1)} %get-tuple-element.109, bf16[4,768]{1,0:T(4,128)(2,1)S(1)} %get-tuple-element.110, bf16[4,768]{1,0:T(4,128)(2,1)S(1)} %get-tuple-element.111), kind=kOutput, calls=%fused_computation.54 | convolution fusion | flops 127457280 | bytes 10967040 | tf_op jit(solution)/shard_map/dot_general | solution.py:120
  19.0 0.9 fusion.9
  20.5 1.5 copy.62
  22.0 19.6 %all-to-all-done = bf16[64,16,768]{2,1,0:T(8,128)(2,1)} async-done(((bf16[64,16,768]{2,1,0:T(8,128)(2,1)}), bf16[64,16,768]{2,1,0:T(8,128)(2,1)}, u32[]{:S(2)}, u32[]{:S(2)}) %all-to-all-start) | async-done | bytes 1572896 | tf_op jit(solution)/shard_map/all_to_all | solution.py:1042
  41.6 51.6 %space_forward.1 = (bf16[4,256,768]{2,1,0:T(8,128)(2,1)}, bf16[4,256,2304]{2,1,0:T(8,128)(2,1)}, bf16[64,16,768]{2,1,0:T(8,128)(2,1)}, f32[4,6,256,128]{3,2,1,0:T(8,128)}) custom-call(bf16[16,4,16,768]{3,2,1,0:T(8,128)(2,1)} %bitcast.x_ref.refs_3_, f32[4,2,768]{2,1,0:T(2,128)} %reshape.108.mod_ref.refs_5_, bf16[768,2304]{1,0:T(8,128)(2,1)} %refs_6_.1), custom_call_target="tpu_custom_call" | custom-call | flops 4429185024 | bytes 12976128 | tf_op jit(solution)/shard_map/space_forward/pallas_call | solution.py:843
  93.2 4.7 %fusion.86 = (bf16[64,16,768]{2,0,1:T(8,128)(2,1)}, bf16[16,64,768]{2,1,0:T(8,128)(2,1)}, bf16[16,64,768]{2,1,0:T(8,128)(2,1)}) fusion(bf16[64,16,768]{2,1,0:T(8,128)(2,1)} %get-tuple-element.37, bf16[64,16,768]{2,1,0:T(8,128)(2,1)} %param.25), kind=kLoop, calls=%fused_computation.121 | loop fusion | bytes 7864320 | tf_op jit(solution)/shard_map/space_forward/pallas_call | solution.py:843
  97.9 106.8 %middle.1 = (bf16[16,64,768]{2,1,0:T(8,128)(2,1)}, bf16[1024,3072]{1,0:T(8,128)(2,1)}, bf16[1024,768]{1,0:T(8,128)(2,1)}, bf16[1024,768]{1,0:T(8,128)(2,1)}, bf1...) custom-call(bf16[16,64,768]{2,1,0:T(8,128)(2,1)} %get-tuple-element., ...), custom_call_target="tpu_custom_call" | custom-call | flops 31406948352 | bytes 40960000 | tf_op jit(solution)/shard_map/middle/pallas_call | solution.py:960
  204.7 3.4 copy.51
  208.1 7.0 %all-to-all-start.1 = ((bf16[64,16,768]{2,1,0:T(8,128)(2,1)}), bf16[64,16,768]{2,1,0:T(8,128)(2,1)}, u32[]{:S(2)}, u32[]{:S(2)}) async-start(bf16[64,16,768]{2,1,0:T(8,128)(2,1)} %copy.51), calls=%async_computation.1 | async-start | bytes 3145728 | tf_op jit(solution)/shard_map/all_to_all | solution.py:1042
  215.3 1.3 copy-done.3
  216.6 2.0 copy.53
  218.6 2.5 convolution_convert_fusion.3
  221.1 2.5 convolution_convert_fusion.4
  223.6 6.9 %convolution_convert_fusion.1 = bf16[768,3072]{1,0:T(8,128)(2,1)} fusion(bf16[1024,768]{1,0:T(8,128)(2,1)S(1)} %copy-done.20, bf16[1024,3072]{1,0:T(8,128)(2,1)S(1)} %bitcast.71), kind=kOutput, calls=%fused_computation.1 | convolution fusion | flops 4834197504 | bytes 12582912 | tf_op jit(solution)/shard_map/rd,rk->dk/dot_general | solution.py:51
  230.5 1.2 fusion.25.refs_8_
  231.8 5.3 %convolution_convert_fusion.2 = bf16[768,2304]{1,0:T(8,128)(2,1)} fusion(bf16[1024,768]{1,0:T(8,128)(2,1)S(1)} %copy-done.21, bf16[1024,2304]{1,0:T(8,128)(2,1)S(1)} %bitcast.73), kind=kOutput, calls=%fused_computation.2 | convolution fusion | flops 3625648128 | bytes 9830400 | tf_op jit(solution)/shard_map/rd,rk->dk/dot_general | solution.py:51
  237.2 7.0 %convolution_convert_fusion = bf16[3072,768]{1,0:T(8,128)(2,1)} fusion(bf16[1024,3072]{1,0:T(8,128)(2,1)S(1)} %bitcast.75, bf16[1024,768]{1,0:T(8,128)(2,1)S(1)} %copy-done.22), kind=kOutput, calls=%fused_computation | convolution fusion | flops 4834197504 | bytes 12582912 | tf_op jit(solution)/shard_map/rd,rk->dk/dot_general | solution.py:51
  244.1 2.9 all-to-all-done.1
  247.7 138.4 %space_backward.1 = (bf16[64,16,768]{2,1,0:T(8,128)(2,1)}, f32[2,4,6912]{2,1,0:T(4,128)}, f32[48,3072]{1,0:T(8,128)}, f32[192,768]{1,0:T(8,128)}, f32[48,2304]{1...) custom-call(bf16[16,4,16,768]{3,2,1,0:T(8,128)(2,1)} %bitcast.11.refs_0_, ...), custom_call_target="tpu_custom_call" | custom-call | flops 9261023232 | bytes 46792704 | tf_op jit(solution)/shard_map/space_backward/pallas_call | solution.py:893
  386.2 1.0 reshape.118
  387.2 7.0 %fusion.1 = f32[24,768]{1,0:T(8,128)S(1)} fusion(bf16[768,6912]{1,0:T(8,128)(2,1)} %param.18, bf16[8,6912]{1,0:T(8,128)(2,1)S(1)} %get-tuple-element.117, bf16[8,6912]{1,0:T(8,128)(2,1)S(1)} %get-tuple-element.118, bf16[8,6912]{1,0:T(8,128)(2,1)S(1)} %get-tuple-element.116), kind=kOutput, calls=%fused_computation.11 | convolution fusion | flops 255799296 | bytes 11022336 | tf_op jit(solution)/shard_map/dot_general | solution.py:120
  394.3 1.1 fusion.68
  395.4 2.4 fusion.66
  397.8 0.8 pad_maximum_fusion
  399.0 1.0 fusion.29
  400.0 2.9 fusion
  403.5 0.8 copy.70
  404.9 0.8 copy.72
  405.8 0.8 copy.73
  (88 shorter events, 5.4 us)
Async XLA Ops:
  0.6 12.5 %copy-start = (bf16[768,768]{1,0:T(8,128)(2,1)S(1)}, bf16[768,768]{1,0:T(8,128)(2,1)}, u32[]{:S(2)}) copy-start(bf16[768,768]{1,0:T(8,128)(2,1)} %param.17) | copy-start | bytes 3538948
  0.7 9.1 %copy-start.1 = (bf16[64,16,768]{2,1,0:T(8,128)(2,1)S(1)}, bf16[64,16,768]{2,1,0:T(8,128)(2,1)}, u32[]{:S(2)}) copy-start(bf16[64,16,768]{2,1,0:T(8,128)(2,1)} %param.13) | copy-start | bytes 4718596
  0.7 12.0 %collective-permute-start = (s32[4]{0:T(128)}, s32[4]{0:T(128)S(1)}, u32[]{:S(2)}, u32[]{:S(2)}) collective-permute-start(s32[4]{0:T(128)} %bitcast.62), channel_id=1, source_target_pairs={{0,16},{16,0},{1,17},{17,1},{2,18},{18,2},{3,19},{19,3},{4,20},{20... | collective-permute-start | bytes 56 | tf_op jit(solution)/shard_map/ppermute | solution.py:100
  3.7 37.9 %all-to-all-start = ((bf16[64,16,768]{2,1,0:T(8,128)(2,1)}), bf16[64,16,768]{2,1,0:T(8,128)(2,1)}, u32[]{:S(2)}, u32[]{:S(2)}) async-start(bf16[64,16,768]{2,1,0:T(8,128)(2,1)} %param.13), calls=%async_computation | async-start | bytes 3145728 | tf_op jit(solution)/shard_map/all_to_all | solution.py:1042
  9.7 1.7 copy-start.15
  9.7 2.9 copy-start.16
  9.7 3.1 copy-start.10
  208.1 7.1 %copy-start.6 = (f32[7,64,768]{2,1,0:T(8,128)S(1)}, f32[7,64,768]{2,1,0:T(8,128)}, u32[]{:S(2)}) copy-start(f32[7,64,768]{2,1,0:T(8,128)} %get-tuple-element.44) | copy-start | bytes 4128772
  208.1 39.0 %all-to-all-start.1 = ((bf16[64,16,768]{2,1,0:T(8,128)(2,1)}), bf16[64,16,768]{2,1,0:T(8,128)(2,1)}, u32[]{:S(2)}, u32[]{:S(2)}) async-start(bf16[64,16,768]{2,1,0:T(8,128)(2,1)} %copy.51), calls=%async_computation.1 | async-start | bytes 3145728 | tf_op jit(solution)/shard_map/all_to_all | solution.py:1042
  215.2 1.4 copy-start.3
  216.6 2.0 copy-start.18
  216.6 2.0 copy-start.19
  218.6 2.5 copy-start.5
  218.6 2.5 copy-start.17
  218.6 5.0 %slice-start = ((s8[6291456]{0:T(1024)(128)(4,1)}), s8[4194304]{0:T(1024)(128)(4,1)S(1)}, s32[]{:S(2)}) async-start(s8[6291456]{0:T(1024)(128)(4,1)} %bitcast.70), calls=%async_computation.2 | async-start | bytes 8388608
  218.6 5.0 %copy-start.20 = (bf16[1024,768]{1,0:T(8,128)(2,1)S(1)}, bf16[1024,768]{1,0:T(8,128)(2,1)}, u32[]{:S(2)}) copy-start(bf16[1024,768]{1,0:T(8,128)(2,1)} %get-tuple-element.45) | copy-start | bytes 4718596
  221.1 2.5 slice-start.1
  221.1 10.7 %slice-start.2 = ((s8[4718592]{0:T(1024)(128)(4,1)}), s8[4194304]{0:T(1024)(128)(4,1)S(1)}, s32[]{:S(2)}) async-start(s8[4718592]{0:T(1024)(128)(4,1)} %bitcast.72), calls=%async_computation.4 | async-start | bytes 8388608
  223.6 8.2 %slice-start.3 = ((s8[4718592]{0:T(1024)(128)(4,1)}), s8[524288]{0:T(1024)(128)(4,1)S(1)}, s32[]{:S(2)}) async-start(s8[4718592]{0:T(1024)(128)(4,1)} %bitcast.72), calls=%async_computation.5 | async-start | bytes 1048576
  223.6 8.2 %copy-start.21 = (bf16[1024,768]{1,0:T(8,128)(2,1)S(1)}, bf16[1024,768]{1,0:T(8,128)(2,1)}, u32[]{:S(2)}) copy-start(bf16[1024,768]{1,0:T(8,128)(2,1)} %get-tuple-element.49) | copy-start | bytes 4718596
  230.5 6.6 %slice-start.4 = ((s8[6291456]{0:T(1024)(128)(4,1)}), s8[2097152]{0:T(1024)(128)(4,1)S(1)}, s32[]{:S(2)}) async-start(s8[6291456]{0:T(1024)(128)(4,1)} %bitcast.74), calls=%async_computation.6 | async-start | bytes 4194304
  231.8 5.4 %slice-start.5 = ((s8[6291456]{0:T(1024)(128)(4,1)}), s8[4194304]{0:T(1024)(128)(4,1)S(1)}, s32[]{:S(2)}) async-start(s8[6291456]{0:T(1024)(128)(4,1)} %bitcast.74), calls=%async_computation.7 | async-start | bytes 8388608
  231.8 5.4 %copy-start.22 = (bf16[1024,768]{1,0:T(8,128)(2,1)S(1)}, bf16[1024,768]{1,0:T(8,128)(2,1)}, u32[]{:S(2)}) copy-start(bf16[1024,768]{1,0:T(8,128)(2,1)} %get-tuple-element.48) | copy-start | bytes 4718596
  387.2 12.7 %copy-start.4 = (bf16[64,16,768]{2,1,0:T(8,128)(2,1)S(1)}, bf16[64,16,768]{2,1,0:T(8,128)(2,1)}, u32[]{:S(2)}) copy-start(bf16[64,16,768]{2,1,0:T(8,128)(2,1)} %get-tuple-element.54) | copy-start | bytes 4718596
  394.3 3.5 copy-start.11
  394.3 3.5 copy-start.12
  395.4 4.6 %copy-start.2 = (f32[16,64,768]{2,1,0:T(8,128)S(1)}, f32[16,64,768]{2,1,0:T(8,128)}, u32[]{:S(2)}) copy-start(f32[16,64,768]{2,1,0:T(8,128)} %get-tuple-element.39) | copy-start | bytes 9437188
  399.9 2.9 copy-start.14
  400.0 3.6 copy-start.9
  400.0 4.3 %copy-start.13 = (f32[48,768]{1,0:T(8,128)S(1)}, f32[48,768]{1,0:T(8,128)}, u32[]{:S(2)}) copy-start(f32[48,768]{1,0:T(8,128)} %get-tuple-element.147) | copy-start | bytes 442372
  402.8 2.1 copy-start.8
  402.9 2.9 copy-start.7
